TPU v7x, 32 devices: a whole 2x2x4 slice. The times are simulated.
32 devices in a mesh: seq: 8 (over z, x), dp: 4 (over y, core).
Axes of the slice: x: 2, y: 2, z: 4, core: 2. Of those that a mesh axis runs over, the one named last changes fastest.
Arguments:
- queries: bfloat16 [8192, 4096], P(('dp', 'seq')), parts along dimension 0, may hold values from -6 to 6
- keys: bfloat16 [8192, 4096], P(('dp', 'seq')), parts along dimension 0, may hold values from -6 to 6
- values: bfloat16 [8192, 4096], P(('dp', 'seq')), parts along dimension 0, may hold values from -6 to 6
- gain: float32 [4096], replicated, may hold values from 0.1 to 1.9
- cotangent: bfloat16 [8192, 4096], P(('dp', 'seq')), parts along dimension 0, may hold values from -6 to 6
Outputs:
- key_grad: bfloat16 [8192, 4096], P(('dp', 'seq')), parts along dimension 0
- value_grad: bfloat16 [8192, 4096], P(('dp', 'seq')), parts along dimension 0
There are 4 independent parts, one for each index of `dp`. A program takes and returns all parts, laid end to end along the dimension named above; an argument that names none is the same for every part. Nothing has to cross between parts.
All inputs are finite; a program needn't handle non-finite values.
Results may differ from a plain program's by a relative error of at most 0.0059.
Values may be sent and summed in bfloat16 or wider, within the bound.
No kernel may reach another device: no remote copies, remote signals or barrier semaphores. Data moves between devices by JAX's collectives and lax.ppermute only.
A program may use at most 64 MiB of HBM per device.

v0:
```python
from functools import partial

import jax
import jax.numpy as jnp
from jax import lax
from jax.sharding import PartitionSpec as P

DH = 128


epsilon = 1e-05


def rms_norm(attended, gain):
    mean_square = jnp.mean(attended * attended, axis=-1, keepdims=True) + epsilon
    return attended * lax.rsqrt(mean_square) * gain


def spread_forward(states):
    stacked = states.reshape(1, states.shape[0] * states.shape[1], states.shape[2])
    running = jnp.cumsum(
        lax.all_to_all(stacked, "seq", split_axis=1, concat_axis=0, tiled=True), axis=0
    )
    before = jnp.concatenate([jnp.zeros_like(running[:1]), running[:-1]], axis=0)
    merged = lax.all_to_all(
        before.astype(jnp.bfloat16), "seq", split_axis=0, concat_axis=1, tiled=True
    )
    return merged.reshape(states.shape)


def spread_backward(states):
    stacked = states.reshape(1, states.shape[0] * states.shape[1], states.shape[2])
    running = jnp.cumsum(
        lax.all_to_all(stacked, "seq", split_axis=1, concat_axis=0, tiled=True)[::-1], axis=0
    )[::-1]
    after = jnp.concatenate([running[1:], jnp.zeros_like(running[:1])], axis=0)
    merged = lax.all_to_all(
        after.astype(jnp.bfloat16), "seq", split_axis=0, concat_axis=1, tiled=True
    )
    return merged.reshape(states.shape)


def shards(queries, keys, values, gain, cotangent):
    tok_rows = queries.shape[0]
    head_count = queries.shape[1] // DH
    head_shape = (tok_rows, head_count, DH)
    query_heads = queries.reshape(head_shape)
    key_heads = keys.reshape(head_shape)
    value_heads = values.reshape(head_shape)
    positions = jnp.arange(tok_rows)
    causal_mask = (positions[:, None] >= positions[None, :])[None]
    later_mask = (positions[:, None] <= positions[None, :])[None]
    states = jnp.einsum("thd,the->hde", key_heads, value_heads, preferred_element_type=jnp.float32)
    scores = jnp.einsum("thd,shd->hts", query_heads, key_heads, preferred_element_type=jnp.float32)
    weights = jnp.where(causal_mask, scores, 0.0).astype(jnp.bfloat16)
    local_term = jnp.einsum(
        "hts,she->the", weights, value_heads, preferred_element_type=jnp.float32
    )
    prefix_round = spread_forward(states)
    cross_term = jnp.einsum(
        "thd,hde->the", query_heads, prefix_round, preferred_element_type=jnp.float32
    )
    attended = (cross_term + local_term).reshape(tok_rows, head_count * DH)
    _, pullback = jax.vjp(partial(rms_norm, gain=gain), attended)
    (grad_out,) = pullback(cotangent.astype(jnp.float32))
    grad_heads = grad_out.astype(jnp.bfloat16).reshape(head_shape)
    grad_states = jnp.einsum(
        "thd,the->hde", query_heads, grad_heads, preferred_element_type=jnp.float32
    )
    key_scores = jnp.einsum(
        "shd,thd->hst", key_heads, query_heads, preferred_element_type=jnp.float32
    )
    key_weights = jnp.where(later_mask, key_scores, 0.0).astype(jnp.bfloat16)
    value_scores = jnp.einsum(
        "she,the->hst", value_heads, grad_heads, preferred_element_type=jnp.float32
    )
    value_weights = jnp.where(later_mask, value_scores, 0.0).astype(jnp.bfloat16)
    key_local = jnp.einsum(
        "hst,thd->shd", value_weights, query_heads, preferred_element_type=jnp.float32
    )
    value_local = jnp.einsum(
        "hst,the->she", key_weights, grad_heads, preferred_element_type=jnp.float32
    )
    suffix_round = spread_backward(grad_states)
    key_out = key_local + jnp.einsum(
        "she,hde->shd", value_heads, suffix_round, preferred_element_type=jnp.float32
    )
    value_out = value_local + jnp.einsum(
        "shd,hde->she", key_heads, suffix_round, preferred_element_type=jnp.float32
    )
    key_grad = key_out.reshape(tok_rows, head_count * DH).astype(jnp.bfloat16)
    value_grad = value_out.reshape(tok_rows, head_count * DH).astype(jnp.bfloat16)
    return (key_grad, value_grad)


def solution(mesh):
    return jax.shard_map(
        shards,
        mesh=mesh,
        in_specs=(
            P(("dp", "seq"), None),
            P(("dp", "seq"), None),
            P(("dp", "seq"), None),
            P(),
            P(("dp", "seq"), None),
        ),
        out_specs=(P(("dp", "seq"), None), P(("dp", "seq"), None)),
        check_vma=False,
    )
```

profile of v0, /device:TPU:0, one launch (start us, length us, event | category | flops | bytes accessed | tf_op | source)
XLA Modules:
  0.0 222.2 jit_solution(17062946296529970006)
XLA Ops:
  0.6 0.0 copy-start
  0.6 1.6 copy-done
  2.2 2.4 %fusion.24 = f32[32,128,128]{2,1,0:T(8,128)S(1)} fusion(bf16[256,4096]{1,0:T(8,128)(2,1)} %param.6, bf16[256,4096]{1,0:T(8,128)(2,1)S(1)} %copy-done), kind=kOutput, calls=%fused_computation.28 | convolution fusion | flops 268435456 | bytes 6291456 | tf_op jit(solution)/shard_map/thd,the->hde/dot_general | solution.py:53
  4.6 55.3 %all_to_all.42 = f32[1,4096,128]{2,0,1:T(1,128)S(1)} all-to-all(f32[1,4096,128]{2,0,1:T(1,128)S(1)} %bitcast.124), channel_id=1, replica_groups=mesh['seq'=8,'dp'=4] {'seq'}, dimensions={1} | all-to-all | bytes 4194304 | tf_op jit(solution)/shard_map/all_to_all | solution.py:22
  59.9 0.2 fusion.56
  60.1 0.1 slice.17
  60.1 1.1 concatenate.6
  61.2 3.6 %all-to-all-start.1 = ((bf16[8,512,128]{2,1,0:T(8,128)(2,1)}), bf16[8,512,128]{2,1,0:T(8,128)(2,1)S(1)}, u32[]{:S(2)}, u32[]{:S(2)}) async-start(bf16[8,512,128]{2,1,0:T(8,128)(2,1)} %concatenate.6), calls=%async_computation.1 | async-start | bytes 2097152 | tf_op jit(solution)/shard_map/all_to_all | solution.py:25
  64.8 3.4 %copy.70 = bf16[32,8,32,128]{3,2,1,0:T(8,128)(2,1)} copy(bf16[32,8,32,128]{3,1,2,0:T(8,128)(2,1)} %bitcast.129) | data formatting | bytes 4194304
  68.2 4.3 %copy.51 = bf16[256,32,128]{0,2,1:T(8,128)(2,1)} copy(bf16[256,32,128]{2,1,0:T(8,128)(2,1)} %bitcast.128) | data formatting | bytes 4194304 | tf_op jit(solution)/shard_map/reshape | solution.py:47
  72.5 6.7 %fusion.2 = f32[32,256,128]{1,2,0:T(8,128)} fusion(pred[256,256]{1,0:T(8,128)(4,1)S(1)} %iota_compare_fusion, bf16[256,4096]{1,0:T(8,128)(2,1)} %param.5, bf16[256,4096]{1,0:T(8,128)(2,1)} %param.6, bf16[256,4096]{1,0:T(8,128)(2,1)S(1)} %copy-done), kind=kOutput, calls=%fused_computation.6 | convolution fusion | flops 1077936128 | bytes 10551296 | tf_op jit(solution)/shard_map/hts,she->the/dot_general | solution.py:56
  79.2 11.2 %all-to-all-done.1 = bf16[8,512,128]{2,1,0:T(8,128)(2,1)S(1)} async-done(((bf16[8,512,128]{2,1,0:T(8,128)(2,1)}), bf16[8,512,128]{2,1,0:T(8,128)(2,1)S(1)}, u32[]{:S(2)}, u32[]{:S(2)}) %all-to-all-start.1) | async-done | bytes 1048608 | tf_op jit(solution)/shard_map/all_to_all | solution.py:25
  90.4 5.6 %multiply_reduce_fusion.1 = (f32[256]{0:T(256)S(1)}, f32[256,32,128]{0,2,1:T(8,128)}) fusion(f32[32,256,128]{1,2,0:T(8,128)} %fusion.2, bf16[32,128,128]{2,1,0:T(8,128)(2,1)S(1)} %bitcast.132, bf16[256,4096]{1,0:T(8,128)(2,1)} %param.5), kind=kOutput, calls=%fused_computation.14 | convolution fusion | flops 271580928 | bytes 11535360 | tf_op jit(solution)/shard_map/thd,hde->the/dot_general | solution.py:60
  96.0 0.0 copy-start.3
  96.0 5.7 %copy.47 = f32[256,4096]{1,0:T(8,128)} copy(f32[256,4096]{0,1:T(8,128)} %bitcast.118) | data formatting | bytes 8388608 | tf_op jit(solution)/shard_map/reshape | solution.py:63
  101.6 0.0 copy-done.3
  101.6 0.0 copy-start.1
  101.6 0.0 copy-start.2
  101.6 3.6 %multiply_reduce_fusion = f32[256]{0:T(256)S(1)} fusion(f32[256,4096]{1,0:T(8,128)} %copy.47, bf16[256,4096]{1,0:T(8,128)(2,1)} %param.9, f32[4096]{0:T(1024)S(1)} %copy-done.3), kind=kLoop, calls=%fused_computation.13 | loop fusion | flops 4194048 | bytes 6308864 | tf_op jit(solution)/shard_map/transpose(jvp())/reduce_sum | solution.py:16
  105.3 0.4 copy-done.1
  105.7 0.7 copy-done.2
  106.4 2.5 %fusion.1 = bf16[256,4096]{1,0:T(8,128)(2,1)} fusion(f32[256,4096]{1,0:T(8,128)S(1)} %copy-done.1, bf16[256,4096]{1,0:T(8,128)(2,1)S(1)} %copy-done.2, f32[256]{0:T(256)S(1)} %get-tuple-element.9, f32[256]{0:T(256)S(1)} %get-tuple-element.8, f32[4096]{0:T(1024)S(1)} %copy-done.3), kind=kLoop, calls=%fused_computation.5 | loop fusion | flops 7340032 | bytes 8407040 | tf_op jit(solution)/shard_map/convert_element_type | solution.py:66
  108.9 4.1 %copy.66 = bf16[256,4096]{0,1:T(8,128)(2,1)} copy(bf16[256,4096]{1,0:T(8,128)(2,1)} %fusion.1) | data formatting | bytes 4194304 | tf_op jit(solution)/shard_map/reshape | solution.py:66
  113.0 2.9 %fusion.58 = f32[32,128,128]{1,2,0:T(8,128)S(1)} fusion(bf16[256,32,128]{0,2,1:T(8,128)(2,1)} %copy.51, bf16[256,32,128]{0,2,1:T(8,128)(2,1)} %bitcast.121), kind=kOutput, calls=%fused_computation.60 | convolution fusion | flops 268435456 | bytes 6291456 | tf_op jit(solution)/shard_map/thd,the->hde/dot_general | solution.py:67
  115.9 51.7 %all_to_all.43 = f32[1,4096,128]{2,0,1:T(1,128)} all-to-all(f32[1,4096,128]{2,0,1:T(1,128)S(1)} %bitcast.125), channel_id=1, replica_groups=mesh['seq'=8,'dp'=4] {'seq'}, dimensions={1} | all-to-all | bytes 4194304 | tf_op jit(solution)/shard_map/all_to_all | solution.py:34
  167.6 3.1 %rev.4 = f32[8,512,128]{2,1,0:T(8,128)} reverse(f32[8,512,128]{2,1,0:T(8,128)} %bitcast.127), dimensions={0} | reverse | bytes 4194304 | tf_op jit(solution)/shard_map/rev | solution.py:34
  170.6 1.7 fusion.57
  172.4 1.0 slice.14
  173.4 1.2 slice.18
  174.6 1.1 concatenate.7
  175.7 3.7 %all-to-all-start.3 = ((bf16[8,512,128]{2,1,0:T(8,128)(2,1)}), bf16[8,512,128]{2,1,0:T(8,128)(2,1)S(1)}, u32[]{:S(2)}, u32[]{:S(2)}) async-start(bf16[8,512,128]{2,1,0:T(8,128)(2,1)} %concatenate.7), calls=%async_computation.3 | async-start | bytes 2097152 | tf_op jit(solution)/shard_map/all_to_all | solution.py:37
  179.5 6.7 %fusion.4 = f32[32,256,128]{1,2,0:T(8,128)} fusion(bf16[256,32,128]{0,2,1:T(8,128)(2,1)} %copy.51, pred[256,256]{1,0:T(8,128)(4,1)S(1)} %iota_compare_fusion.1, bf16[256,32,128]{0,2,1:T(8,128)(2,1)} %bitcast.122, bf16[256,4096]{1,0:T(8,128)(2,1)S(1)} %copy-done), kind=kOutput, calls=%fused_computation.8 | convolution fusion | flops 1077936128 | bytes 10551296 | tf_op jit(solution)/shard_map/hst,thd->shd/dot_general | solution.py:78
  186.2 7.4 %fusion.3 = f32[32,128,256]{2,1,0:T(8,128)} fusion(bf16[256,32,128]{0,2,1:T(8,128)(2,1)} %bitcast.123, pred[256,256]{1,0:T(8,128)(4,1)S(1)} %iota_compare_fusion.1, bf16[256,4096]{1,0:T(8,128)(2,1)} %param.5, bf16[256,4096]{1,0:T(8,128)(2,1)} %param.6), kind=kOutput, calls=%fused_computation.7 | convolution fusion | flops 1077936128 | bytes 10551296 | tf_op jit(solution)/shard_map/hst,the->she/dot_general | solution.py:81
  193.6 11.4 %all-to-all-done.3 = bf16[8,512,128]{2,1,0:T(8,128)(2,1)S(1)} async-done(((bf16[8,512,128]{2,1,0:T(8,128)(2,1)}), bf16[8,512,128]{2,1,0:T(8,128)(2,1)S(1)}, u32[]{:S(2)}, u32[]{:S(2)}) %all-to-all-start.3) | async-done | bytes 1048608 | tf_op jit(solution)/shard_map/all_to_all | solution.py:37
  204.9 4.2 %fusion.6 = bf16[256,32,128]{0,2,1:T(8,128)(2,1)} fusion(f32[32,256,128]{1,2,0:T(8,128)} %fusion.4, bf16[32,128,128]{2,1,0:T(8,128)(2,1)S(1)} %bitcast.119, bf16[256,4096]{1,0:T(8,128)(2,1)S(1)} %copy-done), kind=kOutput, calls=%fused_computation.10 | convolution fusion | flops 270532608 | bytes 9437184 | tf_op jit(solution)/shard_map/she,hde->shd/dot_general | solution.py:85
  209.2 4.1 %copy.61 = bf16[256,4096]{1,0:T(8,128)(2,1)} copy(bf16[256,4096]{0,1:T(8,128)(2,1)} %bitcast.131) | data formatting | bytes 4194304
  213.2 4.9 %add_convert_fusion = bf16[32,128,256]{2,1,0:T(8,128)(2,1)} fusion(f32[32,128,256]{2,1,0:T(8,128)} %fusion.3, bf16[32,128,128]{2,1,0:T(8,128)(2,1)S(1)} %bitcast.120, bf16[256,4096]{1,0:T(8,128)(2,1)} %param.6), kind=kOutput, calls=%fused_computation.12 | convolution fusion | flops 270532608 | bytes 9437184 | tf_op jit(solution)/shard_map/shd,hde->she/dot_general | solution.py:88
  218.2 4.1 %copy.62 = bf16[256,4096]{1,0:T(8,128)(2,1)} copy(bf16[256,4096]{0,1:T(8,128)(2,1)} %bitcast.130) | data formatting | bytes 4194304
  (3 shorter events, 0.1 us)
Async XLA Ops:
  0.6 1.6 copy-start
  61.2 29.2 %all-to-all-start.1 = ((bf16[8,512,128]{2,1,0:T(8,128)(2,1)}), bf16[8,512,128]{2,1,0:T(8,128)(2,1)S(1)}, u32[]{:S(2)}, u32[]{:S(2)}) async-start(bf16[8,512,128]{2,1,0:T(8,128)(2,1)} %concatenate.6), calls=%async_computation.1 | async-start | bytes 2097152 | tf_op jit(solution)/shard_map/all_to_all | solution.py:25
  96.0 5.7 %copy-start.3 = (f32[4096]{0:T(1024)S(1)}, f32[4096]{0:T(1024)}, u32[]{:S(2)}) copy-start(f32[4096]{0:T(1024)} %param.8) | copy-start | bytes 49156
  101.6 4.1 %copy-start.1 = (f32[256,4096]{1,0:T(8,128)S(1)}, f32[256,4096]{1,0:T(8,128)}, u32[]{:S(2)}) copy-start(f32[256,4096]{1,0:T(8,128)} %copy.47) | copy-start | bytes 12582916
  101.6 4.7 %copy-start.2 = (bf16[256,4096]{1,0:T(8,128)(2,1)S(1)}, bf16[256,4096]{1,0:T(8,128)(2,1)}, u32[]{:S(2)}) copy-start(bf16[256,4096]{1,0:T(8,128)(2,1)} %param.9) | copy-start | bytes 6291460
  175.7 29.3 %all-to-all-start.3 = ((bf16[8,512,128]{2,1,0:T(8,128)(2,1)}), bf16[8,512,128]{2,1,0:T(8,128)(2,1)S(1)}, u32[]{:S(2)}, u32[]{:S(2)}) async-start(bf16[8,512,128]{2,1,0:T(8,128)(2,1)} %concatenate.7), calls=%async_computation.3 | async-start | bytes 2097152 | tf_op jit(solution)/shard_map/all_to_all | solution.py:37
where the time goes:
time: 223 us; the launch traced here: 222 us
  blocking collectives  107 us (48%)
  matrix products  40.9 us (18%)
  local copies, waits for them, and re-layouts  35.6 us (16%)
  waiting for transfers between devices  22.6 us (10%)
  other arithmetic  8.13 us (4%)
  starting transfers between devices  7.33 us (3%)
    all_to_all x1, blocking collectives, spread_forward(): lax.all_to_all(stacked, 'seq', split_axis=1, concat_axis=0, tiled=True)  55.3 us
    all_to_all x1, blocking collectives, spread_backward(): lax.all_to_all(stacked, 'seq', split_axis=1, concat_axis=0, tiled=True)  51.7 us
    unnamed x11, local copies, waits for them, and re-layouts  14.2 us
    all_to_all x1, waiting for transfers between devices, spread_backward(): lax.all_to_all(after.astype(jnp.bfloat16), 'seq', split_axis=0, concat_ax...  11.4 us
    all_to_all x1, waiting for transfers between devices, spread_forward(): lax.all_to_all(before.astype(jnp.bfloat16), 'seq', split_axis=0, concat_a...  11.2 us
    dot_general x1, matrix products, shards(): jnp.einsum('hst,the->she', key_weights, grad_heads, preferred_element_typ...  7.35 us
    dot_general x1, matrix products, shards(): jnp.einsum('hst,thd->shd', value_weights, query_heads, preferred_element_...  6.74 us
    dot_general x1, matrix products, shards(): jnp.einsum('hts,she->the', weights, value_heads, preferred_element_type=j...  6.73 us
  transfers between devices with their start and end apart: 2, of which 2 were waited for; matrix products, arithmetic and copies ran while one was open for 13% of the time, Pallas kernels for 0%

commit v1 on v0

v1 whole, which is shorter than its diff:
```python
from functools import partial

import jax
import jax.numpy as jnp
from jax import lax
from jax.experimental import pallas as pl
from jax.experimental.pallas import tpu as pltpu
from jax.sharding import PartitionSpec as P

DH = 128
EPS = 1e-05
CHUNKS = 2
F32 = jnp.float32
BF16 = jnp.bfloat16
NT = (((1,), (1,)), ((), ()))
NN = (((1,), (0,)), ((), ()))
TN = (((0,), (0,)), ((), ()))


def mm(a, b, dims):
    return lax.dot_general(a, b, dims, preferred_element_type=F32)


def head(h):
    return slice(h * DH, (h + 1) * DH)


def lower_mask(t):
    rows = lax.broadcasted_iota(jnp.int32, (t, t), 0)
    cols = lax.broadcasted_iota(jnp.int32, (t, t), 1)
    return rows >= cols


def state_kernel(heads, m_ref, a_ref, b_ref, *outs):
    step = pl.program_id(0)
    for j, out in enumerate(outs):
        @pl.when(step == j)
        def _():
            for h in range(heads):
                out[head(h), :] = mm(a_ref[:, head(h)], b_ref[:, head(h)], TN).astype(BF16)


def local_kernel(heads, q_ref, k_ref, v_ref, out_ref):
    mask = lower_mask(q_ref.shape[0])
    for h in range(heads):
        scores = mm(q_ref[:, head(h)], k_ref[:, head(h)], NT)
        weights = jnp.where(mask, scores, 0.0).astype(BF16)
        out_ref[:, head(h)] = mm(weights, v_ref[:, head(h)], NN)


def attend_kernel(heads, m_ref, q_ref, loc_ref, c_ref, gain_ref, *rest):
    count = len(rest) - 3
    prefixes, (att_ref, ss_ref, sc_ref) = rest[:count], rest[count:]
    step = pl.program_id(0)

    @pl.when(step == 0)
    def _():
        ss_ref[...] = jnp.zeros_like(ss_ref)
        sc_ref[...] = jnp.zeros_like(sc_ref)

    for j, pre in enumerate(prefixes):
        @pl.when(step == j)
        def _():
            ss = ss_ref[...]
            sc = sc_ref[...]
            for h in range(heads):
                att = loc_ref[:, head(h)] + mm(q_ref[:, head(h)], pre[head(h), :], NN)
                att_ref[:, head(h)] = att
                ss = ss + att * att
                sc = sc + att * (c_ref[:, head(h)].astype(F32) * gain_ref[:, head(h)])
            ss_ref[...] = ss
            sc_ref[...] = sc


def grad_kernel(heads, width, m_ref, q_ref, att_ref, c_ref, gain_ref, *rest):
    sums, rest = rest[: 2 * CHUNKS], rest[2 * CHUNKS :]
    g_ref, outs, (r_ref, s_ref) = rest[0], rest[1:-2], rest[-2:]
    step = pl.program_id(0)

    @pl.when(step == 0)
    def _():
        ss = sums[0][...]
        sc = sums[1][...]
        for i in range(1, CHUNKS):
            ss = ss + sums[2 * i][...]
            sc = sc + sums[2 * i + 1][...]
        ss = jnp.sum(ss, axis=1, keepdims=True) / width
        sc = jnp.sum(sc, axis=1, keepdims=True) / width
        r = lax.rsqrt(ss + EPS)
        r_ref[...] = jnp.broadcast_to(r, r_ref.shape)
        s_ref[...] = jnp.broadcast_to(r * r * r * sc, s_ref.shape)

    for j, out in enumerate(outs):
        @pl.when(step == j)
        def _():
            r = r_ref[...]
            s = s_ref[...]
            for h in range(heads):
                u = c_ref[:, head(h)].astype(F32) * gain_ref[:, head(h)]
                g = (u * r - att_ref[:, head(h)] * s).astype(BF16)
                g_ref[:, head(h)] = g
                out[head(h), :] = mm(q_ref[:, head(h)], g, TN).astype(BF16)


def back_local_kernel(heads, q_ref, k_ref, v_ref, g_ref, kl_ref, vl_ref):
    t = q_ref.shape[0]
    rows = lax.broadcasted_iota(jnp.int32, (t, t), 0)
    cols = lax.broadcasted_iota(jnp.int32, (t, t), 1)
    mask = rows <= cols
    for h in range(heads):
        q, k, v, g = (ref[:, head(h)] for ref in (q_ref, k_ref, v_ref, g_ref))
        vw = jnp.where(mask, mm(v, g, NT), 0.0).astype(BF16)
        kl_ref[:, head(h)] = mm(vw, q, NN)
        kw = jnp.where(mask, mm(k, q, NT), 0.0).astype(BF16)
        vl_ref[:, head(h)] = mm(kw, g, NN)


def finish_kernel(heads, count, m_ref, k_ref, v_ref, kl_ref, vl_ref, *rest):
    kg_ref, vg_ref = rest[-2:]
    step = pl.program_id(0)
    for j, suf in enumerate(rest[:count]):
        @pl.when(step == j)
        def _():
            for h in range(heads):
                s = suf[head(h), :]
                kg_ref[:, head(h)] = (kl_ref[:, head(h)] + mm(v_ref[:, head(h)], s, NT)).astype(BF16)
                vg_ref[:, head(h)] = (vl_ref[:, head(h)] + mm(k_ref[:, head(h)], s, NN)).astype(BF16)


def exchange(parts, n):
    m = len(parts)
    out = [parts[0]] + [None] * (m - 1)
    for j in range(m - 1, 0, -1):
        perm = [(i, (i // m) * m + ((i % m) ^ j)) for i in range(n)]
        out[j] = lax.ppermute(parts[j], "seq", perm)
    return out


def carry_groups(total, n, m, forward):
    groups = n // m

    def shift(x, by):
        step = by * m
        if forward:
            perm = [(i, i + step) for i in range(n - step)]
        else:
            perm = [(i + step, i) for i in range(n - step)]
        return lax.ppermute(x, "seq", perm)

    if groups == 1:
        return None
    if groups == 2:
        return shift(total.astype(BF16), 1).astype(F32)
    run = shift(total, 1)
    by = 1
    while by < groups - 1:
        run = run + shift(run, by)
        by *= 2
    return run


def spread(states, n, member, forward):
    m = len(states)
    got = exchange(states, n)
    got = [x.astype(F32) for x in got]
    carry = carry_groups(sum(got), n, m, forward)
    back = []
    for j in range(m):
        target = member ^ j
        acc = carry
        for i in range(m):
            source = member ^ i
            if i == j:
                continue
            take = (source < target) if forward else (source > target)
            term = jnp.where(take, got[i], 0.0)
            acc = term if acc is None else acc + term
        if acc is None:
            acc = jnp.zeros_like(got[0])
        back.append(acc.astype(BF16))
    return exchange(back, n)


def shards(n, queries, keys, values, gain, cotangent):
    rows, width = queries.shape
    m = 4 if n % 4 == 0 else (2 if n % 2 == 0 else 1)
    part = width // (CHUNKS * m)
    half = width // CHUNKS
    heads = part // DH
    member = lax.axis_index("seq") % m
    mem = member.reshape(1).astype(jnp.int32)
    gain2 = gain.reshape(1, width)
    stat = jax.ShapeDtypeStruct((rows, DH), F32)
    state = jax.ShapeDtypeStruct((part, DH), BF16)

    def cols(c, r=rows):
        return pl.BlockSpec((r, part), lambda j, s: (0, c * m + (s[0] ^ j)))

    def cols_half(r=rows):
        return pl.BlockSpec((r, part), lambda j, s: (0, s[0] ^ j))

    whole_state = pl.BlockSpec((part, DH), lambda j, s: (0, 0))
    whole_stat = pl.BlockSpec((rows, DH), lambda j, s: (0, 0))

    def call(kernel, args, in_specs, out_specs, out_shape, flops, nbytes, scratch=(), alias={}):
        return pl.pallas_call(
            kernel,
            out_shape=out_shape,
            grid_spec=pltpu.PrefetchScalarGridSpec(
                num_scalar_prefetch=1, grid=(m,), in_specs=in_specs, out_specs=out_specs, scratch_shapes=scratch
            ),
            input_output_aliases=alias,
            compiler_params=pltpu.CompilerParams(dimension_semantics=("arbitrary",), vmem_limit_bytes=24 << 20),
            cost_estimate=pl.CostEstimate(flops=flops, bytes_accessed=nbytes, transcendentals=0),
        )(mem, *args)

    unit = 2 * rows * DH * half

    def states_of(c, a, b):
        return call(partial(state_kernel, heads), (a, b), [cols(c), cols(c)], [whole_state] * m, [state] * m,
                    unit, 4 * rows * half + 2 * DH * half)

    plain = pl.BlockSpec((rows, part), lambda j: (0, j))

    def grid_call(kernel, args, outs, flops, nbytes):
        return pl.pallas_call(
            kernel,
            grid=(width // part,),
            in_specs=[plain] * len(args),
            out_specs=[plain] * outs,
            out_shape=[jax.ShapeDtypeStruct((rows, width), F32)] * outs,
            compiler_params=pltpu.CompilerParams(dimension_semantics=("arbitrary",), vmem_limit_bytes=24 << 20),
            cost_estimate=pl.CostEstimate(flops=flops, bytes_accessed=nbytes, transcendentals=0),
        )(*args)

    state_parts = [states_of(c, keys, values) for c in range(CHUNKS)]
    prefix = [spread(s, n, member, True) for s in state_parts]
    (local,) = grid_call(partial(local_kernel, heads), (queries, keys, values), 1, 8 * unit, 10 * rows * width)

    attended, sums = [], []
    for c in range(CHUNKS):
        att, ss, sc = call(
            partial(attend_kernel, heads),
            (queries, local, cotangent, gain2, *prefix[c]),
            [cols(c), cols(c), cols(c), cols(c, 1)] + [whole_state] * m,
            [cols_half(), whole_stat, whole_stat],
            [jax.ShapeDtypeStruct((rows, half), F32), stat, stat],
            unit, 12 * rows * half,
        )
        attended.append(att)
        sums += [ss, sc]

    grads, grad_parts = [], []
    for c in range(CHUNKS):
        g, *parts = call(
            partial(grad_kernel, heads, width),
            (queries, attended[c], cotangent, gain2, *sums),
            [cols(c), cols_half(), cols(c), cols(c, 1)] + [whole_stat] * (2 * CHUNKS),
            [cols_half()] + [whole_state] * m,
            [jax.ShapeDtypeStruct((rows, half), BF16)] + [state] * m,
            unit, 10 * rows * half,
            scratch=[pltpu.VMEM((rows, DH), F32)] * 2,
        )
        grads.append(g)
        grad_parts.append(parts)

    suffix = [spread(s, n, member, False) for s in grad_parts]
    blocks = half // part
    local_grads = []
    for c in range(CHUNKS):
        col = pl.BlockSpec((rows, part), lambda j, c=c: (0, c * blocks + j))
        own = pl.BlockSpec((rows, part), lambda j: (0, j))
        local_grads.append(pl.pallas_call(
            partial(back_local_kernel, heads),
            grid=(blocks,),
            in_specs=[col, col, col, own],
            out_specs=[own, own],
            out_shape=[jax.ShapeDtypeStruct((rows, half), F32)] * 2,
            compiler_params=pltpu.CompilerParams(dimension_semantics=("arbitrary",), vmem_limit_bytes=24 << 20),
            cost_estimate=pl.CostEstimate(flops=8 * unit, bytes_accessed=16 * rows * half, transcendentals=0),
        )(queries, keys, values, grads[c]))

    outs = ()
    out_shape = [jax.ShapeDtypeStruct((rows, width), BF16)] * 2
    for c in range(CHUNKS):
        base = 5 + m
        outs = call(
            partial(finish_kernel, heads, m),
            (keys, values, *local_grads[c], *suffix[c], *outs),
            [cols(c), cols(c), cols_half(), cols_half()] + [whole_state] * m
            + [pl.BlockSpec(memory_space=pl.ANY)] * len(outs),
            [cols(c), cols(c)],
            out_shape,
            2 * unit, 16 * rows * half,
            alias={base: 0, base + 1: 1} if outs else {},
        )
    return tuple(outs)


def solution(mesh):
    spec = P(("dp", "seq"), None)
    return jax.shard_map(
        partial(shards, mesh.shape["seq"]),
        mesh=mesh,
        in_specs=(spec, spec, spec, P(), spec),
        out_specs=(spec, spec),
        check_vma=False,
    )
```

time: 223 us -> 106 us (0.48)
  blocking collectives: 107 us -> 0 us
  matrix products: 40.9 us -> 0 us
  starting transfers between devices: 7.33 us -> 46.1 us
  Pallas kernels: 0 us -> 31.3 us
  local copies, waits for them, and re-layouts: 35.6 us -> 12.7 us
  waiting for transfers between devices: 22.6 us -> 8.76 us
  other arithmetic: 8.13 us -> 5.44 us
    all_to_all x2 -> x0, blocking collectives: 107 us -> none  [the longest x1 55.3 us: spread_forward(): lax.all_to_all(stacked, 'seq', split_axis=1, concat_axis=0, tiled=True)]
    ppermute x0 -> x28, starting transfers between devices: none -> 46.1 us  [the longest x24 35.5 us: exchange(): out[j] = lax.ppermute(parts[j], 'seq', perm)]
    dot_general x8 -> x0, matrix products: 40.9 us -> none  [the longest x1 7.35 us: shards(): jnp.einsum('hst,the->she', key_weights, grad_heads, preferred_element_typ...]
    pallas_call x0 -> x11, Pallas kernels: none -> 31.3 us  [the longest x8 16.8 us: call(): pl.pallas_call(kernel, out_shape=out_shape, grid_spec=pltpu.PrefetchScala...]
    all_to_all x2 -> x0, waiting for transfers between devices: 22.6 us -> none  [the longest x1 11.4 us: spread_backward(): lax.all_to_all(after.astype(jnp.bfloat16), 'seq', split_axis=0, concat_ax...]
    reshape x3 -> x0, local copies, waits for them, and re-layouts: 14 us -> none  [the longest x1 5.66 us: shards(): attended = (cross_term + local_term).reshape(tok_rows, head_count * DH)]
    ppermute x0 -> x28, waiting for transfers between devices: none -> 8.76 us  [the longest x24 6.06 us: exchange(): out[j] = lax.ppermute(parts[j], 'seq', perm)]
    all_to_all x2 -> x0, starting transfers between devices: 7.33 us -> none  [the longest x1 3.74 us: spread_backward(): lax.all_to_all(after.astype(jnp.bfloat16), 'seq', split_axis=0, concat_ax...]
  transfers between devices with their start and end apart: 2 -> 28, of which waited for: 2 -> 4; matrix products, arithmetic and copies ran while one was open for 13% -> 5% of each run, Pallas kernels for 0% -> 21%
where the time goes in v1:
time: 106 us; the launch traced here: 105 us
  starting transfers between devices  46.1 us (43%)
  Pallas kernels  31.3 us (30%)
  local copies, waits for them, and re-layouts  12.7 us (12%)
  waiting for transfers between devices  8.76 us (8%)
  other arithmetic  5.44 us (5%)
    ppermute x24, starting transfers between devices, exchange(): out[j] = lax.ppermute(parts[j], 'seq', perm)  35.5 us
    pallas_call x8, Pallas kernels, call(): pl.pallas_call(kernel, out_shape=out_shape, grid_spec=pltpu.PrefetchScala...  16.8 us
    unnamed x32, local copies, waits for them, and re-layouts  12.7 us
    ppermute x4, starting transfers between devices, shift(): return lax.ppermute(x, 'seq', perm)  10.5 us
    pallas_call x2, Pallas kernels, shards(): pl.pallas_call(partial(back_local_kernel, heads), grid=(blocks,), in_spec...  8.56 us
    ppermute x24, waiting for transfers between devices, exchange(): out[j] = lax.ppermute(parts[j], 'seq', perm)  6.06 us
    pallas_call x1, Pallas kernels, grid_call(): pl.pallas_call(kernel, grid=(width // part,), in_specs=[plain] * len(args...  5.96 us
    convert_element_type x4, other arithmetic, spread(): back.append(acc.astype(BF16))  3.15 us
  transfers between devices with their start and end apart: 28, of which 4 were waited for; matrix products, arithmetic and copies ran while one was open for 5% of the time, Pallas kernels for 21%

profile of v1, /device:TPU:0, one launch (start us, length us, event | category | flops | bytes accessed | tf_op | source)
XLA Modules:
  0.0 105.2 jit_solution(6755818216494815552)
XLA Ops:
  0.7 1.6 %copy-done.1 = bf16[256,4096]{1,0:T(8,128)(2,1)S(1)} copy-done((bf16[256,4096]{1,0:T(8,128)(2,1)S(1)}, bf16[256,4096]{1,0:T(8,128)(2,1)}, u32[]{:S(2)}) %copy-start.1) | copy-done | bytes 2097176
  2.2 1.6 %copy-done.4 = bf16[256,4096]{1,0:T(8,128)(2,1)S(1)} copy-done((bf16[256,4096]{1,0:T(8,128)(2,1)S(1)}, bf16[256,4096]{1,0:T(8,128)(2,1)}, u32[]{:S(2)}) %copy-start.4) | copy-done | bytes 2097176
  3.8 1.4 %shard_map.71 = (bf16[512,128]{1,0:T(8,128)(2,1)S(1)}, bf16[512,128]{1,0:T(8,128)(2,1)S(1)}, bf16[512,128]{1,0:T(8,128)(2,1)S(1)}, bf16[512,128]{1,0:T(8,128)(2,1)S(1)}) custom-call(s32[1]{0:T(128)} %bitcast.m_ref, bf16[256,4096]{1,0:T(8,128)(2,1)S(1)} %copy-done.1, bf16[256,4096]{1,0:T(8,128)(2,1)S(1)} %copy-done.4), custom_call_target="tpu_custom_call" | custom-call | flops 134217728 | bytes 2621440 | tf_op jit(solution)/shard_map/pallas_call | solution.py:206
  5.2 3.0 %collective-permute-start.7 = (bf16[512,128]{1,0:T(8,128)(2,1)S(1)}, bf16[512,128]{1,0:T(8,128)(2,1)S(1)}, u32[]{:S(2)}, u32[]{:S(2)}) collective-permute-start(bf16[512,128]{1,0:T(8,128)(2,1)S(1)} %get-tuple-element.38), channel_id=1, source_target_pairs={{0,4},{4,0},{8,12},{12,8},{16,20},{20,16},{24,28},{28,24},{1,5},{5... | collective-permute-start | bytes 393224 | tf_op jit(solution)/shard_map/ppermute | solution.py:135
  8.2 1.6 %collective-permute-start.8 = (bf16[512,128]{1,0:T(8,128)(2,1)S(1)}, bf16[512,128]{1,0:T(8,128)(2,1)}, u32[]{:S(2)}, u32[]{:S(2)}) collective-permute-start(bf16[512,128]{1,0:T(8,128)(2,1)S(1)} %get-tuple-element.39), channel_id=1, source_target_pairs={{0,8},{4,12},{8,0},{12,4},{16,24},{20,28},{24,16},{28,20},{1,9},{5... | collective-permute-start | bytes 393224 | tf_op jit(solution)/shard_map/ppermute | solution.py:135
  9.8 1.4 %shard_map.69 = (bf16[512,128]{1,0:T(8,128)(2,1)S(1)}, bf16[512,128]{1,0:T(8,128)(2,1)S(1)}, bf16[512,128]{1,0:T(8,128)(2,1)S(1)}, bf16[512,128]{1,0:T(8,128)(2,1)S(1)}) custom-call(s32[1]{0:T(128)} %bitcast.m_ref, bf16[256,4096]{1,0:T(8,128)(2,1)S(1)} %copy-done.1, bf16[256,4096]{1,0:T(8,128)(2,1)S(1)} %copy-done.4), custom_call_target="tpu_custom_call" | custom-call | flops 134217728 | bytes 2621440 | tf_op jit(solution)/shard_map/pallas_call | solution.py:206
  11.2 2.0 %collective-permute-start = (bf16[512,128]{1,0:T(8,128)(2,1)S(1)}, bf16[512,128]{1,0:T(8,128)(2,1)S(1)}, u32[]{:S(2)}, u32[]{:S(2)}) collective-permute-start(bf16[512,128]{1,0:T(8,128)(2,1)S(1)} %get-tuple-element.33), channel_id=1, source_target_pairs={{0,4},{4,0},{8,12},{12,8},{16,20},{20,16},{24,28},{28,24},{1,5},{5... | collective-permute-start | bytes 393224 | tf_op jit(solution)/shard_map/ppermute | solution.py:135
  13.2 1.6 %collective-permute-start.1 = (bf16[512,128]{1,0:T(8,128)(2,1)S(1)}, bf16[512,128]{1,0:T(8,128)(2,1)S(1)}, u32[]{:S(2)}, u32[]{:S(2)}) collective-permute-start(bf16[512,128]{1,0:T(8,128)(2,1)S(1)} %get-tuple-element.34), channel_id=1, source_target_pairs={{0,8},{4,12},{8,0},{12,4},{16,24},{20,28},{24,16},{28,20},{1,9},{5... | collective-permute-start | bytes 393224 | tf_op jit(solution)/shard_map/ppermute | solution.py:135
  14.8 2.5 %collective-permute-done.9 = bf16[512,128]{1,0:T(8,128)(2,1)} collective-permute-done((bf16[512,128]{1,0:T(8,128)(2,1)S(1)}, bf16[512,128]{1,0:T(8,128)(2,1)}, u32[]{:S(2)}, u32[]{:S(2)}) %collective-permute-start.9) | collective-permute-done | bytes 131104 | tf_op jit(solution)/shard_map/ppermute | solution.py:135
  17.3 1.0 fusion.25
  18.3 4.5 %collective-permute-start.10 = (bf16[512,128]{1,0:T(8,128)(2,1)S(1)}, bf16[512,128]{1,0:T(8,128)(2,1)S(1)}, u32[]{:S(2)}, u32[]{:S(2)}) collective-permute-start(bf16[512,128]{1,0:T(8,128)(2,1)S(1)} %fusion.25), channel_id=1, source_target_pairs={{0,16},{4,20},{8,24},{12,28},{1,17},{5,21},{9,25},{13,29},{2,18},{... | collective-permute-start | bytes 393224 | tf_op jit(solution)/shard_map/ppermute | solution.py:148
  22.9 3.3 %collective-permute-start.3 = (bf16[512,128]{1,0:T(8,128)(2,1)S(1)}, bf16[512,128]{1,0:T(8,128)(2,1)S(1)}, u32[]{:S(2)}, u32[]{:S(2)}) collective-permute-start(bf16[512,128]{1,0:T(8,128)(2,1)S(1)} %fusion.12), channel_id=1, source_target_pairs={{0,16},{4,20},{8,24},{12,28},{1,17},{5,21},{9,25},{13,29},{2,18},{... | collective-permute-start | bytes 393224 | tf_op jit(solution)/shard_map/ppermute | solution.py:148
  26.2 1.3 %fusion.18 = (bf16[512,128]{1,0:T(8,128)(2,1)S(1)}, bf16[512,128]{1,0:T(8,128)(2,1)S(1)}, bf16[512,128]{1,0:T(8,128)(2,1)S(1)}, bf16[512,128]{1,0:T(8,128)(2,1)S(1)}) fusion(bf16[512,128]{1,0:T(8,128)(2,1)S(1)} %collective-permute-done.7, bf16[512,128]{1,0:T(8,128)(2,1)} %collective-permute-done.8, bf16[512,128]{1,0:T(8,128)(2,1)S(1)} %get-tuple-element.37, ...), kind=kLoop, calls=%fused_computation.94 | loop fusion | flops 2162688 | bytes 1179660 | tf_op jit(solution)/shard_map/convert_element_type | solution.py:180
  27.5 2.0 %collective-permute-start.11 = (bf16[512,128]{1,0:T(8,128)(2,1)S(1)}, bf16[512,128]{1,0:T(8,128)(2,1)S(1)}, u32[]{:S(2)}, u32[]{:S(2)}) collective-permute-start(bf16[512,128]{1,0:T(8,128)(2,1)S(1)} %get-tuple-element.71), channel_id=1, source_target_pairs={{0,4},{4,0},{8,12},{12,8},{16,20},{20,16},{24,28},{28,24},{1,5},{5... | collective-permute-start | bytes 393224 | tf_op jit(solution)/shard_map/ppermute | solution.py:135
  29.5 5.9 %collective-permute-start.12 = (bf16[512,128]{1,0:T(8,128)(2,1)S(1)}, bf16[512,128]{1,0:T(8,128)(2,1)S(1)}, u32[]{:S(2)}, u32[]{:S(2)}) collective-permute-start(bf16[512,128]{1,0:T(8,128)(2,1)S(1)} %get-tuple-element.73), channel_id=1, source_target_pairs={{0,8},{4,12},{8,0},{12,4},{16,24},{20,28},{24,16},{28,20},{1,9},{5... | collective-permute-start | bytes 393224 | tf_op jit(solution)/shard_map/ppermute | solution.py:135
  35.7 1.5 %collective-permute-start.4 = (bf16[512,128]{1,0:T(8,128)(2,1)S(1)}, bf16[512,128]{1,0:T(8,128)(2,1)S(1)}, u32[]{:S(2)}, u32[]{:S(2)}) collective-permute-start(bf16[512,128]{1,0:T(8,128)(2,1)S(1)} %get-tuple-element.75), channel_id=1, source_target_pairs={{0,4},{4,0},{8,12},{12,8},{16,20},{20,16},{24,28},{28,24},{1,5},{5... | collective-permute-start | bytes 393224 | tf_op jit(solution)/shard_map/ppermute | solution.py:135
  37.2 2.0 %collective-permute-start.5 = (bf16[512,128]{1,0:T(8,128)(2,1)S(1)}, bf16[512,128]{1,0:T(8,128)(2,1)S(1)}, u32[]{:S(2)}, u32[]{:S(2)}) collective-permute-start(bf16[512,128]{1,0:T(8,128)(2,1)S(1)} %get-tuple-element.77), channel_id=1, source_target_pairs={{0,8},{4,12},{8,0},{12,4},{16,24},{20,28},{24,16},{28,20},{1,9},{5... | collective-permute-start | bytes 393224 | tf_op jit(solution)/shard_map/ppermute | solution.py:135
  39.3 1.8 %collective-permute-start.6 = (bf16[512,128]{1,0:T(8,128)(2,1)S(1)}, bf16[512,128]{1,0:T(8,128)(2,1)S(1)}, u32[]{:S(2)}, u32[]{:S(2)}) collective-permute-start(bf16[512,128]{1,0:T(8,128)(2,1)S(1)} %get-tuple-element.74), channel_id=1, source_target_pairs={{0,12},{4,8},{8,4},{12,0},{16,28},{20,24},{24,20},{28,16},{1,13},{... | collective-permute-start | bytes 393224 | tf_op jit(solution)/shard_map/ppermute | solution.py:135
  41.0 1.6 %copy-done.2 = bf16[256,4096]{1,0:T(8,128)(2,1)S(1)} copy-done((bf16[256,4096]{1,0:T(8,128)(2,1)S(1)}, bf16[256,4096]{1,0:T(8,128)(2,1)}, u32[]{:S(2)}) %copy-start.2) | copy-done | bytes 2097176
  42.6 1.6 %copy-done.5 = bf16[256,4096]{1,0:T(8,128)(2,1)S(1)} copy-done((bf16[256,4096]{1,0:T(8,128)(2,1)S(1)}, bf16[256,4096]{1,0:T(8,128)(2,1)}, u32[]{:S(2)}) %copy-start.5) | copy-done | bytes 2097176
  44.2 6.0 %shard_map.68.loc_ref = f32[256,4096]{1,0:T(8,128)S(1)} custom-call(bf16[256,4096]{1,0:T(8,128)(2,1)S(1)} %copy-done, bf16[256,4096]{1,0:T(8,128)(2,1)S(1)} %copy-done.2, bf16[256,4096]{1,0:T(8,128)(2,1)S(1)} %copy-done.5), custom_call_target="tpu_custom_call" | custom-call | flops 1073741824 | bytes 10485760 | tf_op jit(solution)/shard_map/pallas_call | solution.py:226
  50.2 1.7 %shard_map.72 = (f32[256,2048]{1,0:T(8,128)S(1)}, f32[256,128]{1,0:T(8,128)S(1)}, f32[256,128]{1,0:T(8,128)S(1)}) custom-call(s32[1]{0:T(128)} %bitcast.m_ref, bf16[256,4096]{1,0:T(8,128)(2,1)S(1)} %copy-done, f32[256,4096]{1,0:T(8,128)S(1)} %shard_map.68.loc_ref, bf16[256,4096]{1,0:T(8,128)(2,1)S(1)} %copy-done.7, f32[1,4096]{1,0:T(1,128)S(1)} %bitcast.2, ...), custom_call_target="tpu_custom_call" | custom-call | flops 134217728 | bytes 6291456 | tf_op jit(solution)/shard_map/pallas_call | solution.py:206
  52.0 1.7 %shard_map.70 = (f32[256,2048]{1,0:T(8,128)S(1)}, f32[256,128]{1,0:T(8,128)S(1)}, f32[256,128]{1,0:T(8,128)S(1)}) custom-call(s32[1]{0:T(128)} %bitcast.m_ref, bf16[256,4096]{1,0:T(8,128)(2,1)S(1)} %copy-done, f32[256,4096]{1,0:T(8,128)S(1)} %shard_map.68.loc_ref, bf16[256,4096]{1,0:T(8,128)(2,1)S(1)} %copy-done.7, f32[1,4096]{1,0:T(1,128)S(1)} %bitcast.3, ...), custom_call_target="tpu_custom_call" | custom-call | flops 134217728 | bytes 6291456 | tf_op jit(solution)/shard_map/pallas_call | solution.py:206
  53.7 1.3 %copy-done.9 = f32[256,2048]{1,0:T(8,128)} copy-done((f32[256,2048]{1,0:T(8,128)}, f32[256,2048]{1,0:T(8,128)S(1)}, u32[]{:S(2)}) %copy-start.9) | copy-done | bytes 2097176
  55.0 2.7 %shard_map.75 = (bf16[256,2048]{1,0:T(8,128)(2,1)S(1)}, bf16[512,128]{1,0:T(8,128)(2,1)S(1)}, bf16[512,128]{1,0:T(8,128)(2,1)}, bf16[512,128]{1,0:T(8,128)(2,1)}, bf16[512,128]{1,0:T(8,128)(2,1)}) custom-call(s32[1]{0:T(128)} %bitcast.m_ref, bf16[256,4096]{1,0:T(8,128)(2,1)S(1)} %copy-done, f32[256,2048]{1,0:T(8,128)S(1)} %get-tuple-element.52.att_ref, ...), custom_call_target="tpu_custom_call" | custom-call | flops 134217728 | bytes 5242880 | tf_op jit(solution)/shard_map/pallas_call | solution.py:206
  57.9 1.5 %collective-permute-start.22 = (bf16[512,128]{1,0:T(8,128)(2,1)}, bf16[512,128]{1,0:T(8,128)(2,1)}, u32[]{:S(2)}, u32[]{:S(2)}) collective-permute-start(bf16[512,128]{1,0:T(8,128)(2,1)} %get-tuple-element.58), channel_id=1, source_target_pairs={{0,8},{4,12},{8,0},{12,4},{16,24},{20,28},{24,16},{28,20},{1,9},{5... | collective-permute-start | bytes 393224 | tf_op jit(solution)/shard_map/ppermute | solution.py:135
  59.4 1.8 %collective-permute-start.23 = (bf16[512,128]{1,0:T(8,128)(2,1)}, bf16[512,128]{1,0:T(8,128)(2,1)}, u32[]{:S(2)}, u32[]{:S(2)}) collective-permute-start(bf16[512,128]{1,0:T(8,128)(2,1)} %get-tuple-element.59), channel_id=1, source_target_pairs={{0,12},{4,8},{8,4},{12,0},{16,28},{20,24},{24,20},{28,16},{1,13},{... | collective-permute-start | bytes 393224 | tf_op jit(solution)/shard_map/ppermute | solution.py:135
  61.2 1.6 %copy-done.8 = bf16[256,4096]{1,0:T(8,128)(2,1)S(1)} copy-done((bf16[256,4096]{1,0:T(8,128)(2,1)S(1)}, bf16[256,4096]{1,0:T(8,128)(2,1)}, u32[]{:S(2)}) %copy-start.8) | copy-done | bytes 2097176
  62.8 1.6 %copy-done.10 = f32[256,2048]{1,0:T(8,128)S(1)} copy-done((f32[256,2048]{1,0:T(8,128)S(1)}, f32[256,2048]{1,0:T(8,128)}, u32[]{:S(2)}) %copy-start.10) | copy-done | bytes 2097176
  64.4 0.9 copy-done.12
  65.3 0.9 copy-done.14
  66.2 1.9 %shard_map.73 = (bf16[256,2048]{1,0:T(8,128)(2,1)S(1)}, bf16[512,128]{1,0:T(8,128)(2,1)S(1)}, bf16[512,128]{1,0:T(8,128)(2,1)S(1)}, bf16[512,128]{1,0:T(8,128)(2,1)S(1)}, bf16[512,128]{1,0:T(8,128)(2,1)S(1)}) custom-call(s32[1]{0:T(128)} %bitcast.m_ref, bf16[256,4096]{1,0:T(8,128)(2,1)S(1)} %copy-done, f32[256,2048]{1,0:T(8,128)S(1)} %copy-done.10, ...), custom_call_target="tpu_custom_call" | custom-call | flops 134217728 | bytes 5242880 | tf_op jit(solution)/shard_map/pallas_call | solution.py:206
  68.5 1.5 %collective-permute-start.15 = (bf16[512,128]{1,0:T(8,128)(2,1)S(1)}, bf16[512,128]{1,0:T(8,128)(2,1)S(1)}, u32[]{:S(2)}, u32[]{:S(2)}) collective-permute-start(bf16[512,128]{1,0:T(8,128)(2,1)S(1)} %get-tuple-element.50), channel_id=1, source_target_pairs={{0,8},{4,12},{8,0},{12,4},{16,24},{20,28},{24,16},{28,20},{1,9},{5... | collective-permute-start | bytes 393224 | tf_op jit(solution)/shard_map/ppermute | solution.py:135
  70.0 1.8 %collective-permute-start.16 = (bf16[512,128]{1,0:T(8,128)(2,1)S(1)}, bf16[512,128]{1,0:T(8,128)(2,1)S(1)}, u32[]{:S(2)}, u32[]{:S(2)}) collective-permute-start(bf16[512,128]{1,0:T(8,128)(2,1)S(1)} %get-tuple-element.51), channel_id=1, source_target_pairs={{0,12},{4,8},{8,4},{12,0},{16,28},{20,24},{24,20},{28,16},{1,13},{... | collective-permute-start | bytes 393224 | tf_op jit(solution)/shard_map/ppermute | solution.py:135
  71.7 1.1 %fusion.51 = bf16[512,128]{1,0:T(8,128)(2,1)S(1)} fusion(bf16[512,128]{1,0:T(8,128)(2,1)} %collective-permute-done.23, bf16[512,128]{1,0:T(8,128)(2,1)} %collective-permute-done.22, bf16[512,128]{1,0:T(8,128)(2,1)} %collective-permute-done.21, bf16[512,128]{1,0:T(8,128)(2,1)S(1)} %get-tuple-element.56), kind=kLoop, calls=%fused_computation.127 | loop fusion | flops 524288 | bytes 655360 | tf_op jit(solution)/shard_map/convert_element_type | solution.py:153
  72.8 1.3 %collective-permute-start.24 = (bf16[512,128]{1,0:T(8,128)(2,1)S(1)}, bf16[512,128]{1,0:T(8,128)(2,1)S(1)}, u32[]{:S(2)}, u32[]{:S(2)}) collective-permute-start(bf16[512,128]{1,0:T(8,128)(2,1)S(1)} %fusion.51), channel_id=1, source_target_pairs={{16,0},{20,4},{24,8},{28,12},{17,1},{21,5},{25,9},{29,13},{18,2},{... | collective-permute-start | bytes 393224 | tf_op jit(solution)/shard_map/ppermute | solution.py:148
  74.2 3.5 %collective-permute-done.16 = bf16[512,128]{1,0:T(8,128)(2,1)S(1)} collective-permute-done((bf16[512,128]{1,0:T(8,128)(2,1)S(1)}, bf16[512,128]{1,0:T(8,128)(2,1)S(1)}, u32[]{:S(2)}, u32[]{:S(2)}) %collective-permute-start.16) | collective-permute-done | bytes 131104 | tf_op jit(solution)/shard_map/ppermute | solution.py:135
  77.7 1.5 %collective-permute-start.17 = (bf16[512,128]{1,0:T(8,128)(2,1)S(1)}, bf16[512,128]{1,0:T(8,128)(2,1)S(1)}, u32[]{:S(2)}, u32[]{:S(2)}) collective-permute-start(bf16[512,128]{1,0:T(8,128)(2,1)S(1)} %fusion.38), channel_id=1, source_target_pairs={{16,0},{20,4},{24,8},{28,12},{17,1},{21,5},{25,9},{29,13},{18,2},{... | collective-permute-start | bytes 393224 | tf_op jit(solution)/shard_map/ppermute | solution.py:148
  79.2 2.2 %collective-permute-done.24 = bf16[512,128]{1,0:T(8,128)(2,1)S(1)} collective-permute-done((bf16[512,128]{1,0:T(8,128)(2,1)S(1)}, bf16[512,128]{1,0:T(8,128)(2,1)S(1)}, u32[]{:S(2)}, u32[]{:S(2)}) %collective-permute-start.24) | collective-permute-done | bytes 131104 | tf_op jit(solution)/shard_map/ppermute | solution.py:148
  81.4 1.3 %fusion.44 = (bf16[512,128]{1,0:T(8,128)(2,1)S(1)}, bf16[512,128]{1,0:T(8,128)(2,1)S(1)}, bf16[512,128]{1,0:T(8,128)(2,1)S(1)}, bf16[512,128]{1,0:T(8,128)(2,1)S(1)}) fusion(bf16[512,128]{1,0:T(8,128)(2,1)} %collective-permute-done.21, bf16[512,128]{1,0:T(8,128)(2,1)} %collective-permute-done.22, bf16[512,128]{1,0:T(8,128)(2,1)S(1)} %get-tuple-element.56, ...), kind=kLoop, calls=%fused_computation.120 | loop fusion | flops 2162688 | bytes 1179660 | tf_op jit(solution)/shard_map/convert_element_type | solution.py:180
  83.1 2.6 %collective-permute-start.26 = (bf16[512,128]{1,0:T(8,128)(2,1)S(1)}, bf16[512,128]{1,0:T(8,128)(2,1)S(1)}, u32[]{:S(2)}, u32[]{:S(2)}) collective-permute-start(bf16[512,128]{1,0:T(8,128)(2,1)S(1)} %get-tuple-element.65), channel_id=1, source_target_pairs={{0,8},{4,12},{8,0},{12,4},{16,24},{20,28},{24,16},{28,20},{1,9},{5... | collective-permute-start | bytes 393224 | tf_op jit(solution)/shard_map/ppermute | solution.py:135
  87.1 0.7 collective-permute-start.18
  87.7 1.9 %collective-permute-start.19 = (bf16[512,128]{1,0:T(8,128)(2,1)S(1)}, bf16[512,128]{1,0:T(8,128)(2,1)S(1)}, u32[]{:S(2)}, u32[]{:S(2)}) collective-permute-start(bf16[512,128]{1,0:T(8,128)(2,1)S(1)} %get-tuple-element.69), channel_id=1, source_target_pairs={{0,8},{4,12},{8,0},{12,4},{16,24},{20,28},{24,16},{28,20},{1,9},{5... | collective-permute-start | bytes 393224 | tf_op jit(solution)/shard_map/ppermute | solution.py:135
  89.6 1.0 collective-permute-start.20
  90.6 4.3 %shard_map.76 = (f32[256,2048]{1,0:T(8,128)S(1)}, f32[256,2048]{1,0:T(8,128)S(1)}) custom-call(bf16[256,4096]{1,0:T(8,128)(2,1)S(1)} %copy-done, bf16[256,4096]{1,0:T(8,128)(2,1)S(1)} %copy-done.3, bf16[256,4096]{1,0:T(8,128)(2,1)S(1)} %copy-done.6, bf16[256,2048]{1,0:T(8,128)(2,1)S(1)} %get-tuple-element.53.g_ref), custom_call_target="tpu_custom_call" | custom-call | flops 1073741824 | bytes 8388608 | tf_op jit(solution)/shard_map/pallas_call | solution.py:273
  94.9 4.3 %shard_map.74 = (f32[256,2048]{1,0:T(8,128)S(1)}, f32[256,2048]{1,0:T(8,128)S(1)}) custom-call(bf16[256,4096]{1,0:T(8,128)(2,1)S(1)} %copy-done, bf16[256,4096]{1,0:T(8,128)(2,1)S(1)} %copy-done.3, bf16[256,4096]{1,0:T(8,128)(2,1)S(1)} %copy-done.6, bf16[256,2048]{1,0:T(8,128)(2,1)S(1)} %get-tuple-element.45.g_ref), custom_call_target="tpu_custom_call" | custom-call | flops 1073741824 | bytes 8388608 | tf_op jit(solution)/shard_map/pallas_call | solution.py:273
  99.2 3.0 %shard_map.77 = (bf16[256,4096]{1,0:T(8,128)(2,1)}, bf16[256,4096]{1,0:T(8,128)(2,1)}) custom-call(s32[1]{0:T(128)} %bitcast.m_ref, bf16[256,4096]{1,0:T(8,128)(2,1)S(1)} %copy-done.3, bf16[256,4096]{1,0:T(8,128)(2,1)S(1)} %copy-done.6, f32[256,2048]{1,0:T(8,128)S(1)} %get-tuple-element.54.kl_ref, f32[256,2048]{1,0:T(8,128)S(1)} %get-tuple-element.55.vl_ref, ...), custom_call_target="tpu_custom_call" | custom-call | flops 268435456 | bytes 8388608 | tf_op jit(solution)/shard_map/pallas_call | solution.py:206
  102.2 3.0 %shard_map.78 = (bf16[256,4096]{1,0:T(8,128)(2,1)}, bf16[256,4096]{1,0:T(8,128)(2,1)}) custom-call(s32[1]{0:T(128)} %bitcast.m_ref, bf16[256,4096]{1,0:T(8,128)(2,1)S(1)} %copy-done.3, bf16[256,4096]{1,0:T(8,128)(2,1)S(1)} %copy-done.6, f32[256,2048]{1,0:T(8,128)S(1)} %get-tuple-element.46.kl_ref, ...), custom_call_target="tpu_custom_call", output_to_operand_aliasing={{0}: (9, {}), {1}: (10, {})} | custom-call | flops 268435456 | bytes 8388608 | tf_op jit(solution)/shard_map/pallas_call | solution.py:206
  (59 shorter events, 2.8 us)
Async XLA Ops:
  0.6 1.6 %copy-start.1 = (bf16[256,4096]{1,0:T(8,128)(2,1)S(1)}, bf16[256,4096]{1,0:T(8,128)(2,1)}, u32[]{:S(2)}) copy-start(bf16[256,4096]{1,0:T(8,128)(2,1)} %k_ref.9) | copy-start | bytes 6291460
  2.2 1.6 %copy-start.4 = (bf16[256,4096]{1,0:T(8,128)(2,1)S(1)}, bf16[256,4096]{1,0:T(8,128)(2,1)}, u32[]{:S(2)}) copy-start(bf16[256,4096]{1,0:T(8,128)(2,1)} %v_ref.9) | copy-start | bytes 6291460
  5.2 9.5 %collective-permute-start.7 = (bf16[512,128]{1,0:T(8,128)(2,1)S(1)}, bf16[512,128]{1,0:T(8,128)(2,1)S(1)}, u32[]{:S(2)}, u32[]{:S(2)}) collective-permute-start(bf16[512,128]{1,0:T(8,128)(2,1)S(1)} %get-tuple-element.38), channel_id=1, source_target_pairs={{0,4},{4,0},{8,12},{12,8},{16,20},{20,16},{24,28},{28,24},{1,5},{5... | collective-permute-start | bytes 393224 | tf_op jit(solution)/shard_map/ppermute | solution.py:135
  8.2 6.5 %collective-permute-start.8 = (bf16[512,128]{1,0:T(8,128)(2,1)S(1)}, bf16[512,128]{1,0:T(8,128)(2,1)}, u32[]{:S(2)}, u32[]{:S(2)}) collective-permute-start(bf16[512,128]{1,0:T(8,128)(2,1)S(1)} %get-tuple-element.39), channel_id=1, source_target_pairs={{0,8},{4,12},{8,0},{12,4},{16,24},{20,28},{24,16},{28,20},{1,9},{5... | collective-permute-start | bytes 393224 | tf_op jit(solution)/shard_map/ppermute | solution.py:135
  9.8 7.5 %collective-permute-start.9 = (bf16[512,128]{1,0:T(8,128)(2,1)S(1)}, bf16[512,128]{1,0:T(8,128)(2,1)}, u32[]{:S(2)}, u32[]{:S(2)}) collective-permute-start(bf16[512,128]{1,0:T(8,128)(2,1)S(1)} %get-tuple-element.40), channel_id=1, source_target_pairs={{0,12},{4,8},{8,4},{12,0},{16,28},{20,24},{24,20},{28,16},{1,13},{... | collective-permute-start | bytes 393224 | tf_op jit(solution)/shard_map/ppermute | solution.py:135
  11.2 29.9 %copy-start = (bf16[256,4096]{1,0:T(8,128)(2,1)S(1)}, bf16[256,4096]{1,0:T(8,128)(2,1)}, u32[]{:S(2)}) copy-start(bf16[256,4096]{1,0:T(8,128)(2,1)} %q_ref.13) | copy-start | bytes 6291460
  11.2 11.6 %collective-permute-start = (bf16[512,128]{1,0:T(8,128)(2,1)S(1)}, bf16[512,128]{1,0:T(8,128)(2,1)S(1)}, u32[]{:S(2)}, u32[]{:S(2)}) collective-permute-start(bf16[512,128]{1,0:T(8,128)(2,1)S(1)} %get-tuple-element.33), channel_id=1, source_target_pairs={{0,4},{4,0},{8,12},{12,8},{16,20},{20,16},{24,28},{28,24},{1,5},{5... | collective-permute-start | bytes 393224 | tf_op jit(solution)/shard_map/ppermute | solution.py:135
  13.2 9.7 %collective-permute-start.1 = (bf16[512,128]{1,0:T(8,128)(2,1)S(1)}, bf16[512,128]{1,0:T(8,128)(2,1)S(1)}, u32[]{:S(2)}, u32[]{:S(2)}) collective-permute-start(bf16[512,128]{1,0:T(8,128)(2,1)S(1)} %get-tuple-element.34), channel_id=1, source_target_pairs={{0,8},{4,12},{8,0},{12,4},{16,24},{20,28},{24,16},{28,20},{1,9},{5... | collective-permute-start | bytes 393224 | tf_op jit(solution)/shard_map/ppermute | solution.py:135
  14.7 8.1 %collective-permute-start.2 = (bf16[512,128]{1,0:T(8,128)(2,1)S(1)}, bf16[512,128]{1,0:T(8,128)(2,1)S(1)}, u32[]{:S(2)}, u32[]{:S(2)}) collective-permute-start(bf16[512,128]{1,0:T(8,128)(2,1)S(1)} %get-tuple-element.35), channel_id=1, source_target_pairs={{0,12},{4,8},{8,4},{12,0},{16,28},{20,24},{24,20},{28,16},{1,13},{... | collective-permute-start | bytes 393224 | tf_op jit(solution)/shard_map/ppermute | solution.py:135
  18.3 7.9 %collective-permute-start.10 = (bf16[512,128]{1,0:T(8,128)(2,1)S(1)}, bf16[512,128]{1,0:T(8,128)(2,1)S(1)}, u32[]{:S(2)}, u32[]{:S(2)}) collective-permute-start(bf16[512,128]{1,0:T(8,128)(2,1)S(1)} %fusion.25), channel_id=1, source_target_pairs={{0,16},{4,20},{8,24},{12,28},{1,17},{5,21},{9,25},{13,29},{2,18},{... | collective-permute-start | bytes 393224 | tf_op jit(solution)/shard_map/ppermute | solution.py:148
  22.9 12.5 %collective-permute-start.3 = (bf16[512,128]{1,0:T(8,128)(2,1)S(1)}, bf16[512,128]{1,0:T(8,128)(2,1)S(1)}, u32[]{:S(2)}, u32[]{:S(2)}) collective-permute-start(bf16[512,128]{1,0:T(8,128)(2,1)S(1)} %fusion.12), channel_id=1, source_target_pairs={{0,16},{4,20},{8,24},{12,28},{1,17},{5,21},{9,25},{13,29},{2,18},{... | collective-permute-start | bytes 393224 | tf_op jit(solution)/shard_map/ppermute | solution.py:148
  27.5 11.8 %collective-permute-start.11 = (bf16[512,128]{1,0:T(8,128)(2,1)S(1)}, bf16[512,128]{1,0:T(8,128)(2,1)S(1)}, u32[]{:S(2)}, u32[]{:S(2)}) collective-permute-start(bf16[512,128]{1,0:T(8,128)(2,1)S(1)} %get-tuple-element.71), channel_id=1, source_target_pairs={{0,4},{4,0},{8,12},{12,8},{16,20},{20,16},{24,28},{28,24},{1,5},{5... | collective-permute-start | bytes 393224 | tf_op jit(solution)/shard_map/ppermute | solution.py:135
  29.5 20.7 %collective-permute-start.12 = (bf16[512,128]{1,0:T(8,128)(2,1)S(1)}, bf16[512,128]{1,0:T(8,128)(2,1)S(1)}, u32[]{:S(2)}, u32[]{:S(2)}) collective-permute-start(bf16[512,128]{1,0:T(8,128)(2,1)S(1)} %get-tuple-element.73), channel_id=1, source_target_pairs={{0,8},{4,12},{8,0},{12,4},{16,24},{20,28},{24,16},{28,20},{1,9},{5... | collective-permute-start | bytes 393224 | tf_op jit(solution)/shard_map/ppermute | solution.py:135
  35.4 14.8 %collective-permute-start.13 = (bf16[512,128]{1,0:T(8,128)(2,1)S(1)}, bf16[512,128]{1,0:T(8,128)(2,1)S(1)}, u32[]{:S(2)}, u32[]{:S(2)}) collective-permute-start(bf16[512,128]{1,0:T(8,128)(2,1)S(1)} %get-tuple-element.70), channel_id=1, source_target_pairs={{0,12},{4,8},{8,4},{12,0},{16,28},{20,24},{24,20},{28,16},{1,13},{... | collective-permute-start | bytes 393224 | tf_op jit(solution)/shard_map/ppermute | solution.py:135
  35.7 16.2 %collective-permute-start.4 = (bf16[512,128]{1,0:T(8,128)(2,1)S(1)}, bf16[512,128]{1,0:T(8,128)(2,1)S(1)}, u32[]{:S(2)}, u32[]{:S(2)}) collective-permute-start(bf16[512,128]{1,0:T(8,128)(2,1)S(1)} %get-tuple-element.75), channel_id=1, source_target_pairs={{0,4},{4,0},{8,12},{12,8},{16,20},{20,16},{24,28},{28,24},{1,5},{5... | collective-permute-start | bytes 393224 | tf_op jit(solution)/shard_map/ppermute | solution.py:135
  37.2 14.7 %collective-permute-start.5 = (bf16[512,128]{1,0:T(8,128)(2,1)S(1)}, bf16[512,128]{1,0:T(8,128)(2,1)S(1)}, u32[]{:S(2)}, u32[]{:S(2)}) collective-permute-start(bf16[512,128]{1,0:T(8,128)(2,1)S(1)} %get-tuple-element.77), channel_id=1, source_target_pairs={{0,8},{4,12},{8,0},{12,4},{16,24},{20,28},{24,16},{28,20},{1,9},{5... | collective-permute-start | bytes 393224 | tf_op jit(solution)/shard_map/ppermute | solution.py:135
  39.3 12.7 %collective-permute-start.6 = (bf16[512,128]{1,0:T(8,128)(2,1)S(1)}, bf16[512,128]{1,0:T(8,128)(2,1)S(1)}, u32[]{:S(2)}, u32[]{:S(2)}) collective-permute-start(bf16[512,128]{1,0:T(8,128)(2,1)S(1)} %get-tuple-element.74), channel_id=1, source_target_pairs={{0,12},{4,8},{8,4},{12,0},{16,28},{20,24},{24,20},{28,16},{1,13},{... | collective-permute-start | bytes 393224 | tf_op jit(solution)/shard_map/ppermute | solution.py:135
  41.0 1.6 %copy-start.2 = (bf16[256,4096]{1,0:T(8,128)(2,1)S(1)}, bf16[256,4096]{1,0:T(8,128)(2,1)}, u32[]{:S(2)}) copy-start(bf16[256,4096]{1,0:T(8,128)(2,1)} %k_ref.9) | copy-start | bytes 6291460
  42.6 1.6 %copy-start.5 = (bf16[256,4096]{1,0:T(8,128)(2,1)S(1)}, bf16[256,4096]{1,0:T(8,128)(2,1)}, u32[]{:S(2)}) copy-start(bf16[256,4096]{1,0:T(8,128)(2,1)} %v_ref.9) | copy-start | bytes 6291460
  44.2 6.0 %copy-start.7 = (bf16[256,4096]{1,0:T(8,128)(2,1)S(1)}, bf16[256,4096]{1,0:T(8,128)(2,1)}, u32[]{:S(2)}) copy-start(bf16[256,4096]{1,0:T(8,128)(2,1)} %c_ref.7) | copy-start | bytes 6291460
  44.2 6.0 %copy-start.15 = (f32[4096]{0:T(1024)S(1)}, f32[4096]{0:T(1024)}, u32[]{:S(2)}) copy-start(f32[4096]{0:T(1024)} %param.8) | copy-start | bytes 49156
  53.7 1.3 %copy-start.9 = (f32[256,2048]{1,0:T(8,128)}, f32[256,2048]{1,0:T(8,128)S(1)}, u32[]{:S(2)}) copy-start(f32[256,2048]{1,0:T(8,128)S(1)} %get-tuple-element.36.att_ref) | copy-start | bytes 6291460
  55.0 2.7 %copy-start.11 = (f32[256,128]{1,0:T(8,128)}, f32[256,128]{1,0:T(8,128)S(1)}, u32[]{:S(2)}) copy-start(f32[256,128]{1,0:T(8,128)S(1)} %get-tuple-element.43.rest_2_) | copy-start | bytes 393220
  55.0 2.7 %copy-start.13 = (f32[256,128]{1,0:T(8,128)}, f32[256,128]{1,0:T(8,128)S(1)}, u32[]{:S(2)}) copy-start(f32[256,128]{1,0:T(8,128)S(1)} %get-tuple-element.44.rest_3_) | copy-start | bytes 393220
  57.7 12.2 %collective-permute-start.21 = (bf16[512,128]{1,0:T(8,128)(2,1)}, bf16[512,128]{1,0:T(8,128)(2,1)}, u32[]{:S(2)}, u32[]{:S(2)}) collective-permute-start(bf16[512,128]{1,0:T(8,128)(2,1)} %get-tuple-element.57), channel_id=1, source_target_pairs={{0,4},{4,0},{8,12},{12,8},{16,20},{20,16},{24,28},{28,24},{1,5},{5... | collective-permute-start | bytes 393224 | tf_op jit(solution)/shard_map/ppermute | solution.py:135
  57.9 13.8 %collective-permute-start.22 = (bf16[512,128]{1,0:T(8,128)(2,1)}, bf16[512,128]{1,0:T(8,128)(2,1)}, u32[]{:S(2)}, u32[]{:S(2)}) collective-permute-start(bf16[512,128]{1,0:T(8,128)(2,1)} %get-tuple-element.58), channel_id=1, source_target_pairs={{0,8},{4,12},{8,0},{12,4},{16,24},{20,28},{24,16},{28,20},{1,9},{5... | collective-permute-start | bytes 393224 | tf_op jit(solution)/shard_map/ppermute | solution.py:135
  59.4 12.3 %collective-permute-start.23 = (bf16[512,128]{1,0:T(8,128)(2,1)}, bf16[512,128]{1,0:T(8,128)(2,1)}, u32[]{:S(2)}, u32[]{:S(2)}) collective-permute-start(bf16[512,128]{1,0:T(8,128)(2,1)} %get-tuple-element.59), channel_id=1, source_target_pairs={{0,12},{4,8},{8,4},{12,0},{16,28},{20,24},{24,20},{28,16},{1,13},{... | collective-permute-start | bytes 393224 | tf_op jit(solution)/shard_map/ppermute | solution.py:135
  61.2 1.6 %copy-start.8 = (bf16[256,4096]{1,0:T(8,128)(2,1)S(1)}, bf16[256,4096]{1,0:T(8,128)(2,1)}, u32[]{:S(2)}) copy-start(bf16[256,4096]{1,0:T(8,128)(2,1)} %c_ref.7) | copy-start | bytes 6291460
  62.8 1.6 %copy-start.10 = (f32[256,2048]{1,0:T(8,128)S(1)}, f32[256,2048]{1,0:T(8,128)}, u32[]{:S(2)}) copy-start(f32[256,2048]{1,0:T(8,128)} %copy-done.9) | copy-start | bytes 6291460
  64.4 0.9 copy-start.12
  65.3 0.9 copy-start.14
  66.2 24.4 %copy-start.6 = (bf16[256,4096]{1,0:T(8,128)(2,1)S(1)}, bf16[256,4096]{1,0:T(8,128)(2,1)}, u32[]{:S(2)}) copy-start(bf16[256,4096]{1,0:T(8,128)(2,1)} %v_ref.9) | copy-start | bytes 6291460
  68.2 22.5 %copy-start.3 = (bf16[256,4096]{1,0:T(8,128)(2,1)S(1)}, bf16[256,4096]{1,0:T(8,128)(2,1)}, u32[]{:S(2)}) copy-start(bf16[256,4096]{1,0:T(8,128)(2,1)} %k_ref.9) | copy-start | bytes 6291460
  68.2 6.0 %collective-permute-start.14 = (bf16[512,128]{1,0:T(8,128)(2,1)S(1)}, bf16[512,128]{1,0:T(8,128)(2,1)S(1)}, u32[]{:S(2)}, u32[]{:S(2)}) collective-permute-start(bf16[512,128]{1,0:T(8,128)(2,1)S(1)} %get-tuple-element.49), channel_id=1, source_target_pairs={{0,4},{4,0},{8,12},{12,8},{16,20},{20,16},{24,28},{28,24},{1,5},{5... | collective-permute-start | bytes 393224 | tf_op jit(solution)/shard_map/ppermute | solution.py:135
  68.5 5.7 %collective-permute-start.15 = (bf16[512,128]{1,0:T(8,128)(2,1)S(1)}, bf16[512,128]{1,0:T(8,128)(2,1)S(1)}, u32[]{:S(2)}, u32[]{:S(2)}) collective-permute-start(bf16[512,128]{1,0:T(8,128)(2,1)S(1)} %get-tuple-element.50), channel_id=1, source_target_pairs={{0,8},{4,12},{8,0},{12,4},{16,24},{20,28},{24,16},{28,20},{1,9},{5... | collective-permute-start | bytes 393224 | tf_op jit(solution)/shard_map/ppermute | solution.py:135
  70.0 7.7 %collective-permute-start.16 = (bf16[512,128]{1,0:T(8,128)(2,1)S(1)}, bf16[512,128]{1,0:T(8,128)(2,1)S(1)}, u32[]{:S(2)}, u32[]{:S(2)}) collective-permute-start(bf16[512,128]{1,0:T(8,128)(2,1)S(1)} %get-tuple-element.51), channel_id=1, source_target_pairs={{0,12},{4,8},{8,4},{12,0},{16,28},{20,24},{24,20},{28,16},{1,13},{... | collective-permute-start | bytes 393224 | tf_op jit(solution)/shard_map/ppermute | solution.py:135
  72.8 8.5 %collective-permute-start.24 = (bf16[512,128]{1,0:T(8,128)(2,1)S(1)}, bf16[512,128]{1,0:T(8,128)(2,1)S(1)}, u32[]{:S(2)}, u32[]{:S(2)}) collective-permute-start(bf16[512,128]{1,0:T(8,128)(2,1)S(1)} %fusion.51), channel_id=1, source_target_pairs={{16,0},{20,4},{24,8},{28,12},{17,1},{21,5},{25,9},{29,13},{18,2},{... | collective-permute-start | bytes 393224 | tf_op jit(solution)/shard_map/ppermute | solution.py:148
  77.7 9.0 %collective-permute-start.17 = (bf16[512,128]{1,0:T(8,128)(2,1)S(1)}, bf16[512,128]{1,0:T(8,128)(2,1)S(1)}, u32[]{:S(2)}, u32[]{:S(2)}) collective-permute-start(bf16[512,128]{1,0:T(8,128)(2,1)S(1)} %fusion.38), channel_id=1, source_target_pairs={{16,0},{20,4},{24,8},{28,12},{17,1},{21,5},{25,9},{29,13},{18,2},{... | collective-permute-start | bytes 393224 | tf_op jit(solution)/shard_map/ppermute | solution.py:148
  82.7 6.9 %collective-permute-start.25 = (bf16[512,128]{1,0:T(8,128)(2,1)S(1)}, bf16[512,128]{1,0:T(8,128)(2,1)S(1)}, u32[]{:S(2)}, u32[]{:S(2)}) collective-permute-start(bf16[512,128]{1,0:T(8,128)(2,1)S(1)} %get-tuple-element.63), channel_id=1, source_target_pairs={{0,4},{4,0},{8,12},{12,8},{16,20},{20,16},{24,28},{28,24},{1,5},{5... | collective-permute-start | bytes 393224 | tf_op jit(solution)/shard_map/ppermute | solution.py:135
  83.1 16.0 %collective-permute-start.26 = (bf16[512,128]{1,0:T(8,128)(2,1)S(1)}, bf16[512,128]{1,0:T(8,128)(2,1)S(1)}, u32[]{:S(2)}, u32[]{:S(2)}) collective-permute-start(bf16[512,128]{1,0:T(8,128)(2,1)S(1)} %get-tuple-element.65), channel_id=1, source_target_pairs={{0,8},{4,12},{8,0},{12,4},{16,24},{20,28},{24,16},{28,20},{1,9},{5... | collective-permute-start | bytes 393224 | tf_op jit(solution)/shard_map/ppermute | solution.py:135
  85.8 13.4 %collective-permute-start.27 = (bf16[512,128]{1,0:T(8,128)(2,1)S(1)}, bf16[512,128]{1,0:T(8,128)(2,1)S(1)}, u32[]{:S(2)}, u32[]{:S(2)}) collective-permute-start(bf16[512,128]{1,0:T(8,128)(2,1)S(1)} %get-tuple-element.62), channel_id=1, source_target_pairs={{0,12},{4,8},{8,4},{12,0},{16,28},{20,24},{24,20},{28,16},{1,13},{... | collective-permute-start | bytes 393224 | tf_op jit(solution)/shard_map/ppermute | solution.py:135
  87.1 15.2 %collective-permute-start.18 = (bf16[512,128]{1,0:T(8,128)(2,1)S(1)}, bf16[512,128]{1,0:T(8,128)(2,1)S(1)}, u32[]{:S(2)}, u32[]{:S(2)}) collective-permute-start(bf16[512,128]{1,0:T(8,128)(2,1)S(1)} %get-tuple-element.67), channel_id=1, source_target_pairs={{0,4},{4,0},{8,12},{12,8},{16,20},{20,16},{24,28},{28,24},{1,5},{5... | collective-permute-start | bytes 393224 | tf_op jit(solution)/shard_map/ppermute | solution.py:135
  87.7 14.5 %collective-permute-start.19 = (bf16[512,128]{1,0:T(8,128)(2,1)S(1)}, bf16[512,128]{1,0:T(8,128)(2,1)S(1)}, u32[]{:S(2)}, u32[]{:S(2)}) collective-permute-start(bf16[512,128]{1,0:T(8,128)(2,1)S(1)} %get-tuple-element.69), channel_id=1, source_target_pairs={{0,8},{4,12},{8,0},{12,4},{16,24},{20,28},{24,16},{28,20},{1,9},{5... | collective-permute-start | bytes 393224 | tf_op jit(solution)/shard_map/ppermute | solution.py:135
  89.6 12.6 %collective-permute-start.20 = (bf16[512,128]{1,0:T(8,128)(2,1)S(1)}, bf16[512,128]{1,0:T(8,128)(2,1)S(1)}, u32[]{:S(2)}, u32[]{:S(2)}) collective-permute-start(bf16[512,128]{1,0:T(8,128)(2,1)S(1)} %get-tuple-element.66), channel_id=1, source_target_pairs={{0,12},{4,8},{8,4},{12,0},{16,28},{20,24},{24,20},{28,16},{1,13},{... | collective-permute-start | bytes 393224 | tf_op jit(solution)/shard_map/ppermute | solution.py:135

commit v2 on v1

--- a/solution.py
+++ b/solution.py
@@ -159,11 +159,13 @@
     return run
 
 
-def spread(states, n, member, forward):
+def spread(states, n, member, forward, filler):
     m = len(states)
     got = exchange(states, n)
+    got, first = lax.optimization_barrier((got, filler[0]))
     got = [x.astype(F32) for x in got]
     carry = carry_groups(sum(got), n, m, forward)
+    carry, second = lax.optimization_barrier((carry, filler[1]))
     back = []
     for j in range(m):
         target = member ^ j
@@ -178,11 +180,14 @@
         if acc is None:
             acc = jnp.zeros_like(got[0])
         back.append(acc.astype(BF16))
-    return exchange(back, n)
+    return exchange(back, n), first, second
 
 
 def shards(n, queries, keys, values, gain, cotangent):
     rows, width = queries.shape
+    queries, keys, values, cotangent = (
+        pltpu.with_memory_space_constraint(x, pltpu.HBM) for x in (queries, keys, values, cotangent)
+    )
     m = 4 if n % 4 == 0 else (2 if n % 2 == 0 else 1)
     part = width // (CHUNKS * m)
     half = width // CHUNKS
@@ -220,29 +225,37 @@
         return call(partial(state_kernel, heads), (a, b), [cols(c), cols(c)], [whole_state] * m, [state] * m,
                     unit, 4 * rows * half + 2 * DH * half)
 
-    plain = pl.BlockSpec((rows, part), lambda j: (0, j))
-
-    def grid_call(kernel, args, outs, flops, nbytes):
+    state_parts = [states_of(c, keys, values) for c in range(CHUNKS)]
+
+    def on_half(kernel, c, args, own_args, outs):
+        col = pl.BlockSpec((rows, part), lambda j: (0, c * m + j))
+        own = pl.BlockSpec((rows, part), lambda j: (0, j))
         return pl.pallas_call(
-            kernel,
-            grid=(width // part,),
-            in_specs=[plain] * len(args),
-            out_specs=[plain] * outs,
-            out_shape=[jax.ShapeDtypeStruct((rows, width), F32)] * outs,
+            partial(kernel, heads),
+            grid=(m,),
+            in_specs=[col] * len(args) + [own] * len(own_args),
+            out_specs=[own] * outs,
+            out_shape=[jax.ShapeDtypeStruct((rows, half), F32)] * outs,
             compiler_params=pltpu.CompilerParams(dimension_semantics=("arbitrary",), vmem_limit_bytes=24 << 20),
-            cost_estimate=pl.CostEstimate(flops=flops, bytes_accessed=nbytes, transcendentals=0),
-        )(*args)
-
-    state_parts = [states_of(c, keys, values) for c in range(CHUNKS)]
-    prefix = [spread(s, n, member, True) for s in state_parts]
-    (local,) = grid_call(partial(local_kernel, heads), (queries, keys, values), 1, 8 * unit, 10 * rows * width)
+            cost_estimate=pl.CostEstimate(
+                flops=4 * unit * outs, bytes_accessed=8 * rows * half * outs, transcendentals=0
+            ),
+        )(*args, *own_args)
+
+    local = [on_half(local_kernel, c, (queries, keys, values), (), 1) for c in range(CHUNKS)]
+    prefix = []
+    for c in range(CHUNKS):
+        filler = ((local[0], []), ([], local[1]))[c]
+        pre, first, second = spread(state_parts[c], n, member, True, filler)
+        local[c] = (first, second)[c]
+        prefix.append(pre)
 
     attended, sums = [], []
     for c in range(CHUNKS):
         att, ss, sc = call(
             partial(attend_kernel, heads),
-            (queries, local, cotangent, gain2, *prefix[c]),
-            [cols(c), cols(c), cols(c), cols(c, 1)] + [whole_state] * m,
+            (queries, *local[c], cotangent, gain2, *prefix[c]),
+            [cols(c), cols_half(), cols(c), cols(c, 1)] + [whole_state] * m,
             [cols_half(), whole_stat, whole_stat],
             [jax.ShapeDtypeStruct((rows, half), F32), stat, stat],
             unit, 12 * rows * half,
@@ -264,21 +277,13 @@
         grads.append(g)
         grad_parts.append(parts)
 
-    suffix = [spread(s, n, member, False) for s in grad_parts]
-    blocks = half // part
-    local_grads = []
-    for c in range(CHUNKS):
-        col = pl.BlockSpec((rows, part), lambda j, c=c: (0, c * blocks + j))
-        own = pl.BlockSpec((rows, part), lambda j: (0, j))
-        local_grads.append(pl.pallas_call(
-            partial(back_local_kernel, heads),
-            grid=(blocks,),
-            in_specs=[col, col, col, own],
-            out_specs=[own, own],
-            out_shape=[jax.ShapeDtypeStruct((rows, half), F32)] * 2,
-            compiler_params=pltpu.CompilerParams(dimension_semantics=("arbitrary",), vmem_limit_bytes=24 << 20),
-            cost_estimate=pl.CostEstimate(flops=8 * unit, bytes_accessed=16 * rows * half, transcendentals=0),
-        )(queries, keys, values, grads[c]))
+    local_grads = [on_half(back_local_kernel, c, (queries, keys, values), (grads[c],), 2) for c in range(CHUNKS)]
+    suffix = []
+    for c in range(CHUNKS):
+        filler = ((local_grads[0], []), ([], local_grads[1]))[c]
+        suf, first, second = spread(grad_parts[c], n, member, False, filler)
+        local_grads[c] = (first, second)[c]
+        suffix.append(suf)
 
     outs = ()
     out_shape = [jax.ShapeDtypeStruct((rows, width), BF16)] * 2

time: 106 us -> 116 us (1.094)
  Pallas kernels: 31.3 us -> 47.7 us
  local copies, waits for them, and re-layouts: 12.7 us -> 3.13 us
  waiting for transfers between devices: 8.76 us -> 17.6 us
  starting transfers between devices: 46.1 us -> 42.4 us
  other arithmetic: 5.44 us -> 3.33 us
    pallas_call x8, Pallas kernels: 16.8 us -> 28.5 us  [call(): pl.pallas_call(kernel, out_shape=out_shape, grid_spec=pltpu.PrefetchScala...]
    unnamed x32 -> x18, local copies, waits for them, and re-layouts: 12.7 us -> 3.13 us
    ppermute x4, waiting for transfers between devices: 2.69 us -> 10.2 us  [shift(): return lax.ppermute(x, 'seq', perm)]
    pallas_call x3 -> x4, Pallas kernels: 14.5 us -> 19.2 us  [on_half(): pl.pallas_call(partial(kernel, heads), grid=(m,), in_specs=[col] * len(ar...]
    ppermute x24, starting transfers between devices: 35.5 us -> 33.5 us  [exchange(): out[j] = lax.ppermute(parts[j], 'seq', perm)]
    ppermute x4, starting transfers between devices: 10.5 us -> 8.97 us  [shift(): return lax.ppermute(x, 'seq', perm)]
    ppermute x24, waiting for transfers between devices: 6.06 us -> 7.39 us  [exchange(): out[j] = lax.ppermute(parts[j], 'seq', perm)]
  transfers between devices with their start and end apart: 28 -> 28, of which waited for: 4 -> 7; matrix products, arithmetic and copies ran while one was open for 5% -> 3% of each run, Pallas kernels for 21% -> 29%
where the time goes in v2:
time: 116 us; the launch traced here: 115 us
  Pallas kernels  47.7 us (41%)
  starting transfers between devices  42.4 us (37%)
  waiting for transfers between devices  17.6 us (15%)
  other arithmetic  3.33 us (3%)
  local copies, waits for them, and re-layouts  3.13 us (3%)
    ppermute x24, starting transfers between devices, exchange(): out[j] = lax.ppermute(parts[j], 'seq', perm)  33.5 us
    pallas_call x8, Pallas kernels, call(): pl.pallas_call(kernel, out_shape=out_shape, grid_spec=pltpu.PrefetchScala...  28.5 us
    pallas_call x4, Pallas kernels, on_half(): pl.pallas_call(partial(kernel, heads), grid=(m,), in_specs=[col] * len(ar...  19.2 us
    ppermute x4, waiting for transfers between devices, shift(): return lax.ppermute(x, 'seq', perm)  10.2 us
    ppermute x4, starting transfers between devices, shift(): return lax.ppermute(x, 'seq', perm)  8.97 us
    ppermute x24, waiting for transfers between devices, exchange(): out[j] = lax.ppermute(parts[j], 'seq', perm)  7.39 us
    unnamed x18, local copies, waits for them, and re-layouts  3.13 us
  transfers between devices with their start and end apart: 28, of which 7 were waited for; matrix products, arithmetic and copies ran while one was open for 3% of the time, Pallas kernels for 29%

profile of v2, /device:TPU:0, one launch (start us, length us, event | category | flops | bytes accessed | tf_op | source)
XLA Modules:
  0.0 115.2 jit_solution(11618225964420562297)
XLA Ops:
  0.6 3.0 %shard_map.68 = (bf16[512,128]{1,0:T(8,128)(2,1)S(1)}, bf16[512,128]{1,0:T(8,128)(2,1)S(1)}, bf16[512,128]{1,0:T(8,128)(2,1)S(1)}, bf16[512,128]{1,0:T(8,128)(2,1)S(1)}) custom-call(s32[1]{0:T(128)} %bitcast.m_ref, bf16[256,4096]{1,0:T(8,128)(2,1)} %k_ref.11, bf16[256,4096]{1,0:T(8,128)(2,1)} %v_ref.11), custom_call_target="tpu_custom_call" | custom-call | flops 134217728 | bytes 2621440 | tf_op jit(solution)/shard_map/pallas_call | solution.py:211
  3.7 3.0 %collective-permute-start = (bf16[512,128]{1,0:T(8,128)(2,1)S(1)}, bf16[512,128]{1,0:T(8,128)(2,1)S(1)}, u32[]{:S(2)}, u32[]{:S(2)}) collective-permute-start(bf16[512,128]{1,0:T(8,128)(2,1)S(1)} %get-tuple-element.57), channel_id=1, source_target_pairs={{0,4},{4,0},{8,12},{12,8},{16,20},{20,16},{24,28},{28,24},{1,5},{5... | collective-permute-start | bytes 393224 | tf_op jit(solution)/shard_map/ppermute | solution.py:135
  6.7 1.6 %collective-permute-start.1 = (bf16[512,128]{1,0:T(8,128)(2,1)S(1)}, bf16[512,128]{1,0:T(8,128)(2,1)S(1)}, u32[]{:S(2)}, u32[]{:S(2)}) collective-permute-start(bf16[512,128]{1,0:T(8,128)(2,1)S(1)} %get-tuple-element.58), channel_id=1, source_target_pairs={{0,8},{4,12},{8,0},{12,4},{16,24},{20,28},{24,16},{28,20},{1,9},{5... | collective-permute-start | bytes 393224 | tf_op jit(solution)/shard_map/ppermute | solution.py:135
  8.2 3.0 %shard_map.71 = (bf16[512,128]{1,0:T(8,128)(2,1)S(1)}, bf16[512,128]{1,0:T(8,128)(2,1)S(1)}, bf16[512,128]{1,0:T(8,128)(2,1)S(1)}, bf16[512,128]{1,0:T(8,128)(2,1)S(1)}) custom-call(s32[1]{0:T(128)} %bitcast.m_ref, bf16[256,4096]{1,0:T(8,128)(2,1)} %k_ref.11, bf16[256,4096]{1,0:T(8,128)(2,1)} %v_ref.11), custom_call_target="tpu_custom_call" | custom-call | flops 134217728 | bytes 2621440 | tf_op jit(solution)/shard_map/pallas_call | solution.py:211
  11.2 2.0 %collective-permute-start.7 = (bf16[512,128]{1,0:T(8,128)(2,1)S(1)}, bf16[512,128]{1,0:T(8,128)(2,1)S(1)}, u32[]{:S(2)}, u32[]{:S(2)}) collective-permute-start(bf16[512,128]{1,0:T(8,128)(2,1)S(1)} %get-tuple-element.68), channel_id=1, source_target_pairs={{0,4},{4,0},{8,12},{12,8},{16,20},{20,16},{24,28},{28,24},{1,5},{5... | collective-permute-start | bytes 393224 | tf_op jit(solution)/shard_map/ppermute | solution.py:135
  13.2 1.6 %collective-permute-start.8 = (bf16[512,128]{1,0:T(8,128)(2,1)S(1)}, bf16[512,128]{1,0:T(8,128)(2,1)S(1)}, u32[]{:S(2)}, u32[]{:S(2)}) collective-permute-start(bf16[512,128]{1,0:T(8,128)(2,1)S(1)} %get-tuple-element.69), channel_id=1, source_target_pairs={{0,8},{4,12},{8,0},{12,4},{16,24},{20,28},{24,16},{28,20},{1,9},{5... | collective-permute-start | bytes 393224 | tf_op jit(solution)/shard_map/ppermute | solution.py:135
  14.8 4.3 %shard_map.72.loc_ref = f32[256,2048]{1,0:T(8,128)S(1)} custom-call(bf16[256,4096]{1,0:T(8,128)(2,1)} %q_ref.15, bf16[256,4096]{1,0:T(8,128)(2,1)} %k_ref.11, bf16[256,4096]{1,0:T(8,128)(2,1)} %v_ref.11), custom_call_target="tpu_custom_call" | custom-call | flops 536870912 | bytes 4194304 | tf_op jit(solution)/shard_map/pallas_call | solution.py:233
  19.2 4.4 %shard_map.69.loc_ref = f32[256,2048]{1,0:T(8,128)S(1)} custom-call(bf16[256,4096]{1,0:T(8,128)(2,1)} %q_ref.15, bf16[256,4096]{1,0:T(8,128)(2,1)} %k_ref.11, bf16[256,4096]{1,0:T(8,128)(2,1)} %v_ref.11), custom_call_target="tpu_custom_call" | custom-call | flops 536870912 | bytes 4194304 | tf_op jit(solution)/shard_map/pallas_call | solution.py:233
  23.7 4.9 %collective-permute-start.10 = (bf16[512,128]{1,0:T(8,128)(2,1)S(1)}, bf16[512,128]{1,0:T(8,128)(2,1)S(1)}, u32[]{:S(2)}, u32[]{:S(2)}) collective-permute-start(bf16[512,128]{1,0:T(8,128)(2,1)S(1)} %fusion.33), channel_id=1, source_target_pairs={{0,16},{4,20},{8,24},{12,28},{1,17},{5,21},{9,25},{13,29},{2,18},{... | collective-permute-start | bytes 393224 | tf_op jit(solution)/shard_map/ppermute | solution.py:148
  28.7 1.3 %collective-permute-start.3 = (bf16[512,128]{1,0:T(8,128)(2,1)S(1)}, bf16[512,128]{1,0:T(8,128)(2,1)S(1)}, u32[]{:S(2)}, u32[]{:S(2)}) collective-permute-start(bf16[512,128]{1,0:T(8,128)(2,1)S(1)} %fusion.16), channel_id=1, source_target_pairs={{0,16},{4,20},{8,24},{12,28},{1,17},{5,21},{9,25},{13,29},{2,18},{... | collective-permute-start | bytes 393224 | tf_op jit(solution)/shard_map/ppermute | solution.py:148
  30.0 1.1 collective-permute-done.10
  31.1 0.3 fusion.28
  31.4 6.7 %collective-permute-start.13 = (bf16[512,128]{1,0:T(8,128)(2,1)S(1)}, bf16[512,128]{1,0:T(8,128)(2,1)S(1)}, u32[]{:S(2)}, u32[]{:S(2)}) collective-permute-start(bf16[512,128]{1,0:T(8,128)(2,1)S(1)} %get-tuple-element.118), channel_id=1, source_target_pairs={{0,12},{4,8},{8,4},{12,0},{16,28},{20,24},{24,20},{28,16},{1,13},{... | collective-permute-start | bytes 393224 | tf_op jit(solution)/shard_map/ppermute | solution.py:135
  38.1 0.6 collective-permute-start.11
  38.8 0.3 fusion.11
  39.1 2.9 %collective-permute-start.6 = (bf16[512,128]{1,0:T(8,128)(2,1)S(1)}, bf16[512,128]{1,0:T(8,128)(2,1)S(1)}, u32[]{:S(2)}, u32[]{:S(2)}) collective-permute-start(bf16[512,128]{1,0:T(8,128)(2,1)S(1)} %get-tuple-element.122), channel_id=1, source_target_pairs={{0,12},{4,8},{8,4},{12,0},{16,28},{20,24},{24,20},{28,16},{1,13},{... | collective-permute-start | bytes 393224 | tf_op jit(solution)/shard_map/ppermute | solution.py:135
  42.0 0.4 collective-permute-done.13.rest_3_
  42.7 2.2 %collective-permute-done.12.rest_2_ = bf16[512,128]{1,0:T(8,128)(2,1)S(1)} collective-permute-done((bf16[512,128]{1,0:T(8,128)(2,1)S(1)}, bf16[512,128]{1,0:T(8,128)(2,1)S(1)}, u32[]{:S(2)}, u32[]{:S(2)}) %collective-permute-start.12) | collective-permute-done | bytes 131104 | tf_op jit(solution)/shard_map/ppermute | solution.py:135
  44.8 2.5 %collective-permute-done.11.rest_1_ = bf16[512,128]{1,0:T(8,128)(2,1)S(1)} collective-permute-done((bf16[512,128]{1,0:T(8,128)(2,1)S(1)}, bf16[512,128]{1,0:T(8,128)(2,1)S(1)}, u32[]{:S(2)}, u32[]{:S(2)}) %collective-permute-start.11) | collective-permute-done | bytes 131104 | tf_op jit(solution)/shard_map/ppermute | solution.py:135
  47.4 3.1 %shard_map.73 = (f32[256,2048]{1,0:T(8,128)S(1)}, f32[256,128]{1,0:T(8,128)S(1)}, f32[256,128]{1,0:T(8,128)S(1)}) custom-call(s32[1]{0:T(128)} %bitcast.m_ref, bf16[256,4096]{1,0:T(8,128)(2,1)} %q_ref.15, f32[256,2048]{1,0:T(8,128)S(1)} %shard_map.72.loc_ref, bf16[256,4096]{1,0:T(8,128)(2,1)} %c_ref.7, f32[1,4096]{1,0:T(1,128)S(1)} %bitcast.2, ...), custom_call_target="tpu_custom_call" | custom-call | flops 134217728 | bytes 6291456 | tf_op jit(solution)/shard_map/pallas_call | solution.py:211
  50.5 3.2 %shard_map.70 = (f32[256,2048]{1,0:T(8,128)S(1)}, f32[256,128]{1,0:T(8,128)S(1)}, f32[256,128]{1,0:T(8,128)S(1)}) custom-call(s32[1]{0:T(128)} %bitcast.m_ref, bf16[256,4096]{1,0:T(8,128)(2,1)} %q_ref.15, f32[256,2048]{1,0:T(8,128)S(1)} %shard_map.69.loc_ref, bf16[256,4096]{1,0:T(8,128)(2,1)} %c_ref.7, f32[1,4096]{1,0:T(1,128)S(1)} %bitcast.3, ...), custom_call_target="tpu_custom_call" | custom-call | flops 134217728 | bytes 6291456 | tf_op jit(solution)/shard_map/pallas_call | solution.py:211
  53.8 4.1 %shard_map.74 = (bf16[256,2048]{1,0:T(8,128)(2,1)S(1)}, bf16[512,128]{1,0:T(8,128)(2,1)S(1)}, bf16[512,128]{1,0:T(8,128)(2,1)}, bf16[512,128]{1,0:T(8,128)(2,1)S(1)}, bf16[512,128]{1,0:T(8,128)(2,1)S(1)}) custom-call(s32[1]{0:T(128)} %bitcast.m_ref, bf16[256,4096]{1,0:T(8,128)(2,1)} %q_ref.15, f32[256,2048]{1,0:T(8,128)S(1)} %get-tuple-element.66.att_ref, ...), custom_call_target="tpu_custom_call" | custom-call | flops 134217728 | bytes 5242880 | tf_op jit(solution)/shard_map/pallas_call | solution.py:211
  57.9 0.6 copy-done.5
  58.5 0.6 copy-done.7
  59.4 0.9 copy-done.1
  60.3 0.9 copy-done.3
  61.2 3.4 %shard_map.76 = (bf16[256,2048]{1,0:T(8,128)(2,1)S(1)}, bf16[512,128]{1,0:T(8,128)(2,1)S(1)}, bf16[512,128]{1,0:T(8,128)(2,1)S(1)}, bf16[512,128]{1,0:T(8,128)(2,1)S(1)}, bf16[512,128]{1,0:T(8,128)(2,1)S(1)}) custom-call(s32[1]{0:T(128)} %bitcast.m_ref, bf16[256,4096]{1,0:T(8,128)(2,1)} %q_ref.15, f32[256,2048]{1,0:T(8,128)S(1)} %get-tuple-element.94.att_ref, ...), custom_call_target="tpu_custom_call" | custom-call | flops 134217728 | bytes 5242880 | tf_op jit(solution)/shard_map/pallas_call | solution.py:211
  64.6 1.9 %collective-permute-start.21 = (bf16[512,128]{1,0:T(8,128)(2,1)S(1)}, bf16[512,128]{1,0:T(8,128)(2,1)S(1)}, u32[]{:S(2)}, u32[]{:S(2)}) collective-permute-start(bf16[512,128]{1,0:T(8,128)(2,1)S(1)} %get-tuple-element.96), channel_id=1, source_target_pairs={{0,4},{4,0},{8,12},{12,8},{16,20},{20,16},{24,28},{28,24},{1,5},{5... | collective-permute-start | bytes 393224 | tf_op jit(solution)/shard_map/ppermute | solution.py:135
  66.5 2.1 %collective-permute-start.22 = (bf16[512,128]{1,0:T(8,128)(2,1)S(1)}, bf16[512,128]{1,0:T(8,128)(2,1)S(1)}, u32[]{:S(2)}, u32[]{:S(2)}) collective-permute-start(bf16[512,128]{1,0:T(8,128)(2,1)S(1)} %get-tuple-element.97), channel_id=1, source_target_pairs={{0,8},{4,12},{8,0},{12,4},{16,24},{20,28},{24,16},{28,20},{1,9},{5... | collective-permute-start | bytes 393224 | tf_op jit(solution)/shard_map/ppermute | solution.py:135
  68.7 2.0 %collective-permute-start.15 = (bf16[512,128]{1,0:T(8,128)(2,1)S(1)}, bf16[512,128]{1,0:T(8,128)(2,1)S(1)}, u32[]{:S(2)}, u32[]{:S(2)}) collective-permute-start(bf16[512,128]{1,0:T(8,128)(2,1)S(1)} %copy-done.8), channel_id=1, source_target_pairs={{0,8},{4,12},{8,0},{12,4},{16,24},{20,28},{24,16},{28,20},{1,9},{5... | collective-permute-start | bytes 393224 | tf_op jit(solution)/shard_map/ppermute | solution.py:135
  70.7 0.9 collective-permute-start.16
  71.6 5.2 %shard_map.77 = (f32[256,2048]{1,0:T(8,128)S(1)}, f32[256,2048]{1,0:T(8,128)S(1)}) custom-call(bf16[256,4096]{1,0:T(8,128)(2,1)} %q_ref.15, bf16[256,4096]{1,0:T(8,128)(2,1)} %k_ref.11, bf16[256,4096]{1,0:T(8,128)(2,1)} %v_ref.11, bf16[256,2048]{1,0:T(8,128)(2,1)S(1)} %get-tuple-element.99.g_ref), custom_call_target="tpu_custom_call" | custom-call | flops 1073741824 | bytes 8388608 | tf_op jit(solution)/shard_map/pallas_call | solution.py:233
  76.9 5.3 %shard_map.75 = (f32[256,2048]{1,0:T(8,128)S(1)}, f32[256,2048]{1,0:T(8,128)S(1)}) custom-call(bf16[256,4096]{1,0:T(8,128)(2,1)} %q_ref.15, bf16[256,4096]{1,0:T(8,128)(2,1)} %k_ref.11, bf16[256,4096]{1,0:T(8,128)(2,1)} %v_ref.11, bf16[256,2048]{1,0:T(8,128)(2,1)S(1)} %get-tuple-element.88.g_ref), custom_call_target="tpu_custom_call" | custom-call | flops 1073741824 | bytes 8388608 | tf_op jit(solution)/shard_map/pallas_call | solution.py:233
  82.3 1.3 %collective-permute-start.24 = (bf16[512,128]{1,0:T(8,128)(2,1)S(1)}, bf16[512,128]{1,0:T(8,128)(2,1)S(1)}, u32[]{:S(2)}, u32[]{:S(2)}) collective-permute-start(bf16[512,128]{1,0:T(8,128)(2,1)S(1)} %fusion.67), channel_id=1, source_target_pairs={{16,0},{20,4},{24,8},{28,12},{17,1},{21,5},{25,9},{29,13},{18,2},{... | collective-permute-start | bytes 393224 | tf_op jit(solution)/shard_map/ppermute | solution.py:148
  83.6 1.0 fusion.50
  84.6 1.5 %collective-permute-start.17 = (bf16[512,128]{1,0:T(8,128)(2,1)S(1)}, bf16[512,128]{1,0:T(8,128)(2,1)S(1)}, u32[]{:S(2)}, u32[]{:S(2)}) collective-permute-start(bf16[512,128]{1,0:T(8,128)(2,1)S(1)} %fusion.50), channel_id=1, source_target_pairs={{16,0},{20,4},{24,8},{28,12},{17,1},{21,5},{25,9},{29,13},{18,2},{... | collective-permute-start | bytes 393224 | tf_op jit(solution)/shard_map/ppermute | solution.py:148
  86.0 9.1 %collective-permute-done.24 = bf16[512,128]{1,0:T(8,128)(2,1)S(1)} collective-permute-done((bf16[512,128]{1,0:T(8,128)(2,1)S(1)}, bf16[512,128]{1,0:T(8,128)(2,1)S(1)}, u32[]{:S(2)}, u32[]{:S(2)}) %collective-permute-start.24) | collective-permute-done | bytes 131104 | tf_op jit(solution)/shard_map/ppermute | solution.py:148
  95.2 0.3 fusion.62
  95.5 3.1 %collective-permute-start.26 = (bf16[512,128]{1,0:T(8,128)(2,1)S(1)}, bf16[512,128]{1,0:T(8,128)(2,1)S(1)}, u32[]{:S(2)}, u32[]{:S(2)}) collective-permute-start(bf16[512,128]{1,0:T(8,128)(2,1)S(1)} %get-tuple-element.111), channel_id=1, source_target_pairs={{0,8},{4,12},{8,0},{12,4},{16,24},{20,28},{24,16},{28,20},{1,9},{5... | collective-permute-start | bytes 393224 | tf_op jit(solution)/shard_map/ppermute | solution.py:135
  98.6 0.4 collective-permute-start.25
  99.0 1.2 %fusion.45 = (bf16[512,128]{1,0:T(8,128)(2,1)S(1)}, bf16[512,128]{1,0:T(8,128)(2,1)S(1)}, bf16[512,128]{1,0:T(8,128)(2,1)S(1)}, bf16[512,128]{1,0:T(8,128)(2,1)S(1)}) fusion(f32[512,128]{1,0:T(8,128)S(1)} %convert_element_type.145, bf16[512,128]{1,0:T(8,128)(2,1)S(1)} %get-tuple-element.84, bf16[512,128]{1,0:T(8,128)(2,1)} %collective-permute-done.14, ...), kind=kLoop, calls=%fused_computation.105 | loop fusion | flops 2097152 | bytes 1310732 | tf_op jit(solution)/shard_map/convert_element_type | solution.py:182
  100.2 1.1 collective-permute-start.20
  101.4 2.0 %collective-permute-start.19 = (bf16[512,128]{1,0:T(8,128)(2,1)S(1)}, bf16[512,128]{1,0:T(8,128)(2,1)S(1)}, u32[]{:S(2)}, u32[]{:S(2)}) collective-permute-start(bf16[512,128]{1,0:T(8,128)(2,1)S(1)} %get-tuple-element.115), channel_id=1, source_target_pairs={{0,8},{4,12},{8,0},{12,4},{16,24},{20,28},{24,16},{28,20},{1,9},{5... | collective-permute-start | bytes 393224 | tf_op jit(solution)/shard_map/ppermute | solution.py:135
  103.4 0.9 collective-permute-start.18
  104.3 1.3 %collective-permute-done.26.rest_2_ = bf16[512,128]{1,0:T(8,128)(2,1)S(1)} collective-permute-done((bf16[512,128]{1,0:T(8,128)(2,1)S(1)}, bf16[512,128]{1,0:T(8,128)(2,1)S(1)}, u32[]{:S(2)}, u32[]{:S(2)}) %collective-permute-start.26) | collective-permute-done | bytes 131104 | tf_op jit(solution)/shard_map/ppermute | solution.py:135
  105.6 0.9 collective-permute-done.25.rest_1_
  106.5 4.3 %shard_map.78 = (bf16[256,4096]{1,0:T(8,128)(2,1)}, bf16[256,4096]{1,0:T(8,128)(2,1)}) custom-call(s32[1]{0:T(128)} %bitcast.m_ref, bf16[256,4096]{1,0:T(8,128)(2,1)} %k_ref.11, bf16[256,4096]{1,0:T(8,128)(2,1)} %v_ref.11, f32[256,2048]{1,0:T(8,128)S(1)} %get-tuple-element.102.kl_ref, f32[256,2048]{1,0:T(8,128)S(1)} %get-tuple-element.103.vl_ref, ...), custom_call_target="tpu_custom_call" | custom-call | flops 268435456 | bytes 8388608 | tf_op jit(solution)/shard_map/pallas_call | solution.py:211
  110.8 4.3 %shard_map.79 = (bf16[256,4096]{1,0:T(8,128)(2,1)}, bf16[256,4096]{1,0:T(8,128)(2,1)}) custom-call(s32[1]{0:T(128)} %bitcast.m_ref, bf16[256,4096]{1,0:T(8,128)(2,1)} %k_ref.11, bf16[256,4096]{1,0:T(8,128)(2,1)} %v_ref.11, f32[256,2048]{1,0:T(8,128)S(1)} %get-tuple-element.91.kl_ref, ...), custom_call_target="tpu_custom_call", output_to_operand_aliasing={{0}: (9, {}), {1}: (10, {})} | custom-call | flops 268435456 | bytes 8388608 | tf_op jit(solution)/shard_map/pallas_call | solution.py:211
  (50 shorter events, 1.0 us)
Async XLA Ops:
  3.7 11.1 %collective-permute-start = (bf16[512,128]{1,0:T(8,128)(2,1)S(1)}, bf16[512,128]{1,0:T(8,128)(2,1)S(1)}, u32[]{:S(2)}, u32[]{:S(2)}) collective-permute-start(bf16[512,128]{1,0:T(8,128)(2,1)S(1)} %get-tuple-element.57), channel_id=1, source_target_pairs={{0,4},{4,0},{8,12},{12,8},{16,20},{20,16},{24,28},{28,24},{1,5},{5... | collective-permute-start | bytes 393224 | tf_op jit(solution)/shard_map/ppermute | solution.py:135
  6.7 16.9 %collective-permute-start.1 = (bf16[512,128]{1,0:T(8,128)(2,1)S(1)}, bf16[512,128]{1,0:T(8,128)(2,1)S(1)}, u32[]{:S(2)}, u32[]{:S(2)}) collective-permute-start(bf16[512,128]{1,0:T(8,128)(2,1)S(1)} %get-tuple-element.58), channel_id=1, source_target_pairs={{0,8},{4,12},{8,0},{12,4},{16,24},{20,28},{24,16},{28,20},{1,9},{5... | collective-permute-start | bytes 393224 | tf_op jit(solution)/shard_map/ppermute | solution.py:135
  8.2 15.3 %collective-permute-start.2 = (bf16[512,128]{1,0:T(8,128)(2,1)S(1)}, bf16[512,128]{1,0:T(8,128)(2,1)S(1)}, u32[]{:S(2)}, u32[]{:S(2)}) collective-permute-start(bf16[512,128]{1,0:T(8,128)(2,1)S(1)} %get-tuple-element.59), channel_id=1, source_target_pairs={{0,12},{4,8},{8,4},{12,0},{16,28},{20,24},{24,20},{28,16},{1,13},{... | collective-permute-start | bytes 393224 | tf_op jit(solution)/shard_map/ppermute | solution.py:135
  11.2 12.3 %collective-permute-start.7 = (bf16[512,128]{1,0:T(8,128)(2,1)S(1)}, bf16[512,128]{1,0:T(8,128)(2,1)S(1)}, u32[]{:S(2)}, u32[]{:S(2)}) collective-permute-start(bf16[512,128]{1,0:T(8,128)(2,1)S(1)} %get-tuple-element.68), channel_id=1, source_target_pairs={{0,4},{4,0},{8,12},{12,8},{16,20},{20,16},{24,28},{28,24},{1,5},{5... | collective-permute-start | bytes 393224 | tf_op jit(solution)/shard_map/ppermute | solution.py:135
  13.2 10.4 %collective-permute-start.8 = (bf16[512,128]{1,0:T(8,128)(2,1)S(1)}, bf16[512,128]{1,0:T(8,128)(2,1)S(1)}, u32[]{:S(2)}, u32[]{:S(2)}) collective-permute-start(bf16[512,128]{1,0:T(8,128)(2,1)S(1)} %get-tuple-element.69), channel_id=1, source_target_pairs={{0,8},{4,12},{8,0},{12,4},{16,24},{20,28},{24,16},{28,20},{1,9},{5... | collective-permute-start | bytes 393224 | tf_op jit(solution)/shard_map/ppermute | solution.py:135
  14.8 8.8 %collective-permute-start.9 = (bf16[512,128]{1,0:T(8,128)(2,1)S(1)}, bf16[512,128]{1,0:T(8,128)(2,1)S(1)}, u32[]{:S(2)}, u32[]{:S(2)}) collective-permute-start(bf16[512,128]{1,0:T(8,128)(2,1)S(1)} %get-tuple-element.70), channel_id=1, source_target_pairs={{0,12},{4,8},{8,4},{12,0},{16,28},{20,24},{24,20},{28,16},{1,13},{... | collective-permute-start | bytes 393224 | tf_op jit(solution)/shard_map/ppermute | solution.py:135
  23.7 23.7 %copy-start.4 = (f32[4096]{0:T(1024)S(1)}, f32[4096]{0:T(1024)}, u32[]{:S(2)}) copy-start(f32[4096]{0:T(1024)} %param.8) | copy-start | bytes 49156
  23.7 7.4 %collective-permute-start.10 = (bf16[512,128]{1,0:T(8,128)(2,1)S(1)}, bf16[512,128]{1,0:T(8,128)(2,1)S(1)}, u32[]{:S(2)}, u32[]{:S(2)}) collective-permute-start(bf16[512,128]{1,0:T(8,128)(2,1)S(1)} %fusion.33), channel_id=1, source_target_pairs={{0,16},{4,20},{8,24},{12,28},{1,17},{5,21},{9,25},{13,29},{2,18},{... | collective-permute-start | bytes 393224 | tf_op jit(solution)/shard_map/ppermute | solution.py:148
  28.7 10.1 %collective-permute-start.3 = (bf16[512,128]{1,0:T(8,128)(2,1)S(1)}, bf16[512,128]{1,0:T(8,128)(2,1)S(1)}, u32[]{:S(2)}, u32[]{:S(2)}) collective-permute-start(bf16[512,128]{1,0:T(8,128)(2,1)S(1)} %fusion.16), channel_id=1, source_target_pairs={{0,16},{4,20},{8,24},{12,28},{1,17},{5,21},{9,25},{13,29},{2,18},{... | collective-permute-start | bytes 393224 | tf_op jit(solution)/shard_map/ppermute | solution.py:148
  31.4 11.0 %collective-permute-start.13 = (bf16[512,128]{1,0:T(8,128)(2,1)S(1)}, bf16[512,128]{1,0:T(8,128)(2,1)S(1)}, u32[]{:S(2)}, u32[]{:S(2)}) collective-permute-start(bf16[512,128]{1,0:T(8,128)(2,1)S(1)} %get-tuple-element.118), channel_id=1, source_target_pairs={{0,12},{4,8},{8,4},{12,0},{16,28},{20,24},{24,20},{28,16},{1,13},{... | collective-permute-start | bytes 393224 | tf_op jit(solution)/shard_map/ppermute | solution.py:135
  38.1 6.7 %collective-permute-start.12 = (bf16[512,128]{1,0:T(8,128)(2,1)S(1)}, bf16[512,128]{1,0:T(8,128)(2,1)S(1)}, u32[]{:S(2)}, u32[]{:S(2)}) collective-permute-start(bf16[512,128]{1,0:T(8,128)(2,1)S(1)} %get-tuple-element.119), channel_id=1, source_target_pairs={{0,8},{4,12},{8,0},{12,4},{16,24},{20,28},{24,16},{28,20},{1,9},{5... | collective-permute-start | bytes 393224 | tf_op jit(solution)/shard_map/ppermute | solution.py:135
  38.1 9.2 %collective-permute-start.11 = (bf16[512,128]{1,0:T(8,128)(2,1)S(1)}, bf16[512,128]{1,0:T(8,128)(2,1)S(1)}, u32[]{:S(2)}, u32[]{:S(2)}) collective-permute-start(bf16[512,128]{1,0:T(8,128)(2,1)S(1)} %get-tuple-element.120), channel_id=1, source_target_pairs={{0,4},{4,0},{8,12},{12,8},{16,20},{20,16},{24,28},{28,24},{1,5},{5... | collective-permute-start | bytes 393224 | tf_op jit(solution)/shard_map/ppermute | solution.py:135
  39.1 11.4 %collective-permute-start.6 = (bf16[512,128]{1,0:T(8,128)(2,1)S(1)}, bf16[512,128]{1,0:T(8,128)(2,1)S(1)}, u32[]{:S(2)}, u32[]{:S(2)}) collective-permute-start(bf16[512,128]{1,0:T(8,128)(2,1)S(1)} %get-tuple-element.122), channel_id=1, source_target_pairs={{0,12},{4,8},{8,4},{12,0},{16,28},{20,24},{24,20},{28,16},{1,13},{... | collective-permute-start | bytes 393224 | tf_op jit(solution)/shard_map/ppermute | solution.py:135
  42.0 8.5 %collective-permute-start.5 = (bf16[512,128]{1,0:T(8,128)(2,1)S(1)}, bf16[512,128]{1,0:T(8,128)(2,1)S(1)}, u32[]{:S(2)}, u32[]{:S(2)}) collective-permute-start(bf16[512,128]{1,0:T(8,128)(2,1)S(1)} %get-tuple-element.123), channel_id=1, source_target_pairs={{0,8},{4,12},{8,0},{12,4},{16,24},{20,28},{24,16},{28,20},{1,9},{5... | collective-permute-start | bytes 393224 | tf_op jit(solution)/shard_map/ppermute | solution.py:135
  42.5 8.1 %collective-permute-start.4 = (bf16[512,128]{1,0:T(8,128)(2,1)S(1)}, bf16[512,128]{1,0:T(8,128)(2,1)S(1)}, u32[]{:S(2)}, u32[]{:S(2)}) collective-permute-start(bf16[512,128]{1,0:T(8,128)(2,1)S(1)} %get-tuple-element.124), channel_id=1, source_target_pairs={{0,4},{4,0},{8,12},{12,8},{16,20},{20,16},{24,28},{28,24},{1,5},{5... | collective-permute-start | bytes 393224 | tf_op jit(solution)/shard_map/ppermute | solution.py:135
  53.7 4.1 %copy-start = (f32[256,128]{1,0:T(8,128)}, f32[256,128]{1,0:T(8,128)S(1)}, u32[]{:S(2)}) copy-start(f32[256,128]{1,0:T(8,128)S(1)} %get-tuple-element.78.rest_2_) | copy-start | bytes 393220
  53.8 4.1 %copy-start.2 = (f32[256,128]{1,0:T(8,128)}, f32[256,128]{1,0:T(8,128)S(1)}, u32[]{:S(2)}) copy-start(f32[256,128]{1,0:T(8,128)S(1)} %get-tuple-element.79.rest_3_) | copy-start | bytes 393220
  57.9 0.7 copy-start.5
  58.5 0.7 copy-start.7
  59.2 11.6 %collective-permute-start.14 = (bf16[512,128]{1,0:T(8,128)(2,1)}, bf16[512,128]{1,0:T(8,128)(2,1)}, u32[]{:S(2)}, u32[]{:S(2)}) collective-permute-start(bf16[512,128]{1,0:T(8,128)(2,1)} %get-tuple-element.81), channel_id=1, source_target_pairs={{0,4},{4,0},{8,12},{12,8},{16,20},{20,16},{24,28},{28,24},{1,5},{5... | collective-permute-start | bytes 393224 | tf_op jit(solution)/shard_map/ppermute | solution.py:135
  59.4 0.9 copy-start.1
  60.3 0.9 copy-start.3
  61.2 7.5 %copy-start.8 = (bf16[512,128]{1,0:T(8,128)(2,1)S(1)}, bf16[512,128]{1,0:T(8,128)(2,1)}, u32[]{:S(2)}) copy-start(bf16[512,128]{1,0:T(8,128)(2,1)} %copy-done.7) | copy-start | bytes 393220
  61.2 9.6 %copy-start.6 = (bf16[512,128]{1,0:T(8,128)(2,1)S(1)}, bf16[512,128]{1,0:T(8,128)(2,1)}, u32[]{:S(2)}) copy-start(bf16[512,128]{1,0:T(8,128)(2,1)} %copy-done.5) | copy-start | bytes 393220
  64.6 17.6 %collective-permute-start.21 = (bf16[512,128]{1,0:T(8,128)(2,1)S(1)}, bf16[512,128]{1,0:T(8,128)(2,1)S(1)}, u32[]{:S(2)}, u32[]{:S(2)}) collective-permute-start(bf16[512,128]{1,0:T(8,128)(2,1)S(1)} %get-tuple-element.96), channel_id=1, source_target_pairs={{0,4},{4,0},{8,12},{12,8},{16,20},{20,16},{24,28},{28,24},{1,5},{5... | collective-permute-start | bytes 393224 | tf_op jit(solution)/shard_map/ppermute | solution.py:135
  66.5 15.7 %collective-permute-start.22 = (bf16[512,128]{1,0:T(8,128)(2,1)S(1)}, bf16[512,128]{1,0:T(8,128)(2,1)S(1)}, u32[]{:S(2)}, u32[]{:S(2)}) collective-permute-start(bf16[512,128]{1,0:T(8,128)(2,1)S(1)} %get-tuple-element.97), channel_id=1, source_target_pairs={{0,8},{4,12},{8,0},{12,4},{16,24},{20,28},{24,16},{28,20},{1,9},{5... | collective-permute-start | bytes 393224 | tf_op jit(solution)/shard_map/ppermute | solution.py:135
  68.6 13.6 %collective-permute-start.23 = (bf16[512,128]{1,0:T(8,128)(2,1)S(1)}, bf16[512,128]{1,0:T(8,128)(2,1)S(1)}, u32[]{:S(2)}, u32[]{:S(2)}) collective-permute-start(bf16[512,128]{1,0:T(8,128)(2,1)S(1)} %get-tuple-element.98), channel_id=1, source_target_pairs={{0,12},{4,8},{8,4},{12,0},{16,28},{20,24},{24,20},{28,16},{1,13},{... | collective-permute-start | bytes 393224 | tf_op jit(solution)/shard_map/ppermute | solution.py:135
  68.7 13.4 %collective-permute-start.15 = (bf16[512,128]{1,0:T(8,128)(2,1)S(1)}, bf16[512,128]{1,0:T(8,128)(2,1)S(1)}, u32[]{:S(2)}, u32[]{:S(2)}) collective-permute-start(bf16[512,128]{1,0:T(8,128)(2,1)S(1)} %copy-done.8), channel_id=1, source_target_pairs={{0,8},{4,12},{8,0},{12,4},{16,24},{20,28},{24,16},{28,20},{1,9},{5... | collective-permute-start | bytes 393224 | tf_op jit(solution)/shard_map/ppermute | solution.py:135
  70.7 11.4 %collective-permute-start.16 = (bf16[512,128]{1,0:T(8,128)(2,1)S(1)}, bf16[512,128]{1,0:T(8,128)(2,1)S(1)}, u32[]{:S(2)}, u32[]{:S(2)}) collective-permute-start(bf16[512,128]{1,0:T(8,128)(2,1)S(1)} %copy-done.6), channel_id=1, source_target_pairs={{0,12},{4,8},{8,4},{12,0},{16,28},{20,24},{24,20},{28,16},{1,13},{... | collective-permute-start | bytes 393224 | tf_op jit(solution)/shard_map/ppermute | solution.py:135
  82.3 12.9 %collective-permute-start.24 = (bf16[512,128]{1,0:T(8,128)(2,1)S(1)}, bf16[512,128]{1,0:T(8,128)(2,1)S(1)}, u32[]{:S(2)}, u32[]{:S(2)}) collective-permute-start(bf16[512,128]{1,0:T(8,128)(2,1)S(1)} %fusion.67), channel_id=1, source_target_pairs={{16,0},{20,4},{24,8},{28,12},{17,1},{21,5},{25,9},{29,13},{18,2},{... | collective-permute-start | bytes 393224 | tf_op jit(solution)/shard_map/ppermute | solution.py:148
  84.6 14.5 %collective-permute-start.17 = (bf16[512,128]{1,0:T(8,128)(2,1)S(1)}, bf16[512,128]{1,0:T(8,128)(2,1)S(1)}, u32[]{:S(2)}, u32[]{:S(2)}) collective-permute-start(bf16[512,128]{1,0:T(8,128)(2,1)S(1)} %fusion.50), channel_id=1, source_target_pairs={{16,0},{20,4},{24,8},{28,12},{17,1},{21,5},{25,9},{29,13},{18,2},{... | collective-permute-start | bytes 393224 | tf_op jit(solution)/shard_map/ppermute | solution.py:148
  95.5 7.9 %collective-permute-start.27 = (bf16[512,128]{1,0:T(8,128)(2,1)S(1)}, bf16[512,128]{1,0:T(8,128)(2,1)S(1)}, u32[]{:S(2)}, u32[]{:S(2)}) collective-permute-start(bf16[512,128]{1,0:T(8,128)(2,1)S(1)} %get-tuple-element.110), channel_id=1, source_target_pairs={{0,12},{4,8},{8,4},{12,0},{16,28},{20,24},{24,20},{28,16},{1,13},{... | collective-permute-start | bytes 393224 | tf_op jit(solution)/shard_map/ppermute | solution.py:135
  95.5 10.1 %collective-permute-start.26 = (bf16[512,128]{1,0:T(8,128)(2,1)S(1)}, bf16[512,128]{1,0:T(8,128)(2,1)S(1)}, u32[]{:S(2)}, u32[]{:S(2)}) collective-permute-start(bf16[512,128]{1,0:T(8,128)(2,1)S(1)} %get-tuple-element.111), channel_id=1, source_target_pairs={{0,8},{4,12},{8,0},{12,4},{16,24},{20,28},{24,16},{28,20},{1,9},{5... | collective-permute-start | bytes 393224 | tf_op jit(solution)/shard_map/ppermute | solution.py:135
  98.6 7.9 %collective-permute-start.25 = (bf16[512,128]{1,0:T(8,128)(2,1)S(1)}, bf16[512,128]{1,0:T(8,128)(2,1)S(1)}, u32[]{:S(2)}, u32[]{:S(2)}) collective-permute-start(bf16[512,128]{1,0:T(8,128)(2,1)S(1)} %get-tuple-element.112), channel_id=1, source_target_pairs={{0,4},{4,0},{8,12},{12,8},{16,20},{20,16},{24,28},{28,24},{1,5},{5... | collective-permute-start | bytes 393224 | tf_op jit(solution)/shard_map/ppermute | solution.py:135
  100.2 10.6 %collective-permute-start.20 = (bf16[512,128]{1,0:T(8,128)(2,1)S(1)}, bf16[512,128]{1,0:T(8,128)(2,1)S(1)}, u32[]{:S(2)}, u32[]{:S(2)}) collective-permute-start(bf16[512,128]{1,0:T(8,128)(2,1)S(1)} %get-tuple-element.114), channel_id=1, source_target_pairs={{0,12},{4,8},{8,4},{12,0},{16,28},{20,24},{24,20},{28,16},{1,13},{... | collective-permute-start | bytes 393224 | tf_op jit(solution)/shard_map/ppermute | solution.py:135
  101.4 9.4 %collective-permute-start.19 = (bf16[512,128]{1,0:T(8,128)(2,1)S(1)}, bf16[512,128]{1,0:T(8,128)(2,1)S(1)}, u32[]{:S(2)}, u32[]{:S(2)}) collective-permute-start(bf16[512,128]{1,0:T(8,128)(2,1)S(1)} %get-tuple-element.115), channel_id=1, source_target_pairs={{0,8},{4,12},{8,0},{12,4},{16,24},{20,28},{24,16},{28,20},{1,9},{5... | collective-permute-start | bytes 393224 | tf_op jit(solution)/shard_map/ppermute | solution.py:135
  103.4 7.4 %collective-permute-start.18 = (bf16[512,128]{1,0:T(8,128)(2,1)S(1)}, bf16[512,128]{1,0:T(8,128)(2,1)S(1)}, u32[]{:S(2)}, u32[]{:S(2)}) collective-permute-start(bf16[512,128]{1,0:T(8,128)(2,1)S(1)} %get-tuple-element.116), channel_id=1, source_target_pairs={{0,4},{4,0},{8,12},{12,8},{16,20},{20,16},{24,28},{28,24},{1,5},{5... | collective-permute-start | bytes 393224 | tf_op jit(solution)/shard_map/ppermute | solution.py:135

commit v3 on v0

v3 whole, which is shorter than its diff:
```python
from functools import partial

import jax
import jax.numpy as jnp
from jax import lax
from jax.experimental import pallas as pl
from jax.experimental.pallas import tpu as pltpu
from jax.sharding import PartitionSpec as P

DH = 128
EPS = 1e-05
CHUNKS = 2
F32 = jnp.float32
BF16 = jnp.bfloat16
NT = (((1,), (1,)), ((), ()))
NN = (((1,), (0,)), ((), ()))
TN = (((0,), (0,)), ((), ()))
VMEM = pl.BlockSpec(memory_space=pltpu.VMEM)
SMEM = pl.BlockSpec(memory_space=pltpu.SMEM)
HBM = pl.BlockSpec(memory_space=pltpu.HBM)
barrier = lax.optimization_barrier


def mm(a, b, dims):
    return lax.dot_general(a, b, dims, preferred_element_type=F32)


def head(h):
    return slice(h * DH, (h + 1) * DH)


def head_at(offset, h):
    return pl.ds(pl.multiple_of(offset + h * DH, DH), DH)


def owned(member, j, part):
    return pl.multiple_of((member ^ j) * part, part)


def mask_of(t, later):
    rows = lax.broadcasted_iota(jnp.int32, (t, t), 0)
    cols = lax.broadcasted_iota(jnp.int32, (t, t), 1)
    return rows <= cols if later else rows >= cols


def state_kernel(chunk, part, m, mem, k_hbm, v_hbm, k_ref, v_ref, *rest):
    outs, sem = rest[:m], rest[m]
    member = mem[0]
    copies = []
    for j in reversed(range(m)):
        at = owned(member, j, part)
        far = pl.multiple_of(chunk * m * part + at, part)
        pair = []
        for i, (src, dst) in enumerate(((k_hbm, k_ref), (v_hbm, v_ref))):
            copy = pltpu.make_async_copy(src.at[:, pl.ds(far, part)], dst.at[:, pl.ds(at, part)], sem.at[i, j])
            copy.start()
            pair.append(copy)
        copies.append((j, at, pair))
    for j, at, pair in copies:
        for copy in pair:
            copy.wait()
        for h in range(part // DH):
            a, b = k_ref[:, head_at(at, h)], v_ref[:, head_at(at, h)]
            outs[j][head(h), :] = mm(a, b, TN).astype(BF16)


def local_kernel(chunk, part, m, k_ref, v_ref, gain_ref, q_hbm, c_hbm, q_ref, u_ref, loc_ref, c_ref, sem):
    copies = []
    for j in range(m):
        at, far = pl.ds(j * part, part), pl.ds((chunk * m + j) * part, part)
        pair = []
        for i, (src, dst) in enumerate(((q_hbm, q_ref), (c_hbm, c_ref))):
            copy = pltpu.make_async_copy(src.at[:, far], dst.at[:, at], sem.at[i, j])
            copy.start()
            pair.append(copy)
        copies.append(pair)
    mask = mask_of(q_ref.shape[0], False)
    for j, pair in enumerate(copies):
        for copy in pair:
            copy.wait()
        for h in range(j * part // DH, (j + 1) * part // DH):
            scores = mm(q_ref[:, head(h)], k_ref[:, head(h)], NT)
            weights = jnp.where(mask, scores, 0.0).astype(BF16)
            loc_ref[:, head(h)] = mm(weights, v_ref[:, head(h)], NN)
            here = head(chunk * m * part // DH + h)
            u_ref[:, head(h)] = c_ref[:, head(h)].astype(F32) * gain_ref[:, here]


def attend_kernel(part, m, mem, q_ref, loc_ref, u_ref, *rest):
    prefixes, (att_ref, ss_ref, su_ref) = rest[:m], rest[m:]
    member = mem[0]
    ss = jnp.zeros(ss_ref.shape, F32)
    su = jnp.zeros(su_ref.shape, F32)
    for j in range(m):
        at = owned(member, j, part)
        for h in range(part // DH):
            here = head_at(at, h)
            att = loc_ref[:, here] + mm(q_ref[:, here], prefixes[j][head(h), :], NN)
            att_ref[:, here] = att
            ss = ss + att * att
            su = su + att * u_ref[:, here]
    ss_ref[...] = ss
    su_ref[...] = su


def grad_kernel(part, m, width, mem, q_ref, att_ref, u_ref, *rest):
    sums, rest = rest[: 2 * CHUNKS], rest[2 * CHUNKS :]
    g_ref, outs = rest[0], rest[1:]
    member = mem[0]
    ss = sums[0][...]
    su = sums[1][...]
    for i in range(1, CHUNKS):
        ss = ss + sums[2 * i][...]
        su = su + sums[2 * i + 1][...]
    ss = jnp.sum(ss, axis=1, keepdims=True) / width
    su = jnp.sum(su, axis=1, keepdims=True) / width
    r = lax.rsqrt(ss + EPS)
    s = jnp.broadcast_to(r * r * r * su, sums[0].shape)
    r = jnp.broadcast_to(r, sums[0].shape)
    for j in reversed(range(m)):
        at = owned(member, j, part)
        for h in range(part // DH):
            here = head_at(at, h)
            g = (u_ref[:, here] * r - att_ref[:, here] * s).astype(BF16)
            g_ref[:, here] = g
            outs[j][head(h), :] = mm(q_ref[:, here], g, TN).astype(BF16)


def back_local_kernel(q_ref, k_ref, v_ref, g_ref, kl_ref, vl_ref):
    mask = mask_of(q_ref.shape[0], True)
    for h in range(q_ref.shape[1] // DH):
        q, k, v, g = (ref[:, head(h)] for ref in (q_ref, k_ref, v_ref, g_ref))
        vw = jnp.where(mask, mm(v, g, NT), 0.0).astype(BF16)
        kl_ref[:, head(h)] = mm(vw, q, NN)
        kw = jnp.where(mask, mm(k, q, NT), 0.0).astype(BF16)
        vl_ref[:, head(h)] = mm(kw, g, NN)


def finish_kernel(chunk, part, m, mem, k_ref, v_ref, kl_ref, vl_ref, *rest):
    suffixes = rest[:m]
    kg_hbm, vg_hbm, kg_ref, vg_ref, sem = rest[-5:]
    member = mem[0]
    copies = []
    for j in range(m):
        at = owned(member, j, part)
        far = pl.multiple_of(chunk * m * part + at, part)
        for h in range(part // DH):
            here = head_at(at, h)
            s = suffixes[j][head(h), :]
            kg_ref[:, here] = (kl_ref[:, here] + mm(v_ref[:, here], s, NT)).astype(BF16)
            vg_ref[:, here] = (vl_ref[:, here] + mm(k_ref[:, here], s, NN)).astype(BF16)
        for i, (src, dst) in enumerate(((kg_ref, kg_hbm), (vg_ref, vg_hbm))):
            copy = pltpu.make_async_copy(src.at[:, pl.ds(at, part)], dst.at[:, pl.ds(far, part)], sem.at[i, j])
            copy.start()
            copies.append(copy)
    for copy in copies:
        copy.wait()


def exchange(parts, n):
    m = len(parts)
    out = [parts[0]] + [None] * (m - 1)
    for j in range(m - 1, 0, -1):
        perm = [(i, (i // m) * m + ((i % m) ^ j)) for i in range(n)]
        out[j] = lax.ppermute(parts[j], "seq", perm)
    return out


def carry_groups(total, n, m, forward):
    groups = n // m

    def shift(x, by):
        step = by * m
        if forward:
            perm = [(i, i + step) for i in range(n - step)]
        else:
            perm = [(i + step, i) for i in range(n - step)]
        return lax.ppermute(x, "seq", perm)

    if groups == 1:
        return jnp.zeros_like(total)
    if groups == 2:
        return shift(total.astype(BF16), 1)
    run = shift(total, 1)
    by = 1
    while by < groups - 1:
        run = run + shift(run, by)
        by *= 2
    return run


def give_back(got, carry, member, forward):
    back = []
    for j in range(len(got)):
        acc = carry.astype(F32)
        for i in range(len(got)):
            if i != j:
                source, target = member ^ i, member ^ j
                take = (source < target) if forward else (source > target)
                acc = acc + jnp.where(take, got[i].astype(F32), 0.0)
        back.append(acc.astype(BF16))
    return back


def total_of(got):
    return sum(x.astype(F32) for x in got)


def scan_chunks(first, second_of, n, member, forward, fill_a, fill_b):
    m = len(first)
    got_a = exchange(first, n)
    second, extra = second_of()
    got_a, second, extra = barrier((got_a, second, extra))
    carry_a = carry_groups(total_of(got_a), n, m, forward)
    got_b = exchange(second, n)
    made_a = fill_a(extra)
    carry_a, made_a, extra = barrier((carry_a, made_a, extra))
    back_a = exchange(give_back(got_a, carry_a, member, forward), n)
    carry_b = carry_groups(total_of(got_b), n, m, forward)
    made_b = fill_b(extra)
    carry_b, made_b = barrier((carry_b, made_b))
    back_b = exchange(give_back(got_b, carry_b, member, forward), n)
    return (back_a, back_b), (made_a, made_b)


def shards(n, queries, keys, values, gain, cotangent):
    rows, width = queries.shape
    queries, keys, values, cotangent = (
        pltpu.with_memory_space_constraint(x, pltpu.HBM) for x in (queries, keys, values, cotangent)
    )
    m = 4 if n % 4 == 0 else (2 if n % 2 == 0 else 1)
    half = width // CHUNKS
    part = half // m
    member = lax.axis_index("seq") % m
    mem = member.reshape(1).astype(jnp.int32)
    gain2 = gain.reshape(1, width)
    wide = pltpu.VMEM((rows, half), F32)
    slim = pltpu.VMEM((rows, half), BF16)
    stat = pltpu.VMEM((rows, DH), F32)
    state = pltpu.VMEM((part, DH), BF16)
    sems = pltpu.SemaphoreType.DMA((2, m))
    unit = 2 * rows * DH * half

    def call(kernel, args, in_specs, out_shape, flops, nbytes, scratch=(), out_specs=None, alias={}):
        return pl.pallas_call(
            kernel,
            in_specs=in_specs,
            out_specs=out_specs or [VMEM] * len(out_shape),
            out_shape=out_shape,
            scratch_shapes=scratch,
            input_output_aliases=alias,
            compiler_params=pltpu.CompilerParams(vmem_limit_bytes=12 << 20),
            cost_estimate=pl.CostEstimate(flops=flops, bytes_accessed=nbytes, transcendentals=0),
        )(*args)

    def states_of(c):
        k, v, *parts = call(
            partial(state_kernel, c, part, m), (mem, keys, values), [SMEM, HBM, HBM],
            [slim, slim] + [state] * m, unit, 6 * rows * half, [sems],
        )
        return parts, (k, v)

    def local_of(c, kv):
        return call(
            partial(local_kernel, c, part, m), (*kv, gain2, queries, cotangent), [VMEM, VMEM, VMEM, HBM, HBM],
            [slim, wide, wide], 4 * unit, 12 * rows * half, [slim, sems],
        )

    kv = [None, None]
    parts_a, kv[0] = states_of(0)

    def second_states():
        parts_b, kv_b = states_of(1)
        return parts_b, (kv[0], kv_b)

    def fill_a(extra):
        kv[0] = extra[0]
        return local_of(0, extra[0])

    def fill_b(extra):
        kv[1] = extra[1]
        return local_of(1, extra[1])

    prefix, made = scan_chunks(parts_a, second_states, n, member, True, fill_a, fill_b)

    attended, sums = [], []
    for c in range(CHUNKS):
        q, u, loc = made[c]
        att, ss, su = call(
            partial(attend_kernel, part, m), (mem, q, loc, u, *prefix[c]), [SMEM] + [VMEM] * (3 + m),
            [wide, stat, stat], unit, 4 * rows * half, alias={2: 0},
        )
        attended.append(att)
        sums += [ss, su]

    def grads_of(c):
        q, u, _ = made[c]
        g, *parts = call(
            partial(grad_kernel, part, m, width), (mem, q, attended[c], u, *sums),
            [SMEM] + [VMEM] * (3 + 2 * CHUNKS), [slim] + [state] * m, unit, 4 * rows * half,
        )
        return parts, (q, *kv[c], g)

    def back_local_of(qkvg):
        return call(back_local_kernel, qkvg, [VMEM] * 4, [wide, wide], 8 * unit, 8 * rows * half)

    parts_a, near_a = grads_of(0)

    def second_grads():
        parts_b, near_b = grads_of(1)
        return parts_b, (near_a, near_b)

    suffix, made = scan_chunks(
        parts_a, second_grads, n, member, False, lambda e: back_local_of(e[0]), lambda e: back_local_of(e[1])
    )

    outs = ()
    for c in range(CHUNKS):
        base = 5 + m
        outs = call(
            partial(finish_kernel, c, part, m), (mem, *kv[c], *made[c], *suffix[c], *outs),
            [SMEM] + [VMEM] * (4 + m) + [HBM] * len(outs),
            [jax.ShapeDtypeStruct((rows, width), BF16)] * 2, 2 * unit, 8 * rows * half, [slim, slim, sems],
            out_specs=[HBM, HBM], alias={base: 0, base + 1: 1} if outs else {},
        )
    return tuple(outs)


def solution(mesh):
    spec = P(("dp", "seq"), None)
    return jax.shard_map(
        partial(shards, mesh.shape["seq"]),
        mesh=mesh,
        in_specs=(spec, spec, spec, P(), spec),
        out_specs=(spec, spec),
        check_vma=False,
    )
```

time: 223 us -> 94.3 us (0.42)
  blocking collectives: 107 us -> 0 us
  matrix products: 40.9 us -> 0 us
  starting transfers between devices: 7.33 us -> 40.8 us
  local copies, waits for them, and re-layouts: 35.6 us -> 8.02 us
  Pallas kernels: 0 us -> 27.4 us
  waiting for transfers between devices: 22.6 us -> 11.3 us
  other arithmetic: 8.13 us -> 5.07 us
    all_to_all x2 -> x0, blocking collectives: 107 us -> none  [the longest x1 55.3 us: spread_forward(): lax.all_to_all(stacked, 'seq', split_axis=1, concat_axis=0, tiled=True)]
    dot_general x8 -> x0, matrix products: 40.9 us -> none  [the longest x1 7.35 us: shards(): jnp.einsum('hst,the->she', key_weights, grad_heads, preferred_element_typ...]
    ppermute x0 -> x28, starting transfers between devices: none -> 40.8 us  [the longest x24 30.2 us: exchange(): out[j] = lax.ppermute(parts[j], 'seq', perm)]
    pallas_call x0 -> x12, Pallas kernels: none -> 27.4 us  [call(): pl.pallas_call(kernel, in_specs=in_specs, out_specs=out_specs or [VMEM] *...]
    all_to_all x2 -> x0, waiting for transfers between devices: 22.6 us -> none  [the longest x1 11.4 us: spread_backward(): lax.all_to_all(after.astype(jnp.bfloat16), 'seq', split_axis=0, concat_ax...]
    reshape x3 -> x0, local copies, waits for them, and re-layouts: 14 us -> none  [the longest x1 5.66 us: shards(): attended = (cross_term + local_term).reshape(tok_rows, head_count * DH)]
    ppermute x0 -> x28, waiting for transfers between devices: none -> 11.3 us  [the longest x24 8.6 us: exchange(): out[j] = lax.ppermute(parts[j], 'seq', perm)]
    all_to_all x2 -> x0, starting transfers between devices: 7.33 us -> none  [the longest x1 3.74 us: spread_backward(): lax.all_to_all(after.astype(jnp.bfloat16), 'seq', split_axis=0, concat_ax...]
  transfers between devices with their start and end apart: 2 -> 28, of which waited for: 2 -> 11; matrix products, arithmetic and copies ran while one was open for 13% -> 5% of each run, Pallas kernels for 0% -> 21%
where the time goes in v3:
time: 94.3 us; the launch traced here: 93.8 us
  starting transfers between devices  40.8 us (43%)
  Pallas kernels  27.4 us (29%)
  waiting for transfers between devices  11.3 us (12%)
  local copies, waits for them, and re-layouts  8.02 us (9%)
  other arithmetic  5.07 us (5%)
  between operations  1.18 us (1%)
    ppermute x24, starting transfers between devices, exchange(): out[j] = lax.ppermute(parts[j], 'seq', perm)  30.2 us
    pallas_call x12, Pallas kernels, call(): pl.pallas_call(kernel, in_specs=in_specs, out_specs=out_specs or [VMEM] *...  27.4 us
    ppermute x4, starting transfers between devices, shift(): return lax.ppermute(x, 'seq', perm)  10.6 us
    ppermute x24, waiting for transfers between devices, exchange(): out[j] = lax.ppermute(parts[j], 'seq', perm)  8.6 us
    unnamed x46, local copies, waits for them, and re-layouts  8.02 us
    convert_element_type x4, other arithmetic, give_back(): back.append(acc.astype(BF16))  3.1 us
    ppermute x4, waiting for transfers between devices, shift(): return lax.ppermute(x, 'seq', perm)  2.71 us
    convert_element_type x4, other arithmetic, carry_groups(): return shift(total.astype(BF16), 1)  1.97 us
  transfers between devices with their start and end apart: 28, of which 11 were waited for; matrix products, arithmetic and copies ran while one was open for 5% of the time, Pallas kernels for 21%

profile of v3, /device:TPU:0, one launch (start us, length us, event | category | flops | bytes accessed | tf_op | source)
XLA Modules:
  0.0 93.8 jit_solution(183407144252594339)
XLA Ops:
  0.6 2.4 %shard_map.68 = (bf16[256,2048]{1,0:T(8,128)(2,1)S(1)}, bf16[256,2048]{1,0:T(8,128)(2,1)S(1)}, bf16[512,128]{1,0:T(8,128)(2,1)S(1)}, bf16[512,128]{1,0:T(8,128)(...) custom-call(s32[1]{0:T(128)} %bitcast.mem, bf16[256,4096]{1,0:T(8,128)(2,1)} %k_hbm.3, ...), custom_call_target="tpu_custom_call" | custom-call | flops 134217728 | bytes 3145728 | tf_op jit(solution)/shard_map/pallas_call | solution.py:245
  3.0 3.0 %collective-permute-start = (bf16[512,128]{1,0:T(8,128)(2,1)S(1)}, bf16[512,128]{1,0:T(8,128)(2,1)S(1)}, u32[]{:S(2)}, u32[]{:S(2)}) collective-permute-start(bf16[512,128]{1,0:T(8,128)(2,1)S(1)} %get-tuple-element.91), channel_id=1, source_target_pairs={{0,4},{4,0},{8,12},{12,8},{16,20},{20,16},{24,28},{28,24},{1,5},{5... | collective-permute-start | bytes 393224 | tf_op jit(solution)/shard_map/ppermute | solution.py:165
  6.1 1.6 %collective-permute-start.1 = (bf16[512,128]{1,0:T(8,128)(2,1)S(1)}, bf16[512,128]{1,0:T(8,128)(2,1)S(1)}, u32[]{:S(2)}, u32[]{:S(2)}) collective-permute-start(bf16[512,128]{1,0:T(8,128)(2,1)S(1)} %get-tuple-element.92), channel_id=1, source_target_pairs={{0,8},{4,12},{8,0},{12,4},{16,24},{20,28},{24,16},{28,20},{1,9},{5... | collective-permute-start | bytes 393224 | tf_op jit(solution)/shard_map/ppermute | solution.py:165
  7.6 2.4 %shard_map.69 = (bf16[256,2048]{1,0:T(8,128)(2,1)S(1)}, bf16[256,2048]{1,0:T(8,128)(2,1)S(1)}, bf16[512,128]{1,0:T(8,128)(2,1)S(1)}, bf16[512,128]{1,0:T(8,128)(...) custom-call(s32[1]{0:T(128)} %bitcast.mem, bf16[256,4096]{1,0:T(8,128)(2,1)} %k_hbm.3, ...), custom_call_target="tpu_custom_call" | custom-call | flops 134217728 | bytes 3145728 | tf_op jit(solution)/shard_map/pallas_call | solution.py:245
  10.0 1.0 %copy-done.2 = bf16[256,2048]{1,0:T(8,128)(2,1)} copy-done((bf16[256,2048]{1,0:T(8,128)(2,1)}, bf16[256,2048]{1,0:T(8,128)(2,1)S(1)}, u32[]{:S(2)}) %copy-start.2) | copy-done | bytes 1048600
  11.1 1.0 %copy-done.5 = bf16[256,2048]{1,0:T(8,128)(2,1)} copy-done((bf16[256,2048]{1,0:T(8,128)(2,1)}, bf16[256,2048]{1,0:T(8,128)(2,1)S(1)}, u32[]{:S(2)}) %copy-start.5) | copy-done | bytes 1048600
  12.4 1.2 %collective-permute-done.2 = bf16[512,128]{1,0:T(8,128)(2,1)S(1)} collective-permute-done((bf16[512,128]{1,0:T(8,128)(2,1)S(1)}, bf16[512,128]{1,0:T(8,128)(2,1)S(1)}, u32[]{:S(2)}, u32[]{:S(2)}) %collective-permute-start.2) | collective-permute-done | bytes 131104 | tf_op jit(solution)/shard_map/ppermute | solution.py:165
  13.6 0.7 fusion.12
  14.3 5.3 %collective-permute-start.3 = (bf16[512,128]{1,0:T(8,128)(2,1)}, bf16[512,128]{1,0:T(8,128)(2,1)}, u32[]{:S(2)}, u32[]{:S(2)}) collective-permute-start(bf16[512,128]{1,0:T(8,128)(2,1)} %fusion.12), channel_id=1, source_target_pairs={{0,16},{4,20},{8,24},{12,28},{1,17},{5,21},{9,25},{13,29},{2,18},{... | collective-permute-start | bytes 393224 | tf_op jit(solution)/shard_map/ppermute | solution.py:178
  19.7 2.5 %collective-permute-start.9 = (bf16[512,128]{1,0:T(8,128)(2,1)S(1)}, bf16[512,128]{1,0:T(8,128)(2,1)S(1)}, u32[]{:S(2)}, u32[]{:S(2)}) collective-permute-start(bf16[512,128]{1,0:T(8,128)(2,1)S(1)} %get-tuple-element.125), channel_id=1, source_target_pairs={{0,12},{4,8},{8,4},{12,0},{16,28},{20,24},{24,20},{28,16},{1,13},{... | collective-permute-start | bytes 393224 | tf_op jit(solution)/shard_map/ppermute | solution.py:165
  23.1 3.8 %shard_map.70 = (bf16[256,2048]{1,0:T(8,128)(2,1)S(1)}, f32[256,2048]{1,0:T(8,128)S(1)}, f32[256,2048]{1,0:T(8,128)S(1)}) custom-call(bf16[256,2048]{1,0:T(8,128)(2,1)S(1)} %get-tuple-element.155.k_ref, bf16[256,2048]{1,0:T(8,128)(2,1)S(1)} %get-tuple-element.156.v_ref, f32[1,4096]{1,0:T(1,128)S(1)} %bitcast.2, bf16[256,4096]{1,0:T(8,128)(2,1)} %q_hbm.3, ...), custom_call_target="tpu_custom_call" | custom-call | flops 536870912 | bytes 6291456 | tf_op jit(solution)/shard_map/pallas_call | solution.py:245
  27.6 2.4 %collective-permute-start.10 = (bf16[512,128]{1,0:T(8,128)(2,1)S(1)}, bf16[512,128]{1,0:T(8,128)(2,1)S(1)}, u32[]{:S(2)}, u32[]{:S(2)}) collective-permute-start(bf16[512,128]{1,0:T(8,128)(2,1)S(1)} %fusion.25), channel_id=1, source_target_pairs={{0,16},{4,20},{8,24},{12,28},{1,17},{5,21},{9,25},{13,29},{2,18},{... | collective-permute-start | bytes 393224 | tf_op jit(solution)/shard_map/ppermute | solution.py:178
  30.0 1.2 %fusion.5 = (bf16[512,128]{1,0:T(8,128)(2,1)S(1)}, bf16[512,128]{1,0:T(8,128)(2,1)S(1)}, bf16[512,128]{1,0:T(8,128)(2,1)S(1)}, bf16[512,128]{1,0:T(8,128)(2,1)S(1)}) fusion(bf16[512,128]{1,0:T(8,128)(2,1)S(1)} %collective-permute-done, bf16[512,128]{1,0:T(8,128)(2,1)S(1)} %collective-permute-done.1, bf16[512,128]{1,0:T(8,128)(2,1)S(1)} %get-tuple-element.102, ...), kind=kLoop, calls=%fused_computation.81 | loop fusion | flops 2162688 | bytes 1179660 | tf_op jit(solution)/shard_map/convert_element_type | solution.py:201
  31.8 2.5 %collective-permute-start.5 = (bf16[512,128]{1,0:T(8,128)(2,1)S(1)}, bf16[512,128]{1,0:T(8,128)(2,1)S(1)}, u32[]{:S(2)}, u32[]{:S(2)}) collective-permute-start(bf16[512,128]{1,0:T(8,128)(2,1)S(1)} %get-tuple-element.193), channel_id=1, source_target_pairs={{0,8},{4,12},{8,0},{12,4},{16,24},{20,28},{24,16},{28,20},{1,9},{5... | collective-permute-start | bytes 393224 | tf_op jit(solution)/shard_map/ppermute | solution.py:165
  34.3 1.0 %collective-permute-start.6 = (bf16[512,128]{1,0:T(8,128)(2,1)S(1)}, bf16[512,128]{1,0:T(8,128)(2,1)S(1)}, u32[]{:S(2)}, u32[]{:S(2)}) collective-permute-start(bf16[512,128]{1,0:T(8,128)(2,1)S(1)} %get-tuple-element.190), channel_id=1, source_target_pairs={{0,12},{4,8},{8,4},{12,0},{16,28},{20,24},{24,20},{28,16},{1,13},{... | collective-permute-start | bytes 393224 | tf_op jit(solution)/shard_map/ppermute | solution.py:165
  35.3 3.7 %shard_map.72 = (bf16[256,2048]{1,0:T(8,128)(2,1)S(1)}, f32[256,2048]{1,0:T(8,128)S(1)}, f32[256,2048]{1,0:T(8,128)S(1)}) custom-call(bf16[256,2048]{1,0:T(8,128)(2,1)S(1)} %copy-done.3, bf16[256,2048]{1,0:T(8,128)(2,1)S(1)} %copy-done.6, f32[1,4096]{1,0:T(1,128)S(1)} %bitcast.3, bf16[256,4096]{1,0:T(8,128)(2,1)} %q_hbm.3, bf16[256,4096]{1,0:T(8,128)(2,1)} %c_hbm.3), custom_call_target="tpu_custom_call" | custom-call | flops 536870912 | bytes 6291456 | tf_op jit(solution)/shard_map/pallas_call | solution.py:245
  39.4 0.6 collective-permute-start.11
  40.0 2.0 %collective-permute-start.12 = (bf16[512,128]{1,0:T(8,128)(2,1)S(1)}, bf16[512,128]{1,0:T(8,128)(2,1)S(1)}, u32[]{:S(2)}, u32[]{:S(2)}) collective-permute-start(bf16[512,128]{1,0:T(8,128)(2,1)S(1)} %get-tuple-element.189), channel_id=1, source_target_pairs={{0,8},{4,12},{8,0},{12,4},{16,24},{20,28},{24,16},{28,20},{1,9},{5... | collective-permute-start | bytes 393224 | tf_op jit(solution)/shard_map/ppermute | solution.py:165
  42.0 1.0 %collective-permute-start.13 = (bf16[512,128]{1,0:T(8,128)(2,1)S(1)}, bf16[512,128]{1,0:T(8,128)(2,1)S(1)}, u32[]{:S(2)}, u32[]{:S(2)}) collective-permute-start(bf16[512,128]{1,0:T(8,128)(2,1)S(1)} %get-tuple-element.186), channel_id=1, source_target_pairs={{0,12},{4,8},{8,4},{12,0},{16,28},{20,24},{24,20},{28,16},{1,13},{... | collective-permute-start | bytes 393224 | tf_op jit(solution)/shard_map/ppermute | solution.py:165
  43.0 1.3 %shard_map.71 = (f32[256,2048]{1,0:T(8,128)S(1)}, f32[256,128]{1,0:T(8,128)S(1)}, f32[256,128]{1,0:T(8,128)S(1)}) custom-call(s32[1]{0:T(128)} %bitcast.mem, bf16[256,2048]{1,0:T(8,128)(2,1)S(1)} %get-tuple-element.154.q_ref, f32[256,2048]{1,0:T(8,128)S(1)} %get-tuple-element.116.loc_ref, ...), custom_call_target="tpu_custom_call", output_to_operand_aliasing={{0}: (2, {})} | custom-call | flops 134217728 | bytes 2097152 | tf_op jit(solution)/shard_map/pallas_call | solution.py:245
  45.0 2.9 %collective-permute-done.13.rest_3_ = bf16[512,128]{1,0:T(8,128)(2,1)S(1)} collective-permute-done((bf16[512,128]{1,0:T(8,128)(2,1)S(1)}, bf16[512,128]{1,0:T(8,128)(2,1)S(1)}, u32[]{:S(2)}, u32[]{:S(2)}) %collective-permute-start.13) | collective-permute-done | bytes 131104 | tf_op jit(solution)/shard_map/ppermute | solution.py:165
  47.9 1.3 %shard_map.73 = (f32[256,2048]{1,0:T(8,128)S(1)}, f32[256,128]{1,0:T(8,128)S(1)}, f32[256,128]{1,0:T(8,128)S(1)}) custom-call(s32[1]{0:T(128)} %bitcast.mem, bf16[256,2048]{1,0:T(8,128)(2,1)S(1)} %get-tuple-element.164.q_ref, f32[256,2048]{1,0:T(8,128)S(1)} %get-tuple-element.130.loc_ref, ...), custom_call_target="tpu_custom_call", output_to_operand_aliasing={{0}: (2, {})} | custom-call | flops 134217728 | bytes 2097152 | tf_op jit(solution)/shard_map/pallas_call | solution.py:245
  49.2 2.0 %shard_map.74 = (bf16[256,2048]{1,0:T(8,128)(2,1)S(1)}, bf16[512,128]{1,0:T(8,128)(2,1)S(1)}, bf16[512,128]{1,0:T(8,128)(2,1)}, bf16[512,128]{1,0:T(8,128)(2,1)}, bf16[512,128]{1,0:T(8,128)(2,1)}) custom-call(s32[1]{0:T(128)} %bitcast.mem, bf16[256,2048]{1,0:T(8,128)(2,1)S(1)} %get-tuple-element.154.q_ref, f32[256,2048]{1,0:T(8,128)S(1)} %get-tuple-element.119.att_ref, ...), custom_call_target="tpu_custom_call" | custom-call | flops 134217728 | bytes 2097152 | tf_op jit(solution)/shard_map/pallas_call | solution.py:245
  51.2 1.0 %copy-done.12 = bf16[256,2048]{1,0:T(8,128)(2,1)} copy-done((bf16[256,2048]{1,0:T(8,128)(2,1)}, bf16[256,2048]{1,0:T(8,128)(2,1)S(1)}, u32[]{:S(2)}) %copy-start.12) | copy-done | bytes 1048600
  52.2 1.5 %collective-permute-start.14 = (bf16[512,128]{1,0:T(8,128)(2,1)}, bf16[512,128]{1,0:T(8,128)(2,1)}, u32[]{:S(2)}, u32[]{:S(2)}) collective-permute-start(bf16[512,128]{1,0:T(8,128)(2,1)} %get-tuple-element.136), channel_id=1, source_target_pairs={{0,4},{4,0},{8,12},{12,8},{16,20},{20,16},{24,28},{28,24},{1,5},{5... | collective-permute-start | bytes 393224 | tf_op jit(solution)/shard_map/ppermute | solution.py:165
  54.1 1.5 %collective-permute-start.16 = (bf16[512,128]{1,0:T(8,128)(2,1)}, bf16[512,128]{1,0:T(8,128)(2,1)}, u32[]{:S(2)}, u32[]{:S(2)}) collective-permute-start(bf16[512,128]{1,0:T(8,128)(2,1)} %get-tuple-element.138), channel_id=1, source_target_pairs={{0,12},{4,8},{8,4},{12,0},{16,28},{20,24},{24,20},{28,16},{1,13},{... | collective-permute-start | bytes 393224 | tf_op jit(solution)/shard_map/ppermute | solution.py:165
  55.7 1.6 %copy-done.9 = f32[256,2048]{1,0:T(8,128)S(1)} copy-done((f32[256,2048]{1,0:T(8,128)S(1)}, f32[256,2048]{1,0:T(8,128)}, u32[]{:S(2)}) %copy-start.9) | copy-done | bytes 2097176
  57.2 1.6 %copy-done.11 = f32[256,2048]{1,0:T(8,128)S(1)} copy-done((f32[256,2048]{1,0:T(8,128)S(1)}, f32[256,2048]{1,0:T(8,128)}, u32[]{:S(2)}) %copy-start.11) | copy-done | bytes 2097176
  58.8 0.9 copy-done.15
  59.7 0.9 copy-done.17
  60.7 1.4 %shard_map.75 = (bf16[256,2048]{1,0:T(8,128)(2,1)S(1)}, bf16[512,128]{1,0:T(8,128)(2,1)S(1)}, bf16[512,128]{1,0:T(8,128)(2,1)S(1)}, bf16[512,128]{1,0:T(8,128)(2,1)S(1)}, bf16[512,128]{1,0:T(8,128)(2,1)S(1)}) custom-call(s32[1]{0:T(128)} %bitcast.mem, bf16[256,2048]{1,0:T(8,128)(2,1)S(1)} %get-tuple-element.164.q_ref, f32[256,2048]{1,0:T(8,128)S(1)} %copy-done.11, ...), custom_call_target="tpu_custom_call" | custom-call | flops 134217728 | bytes 2097152 | tf_op jit(solution)/shard_map/pallas_call | solution.py:245
  62.1 1.5 %collective-permute-start.19 = (bf16[512,128]{1,0:T(8,128)(2,1)S(1)}, bf16[512,128]{1,0:T(8,128)(2,1)S(1)}, u32[]{:S(2)}, u32[]{:S(2)}) collective-permute-start(bf16[512,128]{1,0:T(8,128)(2,1)S(1)} %get-tuple-element.149), channel_id=1, source_target_pairs={{0,12},{4,8},{8,4},{12,0},{16,28},{20,24},{24,20},{28,16},{1,13},{... | collective-permute-start | bytes 393224 | tf_op jit(solution)/shard_map/ppermute | solution.py:165
  63.6 1.5 %collective-permute-start.18 = (bf16[512,128]{1,0:T(8,128)(2,1)S(1)}, bf16[512,128]{1,0:T(8,128)(2,1)S(1)}, u32[]{:S(2)}, u32[]{:S(2)}) collective-permute-start(bf16[512,128]{1,0:T(8,128)(2,1)S(1)} %get-tuple-element.148), channel_id=1, source_target_pairs={{0,8},{4,12},{8,0},{12,4},{16,24},{20,28},{24,16},{28,20},{1,9},{5... | collective-permute-start | bytes 393224 | tf_op jit(solution)/shard_map/ppermute | solution.py:165
  65.6 1.1 %fusion.51 = bf16[512,128]{1,0:T(8,128)(2,1)S(1)} fusion(bf16[512,128]{1,0:T(8,128)(2,1)} %collective-permute-done.16, bf16[512,128]{1,0:T(8,128)(2,1)} %collective-permute-done.15, bf16[512,128]{1,0:T(8,128)(2,1)} %collective-permute-done.14, bf16[512,128]{1,0:T(8,128)(2,1)S(1)} %get-tuple-element.150), kind=kLoop, calls=%fused_computation.127 | loop fusion | flops 524288 | bytes 655360 | tf_op jit(solution)/shard_map/convert_element_type | solution.py:183
  66.8 1.4 %collective-permute-start.21 = (bf16[512,128]{1,0:T(8,128)(2,1)S(1)}, bf16[512,128]{1,0:T(8,128)(2,1)S(1)}, u32[]{:S(2)}, u32[]{:S(2)}) collective-permute-start(bf16[512,128]{1,0:T(8,128)(2,1)S(1)} %fusion.51), channel_id=1, source_target_pairs={{16,0},{20,4},{24,8},{28,12},{17,1},{21,5},{25,9},{29,13},{18,2},{... | collective-permute-start | bytes 393224 | tf_op jit(solution)/shard_map/ppermute | solution.py:178
  68.2 2.6 %shard_map.76 = (f32[256,2048]{1,0:T(8,128)S(1)}, f32[256,2048]{1,0:T(8,128)S(1)}) custom-call(bf16[256,2048]{1,0:T(8,128)(2,1)S(1)} %copy-done.1, bf16[256,2048]{1,0:T(8,128)(2,1)S(1)} %get-tuple-element.155.k_ref, bf16[256,2048]{1,0:T(8,128)(2,1)S(1)} %get-tuple-element.156.v_ref, bf16[256,2048]{1,0:T(8,128)(2,1)S(1)} %copy-done.13), custom_call_target="tpu_custom_call" | custom-call | flops 1073741824 | bytes 4194304 | tf_op jit(solution)/shard_map/pallas_call | solution.py:245
  71.1 1.5 %collective-permute-start.20 = (bf16[512,128]{1,0:T(8,128)(2,1)S(1)}, bf16[512,128]{1,0:T(8,128)(2,1)S(1)}, u32[]{:S(2)}, u32[]{:S(2)}) collective-permute-start(bf16[512,128]{1,0:T(8,128)(2,1)S(1)} %fusion.38), channel_id=1, source_target_pairs={{16,0},{20,4},{24,8},{28,12},{17,1},{21,5},{25,9},{29,13},{18,2},{... | collective-permute-start | bytes 393224 | tf_op jit(solution)/shard_map/ppermute | solution.py:178
  72.6 2.7 %collective-permute-done.21 = bf16[512,128]{1,0:T(8,128)(2,1)S(1)} collective-permute-done((bf16[512,128]{1,0:T(8,128)(2,1)S(1)}, bf16[512,128]{1,0:T(8,128)(2,1)S(1)}, u32[]{:S(2)}, u32[]{:S(2)}) %collective-permute-start.21) | collective-permute-done | bytes 131104 | tf_op jit(solution)/shard_map/ppermute | solution.py:178
  75.3 1.3 %fusion.44 = (bf16[512,128]{1,0:T(8,128)(2,1)S(1)}, bf16[512,128]{1,0:T(8,128)(2,1)S(1)}, bf16[512,128]{1,0:T(8,128)(2,1)S(1)}, bf16[512,128]{1,0:T(8,128)(2,1)S(1)}) fusion(bf16[512,128]{1,0:T(8,128)(2,1)} %collective-permute-done.14, bf16[512,128]{1,0:T(8,128)(2,1)} %collective-permute-done.15, bf16[512,128]{1,0:T(8,128)(2,1)S(1)} %get-tuple-element.150, ...), kind=kLoop, calls=%fused_computation.120 | loop fusion | flops 2162688 | bytes 1179660 | tf_op jit(solution)/shard_map/convert_element_type | solution.py:201
  76.6 2.4 %collective-permute-start.25 = (bf16[512,128]{1,0:T(8,128)(2,1)S(1)}, bf16[512,128]{1,0:T(8,128)(2,1)S(1)}, u32[]{:S(2)}, u32[]{:S(2)}) collective-permute-start(bf16[512,128]{1,0:T(8,128)(2,1)S(1)} %get-tuple-element.179), channel_id=1, source_target_pairs={{0,4},{4,0},{8,12},{12,8},{16,20},{20,16},{24,28},{28,24},{1,5},{5... | collective-permute-start | bytes 393224 | tf_op jit(solution)/shard_map/ppermute | solution.py:165
  79.3 1.2 %collective-permute-start.27 = (bf16[512,128]{1,0:T(8,128)(2,1)S(1)}, bf16[512,128]{1,0:T(8,128)(2,1)S(1)}, u32[]{:S(2)}, u32[]{:S(2)}) collective-permute-start(bf16[512,128]{1,0:T(8,128)(2,1)S(1)} %get-tuple-element.178), channel_id=1, source_target_pairs={{0,12},{4,8},{8,4},{12,0},{16,28},{20,24},{24,20},{28,16},{1,13},{... | collective-permute-start | bytes 393224 | tf_op jit(solution)/shard_map/ppermute | solution.py:165
  80.5 2.6 %shard_map.77 = (f32[256,2048]{1,0:T(8,128)S(1)}, f32[256,2048]{1,0:T(8,128)S(1)}) custom-call(bf16[256,2048]{1,0:T(8,128)(2,1)S(1)} %get-tuple-element.164.q_ref, bf16[256,2048]{1,0:T(8,128)(2,1)S(1)} %copy-done.4, bf16[256,2048]{1,0:T(8,128)(2,1)S(1)} %copy-done.7, bf16[256,2048]{1,0:T(8,128)(2,1)S(1)} %get-tuple-element.167.g_ref), custom_call_target="tpu_custom_call" | custom-call | flops 1073741824 | bytes 4194304 | tf_op jit(solution)/shard_map/pallas_call | solution.py:245
  83.4 2.0 %collective-permute-start.22 = (bf16[512,128]{1,0:T(8,128)(2,1)S(1)}, bf16[512,128]{1,0:T(8,128)(2,1)S(1)}, u32[]{:S(2)}, u32[]{:S(2)}) collective-permute-start(bf16[512,128]{1,0:T(8,128)(2,1)S(1)} %get-tuple-element.183), channel_id=1, source_target_pairs={{0,4},{4,0},{8,12},{12,8},{16,20},{20,16},{24,28},{28,24},{1,5},{5... | collective-permute-start | bytes 393224 | tf_op jit(solution)/shard_map/ppermute | solution.py:165
  85.8 1.2 %collective-permute-start.24 = (bf16[512,128]{1,0:T(8,128)(2,1)S(1)}, bf16[512,128]{1,0:T(8,128)(2,1)S(1)}, u32[]{:S(2)}, u32[]{:S(2)}) collective-permute-start(bf16[512,128]{1,0:T(8,128)(2,1)S(1)} %get-tuple-element.182), channel_id=1, source_target_pairs={{0,12},{4,8},{8,4},{12,0},{16,28},{20,24},{24,20},{28,16},{1,13},{... | collective-permute-start | bytes 393224 | tf_op jit(solution)/shard_map/ppermute | solution.py:165
  87.0 2.0 %shard_map.78 = (bf16[256,4096]{1,0:T(8,128)(2,1)}, bf16[256,4096]{1,0:T(8,128)(2,1)}) custom-call(s32[1]{0:T(128)} %bitcast.mem, bf16[256,2048]{1,0:T(8,128)(2,1)S(1)} %get-tuple-element.155.k_ref, bf16[256,2048]{1,0:T(8,128)(2,1)S(1)} %get-tuple-element.156.v_ref, f32[256,2048]{1,0:T(8,128)S(1)} %get-tuple-element.173.kl_ref, ...), custom_call_target="tpu_custom_call" | custom-call | flops 268435456 | bytes 4194304 | tf_op jit(solution)/shard_map/pallas_call | solution.py:245
  89.0 1.4 %collective-permute-done.23.rest_2_ = bf16[512,128]{1,0:T(8,128)(2,1)S(1)} collective-permute-done((bf16[512,128]{1,0:T(8,128)(2,1)S(1)}, bf16[512,128]{1,0:T(8,128)(2,1)S(1)}, u32[]{:S(2)}, u32[]{:S(2)}) %collective-permute-start.23) | collective-permute-done | bytes 131104 | tf_op jit(solution)/shard_map/ppermute | solution.py:165
  90.4 1.3 %collective-permute-done.24.rest_3_ = bf16[512,128]{1,0:T(8,128)(2,1)S(1)} collective-permute-done((bf16[512,128]{1,0:T(8,128)(2,1)S(1)}, bf16[512,128]{1,0:T(8,128)(2,1)S(1)}, u32[]{:S(2)}, u32[]{:S(2)}) %collective-permute-start.24) | collective-permute-done | bytes 131104 | tf_op jit(solution)/shard_map/ppermute | solution.py:165
  91.7 2.0 %shard_map.79 = (bf16[256,4096]{1,0:T(8,128)(2,1)}, bf16[256,4096]{1,0:T(8,128)(2,1)}) custom-call(s32[1]{0:T(128)} %bitcast.mem, bf16[256,2048]{1,0:T(8,128)(2,1)S(1)} %copy-done.4, bf16[256,2048]{1,0:T(8,128)(2,1)S(1)} %copy-done.7, f32[256,2048]{1,0:T(8,128)S(1)} %get-tuple-element.170.kl_ref, ...), custom_call_target="tpu_custom_call", output_to_operand_aliasing={{0}: (9, {}), {1}: (10, {})} | custom-call | flops 268435456 | bytes 4194304 | tf_op jit(solution)/shard_map/pallas_call | solution.py:245
  (74 shorter events, 6.0 us)
Async XLA Ops:
  3.0 9.0 %collective-permute-start = (bf16[512,128]{1,0:T(8,128)(2,1)S(1)}, bf16[512,128]{1,0:T(8,128)(2,1)S(1)}, u32[]{:S(2)}, u32[]{:S(2)}) collective-permute-start(bf16[512,128]{1,0:T(8,128)(2,1)S(1)} %get-tuple-element.91), channel_id=1, source_target_pairs={{0,4},{4,0},{8,12},{12,8},{16,20},{20,16},{24,28},{28,24},{1,5},{5... | collective-permute-start | bytes 393224 | tf_op jit(solution)/shard_map/ppermute | solution.py:165
  6.1 6.4 %collective-permute-start.1 = (bf16[512,128]{1,0:T(8,128)(2,1)S(1)}, bf16[512,128]{1,0:T(8,128)(2,1)S(1)}, u32[]{:S(2)}, u32[]{:S(2)}) collective-permute-start(bf16[512,128]{1,0:T(8,128)(2,1)S(1)} %get-tuple-element.92), channel_id=1, source_target_pairs={{0,8},{4,12},{8,0},{12,4},{16,24},{20,28},{24,16},{28,20},{1,9},{5... | collective-permute-start | bytes 393224 | tf_op jit(solution)/shard_map/ppermute | solution.py:165
  7.6 15.5 %copy-start.18 = (f32[4096]{0:T(1024)S(1)}, f32[4096]{0:T(1024)}, u32[]{:S(2)}) copy-start(f32[4096]{0:T(1024)} %param.8) | copy-start | bytes 49156
  7.6 6.0 %collective-permute-start.2 = (bf16[512,128]{1,0:T(8,128)(2,1)S(1)}, bf16[512,128]{1,0:T(8,128)(2,1)S(1)}, u32[]{:S(2)}, u32[]{:S(2)}) collective-permute-start(bf16[512,128]{1,0:T(8,128)(2,1)S(1)} %get-tuple-element.93), channel_id=1, source_target_pairs={{0,12},{4,8},{8,4},{12,0},{16,28},{20,24},{24,20},{28,16},{1,13},{... | collective-permute-start | bytes 393224 | tf_op jit(solution)/shard_map/ppermute | solution.py:165
  10.0 1.0 %copy-start.2 = (bf16[256,2048]{1,0:T(8,128)(2,1)}, bf16[256,2048]{1,0:T(8,128)(2,1)S(1)}, u32[]{:S(2)}) copy-start(bf16[256,2048]{1,0:T(8,128)(2,1)S(1)} %get-tuple-element.165.k_ref) | copy-start | bytes 3145732
  11.1 1.0 %copy-start.5 = (bf16[256,2048]{1,0:T(8,128)(2,1)}, bf16[256,2048]{1,0:T(8,128)(2,1)S(1)}, u32[]{:S(2)}) copy-start(bf16[256,2048]{1,0:T(8,128)(2,1)S(1)} %get-tuple-element.166.v_ref) | copy-start | bytes 3145732
  14.3 12.6 %collective-permute-start.3 = (bf16[512,128]{1,0:T(8,128)(2,1)}, bf16[512,128]{1,0:T(8,128)(2,1)}, u32[]{:S(2)}, u32[]{:S(2)}) collective-permute-start(bf16[512,128]{1,0:T(8,128)(2,1)} %fusion.12), channel_id=1, source_target_pairs={{0,16},{4,20},{8,24},{12,28},{1,17},{5,21},{9,25},{13,29},{2,18},{... | collective-permute-start | bytes 393224 | tf_op jit(solution)/shard_map/ppermute | solution.py:178
  19.7 7.3 %collective-permute-start.9 = (bf16[512,128]{1,0:T(8,128)(2,1)S(1)}, bf16[512,128]{1,0:T(8,128)(2,1)S(1)}, u32[]{:S(2)}, u32[]{:S(2)}) collective-permute-start(bf16[512,128]{1,0:T(8,128)(2,1)S(1)} %get-tuple-element.125), channel_id=1, source_target_pairs={{0,12},{4,8},{8,4},{12,0},{16,28},{20,24},{24,20},{28,16},{1,13},{... | collective-permute-start | bytes 393224 | tf_op jit(solution)/shard_map/ppermute | solution.py:165
  22.1 5.2 %collective-permute-start.8 = (bf16[512,128]{1,0:T(8,128)(2,1)S(1)}, bf16[512,128]{1,0:T(8,128)(2,1)S(1)}, u32[]{:S(2)}, u32[]{:S(2)}) collective-permute-start(bf16[512,128]{1,0:T(8,128)(2,1)S(1)} %get-tuple-element.124), channel_id=1, source_target_pairs={{0,8},{4,12},{8,0},{12,4},{16,24},{20,28},{24,16},{28,20},{1,9},{5... | collective-permute-start | bytes 393224 | tf_op jit(solution)/shard_map/ppermute | solution.py:165
  22.6 5.0 %collective-permute-start.7 = (bf16[512,128]{1,0:T(8,128)(2,1)S(1)}, bf16[512,128]{1,0:T(8,128)(2,1)S(1)}, u32[]{:S(2)}, u32[]{:S(2)}) collective-permute-start(bf16[512,128]{1,0:T(8,128)(2,1)S(1)} %get-tuple-element.123), channel_id=1, source_target_pairs={{0,4},{4,0},{8,12},{12,8},{16,20},{20,16},{24,28},{28,24},{1,5},{5... | collective-permute-start | bytes 393224 | tf_op jit(solution)/shard_map/ppermute | solution.py:165
  23.1 12.2 %copy-start.6 = (bf16[256,2048]{1,0:T(8,128)(2,1)S(1)}, bf16[256,2048]{1,0:T(8,128)(2,1)}, u32[]{:S(2)}) copy-start(bf16[256,2048]{1,0:T(8,128)(2,1)} %copy-done.5) | copy-start | bytes 3145732
  26.9 22.2 %copy-start = (bf16[256,2048]{1,0:T(8,128)(2,1)}, bf16[256,2048]{1,0:T(8,128)(2,1)S(1)}, u32[]{:S(2)}) copy-start(bf16[256,2048]{1,0:T(8,128)(2,1)S(1)} %get-tuple-element.154.q_ref) | copy-start | bytes 3145732
  26.9 8.4 %copy-start.3 = (bf16[256,2048]{1,0:T(8,128)(2,1)S(1)}, bf16[256,2048]{1,0:T(8,128)(2,1)}, u32[]{:S(2)}) copy-start(bf16[256,2048]{1,0:T(8,128)(2,1)} %copy-done.2) | copy-start | bytes 3145732
  27.3 7.0 %copy-start.19 = (bf16[512,128]{1,0:T(8,128)(2,1)}, bf16[512,128]{1,0:T(8,128)(2,1)S(1)}, u32[]{:S(2)}) copy-start(bf16[512,128]{1,0:T(8,128)(2,1)S(1)} %collective-permute-done.8) | copy-start | bytes 393220
  27.6 6.8 %copy-start.21 = (bf16[512,128]{1,0:T(8,128)(2,1)}, bf16[512,128]{1,0:T(8,128)(2,1)S(1)}, u32[]{:S(2)}) copy-start(bf16[512,128]{1,0:T(8,128)(2,1)S(1)} %collective-permute-done.7) | copy-start | bytes 393220
  27.6 11.5 %collective-permute-start.10 = (bf16[512,128]{1,0:T(8,128)(2,1)S(1)}, bf16[512,128]{1,0:T(8,128)(2,1)S(1)}, u32[]{:S(2)}, u32[]{:S(2)}) collective-permute-start(bf16[512,128]{1,0:T(8,128)(2,1)S(1)} %fusion.25), channel_id=1, source_target_pairs={{0,16},{4,20},{8,24},{12,28},{1,17},{5,21},{9,25},{13,29},{2,18},{... | collective-permute-start | bytes 393224 | tf_op jit(solution)/shard_map/ppermute | solution.py:178
  31.2 10.8 %collective-permute-start.4 = (bf16[512,128]{1,0:T(8,128)(2,1)S(1)}, bf16[512,128]{1,0:T(8,128)(2,1)S(1)}, u32[]{:S(2)}, u32[]{:S(2)}) collective-permute-start(bf16[512,128]{1,0:T(8,128)(2,1)S(1)} %get-tuple-element.191), channel_id=1, source_target_pairs={{0,4},{4,0},{8,12},{12,8},{16,20},{20,16},{24,28},{28,24},{1,5},{5... | collective-permute-start | bytes 393224 | tf_op jit(solution)/shard_map/ppermute | solution.py:165
  31.8 11.2 %collective-permute-start.5 = (bf16[512,128]{1,0:T(8,128)(2,1)S(1)}, bf16[512,128]{1,0:T(8,128)(2,1)S(1)}, u32[]{:S(2)}, u32[]{:S(2)}) collective-permute-start(bf16[512,128]{1,0:T(8,128)(2,1)S(1)} %get-tuple-element.193), channel_id=1, source_target_pairs={{0,8},{4,12},{8,0},{12,4},{16,24},{20,28},{24,16},{28,20},{1,9},{5... | collective-permute-start | bytes 393224 | tf_op jit(solution)/shard_map/ppermute | solution.py:165
  34.3 8.7 %collective-permute-start.6 = (bf16[512,128]{1,0:T(8,128)(2,1)S(1)}, bf16[512,128]{1,0:T(8,128)(2,1)S(1)}, u32[]{:S(2)}, u32[]{:S(2)}) collective-permute-start(bf16[512,128]{1,0:T(8,128)(2,1)S(1)} %get-tuple-element.190), channel_id=1, source_target_pairs={{0,12},{4,8},{8,4},{12,0},{16,28},{20,24},{24,20},{28,16},{1,13},{... | collective-permute-start | bytes 393224 | tf_op jit(solution)/shard_map/ppermute | solution.py:165
  35.3 3.8 %copy-start.20 = (bf16[512,128]{1,0:T(8,128)(2,1)S(1)}, bf16[512,128]{1,0:T(8,128)(2,1)}, u32[]{:S(2)}) copy-start(bf16[512,128]{1,0:T(8,128)(2,1)} %copy-done.19) | copy-start | bytes 393220
  35.3 3.8 %copy-start.22 = (bf16[512,128]{1,0:T(8,128)(2,1)S(1)}, bf16[512,128]{1,0:T(8,128)(2,1)}, u32[]{:S(2)}) copy-start(bf16[512,128]{1,0:T(8,128)(2,1)} %copy-done.21) | copy-start | bytes 393220
  39.1 8.8 %copy-start.8 = (f32[256,2048]{1,0:T(8,128)}, f32[256,2048]{1,0:T(8,128)S(1)}, u32[]{:S(2)}) copy-start(f32[256,2048]{1,0:T(8,128)S(1)} %get-tuple-element.131.u_ref) | copy-start | bytes 6291460
  39.4 5.0 %collective-permute-start.11 = (bf16[512,128]{1,0:T(8,128)(2,1)S(1)}, bf16[512,128]{1,0:T(8,128)(2,1)S(1)}, u32[]{:S(2)}, u32[]{:S(2)}) collective-permute-start(bf16[512,128]{1,0:T(8,128)(2,1)S(1)} %get-tuple-element.187), channel_id=1, source_target_pairs={{0,4},{4,0},{8,12},{12,8},{16,20},{20,16},{24,28},{28,24},{1,5},{5... | collective-permute-start | bytes 393224 | tf_op jit(solution)/shard_map/ppermute | solution.py:165
  40.0 5.0 %collective-permute-start.12 = (bf16[512,128]{1,0:T(8,128)(2,1)S(1)}, bf16[512,128]{1,0:T(8,128)(2,1)S(1)}, u32[]{:S(2)}, u32[]{:S(2)}) collective-permute-start(bf16[512,128]{1,0:T(8,128)(2,1)S(1)} %get-tuple-element.189), channel_id=1, source_target_pairs={{0,8},{4,12},{8,0},{12,4},{16,24},{20,28},{24,16},{28,20},{1,9},{5... | collective-permute-start | bytes 393224 | tf_op jit(solution)/shard_map/ppermute | solution.py:165
  42.0 5.9 %collective-permute-start.13 = (bf16[512,128]{1,0:T(8,128)(2,1)S(1)}, bf16[512,128]{1,0:T(8,128)(2,1)S(1)}, u32[]{:S(2)}, u32[]{:S(2)}) collective-permute-start(bf16[512,128]{1,0:T(8,128)(2,1)S(1)} %get-tuple-element.186), channel_id=1, source_target_pairs={{0,12},{4,8},{8,4},{12,0},{16,28},{20,24},{24,20},{28,16},{1,13},{... | collective-permute-start | bytes 393224 | tf_op jit(solution)/shard_map/ppermute | solution.py:165
  49.2 2.0 %copy-start.10 = (f32[256,2048]{1,0:T(8,128)}, f32[256,2048]{1,0:T(8,128)S(1)}, u32[]{:S(2)}) copy-start(f32[256,2048]{1,0:T(8,128)S(1)} %get-tuple-element.139.att_ref) | copy-start | bytes 6291460
  49.2 2.0 %copy-start.14 = (f32[256,128]{1,0:T(8,128)}, f32[256,128]{1,0:T(8,128)S(1)}, u32[]{:S(2)}) copy-start(f32[256,128]{1,0:T(8,128)S(1)} %get-tuple-element.133.rest_2_) | copy-start | bytes 393220
  49.2 2.0 %copy-start.16 = (f32[256,128]{1,0:T(8,128)}, f32[256,128]{1,0:T(8,128)S(1)}, u32[]{:S(2)}) copy-start(f32[256,128]{1,0:T(8,128)S(1)} %get-tuple-element.134.rest_3_) | copy-start | bytes 393220
  52.2 9.9 %collective-permute-start.14 = (bf16[512,128]{1,0:T(8,128)(2,1)}, bf16[512,128]{1,0:T(8,128)(2,1)}, u32[]{:S(2)}, u32[]{:S(2)}) collective-permute-start(bf16[512,128]{1,0:T(8,128)(2,1)} %get-tuple-element.136), channel_id=1, source_target_pairs={{0,4},{4,0},{8,12},{12,8},{16,20},{20,16},{24,28},{28,24},{1,5},{5... | collective-permute-start | bytes 393224 | tf_op jit(solution)/shard_map/ppermute | solution.py:165
  53.7 8.4 %collective-permute-start.15 = (bf16[512,128]{1,0:T(8,128)(2,1)}, bf16[512,128]{1,0:T(8,128)(2,1)}, u32[]{:S(2)}, u32[]{:S(2)}) collective-permute-start(bf16[512,128]{1,0:T(8,128)(2,1)} %get-tuple-element.137), channel_id=1, source_target_pairs={{0,8},{4,12},{8,0},{12,4},{16,24},{20,28},{24,16},{28,20},{1,9},{5... | collective-permute-start | bytes 393224 | tf_op jit(solution)/shard_map/ppermute | solution.py:165
  54.1 7.9 %collective-permute-start.16 = (bf16[512,128]{1,0:T(8,128)(2,1)}, bf16[512,128]{1,0:T(8,128)(2,1)}, u32[]{:S(2)}, u32[]{:S(2)}) collective-permute-start(bf16[512,128]{1,0:T(8,128)(2,1)} %get-tuple-element.138), channel_id=1, source_target_pairs={{0,12},{4,8},{8,4},{12,0},{16,28},{20,24},{24,20},{28,16},{1,13},{... | collective-permute-start | bytes 393224 | tf_op jit(solution)/shard_map/ppermute | solution.py:165
  55.7 1.6 %copy-start.9 = (f32[256,2048]{1,0:T(8,128)S(1)}, f32[256,2048]{1,0:T(8,128)}, u32[]{:S(2)}) copy-start(f32[256,2048]{1,0:T(8,128)} %copy-done.8) | copy-start | bytes 6291460
  57.2 1.6 %copy-start.11 = (f32[256,2048]{1,0:T(8,128)S(1)}, f32[256,2048]{1,0:T(8,128)}, u32[]{:S(2)}) copy-start(f32[256,2048]{1,0:T(8,128)} %copy-done.10) | copy-start | bytes 6291460
  60.6 7.6 %copy-start.1 = (bf16[256,2048]{1,0:T(8,128)(2,1)S(1)}, bf16[256,2048]{1,0:T(8,128)(2,1)}, u32[]{:S(2)}) copy-start(bf16[256,2048]{1,0:T(8,128)(2,1)} %copy-done) | copy-start | bytes 3145732
  60.7 7.6 %copy-start.13 = (bf16[256,2048]{1,0:T(8,128)(2,1)S(1)}, bf16[256,2048]{1,0:T(8,128)(2,1)}, u32[]{:S(2)}) copy-start(bf16[256,2048]{1,0:T(8,128)(2,1)} %copy-done.12) | copy-start | bytes 3145732
  62.1 8.7 %collective-permute-start.19 = (bf16[512,128]{1,0:T(8,128)(2,1)S(1)}, bf16[512,128]{1,0:T(8,128)(2,1)S(1)}, u32[]{:S(2)}, u32[]{:S(2)}) collective-permute-start(bf16[512,128]{1,0:T(8,128)(2,1)S(1)} %get-tuple-element.149), channel_id=1, source_target_pairs={{0,12},{4,8},{8,4},{12,0},{16,28},{20,24},{24,20},{28,16},{1,13},{... | collective-permute-start | bytes 393224 | tf_op jit(solution)/shard_map/ppermute | solution.py:165
  63.6 7.4 %collective-permute-start.18 = (bf16[512,128]{1,0:T(8,128)(2,1)S(1)}, bf16[512,128]{1,0:T(8,128)(2,1)S(1)}, u32[]{:S(2)}, u32[]{:S(2)}) collective-permute-start(bf16[512,128]{1,0:T(8,128)(2,1)S(1)} %get-tuple-element.148), channel_id=1, source_target_pairs={{0,8},{4,12},{8,0},{12,4},{16,24},{20,28},{24,16},{28,20},{1,9},{5... | collective-permute-start | bytes 393224 | tf_op jit(solution)/shard_map/ppermute | solution.py:165
  65.1 5.9 %collective-permute-start.17 = (bf16[512,128]{1,0:T(8,128)(2,1)S(1)}, bf16[512,128]{1,0:T(8,128)(2,1)S(1)}, u32[]{:S(2)}, u32[]{:S(2)}) collective-permute-start(bf16[512,128]{1,0:T(8,128)(2,1)S(1)} %get-tuple-element.147), channel_id=1, source_target_pairs={{0,4},{4,0},{8,12},{12,8},{16,20},{20,16},{24,28},{28,24},{1,5},{5... | collective-permute-start | bytes 393224 | tf_op jit(solution)/shard_map/ppermute | solution.py:165
  66.8 13.8 %copy-start.4 = (bf16[256,2048]{1,0:T(8,128)(2,1)S(1)}, bf16[256,2048]{1,0:T(8,128)(2,1)}, u32[]{:S(2)}) copy-start(bf16[256,2048]{1,0:T(8,128)(2,1)} %copy-done.2) | copy-start | bytes 3145732
  66.8 13.7 %copy-start.7 = (bf16[256,2048]{1,0:T(8,128)(2,1)S(1)}, bf16[256,2048]{1,0:T(8,128)(2,1)}, u32[]{:S(2)}) copy-start(bf16[256,2048]{1,0:T(8,128)(2,1)} %copy-done.5) | copy-start | bytes 3145732
  66.8 8.5 %collective-permute-start.21 = (bf16[512,128]{1,0:T(8,128)(2,1)S(1)}, bf16[512,128]{1,0:T(8,128)(2,1)S(1)}, u32[]{:S(2)}, u32[]{:S(2)}) collective-permute-start(bf16[512,128]{1,0:T(8,128)(2,1)S(1)} %fusion.51), channel_id=1, source_target_pairs={{16,0},{20,4},{24,8},{28,12},{17,1},{21,5},{25,9},{29,13},{18,2},{... | collective-permute-start | bytes 393224 | tf_op jit(solution)/shard_map/ppermute | solution.py:178
  71.1 12.0 %collective-permute-start.20 = (bf16[512,128]{1,0:T(8,128)(2,1)S(1)}, bf16[512,128]{1,0:T(8,128)(2,1)S(1)}, u32[]{:S(2)}, u32[]{:S(2)}) collective-permute-start(bf16[512,128]{1,0:T(8,128)(2,1)S(1)} %fusion.38), channel_id=1, source_target_pairs={{16,0},{20,4},{24,8},{28,12},{17,1},{21,5},{25,9},{29,13},{18,2},{... | collective-permute-start | bytes 393224 | tf_op jit(solution)/shard_map/ppermute | solution.py:178
  76.6 9.2 %collective-permute-start.25 = (bf16[512,128]{1,0:T(8,128)(2,1)S(1)}, bf16[512,128]{1,0:T(8,128)(2,1)S(1)}, u32[]{:S(2)}, u32[]{:S(2)}) collective-permute-start(bf16[512,128]{1,0:T(8,128)(2,1)S(1)} %get-tuple-element.179), channel_id=1, source_target_pairs={{0,4},{4,0},{8,12},{12,8},{16,20},{20,16},{24,28},{28,24},{1,5},{5... | collective-permute-start | bytes 393224 | tf_op jit(solution)/shard_map/ppermute | solution.py:165
  79.0 8.0 %collective-permute-start.26 = (bf16[512,128]{1,0:T(8,128)(2,1)S(1)}, bf16[512,128]{1,0:T(8,128)(2,1)S(1)}, u32[]{:S(2)}, u32[]{:S(2)}) collective-permute-start(bf16[512,128]{1,0:T(8,128)(2,1)S(1)} %get-tuple-element.181), channel_id=1, source_target_pairs={{0,8},{4,12},{8,0},{12,4},{16,24},{20,28},{24,16},{28,20},{1,9},{5... | collective-permute-start | bytes 393224 | tf_op jit(solution)/shard_map/ppermute | solution.py:165
  79.3 7.6 %collective-permute-start.27 = (bf16[512,128]{1,0:T(8,128)(2,1)S(1)}, bf16[512,128]{1,0:T(8,128)(2,1)S(1)}, u32[]{:S(2)}, u32[]{:S(2)}) collective-permute-start(bf16[512,128]{1,0:T(8,128)(2,1)S(1)} %get-tuple-element.178), channel_id=1, source_target_pairs={{0,12},{4,8},{8,4},{12,0},{16,28},{20,24},{24,20},{28,16},{1,13},{... | collective-permute-start | bytes 393224 | tf_op jit(solution)/shard_map/ppermute | solution.py:165
  83.4 5.6 %collective-permute-start.22 = (bf16[512,128]{1,0:T(8,128)(2,1)S(1)}, bf16[512,128]{1,0:T(8,128)(2,1)S(1)}, u32[]{:S(2)}, u32[]{:S(2)}) collective-permute-start(bf16[512,128]{1,0:T(8,128)(2,1)S(1)} %get-tuple-element.183), channel_id=1, source_target_pairs={{0,4},{4,0},{8,12},{12,8},{16,20},{20,16},{24,28},{28,24},{1,5},{5... | collective-permute-start | bytes 393224 | tf_op jit(solution)/shard_map/ppermute | solution.py:165
  85.4 5.0 %collective-permute-start.23 = (bf16[512,128]{1,0:T(8,128)(2,1)S(1)}, bf16[512,128]{1,0:T(8,128)(2,1)S(1)}, u32[]{:S(2)}, u32[]{:S(2)}) collective-permute-start(bf16[512,128]{1,0:T(8,128)(2,1)S(1)} %get-tuple-element.185), channel_id=1, source_target_pairs={{0,8},{4,12},{8,0},{12,4},{16,24},{20,28},{24,16},{28,20},{1,9},{5... | collective-permute-start | bytes 393224 | tf_op jit(solution)/shard_map/ppermute | solution.py:165
  85.8 5.9 %collective-permute-start.24 = (bf16[512,128]{1,0:T(8,128)(2,1)S(1)}, bf16[512,128]{1,0:T(8,128)(2,1)S(1)}, u32[]{:S(2)}, u32[]{:S(2)}) collective-permute-start(bf16[512,128]{1,0:T(8,128)(2,1)S(1)} %get-tuple-element.182), channel_id=1, source_target_pairs={{0,12},{4,8},{8,4},{12,0},{16,28},{20,24},{24,20},{28,16},{1,13},{... | collective-permute-start | bytes 393224 | tf_op jit(solution)/shard_map/ppermute | solution.py:165
  (3 other events, 2.8 us)

commit v4 on v3

--- a/solution.py
+++ b/solution.py
@@ -157,6 +157,54 @@
         copy.wait()
 
 
+def total_kernel(*refs):
+    acc = refs[0][...].astype(F32)
+    for ref in refs[1:-1]:
+        acc = acc + ref[...].astype(F32)
+    refs[-1][...] = acc.astype(refs[-1].dtype)
+
+
+def give_back_kernel(m, forward, mem, carry, *refs):
+    got, back = refs[:m], refs[m:]
+    member = mem[0]
+    for j in range(m):
+        acc = carry[...].astype(F32)
+        for i in range(m):
+            if i != j:
+                source, target = member ^ i, member ^ j
+                take = (source < target) if forward else (source > target)
+                acc = acc + jnp.where(take, got[i][...].astype(F32), 0.0)
+        back[j][...] = acc.astype(BF16)
+
+
+def call(kernel, args, in_specs, out_shape, flops, nbytes, scratch=(), out_specs=None, alias={}):
+    return pl.pallas_call(
+        kernel,
+        in_specs=in_specs,
+        out_specs=out_specs or [VMEM] * len(out_shape),
+        out_shape=out_shape,
+        scratch_shapes=scratch,
+        input_output_aliases=alias,
+        compiler_params=pltpu.CompilerParams(vmem_limit_bytes=8 << 20),
+        cost_estimate=pl.CostEstimate(flops=flops, bytes_accessed=nbytes, transcendentals=0),
+    )(*args)
+
+
+def total_of(got, n):
+    m = len(got)
+    wire = BF16 if n // m == 2 else F32
+    (total,) = call(total_kernel, got, [VMEM] * m, [pltpu.VMEM(got[0].shape, wire)], got[0].size, got[0].size)
+    return total
+
+
+def give_back(got, carry, mem, forward):
+    m = len(got)
+    return call(
+        partial(give_back_kernel, m, forward), (mem, carry, *got), [SMEM] + [VMEM] * (m + 1),
+        [pltpu.VMEM(got[0].shape, BF16)] * m, got[0].size, got[0].size,
+    )
+
+
 def exchange(parts, n):
     m = len(parts)
     out = [parts[0]] + [None] * (m - 1)
@@ -180,7 +228,7 @@
     if groups == 1:
         return jnp.zeros_like(total)
     if groups == 2:
-        return shift(total.astype(BF16), 1)
+        return shift(total, 1)
     run = shift(total, 1)
     by = 1
     while by < groups - 1:
@@ -189,37 +237,20 @@
     return run
 
 
-def give_back(got, carry, member, forward):
-    back = []
-    for j in range(len(got)):
-        acc = carry.astype(F32)
-        for i in range(len(got)):
-            if i != j:
-                source, target = member ^ i, member ^ j
-                take = (source < target) if forward else (source > target)
-                acc = acc + jnp.where(take, got[i].astype(F32), 0.0)
-        back.append(acc.astype(BF16))
-    return back
-
-
-def total_of(got):
-    return sum(x.astype(F32) for x in got)
-
-
-def scan_chunks(first, second_of, n, member, forward, fill_a, fill_b):
+def scan_chunks(first, second_of, n, mem, forward, fill_a, fill_b):
     m = len(first)
     got_a = exchange(first, n)
     second, extra = second_of()
     got_a, second, extra = barrier((got_a, second, extra))
-    carry_a = carry_groups(total_of(got_a), n, m, forward)
+    carry_a = carry_groups(total_of(got_a, n), n, m, forward)
     got_b = exchange(second, n)
     made_a = fill_a(extra)
     carry_a, made_a, extra = barrier((carry_a, made_a, extra))
-    back_a = exchange(give_back(got_a, carry_a, member, forward), n)
-    carry_b = carry_groups(total_of(got_b), n, m, forward)
+    back_a = exchange(give_back(got_a, carry_a, mem, forward), n)
+    carry_b = carry_groups(total_of(got_b, n), n, m, forward)
     made_b = fill_b(extra)
     carry_b, made_b = barrier((carry_b, made_b))
-    back_b = exchange(give_back(got_b, carry_b, member, forward), n)
+    back_b = exchange(give_back(got_b, carry_b, mem, forward), n)
     return (back_a, back_b), (made_a, made_b)
 
 
@@ -241,18 +272,6 @@
     sems = pltpu.SemaphoreType.DMA((2, m))
     unit = 2 * rows * DH * half
 
-    def call(kernel, args, in_specs, out_shape, flops, nbytes, scratch=(), out_specs=None, alias={}):
-        return pl.pallas_call(
-            kernel,
-            in_specs=in_specs,
-            out_specs=out_specs or [VMEM] * len(out_shape),
-            out_shape=out_shape,
-            scratch_shapes=scratch,
-            input_output_aliases=alias,
-            compiler_params=pltpu.CompilerParams(vmem_limit_bytes=12 << 20),
-            cost_estimate=pl.CostEstimate(flops=flops, bytes_accessed=nbytes, transcendentals=0),
-        )(*args)
-
     def states_of(c):
         k, v, *parts = call(
             partial(state_kernel, c, part, m), (mem, keys, values), [SMEM, HBM, HBM],
@@ -281,7 +300,7 @@
         kv[1] = extra[1]
         return local_of(1, extra[1])
 
-    prefix, made = scan_chunks(parts_a, second_states, n, member, True, fill_a, fill_b)
+    prefix, made = scan_chunks(parts_a, second_states, n, mem, True, fill_a, fill_b)
 
     attended, sums = [], []
     for c in range(CHUNKS):
@@ -311,7 +330,7 @@
         return parts_b, (near_a, near_b)
 
     suffix, made = scan_chunks(
-        parts_a, second_grads, n, member, False, lambda e: back_local_of(e[0]), lambda e: back_local_of(e[1])
+        parts_a, second_grads, n, mem, False, lambda e: back_local_of(e[0]), lambda e: back_local_of(e[1])
     )
 
     outs = ()

time: 94.3 us -> 91 us (0.965)
  waiting for transfers between devices: 11.3 us -> 22.1 us
  local copies, waits for them, and re-layouts: 8.02 us -> 0.01 us
  other arithmetic: 5.07 us -> 0 us
  starting transfers between devices: 40.8 us -> 38.8 us
  Pallas kernels: 27.4 us -> 28.4 us
    ppermute x24, waiting for transfers between devices: 8.6 us -> 22.1 us  [exchange(): out[j] = lax.ppermute(parts[j], 'seq', perm)]
    unnamed x46 -> x2, local copies, waits for them, and re-layouts: 8.02 us -> 0.01 us
    convert_element_type x8 -> x0, other arithmetic: 5.07 us -> none  [the longest x4 3.1 us: give_back(): back.append(acc.astype(BF16))]
    ppermute x4, waiting for transfers between devices: 2.71 us -> 0.01 us  [shift(): return lax.ppermute(x, 'seq', perm)]
    ppermute x4, starting transfers between devices: 10.6 us -> 9.28 us  [shift(): return lax.ppermute(x, 'seq', perm)]
    pallas_call x12 -> x20, Pallas kernels: 27.4 us -> 28.4 us  [call(): pl.pallas_call(kernel, in_specs=in_specs, out_specs=out_specs or [VMEM] *...]
  transfers between devices with their start and end apart: 28 -> 28, of which waited for: 11 -> 10; matrix products, arithmetic and copies ran while one was open for 5% -> 0% of each run, Pallas kernels for 21% -> 24%
where the time goes in v4:
time: 91 us; the launch traced here: 90.5 us
  starting transfers between devices  38.8 us (43%)
  Pallas kernels  28.4 us (31%)
  waiting for transfers between devices  22.1 us (24%)
  between operations  1.12 us (1%)
    ppermute x24, starting transfers between devices, exchange(): out[j] = lax.ppermute(parts[j], 'seq', perm)  29.6 us
    pallas_call x20, Pallas kernels, call(): pl.pallas_call(kernel, in_specs=in_specs, out_specs=out_specs or [VMEM] *...  28.4 us
    ppermute x24, waiting for transfers between devices, exchange(): out[j] = lax.ppermute(parts[j], 'seq', perm)  22.1 us
    ppermute x4, starting transfers between devices, shift(): return lax.ppermute(x, 'seq', perm)  9.28 us
  transfers between devices with their start and end apart: 28, of which 10 were waited for; matrix products, arithmetic and copies ran while one was open for 0% of the time, Pallas kernels for 24%

profile of v4, /device:TPU:0, one launch (start us, length us, event | category | flops | bytes accessed | tf_op | source)
XLA Modules:
  0.0 90.5 jit_solution(2134043256135789199)
XLA Ops:
  0.6 2.4 %shard_map.68 = (bf16[256,2048]{1,0:T(8,128)(2,1)S(1)}, bf16[256,2048]{1,0:T(8,128)(2,1)S(1)}, bf16[512,128]{1,0:T(8,128)(2,1)S(1)}, bf16[512,128]{1,0:T(8,128)(...) custom-call(s32[1]{0:T(128)} %bitcast.mem, bf16[256,4096]{1,0:T(8,128)(2,1)} %k_hbm.3, ...), custom_call_target="tpu_custom_call" | custom-call | flops 134217728 | bytes 3145728 | tf_op jit(solution)/shard_map/pallas_call | solution.py:181
  3.0 3.0 %collective-permute-start = (bf16[512,128]{1,0:T(8,128)(2,1)S(1)}, bf16[512,128]{1,0:T(8,128)(2,1)S(1)}, u32[]{:S(2)}, u32[]{:S(2)}) collective-permute-start(bf16[512,128]{1,0:T(8,128)(2,1)S(1)} %get-tuple-element.107), channel_id=1, source_target_pairs={{0,4},{4,0},{8,12},{12,8},{16,20},{20,16},{24,28},{28,24},{1,5},{5... | collective-permute-start | bytes 393224 | tf_op jit(solution)/shard_map/ppermute | solution.py:213
  6.1 1.6 %collective-permute-start.1 = (bf16[512,128]{1,0:T(8,128)(2,1)S(1)}, bf16[512,128]{1,0:T(8,128)(2,1)S(1)}, u32[]{:S(2)}, u32[]{:S(2)}) collective-permute-start(bf16[512,128]{1,0:T(8,128)(2,1)S(1)} %get-tuple-element.108), channel_id=1, source_target_pairs={{0,8},{4,12},{8,0},{12,4},{16,24},{20,28},{24,16},{28,20},{1,9},{5... | collective-permute-start | bytes 393224 | tf_op jit(solution)/shard_map/ppermute | solution.py:213
  7.6 2.4 %shard_map.69 = (bf16[256,2048]{1,0:T(8,128)(2,1)S(1)}, bf16[256,2048]{1,0:T(8,128)(2,1)S(1)}, bf16[512,128]{1,0:T(8,128)(2,1)S(1)}, bf16[512,128]{1,0:T(8,128)(...) custom-call(s32[1]{0:T(128)} %bitcast.mem, bf16[256,4096]{1,0:T(8,128)(2,1)} %k_hbm.3, ...), custom_call_target="tpu_custom_call" | custom-call | flops 134217728 | bytes 3145728 | tf_op jit(solution)/shard_map/pallas_call | solution.py:181
  10.1 2.4 %collective-permute-done.1.refs_2_ = bf16[512,128]{1,0:T(8,128)(2,1)S(1)} collective-permute-done((bf16[512,128]{1,0:T(8,128)(2,1)S(1)}, bf16[512,128]{1,0:T(8,128)(2,1)S(1)}, u32[]{:S(2)}, u32[]{:S(2)}) %collective-permute-start.1) | collective-permute-done | bytes 131104 | tf_op jit(solution)/shard_map/ppermute | solution.py:213
  12.4 1.2 %collective-permute-done.2.refs_3_ = bf16[512,128]{1,0:T(8,128)(2,1)S(1)} collective-permute-done((bf16[512,128]{1,0:T(8,128)(2,1)S(1)}, bf16[512,128]{1,0:T(8,128)(2,1)S(1)}, u32[]{:S(2)}, u32[]{:S(2)}) %collective-permute-start.2) | collective-permute-done | bytes 131104 | tf_op jit(solution)/shard_map/ppermute | solution.py:213
  13.6 1.7 %collective-permute-start.7 = (bf16[512,128]{1,0:T(8,128)(2,1)S(1)}, bf16[512,128]{1,0:T(8,128)(2,1)S(1)}, u32[]{:S(2)}, u32[]{:S(2)}) collective-permute-start(bf16[512,128]{1,0:T(8,128)(2,1)S(1)} %get-tuple-element.143), channel_id=1, source_target_pairs={{0,4},{4,0},{8,12},{12,8},{16,20},{20,16},{24,28},{28,24},{1,5},{5... | collective-permute-start | bytes 393224 | tf_op jit(solution)/shard_map/ppermute | solution.py:213
  15.3 1.6 %collective-permute-start.8 = (bf16[512,128]{1,0:T(8,128)(2,1)S(1)}, bf16[512,128]{1,0:T(8,128)(2,1)S(1)}, u32[]{:S(2)}, u32[]{:S(2)}) collective-permute-start(bf16[512,128]{1,0:T(8,128)(2,1)S(1)} %get-tuple-element.144), channel_id=1, source_target_pairs={{0,8},{4,12},{8,0},{12,4},{16,24},{20,28},{24,16},{28,20},{1,9},{5... | collective-permute-start | bytes 393224 | tf_op jit(solution)/shard_map/ppermute | solution.py:213
  16.9 0.3 collective-permute-start.9
  17.2 4.7 %collective-permute-start.3 = (bf16[512,128]{1,0:T(8,128)(2,1)S(1)}, bf16[512,128]{1,0:T(8,128)(2,1)S(1)}, u32[]{:S(2)}, u32[]{:S(2)}) collective-permute-start(bf16[512,128]{1,0:T(8,128)(2,1)S(1)} %shard_map.70), channel_id=1, source_target_pairs={{0,16},{4,20},{8,24},{12,28},{1,17},{5,21},{9,25},{13,29},{2,18},{... | collective-permute-start | bytes 393224 | tf_op jit(solution)/shard_map/ppermute | solution.py:226
  21.9 3.7 %shard_map.71 = (bf16[256,2048]{1,0:T(8,128)(2,1)S(1)}, f32[256,2048]{1,0:T(8,128)S(1)}, f32[256,2048]{1,0:T(8,128)S(1)}) custom-call(bf16[256,2048]{1,0:T(8,128)(2,1)S(1)} %get-tuple-element.179.k_ref, bf16[256,2048]{1,0:T(8,128)(2,1)S(1)} %get-tuple-element.180.v_ref, f32[1,4096]{1,0:T(1,128)S(1)} %bitcast.2, bf16[256,4096]{1,0:T(8,128)(2,1)} %q_hbm.3, ...), custom_call_target="tpu_custom_call" | custom-call | flops 536870912 | bytes 6291456 | tf_op jit(solution)/shard_map/pallas_call | solution.py:181
  25.7 1.8 %collective-permute-start.10 = (bf16[512,128]{1,0:T(8,128)(2,1)S(1)}, bf16[512,128]{1,0:T(8,128)(2,1)S(1)}, u32[]{:S(2)}, u32[]{:S(2)}) collective-permute-start(bf16[512,128]{1,0:T(8,128)(2,1)S(1)} %shard_map.74), channel_id=1, source_target_pairs={{0,16},{4,20},{8,24},{12,28},{1,17},{5,21},{9,25},{13,29},{2,18},{... | collective-permute-start | bytes 393224 | tf_op jit(solution)/shard_map/ppermute | solution.py:226
  27.5 0.4 shard_map.72
  27.9 1.2 %collective-permute-start.4 = (bf16[512,128]{1,0:T(8,128)(2,1)S(1)}, bf16[512,128]{1,0:T(8,128)(2,1)S(1)}, u32[]{:S(2)}, u32[]{:S(2)}) collective-permute-start(bf16[512,128]{1,0:T(8,128)(2,1)S(1)} %get-tuple-element.136), channel_id=1, source_target_pairs={{0,4},{4,0},{8,12},{12,8},{16,20},{20,16},{24,28},{28,24},{1,5},{5... | collective-permute-start | bytes 393224 | tf_op jit(solution)/shard_map/ppermute | solution.py:213
  29.1 2.6 %collective-permute-start.5 = (bf16[512,128]{1,0:T(8,128)(2,1)S(1)}, bf16[512,128]{1,0:T(8,128)(2,1)S(1)}, u32[]{:S(2)}, u32[]{:S(2)}) collective-permute-start(bf16[512,128]{1,0:T(8,128)(2,1)S(1)} %get-tuple-element.137), channel_id=1, source_target_pairs={{0,8},{4,12},{8,0},{12,4},{16,24},{20,28},{24,16},{28,20},{1,9},{5... | collective-permute-start | bytes 393224 | tf_op jit(solution)/shard_map/ppermute | solution.py:213
  31.7 3.7 %shard_map.75 = (bf16[256,2048]{1,0:T(8,128)(2,1)S(1)}, f32[256,2048]{1,0:T(8,128)S(1)}, f32[256,2048]{1,0:T(8,128)S(1)}) custom-call(bf16[256,2048]{1,0:T(8,128)(2,1)S(1)} %get-tuple-element.189.k_ref, bf16[256,2048]{1,0:T(8,128)(2,1)S(1)} %get-tuple-element.190.v_ref, f32[1,4096]{1,0:T(1,128)S(1)} %bitcast.3, bf16[256,4096]{1,0:T(8,128)(2,1)} %q_hbm.3, ...), custom_call_target="tpu_custom_call" | custom-call | flops 536870912 | bytes 6291456 | tf_op jit(solution)/shard_map/pallas_call | solution.py:181
  35.4 0.4 shard_map.76
  35.8 1.5 %collective-permute-start.11 = (bf16[512,128]{1,0:T(8,128)(2,1)S(1)}, bf16[512,128]{1,0:T(8,128)(2,1)S(1)}, u32[]{:S(2)}, u32[]{:S(2)}) collective-permute-start(bf16[512,128]{1,0:T(8,128)(2,1)S(1)} %get-tuple-element.154), channel_id=1, source_target_pairs={{0,4},{4,0},{8,12},{12,8},{16,20},{20,16},{24,28},{28,24},{1,5},{5... | collective-permute-start | bytes 393224 | tf_op jit(solution)/shard_map/ppermute | solution.py:213
  37.3 2.0 %collective-permute-start.12 = (bf16[512,128]{1,0:T(8,128)(2,1)S(1)}, bf16[512,128]{1,0:T(8,128)(2,1)S(1)}, u32[]{:S(2)}, u32[]{:S(2)}) collective-permute-start(bf16[512,128]{1,0:T(8,128)(2,1)S(1)} %get-tuple-element.155), channel_id=1, source_target_pairs={{0,8},{4,12},{8,0},{12,4},{16,24},{20,28},{24,16},{28,20},{1,9},{5... | collective-permute-start | bytes 393224 | tf_op jit(solution)/shard_map/ppermute | solution.py:213
  39.3 1.3 %shard_map.73 = (f32[256,2048]{1,0:T(8,128)S(1)}, f32[256,128]{1,0:T(8,128)S(1)}, f32[256,128]{1,0:T(8,128)S(1)}) custom-call(s32[1]{0:T(128)} %bitcast.mem, bf16[256,2048]{1,0:T(8,128)(2,1)S(1)} %get-tuple-element.178.q_ref, f32[256,2048]{1,0:T(8,128)S(1)} %get-tuple-element.132.loc_ref, ...), custom_call_target="tpu_custom_call", output_to_operand_aliasing={{0}: (2, {})} | custom-call | flops 134217728 | bytes 2097152 | tf_op jit(solution)/shard_map/pallas_call | solution.py:181
  40.6 1.0 %collective-permute-done.11.rest_1_ = bf16[512,128]{1,0:T(8,128)(2,1)S(1)} collective-permute-done((bf16[512,128]{1,0:T(8,128)(2,1)S(1)}, bf16[512,128]{1,0:T(8,128)(2,1)S(1)}, u32[]{:S(2)}, u32[]{:S(2)}) %collective-permute-start.11) | collective-permute-done | bytes 131104 | tf_op jit(solution)/shard_map/ppermute | solution.py:213
  41.6 0.6 collective-permute-done.12.rest_2_
  42.3 2.9 %collective-permute-done.13.rest_3_ = bf16[512,128]{1,0:T(8,128)(2,1)S(1)} collective-permute-done((bf16[512,128]{1,0:T(8,128)(2,1)S(1)}, bf16[512,128]{1,0:T(8,128)(2,1)S(1)}, u32[]{:S(2)}, u32[]{:S(2)}) %collective-permute-start.13) | collective-permute-done | bytes 131104 | tf_op jit(solution)/shard_map/ppermute | solution.py:213
  45.2 1.3 %shard_map.77 = (f32[256,2048]{1,0:T(8,128)S(1)}, f32[256,128]{1,0:T(8,128)S(1)}, f32[256,128]{1,0:T(8,128)S(1)}) custom-call(s32[1]{0:T(128)} %bitcast.mem, bf16[256,2048]{1,0:T(8,128)(2,1)S(1)} %get-tuple-element.188.q_ref, f32[256,2048]{1,0:T(8,128)S(1)} %get-tuple-element.150.loc_ref, ...), custom_call_target="tpu_custom_call", output_to_operand_aliasing={{0}: (2, {})} | custom-call | flops 134217728 | bytes 2097152 | tf_op jit(solution)/shard_map/pallas_call | solution.py:181
  46.5 1.4 %shard_map.78 = (bf16[256,2048]{1,0:T(8,128)(2,1)S(1)}, bf16[512,128]{1,0:T(8,128)(2,1)S(1)}, bf16[512,128]{1,0:T(8,128)(2,1)S(1)}, bf16[512,128]{1,0:T(8,128)(2,1)S(1)}, bf16[512,128]{1,0:T(8,128)(2,1)S(1)}) custom-call(s32[1]{0:T(128)} %bitcast.mem, bf16[256,2048]{1,0:T(8,128)(2,1)S(1)} %get-tuple-element.178.q_ref, ...), custom_call_target="tpu_custom_call" | custom-call | flops 134217728 | bytes 2097152 | tf_op jit(solution)/shard_map/pallas_call | solution.py:181
  47.9 0.5 collective-permute-start.14
  48.4 1.6 %collective-permute-start.15 = (bf16[512,128]{1,0:T(8,128)(2,1)S(1)}, bf16[512,128]{1,0:T(8,128)(2,1)S(1)}, u32[]{:S(2)}, u32[]{:S(2)}) collective-permute-start(bf16[512,128]{1,0:T(8,128)(2,1)S(1)} %get-tuple-element.161), channel_id=1, source_target_pairs={{0,8},{4,12},{8,0},{12,4},{16,24},{20,28},{24,16},{28,20},{1,9},{5... | collective-permute-start | bytes 393224 | tf_op jit(solution)/shard_map/ppermute | solution.py:213
  49.9 1.5 %collective-permute-start.16 = (bf16[512,128]{1,0:T(8,128)(2,1)S(1)}, bf16[512,128]{1,0:T(8,128)(2,1)S(1)}, u32[]{:S(2)}, u32[]{:S(2)}) collective-permute-start(bf16[512,128]{1,0:T(8,128)(2,1)S(1)} %get-tuple-element.162), channel_id=1, source_target_pairs={{0,12},{4,8},{8,4},{12,0},{16,28},{20,24},{24,20},{28,16},{1,13},{... | collective-permute-start | bytes 393224 | tf_op jit(solution)/shard_map/ppermute | solution.py:213
  51.4 1.4 %shard_map.79 = (bf16[256,2048]{1,0:T(8,128)(2,1)S(1)}, bf16[512,128]{1,0:T(8,128)(2,1)S(1)}, bf16[512,128]{1,0:T(8,128)(2,1)S(1)}, bf16[512,128]{1,0:T(8,128)(2,1)S(1)}, bf16[512,128]{1,0:T(8,128)(2,1)S(1)}) custom-call(s32[1]{0:T(128)} %bitcast.mem, bf16[256,2048]{1,0:T(8,128)(2,1)S(1)} %get-tuple-element.188.q_ref, ...), custom_call_target="tpu_custom_call" | custom-call | flops 134217728 | bytes 2097152 | tf_op jit(solution)/shard_map/pallas_call | solution.py:181
  52.8 1.2 %collective-permute-done.14.refs_1_ = bf16[512,128]{1,0:T(8,128)(2,1)S(1)} collective-permute-done((bf16[512,128]{1,0:T(8,128)(2,1)S(1)}, bf16[512,128]{1,0:T(8,128)(2,1)S(1)}, u32[]{:S(2)}, u32[]{:S(2)}) %collective-permute-start.14) | collective-permute-done | bytes 131104 | tf_op jit(solution)/shard_map/ppermute | solution.py:213
  54.0 0.6 collective-permute-done.15.refs_2_
  54.6 5.3 %collective-permute-done.16.refs_3_ = bf16[512,128]{1,0:T(8,128)(2,1)S(1)} collective-permute-done((bf16[512,128]{1,0:T(8,128)(2,1)S(1)}, bf16[512,128]{1,0:T(8,128)(2,1)S(1)}, u32[]{:S(2)}, u32[]{:S(2)}) %collective-permute-start.16) | collective-permute-done | bytes 131104 | tf_op jit(solution)/shard_map/ppermute | solution.py:213
  59.9 0.5 collective-permute-start.18
  60.4 3.0 %collective-permute-start.19 = (bf16[512,128]{1,0:T(8,128)(2,1)S(1)}, bf16[512,128]{1,0:T(8,128)(2,1)S(1)}, u32[]{:S(2)}, u32[]{:S(2)}) collective-permute-start(bf16[512,128]{1,0:T(8,128)(2,1)S(1)} %get-tuple-element.173), channel_id=1, source_target_pairs={{0,12},{4,8},{8,4},{12,0},{16,28},{20,24},{24,20},{28,16},{1,13},{... | collective-permute-start | bytes 393224 | tf_op jit(solution)/shard_map/ppermute | solution.py:213
  63.4 1.3 %collective-permute-start.21 = (bf16[512,128]{1,0:T(8,128)(2,1)S(1)}, bf16[512,128]{1,0:T(8,128)(2,1)S(1)}, u32[]{:S(2)}, u32[]{:S(2)}) collective-permute-start(bf16[512,128]{1,0:T(8,128)(2,1)S(1)} %shard_map.81), channel_id=1, source_target_pairs={{16,0},{20,4},{24,8},{28,12},{17,1},{21,5},{25,9},{29,13},{18,2},{... | collective-permute-start | bytes 393224 | tf_op jit(solution)/shard_map/ppermute | solution.py:226
  64.7 2.6 %shard_map.82 = (f32[256,2048]{1,0:T(8,128)S(1)}, f32[256,2048]{1,0:T(8,128)S(1)}) custom-call(bf16[256,2048]{1,0:T(8,128)(2,1)S(1)} %get-tuple-element.178.q_ref, bf16[256,2048]{1,0:T(8,128)(2,1)S(1)} %get-tuple-element.179.k_ref, bf16[256,2048]{1,0:T(8,128)(2,1)S(1)} %get-tuple-element.180.v_ref, bf16[256,2048]{1,0:T(8,128)(2,1)S(1)} %get-tuple-element.181.g_ref), custom_call_target="tpu_custom_call" | custom-call | flops 1073741824 | bytes 4194304 | tf_op jit(solution)/shard_map/pallas_call | solution.py:181
  67.3 4.6 %collective-permute-done.19.refs_3_ = bf16[512,128]{1,0:T(8,128)(2,1)S(1)} collective-permute-done((bf16[512,128]{1,0:T(8,128)(2,1)S(1)}, bf16[512,128]{1,0:T(8,128)(2,1)S(1)}, u32[]{:S(2)}, u32[]{:S(2)}) %collective-permute-start.19) | collective-permute-done | bytes 131104 | tf_op jit(solution)/shard_map/ppermute | solution.py:213
  72.0 1.5 %collective-permute-start.20 = (bf16[512,128]{1,0:T(8,128)(2,1)S(1)}, bf16[512,128]{1,0:T(8,128)(2,1)S(1)}, u32[]{:S(2)}, u32[]{:S(2)}) collective-permute-start(bf16[512,128]{1,0:T(8,128)(2,1)S(1)} %shard_map.80), channel_id=1, source_target_pairs={{16,0},{20,4},{24,8},{28,12},{17,1},{21,5},{25,9},{29,13},{18,2},{... | collective-permute-start | bytes 393224 | tf_op jit(solution)/shard_map/ppermute | solution.py:226
  73.5 0.4 shard_map.85
  74.0 1.0 %collective-permute-start.26 = (bf16[512,128]{1,0:T(8,128)(2,1)S(1)}, bf16[512,128]{1,0:T(8,128)(2,1)S(1)}, u32[]{:S(2)}, u32[]{:S(2)}) collective-permute-start(bf16[512,128]{1,0:T(8,128)(2,1)S(1)} %get-tuple-element.206), channel_id=1, source_target_pairs={{0,8},{4,12},{8,0},{12,4},{16,24},{20,28},{24,16},{28,20},{1,9},{5... | collective-permute-start | bytes 393224 | tf_op jit(solution)/shard_map/ppermute | solution.py:213
  75.0 2.4 %collective-permute-start.27 = (bf16[512,128]{1,0:T(8,128)(2,1)S(1)}, bf16[512,128]{1,0:T(8,128)(2,1)S(1)}, u32[]{:S(2)}, u32[]{:S(2)}) collective-permute-start(bf16[512,128]{1,0:T(8,128)(2,1)S(1)} %get-tuple-element.207), channel_id=1, source_target_pairs={{0,12},{4,8},{8,4},{12,0},{16,28},{20,24},{24,20},{28,16},{1,13},{... | collective-permute-start | bytes 393224 | tf_op jit(solution)/shard_map/ppermute | solution.py:213
  77.4 2.6 %shard_map.83 = (f32[256,2048]{1,0:T(8,128)S(1)}, f32[256,2048]{1,0:T(8,128)S(1)}) custom-call(bf16[256,2048]{1,0:T(8,128)(2,1)S(1)} %get-tuple-element.188.q_ref, bf16[256,2048]{1,0:T(8,128)(2,1)S(1)} %get-tuple-element.189.k_ref, bf16[256,2048]{1,0:T(8,128)(2,1)S(1)} %get-tuple-element.190.v_ref, bf16[256,2048]{1,0:T(8,128)(2,1)S(1)} %get-tuple-element.191.g_ref), custom_call_target="tpu_custom_call" | custom-call | flops 1073741824 | bytes 4194304 | tf_op jit(solution)/shard_map/pallas_call | solution.py:181
  80.0 0.4 shard_map.84
  80.5 1.0 %collective-permute-start.23 = (bf16[512,128]{1,0:T(8,128)(2,1)S(1)}, bf16[512,128]{1,0:T(8,128)(2,1)S(1)}, u32[]{:S(2)}, u32[]{:S(2)}) collective-permute-start(bf16[512,128]{1,0:T(8,128)(2,1)S(1)} %get-tuple-element.199), channel_id=1, source_target_pairs={{0,8},{4,12},{8,0},{12,4},{16,24},{20,28},{24,16},{28,20},{1,9},{5... | collective-permute-start | bytes 393224 | tf_op jit(solution)/shard_map/ppermute | solution.py:213
  81.5 2.4 %collective-permute-start.24 = (bf16[512,128]{1,0:T(8,128)(2,1)S(1)}, bf16[512,128]{1,0:T(8,128)(2,1)S(1)}, u32[]{:S(2)}, u32[]{:S(2)}) collective-permute-start(bf16[512,128]{1,0:T(8,128)(2,1)S(1)} %get-tuple-element.200), channel_id=1, source_target_pairs={{0,12},{4,8},{8,4},{12,0},{16,28},{20,24},{24,20},{28,16},{1,13},{... | collective-permute-start | bytes 393224 | tf_op jit(solution)/shard_map/ppermute | solution.py:213
  84.0 2.0 %shard_map.86 = (bf16[256,4096]{1,0:T(8,128)(2,1)}, bf16[256,4096]{1,0:T(8,128)(2,1)}) custom-call(s32[1]{0:T(128)} %bitcast.mem, bf16[256,2048]{1,0:T(8,128)(2,1)S(1)} %get-tuple-element.179.k_ref, bf16[256,2048]{1,0:T(8,128)(2,1)S(1)} %get-tuple-element.180.v_ref, f32[256,2048]{1,0:T(8,128)S(1)} %get-tuple-element.201.kl_ref, ...), custom_call_target="tpu_custom_call" | custom-call | flops 268435456 | bytes 4194304 | tf_op jit(solution)/shard_map/pallas_call | solution.py:181
  86.0 2.3 %collective-permute-done.24.rest_3_ = bf16[512,128]{1,0:T(8,128)(2,1)S(1)} collective-permute-done((bf16[512,128]{1,0:T(8,128)(2,1)S(1)}, bf16[512,128]{1,0:T(8,128)(2,1)S(1)}, u32[]{:S(2)}, u32[]{:S(2)}) %collective-permute-start.24) | collective-permute-done | bytes 131104 | tf_op jit(solution)/shard_map/ppermute | solution.py:213
  88.3 2.0 %shard_map.87 = (bf16[256,4096]{1,0:T(8,128)(2,1)}, bf16[256,4096]{1,0:T(8,128)(2,1)}) custom-call(s32[1]{0:T(128)} %bitcast.mem, bf16[256,2048]{1,0:T(8,128)(2,1)S(1)} %get-tuple-element.189.k_ref, bf16[256,2048]{1,0:T(8,128)(2,1)S(1)} %get-tuple-element.190.v_ref, ...), custom_call_target="tpu_custom_call", output_to_operand_aliasing={{0}: (9, {}), {1}: (10, {})} | custom-call | flops 268435456 | bytes 4194304 | tf_op jit(solution)/shard_map/pallas_call | solution.py:181
  (30 shorter events, 0.6 us)
Async XLA Ops:
  3.0 7.0 %collective-permute-start = (bf16[512,128]{1,0:T(8,128)(2,1)S(1)}, bf16[512,128]{1,0:T(8,128)(2,1)S(1)}, u32[]{:S(2)}, u32[]{:S(2)}) collective-permute-start(bf16[512,128]{1,0:T(8,128)(2,1)S(1)} %get-tuple-element.107), channel_id=1, source_target_pairs={{0,4},{4,0},{8,12},{12,8},{16,20},{20,16},{24,28},{28,24},{1,5},{5... | collective-permute-start | bytes 393224 | tf_op jit(solution)/shard_map/ppermute | solution.py:213
  6.1 6.4 %collective-permute-start.1 = (bf16[512,128]{1,0:T(8,128)(2,1)S(1)}, bf16[512,128]{1,0:T(8,128)(2,1)S(1)}, u32[]{:S(2)}, u32[]{:S(2)}) collective-permute-start(bf16[512,128]{1,0:T(8,128)(2,1)S(1)} %get-tuple-element.108), channel_id=1, source_target_pairs={{0,8},{4,12},{8,0},{12,4},{16,24},{20,28},{24,16},{28,20},{1,9},{5... | collective-permute-start | bytes 393224 | tf_op jit(solution)/shard_map/ppermute | solution.py:213
  7.6 14.2 %copy-start = (f32[4096]{0:T(1024)S(1)}, f32[4096]{0:T(1024)}, u32[]{:S(2)}) copy-start(f32[4096]{0:T(1024)} %param.8) | copy-start | bytes 49156
  7.6 6.0 %collective-permute-start.2 = (bf16[512,128]{1,0:T(8,128)(2,1)S(1)}, bf16[512,128]{1,0:T(8,128)(2,1)S(1)}, u32[]{:S(2)}, u32[]{:S(2)}) collective-permute-start(bf16[512,128]{1,0:T(8,128)(2,1)S(1)} %get-tuple-element.109), channel_id=1, source_target_pairs={{0,12},{4,8},{8,4},{12,0},{16,28},{20,24},{24,20},{28,16},{1,13},{... | collective-permute-start | bytes 393224 | tf_op jit(solution)/shard_map/ppermute | solution.py:213
  13.6 12.0 %collective-permute-start.7 = (bf16[512,128]{1,0:T(8,128)(2,1)S(1)}, bf16[512,128]{1,0:T(8,128)(2,1)S(1)}, u32[]{:S(2)}, u32[]{:S(2)}) collective-permute-start(bf16[512,128]{1,0:T(8,128)(2,1)S(1)} %get-tuple-element.143), channel_id=1, source_target_pairs={{0,4},{4,0},{8,12},{12,8},{16,20},{20,16},{24,28},{28,24},{1,5},{5... | collective-permute-start | bytes 393224 | tf_op jit(solution)/shard_map/ppermute | solution.py:213
  15.3 10.3 %collective-permute-start.8 = (bf16[512,128]{1,0:T(8,128)(2,1)S(1)}, bf16[512,128]{1,0:T(8,128)(2,1)S(1)}, u32[]{:S(2)}, u32[]{:S(2)}) collective-permute-start(bf16[512,128]{1,0:T(8,128)(2,1)S(1)} %get-tuple-element.144), channel_id=1, source_target_pairs={{0,8},{4,12},{8,0},{12,4},{16,24},{20,28},{24,16},{28,20},{1,9},{5... | collective-permute-start | bytes 393224 | tf_op jit(solution)/shard_map/ppermute | solution.py:213
  16.9 8.7 %collective-permute-start.9 = (bf16[512,128]{1,0:T(8,128)(2,1)S(1)}, bf16[512,128]{1,0:T(8,128)(2,1)S(1)}, u32[]{:S(2)}, u32[]{:S(2)}) collective-permute-start(bf16[512,128]{1,0:T(8,128)(2,1)S(1)} %get-tuple-element.145), channel_id=1, source_target_pairs={{0,12},{4,8},{8,4},{12,0},{16,28},{20,24},{24,20},{28,16},{1,13},{... | collective-permute-start | bytes 393224 | tf_op jit(solution)/shard_map/ppermute | solution.py:213
  17.2 10.3 %collective-permute-start.3 = (bf16[512,128]{1,0:T(8,128)(2,1)S(1)}, bf16[512,128]{1,0:T(8,128)(2,1)S(1)}, u32[]{:S(2)}, u32[]{:S(2)}) collective-permute-start(bf16[512,128]{1,0:T(8,128)(2,1)S(1)} %shard_map.70), channel_id=1, source_target_pairs={{0,16},{4,20},{8,24},{12,28},{1,17},{5,21},{9,25},{13,29},{2,18},{... | collective-permute-start | bytes 393224 | tf_op jit(solution)/shard_map/ppermute | solution.py:226
  25.7 9.7 %collective-permute-start.10 = (bf16[512,128]{1,0:T(8,128)(2,1)S(1)}, bf16[512,128]{1,0:T(8,128)(2,1)S(1)}, u32[]{:S(2)}, u32[]{:S(2)}) collective-permute-start(bf16[512,128]{1,0:T(8,128)(2,1)S(1)} %shard_map.74), channel_id=1, source_target_pairs={{0,16},{4,20},{8,24},{12,28},{1,17},{5,21},{9,25},{13,29},{2,18},{... | collective-permute-start | bytes 393224 | tf_op jit(solution)/shard_map/ppermute | solution.py:226
  27.9 11.4 %collective-permute-start.4 = (bf16[512,128]{1,0:T(8,128)(2,1)S(1)}, bf16[512,128]{1,0:T(8,128)(2,1)S(1)}, u32[]{:S(2)}, u32[]{:S(2)}) collective-permute-start(bf16[512,128]{1,0:T(8,128)(2,1)S(1)} %get-tuple-element.136), channel_id=1, source_target_pairs={{0,4},{4,0},{8,12},{12,8},{16,20},{20,16},{24,28},{28,24},{1,5},{5... | collective-permute-start | bytes 393224 | tf_op jit(solution)/shard_map/ppermute | solution.py:213
  29.1 10.2 %collective-permute-start.5 = (bf16[512,128]{1,0:T(8,128)(2,1)S(1)}, bf16[512,128]{1,0:T(8,128)(2,1)S(1)}, u32[]{:S(2)}, u32[]{:S(2)}) collective-permute-start(bf16[512,128]{1,0:T(8,128)(2,1)S(1)} %get-tuple-element.137), channel_id=1, source_target_pairs={{0,8},{4,12},{8,0},{12,4},{16,24},{20,28},{24,16},{28,20},{1,9},{5... | collective-permute-start | bytes 393224 | tf_op jit(solution)/shard_map/ppermute | solution.py:213
  31.7 7.7 %collective-permute-start.6 = (bf16[512,128]{1,0:T(8,128)(2,1)S(1)}, bf16[512,128]{1,0:T(8,128)(2,1)S(1)}, u32[]{:S(2)}, u32[]{:S(2)}) collective-permute-start(bf16[512,128]{1,0:T(8,128)(2,1)S(1)} %get-tuple-element.138), channel_id=1, source_target_pairs={{0,12},{4,8},{8,4},{12,0},{16,28},{20,24},{24,20},{28,16},{1,13},{... | collective-permute-start | bytes 393224 | tf_op jit(solution)/shard_map/ppermute | solution.py:213
  35.8 5.9 %collective-permute-start.11 = (bf16[512,128]{1,0:T(8,128)(2,1)S(1)}, bf16[512,128]{1,0:T(8,128)(2,1)S(1)}, u32[]{:S(2)}, u32[]{:S(2)}) collective-permute-start(bf16[512,128]{1,0:T(8,128)(2,1)S(1)} %get-tuple-element.154), channel_id=1, source_target_pairs={{0,4},{4,0},{8,12},{12,8},{16,20},{20,16},{24,28},{28,24},{1,5},{5... | collective-permute-start | bytes 393224 | tf_op jit(solution)/shard_map/ppermute | solution.py:213
  37.3 5.0 %collective-permute-start.12 = (bf16[512,128]{1,0:T(8,128)(2,1)S(1)}, bf16[512,128]{1,0:T(8,128)(2,1)S(1)}, u32[]{:S(2)}, u32[]{:S(2)}) collective-permute-start(bf16[512,128]{1,0:T(8,128)(2,1)S(1)} %get-tuple-element.155), channel_id=1, source_target_pairs={{0,8},{4,12},{8,0},{12,4},{16,24},{20,28},{24,16},{28,20},{1,9},{5... | collective-permute-start | bytes 393224 | tf_op jit(solution)/shard_map/ppermute | solution.py:213
  39.3 5.9 %collective-permute-start.13 = (bf16[512,128]{1,0:T(8,128)(2,1)S(1)}, bf16[512,128]{1,0:T(8,128)(2,1)S(1)}, u32[]{:S(2)}, u32[]{:S(2)}) collective-permute-start(bf16[512,128]{1,0:T(8,128)(2,1)S(1)} %get-tuple-element.156), channel_id=1, source_target_pairs={{0,12},{4,8},{8,4},{12,0},{16,28},{20,24},{24,20},{28,16},{1,13},{... | collective-permute-start | bytes 393224 | tf_op jit(solution)/shard_map/ppermute | solution.py:213
  47.9 6.1 %collective-permute-start.14 = (bf16[512,128]{1,0:T(8,128)(2,1)S(1)}, bf16[512,128]{1,0:T(8,128)(2,1)S(1)}, u32[]{:S(2)}, u32[]{:S(2)}) collective-permute-start(bf16[512,128]{1,0:T(8,128)(2,1)S(1)} %get-tuple-element.160), channel_id=1, source_target_pairs={{0,4},{4,0},{8,12},{12,8},{16,20},{20,16},{24,28},{28,24},{1,5},{5... | collective-permute-start | bytes 393224 | tf_op jit(solution)/shard_map/ppermute | solution.py:213
  48.4 6.2 %collective-permute-start.15 = (bf16[512,128]{1,0:T(8,128)(2,1)S(1)}, bf16[512,128]{1,0:T(8,128)(2,1)S(1)}, u32[]{:S(2)}, u32[]{:S(2)}) collective-permute-start(bf16[512,128]{1,0:T(8,128)(2,1)S(1)} %get-tuple-element.161), channel_id=1, source_target_pairs={{0,8},{4,12},{8,0},{12,4},{16,24},{20,28},{24,16},{28,20},{1,9},{5... | collective-permute-start | bytes 393224 | tf_op jit(solution)/shard_map/ppermute | solution.py:213
  49.9 10.0 %collective-permute-start.16 = (bf16[512,128]{1,0:T(8,128)(2,1)S(1)}, bf16[512,128]{1,0:T(8,128)(2,1)S(1)}, u32[]{:S(2)}, u32[]{:S(2)}) collective-permute-start(bf16[512,128]{1,0:T(8,128)(2,1)S(1)} %get-tuple-element.162), channel_id=1, source_target_pairs={{0,12},{4,8},{8,4},{12,0},{16,28},{20,24},{24,20},{28,16},{1,13},{... | collective-permute-start | bytes 393224 | tf_op jit(solution)/shard_map/ppermute | solution.py:213
  59.9 7.4 %collective-permute-start.17 = (bf16[512,128]{1,0:T(8,128)(2,1)S(1)}, bf16[512,128]{1,0:T(8,128)(2,1)S(1)}, u32[]{:S(2)}, u32[]{:S(2)}) collective-permute-start(bf16[512,128]{1,0:T(8,128)(2,1)S(1)} %get-tuple-element.171), channel_id=1, source_target_pairs={{0,4},{4,0},{8,12},{12,8},{16,20},{20,16},{24,28},{28,24},{1,5},{5... | collective-permute-start | bytes 393224 | tf_op jit(solution)/shard_map/ppermute | solution.py:213
  59.9 7.4 %collective-permute-start.18 = (bf16[512,128]{1,0:T(8,128)(2,1)S(1)}, bf16[512,128]{1,0:T(8,128)(2,1)S(1)}, u32[]{:S(2)}, u32[]{:S(2)}) collective-permute-start(bf16[512,128]{1,0:T(8,128)(2,1)S(1)} %get-tuple-element.172), channel_id=1, source_target_pairs={{0,8},{4,12},{8,0},{12,4},{16,24},{20,28},{24,16},{28,20},{1,9},{5... | collective-permute-start | bytes 393224 | tf_op jit(solution)/shard_map/ppermute | solution.py:213
  60.4 11.5 %collective-permute-start.19 = (bf16[512,128]{1,0:T(8,128)(2,1)S(1)}, bf16[512,128]{1,0:T(8,128)(2,1)S(1)}, u32[]{:S(2)}, u32[]{:S(2)}) collective-permute-start(bf16[512,128]{1,0:T(8,128)(2,1)S(1)} %get-tuple-element.173), channel_id=1, source_target_pairs={{0,12},{4,8},{8,4},{12,0},{16,28},{20,24},{24,20},{28,16},{1,13},{... | collective-permute-start | bytes 393224 | tf_op jit(solution)/shard_map/ppermute | solution.py:213
  63.4 10.1 %collective-permute-start.21 = (bf16[512,128]{1,0:T(8,128)(2,1)S(1)}, bf16[512,128]{1,0:T(8,128)(2,1)S(1)}, u32[]{:S(2)}, u32[]{:S(2)}) collective-permute-start(bf16[512,128]{1,0:T(8,128)(2,1)S(1)} %shard_map.81), channel_id=1, source_target_pairs={{16,0},{20,4},{24,8},{28,12},{17,1},{21,5},{25,9},{29,13},{18,2},{... | collective-permute-start | bytes 393224 | tf_op jit(solution)/shard_map/ppermute | solution.py:226
  72.0 8.0 %collective-permute-start.20 = (bf16[512,128]{1,0:T(8,128)(2,1)S(1)}, bf16[512,128]{1,0:T(8,128)(2,1)S(1)}, u32[]{:S(2)}, u32[]{:S(2)}) collective-permute-start(bf16[512,128]{1,0:T(8,128)(2,1)S(1)} %shard_map.80), channel_id=1, source_target_pairs={{16,0},{20,4},{24,8},{28,12},{17,1},{21,5},{25,9},{29,13},{18,2},{... | collective-permute-start | bytes 393224 | tf_op jit(solution)/shard_map/ppermute | solution.py:226
  73.9 7.6 %collective-permute-start.25 = (bf16[512,128]{1,0:T(8,128)(2,1)S(1)}, bf16[512,128]{1,0:T(8,128)(2,1)S(1)}, u32[]{:S(2)}, u32[]{:S(2)}) collective-permute-start(bf16[512,128]{1,0:T(8,128)(2,1)S(1)} %get-tuple-element.205), channel_id=1, source_target_pairs={{0,4},{4,0},{8,12},{12,8},{16,20},{20,16},{24,28},{28,24},{1,5},{5... | collective-permute-start | bytes 393224 | tf_op jit(solution)/shard_map/ppermute | solution.py:213
  74.0 10.0 %collective-permute-start.26 = (bf16[512,128]{1,0:T(8,128)(2,1)S(1)}, bf16[512,128]{1,0:T(8,128)(2,1)S(1)}, u32[]{:S(2)}, u32[]{:S(2)}) collective-permute-start(bf16[512,128]{1,0:T(8,128)(2,1)S(1)} %get-tuple-element.206), channel_id=1, source_target_pairs={{0,8},{4,12},{8,0},{12,4},{16,24},{20,28},{24,16},{28,20},{1,9},{5... | collective-permute-start | bytes 393224 | tf_op jit(solution)/shard_map/ppermute | solution.py:213
  75.0 8.9 %collective-permute-start.27 = (bf16[512,128]{1,0:T(8,128)(2,1)S(1)}, bf16[512,128]{1,0:T(8,128)(2,1)S(1)}, u32[]{:S(2)}, u32[]{:S(2)}) collective-permute-start(bf16[512,128]{1,0:T(8,128)(2,1)S(1)} %get-tuple-element.207), channel_id=1, source_target_pairs={{0,12},{4,8},{8,4},{12,0},{16,28},{20,24},{24,20},{28,16},{1,13},{... | collective-permute-start | bytes 393224 | tf_op jit(solution)/shard_map/ppermute | solution.py:213
  80.4 5.6 %collective-permute-start.22 = (bf16[512,128]{1,0:T(8,128)(2,1)S(1)}, bf16[512,128]{1,0:T(8,128)(2,1)S(1)}, u32[]{:S(2)}, u32[]{:S(2)}) collective-permute-start(bf16[512,128]{1,0:T(8,128)(2,1)S(1)} %get-tuple-element.198), channel_id=1, source_target_pairs={{0,4},{4,0},{8,12},{12,8},{16,20},{20,16},{24,28},{28,24},{1,5},{5... | collective-permute-start | bytes 393224 | tf_op jit(solution)/shard_map/ppermute | solution.py:213
  80.5 5.4 %collective-permute-start.23 = (bf16[512,128]{1,0:T(8,128)(2,1)S(1)}, bf16[512,128]{1,0:T(8,128)(2,1)S(1)}, u32[]{:S(2)}, u32[]{:S(2)}) collective-permute-start(bf16[512,128]{1,0:T(8,128)(2,1)S(1)} %get-tuple-element.199), channel_id=1, source_target_pairs={{0,8},{4,12},{8,0},{12,4},{16,24},{20,28},{24,16},{28,20},{1,9},{5... | collective-permute-start | bytes 393224 | tf_op jit(solution)/shard_map/ppermute | solution.py:213
  81.5 6.8 %collective-permute-start.24 = (bf16[512,128]{1,0:T(8,128)(2,1)S(1)}, bf16[512,128]{1,0:T(8,128)(2,1)S(1)}, u32[]{:S(2)}, u32[]{:S(2)}) collective-permute-start(bf16[512,128]{1,0:T(8,128)(2,1)S(1)} %get-tuple-element.200), channel_id=1, source_target_pairs={{0,12},{4,8},{8,4},{12,0},{16,28},{20,24},{24,20},{28,16},{1,13},{... | collective-permute-start | bytes 393224 | tf_op jit(solution)/shard_map/ppermute | solution.py:213

commit v5 on v4

--- a/solution.py
+++ b/solution.py
@@ -241,15 +241,14 @@
     m = len(first)
     got_a = exchange(first, n)
     second, extra = second_of()
-    got_a, second, extra = barrier((got_a, second, extra))
-    carry_a = carry_groups(total_of(got_a, n), n, m, forward)
     got_b = exchange(second, n)
     made_a = fill_a(extra)
-    carry_a, made_a, extra = barrier((carry_a, made_a, extra))
-    back_a = exchange(give_back(got_a, carry_a, mem, forward), n)
+    got_b, made_a, extra = barrier((got_b, made_a, extra))
+    carry_a = carry_groups(total_of(got_a, n), n, m, forward)
     carry_b = carry_groups(total_of(got_b, n), n, m, forward)
     made_b = fill_b(extra)
-    carry_b, made_b = barrier((carry_b, made_b))
+    carry_a, made_b = barrier((carry_a, made_b))
+    back_a = exchange(give_back(got_a, carry_a, mem, forward), n)
     back_b = exchange(give_back(got_b, carry_b, mem, forward), n)
     return (back_a, back_b), (made_a, made_b)
 

time: 91 us -> 80.1 us (0.88)
  waiting for transfers between devices: 22.1 us -> 8.24 us
  starting transfers between devices: 38.8 us -> 42 us
    ppermute x24, waiting for transfers between devices: 22.1 us -> 7.82 us  [exchange(): out[j] = lax.ppermute(parts[j], 'seq', perm)]
    ppermute x24, starting transfers between devices: 29.6 us -> 32.4 us  [exchange(): out[j] = lax.ppermute(parts[j], 'seq', perm)]
  transfers between devices with their start and end apart: 28 -> 28, of which waited for: 10 -> 9; matrix products, arithmetic and copies ran while one was open for 0% -> 0% of each run, Pallas kernels for 24% -> 27%
where the time goes in v5:
time: 80.1 us; the launch traced here: 79.8 us
  starting transfers between devices  42 us (52%)
  Pallas kernels  28.5 us (36%)
  waiting for transfers between devices  8.24 us (10%)
  between operations  1.08 us (1%)
    ppermute x24, starting transfers between devices, exchange(): out[j] = lax.ppermute(parts[j], 'seq', perm)  32.4 us
    pallas_call x20, Pallas kernels, call(): pl.pallas_call(kernel, in_specs=in_specs, out_specs=out_specs or [VMEM] *...  28.5 us
    ppermute x4, starting transfers between devices, shift(): return lax.ppermute(x, 'seq', perm)  9.6 us
    ppermute x24, waiting for transfers between devices, exchange(): out[j] = lax.ppermute(parts[j], 'seq', perm)  7.82 us
  transfers between devices with their start and end apart: 28, of which 9 were waited for; matrix products, arithmetic and copies ran while one was open for 0% of the time, Pallas kernels for 27%

profile of v5, /device:TPU:0, one launch (start us, length us, event | category | flops | bytes accessed | tf_op | source)
XLA Modules:
  0.0 79.8 jit_solution(25601956092962450)
XLA Ops:
  0.6 2.4 %shard_map.69 = (bf16[256,2048]{1,0:T(8,128)(2,1)S(1)}, bf16[256,2048]{1,0:T(8,128)(2,1)S(1)}, bf16[512,128]{1,0:T(8,128)(2,1)S(1)}, bf16[512,128]{1,0:T(8,128)(...) custom-call(s32[1]{0:T(128)} %bitcast.mem, bf16[256,4096]{1,0:T(8,128)(2,1)} %k_hbm.3, ...), custom_call_target="tpu_custom_call" | custom-call | flops 134217728 | bytes 3145728 | tf_op jit(solution)/shard_map/pallas_call | solution.py:181
  3.0 3.0 %collective-permute-start.3 = (bf16[512,128]{1,0:T(8,128)(2,1)S(1)}, bf16[512,128]{1,0:T(8,128)(2,1)S(1)}, u32[]{:S(2)}, u32[]{:S(2)}) collective-permute-start(bf16[512,128]{1,0:T(8,128)(2,1)S(1)} %get-tuple-element.101), channel_id=1, source_target_pairs={{0,4},{4,0},{8,12},{12,8},{16,20},{20,16},{24,28},{28,24},{1,5},{5... | collective-permute-start | bytes 393224 | tf_op jit(solution)/shard_map/ppermute | solution.py:213
  6.1 1.6 %collective-permute-start.4 = (bf16[512,128]{1,0:T(8,128)(2,1)S(1)}, bf16[512,128]{1,0:T(8,128)(2,1)S(1)}, u32[]{:S(2)}, u32[]{:S(2)}) collective-permute-start(bf16[512,128]{1,0:T(8,128)(2,1)S(1)} %get-tuple-element.102), channel_id=1, source_target_pairs={{0,8},{4,12},{8,0},{12,4},{16,24},{20,28},{24,16},{28,20},{1,9},{5... | collective-permute-start | bytes 393224 | tf_op jit(solution)/shard_map/ppermute | solution.py:213
  7.6 2.4 %shard_map.68 = (bf16[256,2048]{1,0:T(8,128)(2,1)S(1)}, bf16[256,2048]{1,0:T(8,128)(2,1)S(1)}, bf16[512,128]{1,0:T(8,128)(2,1)S(1)}, bf16[512,128]{1,0:T(8,128)(...) custom-call(s32[1]{0:T(128)} %bitcast.mem, bf16[256,4096]{1,0:T(8,128)(2,1)} %k_hbm.3, ...), custom_call_target="tpu_custom_call" | custom-call | flops 134217728 | bytes 3145728 | tf_op jit(solution)/shard_map/pallas_call | solution.py:181
  10.0 2.0 %collective-permute-start = (bf16[512,128]{1,0:T(8,128)(2,1)S(1)}, bf16[512,128]{1,0:T(8,128)(2,1)S(1)}, u32[]{:S(2)}, u32[]{:S(2)}) collective-permute-start(bf16[512,128]{1,0:T(8,128)(2,1)S(1)} %get-tuple-element.85), channel_id=1, source_target_pairs={{0,4},{4,0},{8,12},{12,8},{16,20},{20,16},{24,28},{28,24},{1,5},{5... | collective-permute-start | bytes 393224 | tf_op jit(solution)/shard_map/ppermute | solution.py:213
  12.0 1.6 %collective-permute-start.1 = (bf16[512,128]{1,0:T(8,128)(2,1)S(1)}, bf16[512,128]{1,0:T(8,128)(2,1)S(1)}, u32[]{:S(2)}, u32[]{:S(2)}) collective-permute-start(bf16[512,128]{1,0:T(8,128)(2,1)S(1)} %get-tuple-element.86), channel_id=1, source_target_pairs={{0,8},{4,12},{8,0},{12,4},{16,24},{20,28},{24,16},{28,20},{1,9},{5... | collective-permute-start | bytes 393224 | tf_op jit(solution)/shard_map/ppermute | solution.py:213
  13.6 0.5 collective-permute-done.5.refs_3_
  14.1 4.7 %collective-permute-start.6 = (bf16[512,128]{1,0:T(8,128)(2,1)S(1)}, bf16[512,128]{1,0:T(8,128)(2,1)S(1)}, u32[]{:S(2)}, u32[]{:S(2)}) collective-permute-start(bf16[512,128]{1,0:T(8,128)(2,1)S(1)} %shard_map.71), channel_id=1, source_target_pairs={{0,16},{4,20},{8,24},{12,28},{1,17},{5,21},{9,25},{13,29},{2,18},{... | collective-permute-start | bytes 393224 | tf_op jit(solution)/shard_map/ppermute | solution.py:226
  18.9 3.7 %shard_map.70 = (bf16[256,2048]{1,0:T(8,128)(2,1)S(1)}, f32[256,2048]{1,0:T(8,128)S(1)}, f32[256,2048]{1,0:T(8,128)S(1)}) custom-call(bf16[256,2048]{1,0:T(8,128)(2,1)S(1)} %get-tuple-element.88.k_ref, bf16[256,2048]{1,0:T(8,128)(2,1)S(1)} %get-tuple-element.89.v_ref, f32[1,4096]{1,0:T(1,128)S(1)} %bitcast.2, bf16[256,4096]{1,0:T(8,128)(2,1)} %q_hbm.3, ...), custom_call_target="tpu_custom_call" | custom-call | flops 536870912 | bytes 6291456 | tf_op jit(solution)/shard_map/pallas_call | solution.py:181
  22.7 2.1 %collective-permute-start.10 = (bf16[512,128]{1,0:T(8,128)(2,1)S(1)}, bf16[512,128]{1,0:T(8,128)(2,1)S(1)}, u32[]{:S(2)}, u32[]{:S(2)}) collective-permute-start(bf16[512,128]{1,0:T(8,128)(2,1)S(1)} %shard_map.75), channel_id=1, source_target_pairs={{0,16},{4,20},{8,24},{12,28},{1,17},{5,21},{9,25},{13,29},{2,18},{... | collective-permute-start | bytes 393224 | tf_op jit(solution)/shard_map/ppermute | solution.py:226
  24.8 3.7 %shard_map.72 = (bf16[256,2048]{1,0:T(8,128)(2,1)S(1)}, f32[256,2048]{1,0:T(8,128)S(1)}, f32[256,2048]{1,0:T(8,128)S(1)}) custom-call(bf16[256,2048]{1,0:T(8,128)(2,1)S(1)} %get-tuple-element.142.k_ref, bf16[256,2048]{1,0:T(8,128)(2,1)S(1)} %get-tuple-element.143.v_ref, f32[1,4096]{1,0:T(1,128)S(1)} %bitcast.3, bf16[256,4096]{1,0:T(8,128)(2,1)} %q_hbm.3, ...), custom_call_target="tpu_custom_call" | custom-call | flops 536870912 | bytes 6291456 | tf_op jit(solution)/shard_map/pallas_call | solution.py:181
  28.5 0.4 shard_map.73
  28.9 0.9 %collective-permute-start.7 = (bf16[512,128]{1,0:T(8,128)(2,1)S(1)}, bf16[512,128]{1,0:T(8,128)(2,1)S(1)}, u32[]{:S(2)}, u32[]{:S(2)}) collective-permute-start(bf16[512,128]{1,0:T(8,128)(2,1)S(1)} %get-tuple-element.109), channel_id=1, source_target_pairs={{0,4},{4,0},{8,12},{12,8},{16,20},{20,16},{24,28},{28,24},{1,5},{5... | collective-permute-start | bytes 393224 | tf_op jit(solution)/shard_map/ppermute | solution.py:213
  29.8 3.0 %collective-permute-start.8 = (bf16[512,128]{1,0:T(8,128)(2,1)S(1)}, bf16[512,128]{1,0:T(8,128)(2,1)S(1)}, u32[]{:S(2)}, u32[]{:S(2)}) collective-permute-start(bf16[512,128]{1,0:T(8,128)(2,1)S(1)} %get-tuple-element.110), channel_id=1, source_target_pairs={{0,8},{4,12},{8,0},{12,4},{16,24},{20,28},{24,16},{28,20},{1,9},{5... | collective-permute-start | bytes 393224 | tf_op jit(solution)/shard_map/ppermute | solution.py:213
  32.8 0.4 shard_map.76
  33.2 1.5 %collective-permute-start.11 = (bf16[512,128]{1,0:T(8,128)(2,1)S(1)}, bf16[512,128]{1,0:T(8,128)(2,1)S(1)}, u32[]{:S(2)}, u32[]{:S(2)}) collective-permute-start(bf16[512,128]{1,0:T(8,128)(2,1)S(1)} %get-tuple-element.123), channel_id=1, source_target_pairs={{0,4},{4,0},{8,12},{12,8},{16,20},{20,16},{24,28},{28,24},{1,5},{5... | collective-permute-start | bytes 393224 | tf_op jit(solution)/shard_map/ppermute | solution.py:213
  34.7 2.0 %collective-permute-start.12 = (bf16[512,128]{1,0:T(8,128)(2,1)S(1)}, bf16[512,128]{1,0:T(8,128)(2,1)S(1)}, u32[]{:S(2)}, u32[]{:S(2)}) collective-permute-start(bf16[512,128]{1,0:T(8,128)(2,1)S(1)} %get-tuple-element.124), channel_id=1, source_target_pairs={{0,8},{4,12},{8,0},{12,4},{16,24},{20,28},{24,16},{28,20},{1,9},{5... | collective-permute-start | bytes 393224 | tf_op jit(solution)/shard_map/ppermute | solution.py:213
  36.7 2.6 %collective-permute-start.13 = (bf16[512,128]{1,0:T(8,128)(2,1)S(1)}, bf16[512,128]{1,0:T(8,128)(2,1)S(1)}, u32[]{:S(2)}, u32[]{:S(2)}) collective-permute-start(bf16[512,128]{1,0:T(8,128)(2,1)S(1)} %get-tuple-element.125), channel_id=1, source_target_pairs={{0,12},{4,8},{8,4},{12,0},{16,28},{20,24},{24,20},{28,16},{1,13},{... | collective-permute-start | bytes 393224 | tf_op jit(solution)/shard_map/ppermute | solution.py:213
  39.4 1.3 %shard_map.74 = (f32[256,2048]{1,0:T(8,128)S(1)}, f32[256,128]{1,0:T(8,128)S(1)}, f32[256,128]{1,0:T(8,128)S(1)}) custom-call(s32[1]{0:T(128)} %bitcast.mem, bf16[256,2048]{1,0:T(8,128)(2,1)S(1)} %get-tuple-element.97.q_ref, f32[256,2048]{1,0:T(8,128)S(1)} %get-tuple-element.98.loc_ref, ...), custom_call_target="tpu_custom_call", output_to_operand_aliasing={{0}: (2, {})} | custom-call | flops 134217728 | bytes 2097152 | tf_op jit(solution)/shard_map/pallas_call | solution.py:181
  40.7 1.9 %collective-permute-done.13.rest_3_ = bf16[512,128]{1,0:T(8,128)(2,1)S(1)} collective-permute-done((bf16[512,128]{1,0:T(8,128)(2,1)S(1)}, bf16[512,128]{1,0:T(8,128)(2,1)S(1)}, u32[]{:S(2)}, u32[]{:S(2)}) %collective-permute-start.13) | collective-permute-done | bytes 131104 | tf_op jit(solution)/shard_map/ppermute | solution.py:213
  42.6 1.3 %shard_map.77 = (f32[256,2048]{1,0:T(8,128)S(1)}, f32[256,128]{1,0:T(8,128)S(1)}, f32[256,128]{1,0:T(8,128)S(1)}) custom-call(s32[1]{0:T(128)} %bitcast.mem, bf16[256,2048]{1,0:T(8,128)(2,1)S(1)} %get-tuple-element.141.q_ref, f32[256,2048]{1,0:T(8,128)S(1)} %get-tuple-element.116.loc_ref, ...), custom_call_target="tpu_custom_call", output_to_operand_aliasing={{0}: (2, {})} | custom-call | flops 134217728 | bytes 2097152 | tf_op jit(solution)/shard_map/pallas_call | solution.py:181
  43.9 1.4 %shard_map.78 = (bf16[256,2048]{1,0:T(8,128)(2,1)S(1)}, bf16[512,128]{1,0:T(8,128)(2,1)S(1)}, bf16[512,128]{1,0:T(8,128)(2,1)S(1)}, bf16[512,128]{1,0:T(8,128)(2,1)S(1)}, bf16[512,128]{1,0:T(8,128)(2,1)S(1)}) custom-call(s32[1]{0:T(128)} %bitcast.mem, bf16[256,2048]{1,0:T(8,128)(2,1)S(1)} %get-tuple-element.97.q_ref, ...), custom_call_target="tpu_custom_call" | custom-call | flops 134217728 | bytes 2097152 | tf_op jit(solution)/shard_map/pallas_call | solution.py:181
  45.3 1.4 %collective-permute-start.14 = (bf16[512,128]{1,0:T(8,128)(2,1)S(1)}, bf16[512,128]{1,0:T(8,128)(2,1)S(1)}, u32[]{:S(2)}, u32[]{:S(2)}) collective-permute-start(bf16[512,128]{1,0:T(8,128)(2,1)S(1)} %get-tuple-element.129), channel_id=1, source_target_pairs={{0,4},{4,0},{8,12},{12,8},{16,20},{20,16},{24,28},{28,24},{1,5},{5... | collective-permute-start | bytes 393224 | tf_op jit(solution)/shard_map/ppermute | solution.py:213
  46.7 1.9 %collective-permute-start.15 = (bf16[512,128]{1,0:T(8,128)(2,1)S(1)}, bf16[512,128]{1,0:T(8,128)(2,1)S(1)}, u32[]{:S(2)}, u32[]{:S(2)}) collective-permute-start(bf16[512,128]{1,0:T(8,128)(2,1)S(1)} %get-tuple-element.130), channel_id=1, source_target_pairs={{0,8},{4,12},{8,0},{12,4},{16,24},{20,28},{24,16},{28,20},{1,9},{5... | collective-permute-start | bytes 393224 | tf_op jit(solution)/shard_map/ppermute | solution.py:213
  48.6 0.2 collective-permute-start.16
  48.9 1.4 %shard_map.80 = (bf16[256,2048]{1,0:T(8,128)(2,1)S(1)}, bf16[512,128]{1,0:T(8,128)(2,1)S(1)}, bf16[512,128]{1,0:T(8,128)(2,1)S(1)}, bf16[512,128]{1,0:T(8,128)(2,1)S(1)}, bf16[512,128]{1,0:T(8,128)(2,1)S(1)}) custom-call(s32[1]{0:T(128)} %bitcast.mem, bf16[256,2048]{1,0:T(8,128)(2,1)S(1)} %get-tuple-element.141.q_ref, ...), custom_call_target="tpu_custom_call" | custom-call | flops 134217728 | bytes 2097152 | tf_op jit(solution)/shard_map/pallas_call | solution.py:181
  50.3 1.4 %collective-permute-start.18 = (bf16[512,128]{1,0:T(8,128)(2,1)S(1)}, bf16[512,128]{1,0:T(8,128)(2,1)S(1)}, u32[]{:S(2)}, u32[]{:S(2)}) collective-permute-start(bf16[512,128]{1,0:T(8,128)(2,1)S(1)} %get-tuple-element.134), channel_id=1, source_target_pairs={{0,4},{4,0},{8,12},{12,8},{16,20},{20,16},{24,28},{28,24},{1,5},{5... | collective-permute-start | bytes 393224 | tf_op jit(solution)/shard_map/ppermute | solution.py:213
  51.7 1.9 %collective-permute-start.19 = (bf16[512,128]{1,0:T(8,128)(2,1)S(1)}, bf16[512,128]{1,0:T(8,128)(2,1)S(1)}, u32[]{:S(2)}, u32[]{:S(2)}) collective-permute-start(bf16[512,128]{1,0:T(8,128)(2,1)S(1)} %get-tuple-element.135), channel_id=1, source_target_pairs={{0,8},{4,12},{8,0},{12,4},{16,24},{20,28},{24,16},{28,20},{1,9},{5... | collective-permute-start | bytes 393224 | tf_op jit(solution)/shard_map/ppermute | solution.py:213
  53.6 0.8 %collective-permute-start.20 = (bf16[512,128]{1,0:T(8,128)(2,1)S(1)}, bf16[512,128]{1,0:T(8,128)(2,1)S(1)}, u32[]{:S(2)}, u32[]{:S(2)}) collective-permute-start(bf16[512,128]{1,0:T(8,128)(2,1)S(1)} %get-tuple-element.136), channel_id=1, source_target_pairs={{0,12},{4,8},{8,4},{12,0},{16,28},{20,24},{24,20},{28,16},{1,13},{... | collective-permute-start | bytes 393224 | tf_op jit(solution)/shard_map/ppermute | solution.py:213
  54.5 1.8 %collective-permute-done.16.refs_3_ = bf16[512,128]{1,0:T(8,128)(2,1)S(1)} collective-permute-done((bf16[512,128]{1,0:T(8,128)(2,1)S(1)}, bf16[512,128]{1,0:T(8,128)(2,1)S(1)}, u32[]{:S(2)}, u32[]{:S(2)}) %collective-permute-start.16) | collective-permute-done | bytes 131104 | tf_op jit(solution)/shard_map/ppermute | solution.py:213
  56.3 1.3 %collective-permute-start.17 = (bf16[512,128]{1,0:T(8,128)(2,1)S(1)}, bf16[512,128]{1,0:T(8,128)(2,1)S(1)}, u32[]{:S(2)}, u32[]{:S(2)}) collective-permute-start(bf16[512,128]{1,0:T(8,128)(2,1)S(1)} %shard_map.79), channel_id=1, source_target_pairs={{16,0},{20,4},{24,8},{28,12},{17,1},{21,5},{25,9},{29,13},{18,2},{... | collective-permute-start | bytes 393224 | tf_op jit(solution)/shard_map/ppermute | solution.py:226
  57.6 2.6 %shard_map.81 = (f32[256,2048]{1,0:T(8,128)S(1)}, f32[256,2048]{1,0:T(8,128)S(1)}) custom-call(bf16[256,2048]{1,0:T(8,128)(2,1)S(1)} %get-tuple-element.97.q_ref, bf16[256,2048]{1,0:T(8,128)(2,1)S(1)} %get-tuple-element.88.k_ref, bf16[256,2048]{1,0:T(8,128)(2,1)S(1)} %get-tuple-element.89.v_ref, bf16[256,2048]{1,0:T(8,128)(2,1)S(1)} %get-tuple-element.137.g_ref), custom_call_target="tpu_custom_call" | custom-call | flops 1073741824 | bytes 4194304 | tf_op jit(solution)/shard_map/pallas_call | solution.py:181
  60.2 0.5 collective-permute-done.20.refs_3_
  60.8 1.5 %collective-permute-start.21 = (bf16[512,128]{1,0:T(8,128)(2,1)S(1)}, bf16[512,128]{1,0:T(8,128)(2,1)S(1)}, u32[]{:S(2)}, u32[]{:S(2)}) collective-permute-start(bf16[512,128]{1,0:T(8,128)(2,1)S(1)} %shard_map.83), channel_id=1, source_target_pairs={{16,0},{20,4},{24,8},{28,12},{17,1},{21,5},{25,9},{29,13},{18,2},{... | collective-permute-start | bytes 393224 | tf_op jit(solution)/shard_map/ppermute | solution.py:226
  62.3 2.6 %shard_map.82 = (f32[256,2048]{1,0:T(8,128)S(1)}, f32[256,2048]{1,0:T(8,128)S(1)}) custom-call(bf16[256,2048]{1,0:T(8,128)(2,1)S(1)} %get-tuple-element.141.q_ref, bf16[256,2048]{1,0:T(8,128)(2,1)S(1)} %get-tuple-element.142.k_ref, bf16[256,2048]{1,0:T(8,128)(2,1)S(1)} %get-tuple-element.143.v_ref, bf16[256,2048]{1,0:T(8,128)(2,1)S(1)} %get-tuple-element.144.g_ref), custom_call_target="tpu_custom_call" | custom-call | flops 1073741824 | bytes 4194304 | tf_op jit(solution)/shard_map/pallas_call | solution.py:181
  65.1 0.4 shard_map.85
  65.4 0.9 %collective-permute-start.25 = (bf16[512,128]{1,0:T(8,128)(2,1)S(1)}, bf16[512,128]{1,0:T(8,128)(2,1)S(1)}, u32[]{:S(2)}, u32[]{:S(2)}) collective-permute-start(bf16[512,128]{1,0:T(8,128)(2,1)S(1)} %get-tuple-element.161), channel_id=1, source_target_pairs={{0,4},{4,0},{8,12},{12,8},{16,20},{20,16},{24,28},{28,24},{1,5},{5... | collective-permute-start | bytes 393224 | tf_op jit(solution)/shard_map/ppermute | solution.py:213
  66.3 2.6 %collective-permute-start.27 = (bf16[512,128]{1,0:T(8,128)(2,1)S(1)}, bf16[512,128]{1,0:T(8,128)(2,1)S(1)}, u32[]{:S(2)}, u32[]{:S(2)}) collective-permute-start(bf16[512,128]{1,0:T(8,128)(2,1)S(1)} %get-tuple-element.163), channel_id=1, source_target_pairs={{0,12},{4,8},{8,4},{12,0},{16,28},{20,24},{24,20},{28,16},{1,13},{... | collective-permute-start | bytes 393224 | tf_op jit(solution)/shard_map/ppermute | solution.py:213
  69.0 0.3 collective-permute-done.21.carry
  69.2 0.4 shard_map.84
  69.6 0.6 collective-permute-start.22
  70.3 0.8 %collective-permute-start.23 = (bf16[512,128]{1,0:T(8,128)(2,1)S(1)}, bf16[512,128]{1,0:T(8,128)(2,1)S(1)}, u32[]{:S(2)}, u32[]{:S(2)}) collective-permute-start(bf16[512,128]{1,0:T(8,128)(2,1)S(1)} %get-tuple-element.155), channel_id=1, source_target_pairs={{0,8},{4,12},{8,0},{12,4},{16,24},{20,28},{24,16},{28,20},{1,9},{5... | collective-permute-start | bytes 393224 | tf_op jit(solution)/shard_map/ppermute | solution.py:213
  71.1 0.7 collective-permute-done.25.rest_1_
  71.7 1.4 %collective-permute-start.24 = (bf16[512,128]{1,0:T(8,128)(2,1)S(1)}, bf16[512,128]{1,0:T(8,128)(2,1)S(1)}, u32[]{:S(2)}, u32[]{:S(2)}) collective-permute-start(bf16[512,128]{1,0:T(8,128)(2,1)S(1)} %get-tuple-element.156), channel_id=1, source_target_pairs={{0,12},{4,8},{8,4},{12,0},{16,28},{20,24},{24,20},{28,16},{1,13},{... | collective-permute-start | bytes 393224 | tf_op jit(solution)/shard_map/ppermute | solution.py:213
  73.2 1.4 %collective-permute-done.27.rest_3_ = bf16[512,128]{1,0:T(8,128)(2,1)S(1)} collective-permute-done((bf16[512,128]{1,0:T(8,128)(2,1)S(1)}, bf16[512,128]{1,0:T(8,128)(2,1)S(1)}, u32[]{:S(2)}, u32[]{:S(2)}) %collective-permute-start.27) | collective-permute-done | bytes 131104 | tf_op jit(solution)/shard_map/ppermute | solution.py:213
  74.6 2.0 %shard_map.86 = (bf16[256,4096]{1,0:T(8,128)(2,1)}, bf16[256,4096]{1,0:T(8,128)(2,1)}) custom-call(s32[1]{0:T(128)} %bitcast.mem, bf16[256,2048]{1,0:T(8,128)(2,1)S(1)} %get-tuple-element.88.k_ref, bf16[256,2048]{1,0:T(8,128)(2,1)S(1)} %get-tuple-element.89.v_ref, f32[256,2048]{1,0:T(8,128)S(1)} %get-tuple-element.157.kl_ref, ...), custom_call_target="tpu_custom_call" | custom-call | flops 268435456 | bytes 4194304 | tf_op jit(solution)/shard_map/pallas_call | solution.py:181
  76.6 1.0 %collective-permute-done.24.rest_3_ = bf16[512,128]{1,0:T(8,128)(2,1)S(1)} collective-permute-done((bf16[512,128]{1,0:T(8,128)(2,1)S(1)}, bf16[512,128]{1,0:T(8,128)(2,1)S(1)}, u32[]{:S(2)}, u32[]{:S(2)}) %collective-permute-start.24) | collective-permute-done | bytes 131104 | tf_op jit(solution)/shard_map/ppermute | solution.py:213
  77.6 2.0 %shard_map.87 = (bf16[256,4096]{1,0:T(8,128)(2,1)}, bf16[256,4096]{1,0:T(8,128)(2,1)}) custom-call(s32[1]{0:T(128)} %bitcast.mem, bf16[256,2048]{1,0:T(8,128)(2,1)S(1)} %get-tuple-element.142.k_ref, bf16[256,2048]{1,0:T(8,128)(2,1)S(1)} %get-tuple-element.143.v_ref, ...), custom_call_target="tpu_custom_call", output_to_operand_aliasing={{0}: (9, {}), {1}: (10, {})} | custom-call | flops 268435456 | bytes 4194304 | tf_op jit(solution)/shard_map/pallas_call | solution.py:181
  (30 shorter events, 0.5 us)
Async XLA Ops:
  3.0 10.5 %collective-permute-start.3 = (bf16[512,128]{1,0:T(8,128)(2,1)S(1)}, bf16[512,128]{1,0:T(8,128)(2,1)S(1)}, u32[]{:S(2)}, u32[]{:S(2)}) collective-permute-start(bf16[512,128]{1,0:T(8,128)(2,1)S(1)} %get-tuple-element.101), channel_id=1, source_target_pairs={{0,4},{4,0},{8,12},{12,8},{16,20},{20,16},{24,28},{28,24},{1,5},{5... | collective-permute-start | bytes 393224 | tf_op jit(solution)/shard_map/ppermute | solution.py:213
  6.1 7.5 %collective-permute-start.4 = (bf16[512,128]{1,0:T(8,128)(2,1)S(1)}, bf16[512,128]{1,0:T(8,128)(2,1)S(1)}, u32[]{:S(2)}, u32[]{:S(2)}) collective-permute-start(bf16[512,128]{1,0:T(8,128)(2,1)S(1)} %get-tuple-element.102), channel_id=1, source_target_pairs={{0,8},{4,12},{8,0},{12,4},{16,24},{20,28},{24,16},{28,20},{1,9},{5... | collective-permute-start | bytes 393224 | tf_op jit(solution)/shard_map/ppermute | solution.py:213
  7.6 11.2 %copy-start = (f32[4096]{0:T(1024)S(1)}, f32[4096]{0:T(1024)}, u32[]{:S(2)}) copy-start(f32[4096]{0:T(1024)} %param.8) | copy-start | bytes 49156
  7.6 6.4 %collective-permute-start.5 = (bf16[512,128]{1,0:T(8,128)(2,1)S(1)}, bf16[512,128]{1,0:T(8,128)(2,1)S(1)}, u32[]{:S(2)}, u32[]{:S(2)}) collective-permute-start(bf16[512,128]{1,0:T(8,128)(2,1)S(1)} %get-tuple-element.103), channel_id=1, source_target_pairs={{0,12},{4,8},{8,4},{12,0},{16,28},{20,24},{24,20},{28,16},{1,13},{... | collective-permute-start | bytes 393224 | tf_op jit(solution)/shard_map/ppermute | solution.py:213
  10.0 12.5 %collective-permute-start = (bf16[512,128]{1,0:T(8,128)(2,1)S(1)}, bf16[512,128]{1,0:T(8,128)(2,1)S(1)}, u32[]{:S(2)}, u32[]{:S(2)}) collective-permute-start(bf16[512,128]{1,0:T(8,128)(2,1)S(1)} %get-tuple-element.85), channel_id=1, source_target_pairs={{0,4},{4,0},{8,12},{12,8},{16,20},{20,16},{24,28},{28,24},{1,5},{5... | collective-permute-start | bytes 393224 | tf_op jit(solution)/shard_map/ppermute | solution.py:213
  12.0 10.6 %collective-permute-start.1 = (bf16[512,128]{1,0:T(8,128)(2,1)S(1)}, bf16[512,128]{1,0:T(8,128)(2,1)S(1)}, u32[]{:S(2)}, u32[]{:S(2)}) collective-permute-start(bf16[512,128]{1,0:T(8,128)(2,1)S(1)} %get-tuple-element.86), channel_id=1, source_target_pairs={{0,8},{4,12},{8,0},{12,4},{16,24},{20,28},{24,16},{28,20},{1,9},{5... | collective-permute-start | bytes 393224 | tf_op jit(solution)/shard_map/ppermute | solution.py:213
  13.6 9.0 %collective-permute-start.2 = (bf16[512,128]{1,0:T(8,128)(2,1)S(1)}, bf16[512,128]{1,0:T(8,128)(2,1)S(1)}, u32[]{:S(2)}, u32[]{:S(2)}) collective-permute-start(bf16[512,128]{1,0:T(8,128)(2,1)S(1)} %get-tuple-element.87), channel_id=1, source_target_pairs={{0,12},{4,8},{8,4},{12,0},{16,28},{20,24},{24,20},{28,16},{1,13},{... | collective-permute-start | bytes 393224 | tf_op jit(solution)/shard_map/ppermute | solution.py:213
  14.1 14.3 %collective-permute-start.6 = (bf16[512,128]{1,0:T(8,128)(2,1)S(1)}, bf16[512,128]{1,0:T(8,128)(2,1)S(1)}, u32[]{:S(2)}, u32[]{:S(2)}) collective-permute-start(bf16[512,128]{1,0:T(8,128)(2,1)S(1)} %shard_map.71), channel_id=1, source_target_pairs={{0,16},{4,20},{8,24},{12,28},{1,17},{5,21},{9,25},{13,29},{2,18},{... | collective-permute-start | bytes 393224 | tf_op jit(solution)/shard_map/ppermute | solution.py:226
  22.7 10.1 %collective-permute-start.10 = (bf16[512,128]{1,0:T(8,128)(2,1)S(1)}, bf16[512,128]{1,0:T(8,128)(2,1)S(1)}, u32[]{:S(2)}, u32[]{:S(2)}) collective-permute-start(bf16[512,128]{1,0:T(8,128)(2,1)S(1)} %shard_map.75), channel_id=1, source_target_pairs={{0,16},{4,20},{8,24},{12,28},{1,17},{5,21},{9,25},{13,29},{2,18},{... | collective-permute-start | bytes 393224 | tf_op jit(solution)/shard_map/ppermute | solution.py:226
  28.9 7.9 %collective-permute-start.7 = (bf16[512,128]{1,0:T(8,128)(2,1)S(1)}, bf16[512,128]{1,0:T(8,128)(2,1)S(1)}, u32[]{:S(2)}, u32[]{:S(2)}) collective-permute-start(bf16[512,128]{1,0:T(8,128)(2,1)S(1)} %get-tuple-element.109), channel_id=1, source_target_pairs={{0,4},{4,0},{8,12},{12,8},{16,20},{20,16},{24,28},{28,24},{1,5},{5... | collective-permute-start | bytes 393224 | tf_op jit(solution)/shard_map/ppermute | solution.py:213
  29.8 9.5 %collective-permute-start.8 = (bf16[512,128]{1,0:T(8,128)(2,1)S(1)}, bf16[512,128]{1,0:T(8,128)(2,1)S(1)}, u32[]{:S(2)}, u32[]{:S(2)}) collective-permute-start(bf16[512,128]{1,0:T(8,128)(2,1)S(1)} %get-tuple-element.110), channel_id=1, source_target_pairs={{0,8},{4,12},{8,0},{12,4},{16,24},{20,28},{24,16},{28,20},{1,9},{5... | collective-permute-start | bytes 393224 | tf_op jit(solution)/shard_map/ppermute | solution.py:213
  32.8 6.5 %collective-permute-start.9 = (bf16[512,128]{1,0:T(8,128)(2,1)S(1)}, bf16[512,128]{1,0:T(8,128)(2,1)S(1)}, u32[]{:S(2)}, u32[]{:S(2)}) collective-permute-start(bf16[512,128]{1,0:T(8,128)(2,1)S(1)} %get-tuple-element.111), channel_id=1, source_target_pairs={{0,12},{4,8},{8,4},{12,0},{16,28},{20,24},{24,20},{28,16},{1,13},{... | collective-permute-start | bytes 393224 | tf_op jit(solution)/shard_map/ppermute | solution.py:213
  33.2 7.5 %collective-permute-start.11 = (bf16[512,128]{1,0:T(8,128)(2,1)S(1)}, bf16[512,128]{1,0:T(8,128)(2,1)S(1)}, u32[]{:S(2)}, u32[]{:S(2)}) collective-permute-start(bf16[512,128]{1,0:T(8,128)(2,1)S(1)} %get-tuple-element.123), channel_id=1, source_target_pairs={{0,4},{4,0},{8,12},{12,8},{16,20},{20,16},{24,28},{28,24},{1,5},{5... | collective-permute-start | bytes 393224 | tf_op jit(solution)/shard_map/ppermute | solution.py:213
  34.7 6.0 %collective-permute-start.12 = (bf16[512,128]{1,0:T(8,128)(2,1)S(1)}, bf16[512,128]{1,0:T(8,128)(2,1)S(1)}, u32[]{:S(2)}, u32[]{:S(2)}) collective-permute-start(bf16[512,128]{1,0:T(8,128)(2,1)S(1)} %get-tuple-element.124), channel_id=1, source_target_pairs={{0,8},{4,12},{8,0},{12,4},{16,24},{20,28},{24,16},{28,20},{1,9},{5... | collective-permute-start | bytes 393224 | tf_op jit(solution)/shard_map/ppermute | solution.py:213
  36.7 5.9 %collective-permute-start.13 = (bf16[512,128]{1,0:T(8,128)(2,1)S(1)}, bf16[512,128]{1,0:T(8,128)(2,1)S(1)}, u32[]{:S(2)}, u32[]{:S(2)}) collective-permute-start(bf16[512,128]{1,0:T(8,128)(2,1)S(1)} %get-tuple-element.125), channel_id=1, source_target_pairs={{0,12},{4,8},{8,4},{12,0},{16,28},{20,24},{24,20},{28,16},{1,13},{... | collective-permute-start | bytes 393224 | tf_op jit(solution)/shard_map/ppermute | solution.py:213
  45.3 8.3 %collective-permute-start.14 = (bf16[512,128]{1,0:T(8,128)(2,1)S(1)}, bf16[512,128]{1,0:T(8,128)(2,1)S(1)}, u32[]{:S(2)}, u32[]{:S(2)}) collective-permute-start(bf16[512,128]{1,0:T(8,128)(2,1)S(1)} %get-tuple-element.129), channel_id=1, source_target_pairs={{0,4},{4,0},{8,12},{12,8},{16,20},{20,16},{24,28},{28,24},{1,5},{5... | collective-permute-start | bytes 393224 | tf_op jit(solution)/shard_map/ppermute | solution.py:213
  46.7 7.7 %collective-permute-start.15 = (bf16[512,128]{1,0:T(8,128)(2,1)S(1)}, bf16[512,128]{1,0:T(8,128)(2,1)S(1)}, u32[]{:S(2)}, u32[]{:S(2)}) collective-permute-start(bf16[512,128]{1,0:T(8,128)(2,1)S(1)} %get-tuple-element.130), channel_id=1, source_target_pairs={{0,8},{4,12},{8,0},{12,4},{16,24},{20,28},{24,16},{28,20},{1,9},{5... | collective-permute-start | bytes 393224 | tf_op jit(solution)/shard_map/ppermute | solution.py:213
  48.6 7.6 %collective-permute-start.16 = (bf16[512,128]{1,0:T(8,128)(2,1)S(1)}, bf16[512,128]{1,0:T(8,128)(2,1)S(1)}, u32[]{:S(2)}, u32[]{:S(2)}) collective-permute-start(bf16[512,128]{1,0:T(8,128)(2,1)S(1)} %get-tuple-element.131), channel_id=1, source_target_pairs={{0,12},{4,8},{8,4},{12,0},{16,28},{20,24},{24,20},{28,16},{1,13},{... | collective-permute-start | bytes 393224 | tf_op jit(solution)/shard_map/ppermute | solution.py:213
  50.3 9.9 %collective-permute-start.18 = (bf16[512,128]{1,0:T(8,128)(2,1)S(1)}, bf16[512,128]{1,0:T(8,128)(2,1)S(1)}, u32[]{:S(2)}, u32[]{:S(2)}) collective-permute-start(bf16[512,128]{1,0:T(8,128)(2,1)S(1)} %get-tuple-element.134), channel_id=1, source_target_pairs={{0,4},{4,0},{8,12},{12,8},{16,20},{20,16},{24,28},{28,24},{1,5},{5... | collective-permute-start | bytes 393224 | tf_op jit(solution)/shard_map/ppermute | solution.py:213
  51.7 8.5 %collective-permute-start.19 = (bf16[512,128]{1,0:T(8,128)(2,1)S(1)}, bf16[512,128]{1,0:T(8,128)(2,1)S(1)}, u32[]{:S(2)}, u32[]{:S(2)}) collective-permute-start(bf16[512,128]{1,0:T(8,128)(2,1)S(1)} %get-tuple-element.135), channel_id=1, source_target_pairs={{0,8},{4,12},{8,0},{12,4},{16,24},{20,28},{24,16},{28,20},{1,9},{5... | collective-permute-start | bytes 393224 | tf_op jit(solution)/shard_map/ppermute | solution.py:213
  53.6 7.1 %collective-permute-start.20 = (bf16[512,128]{1,0:T(8,128)(2,1)S(1)}, bf16[512,128]{1,0:T(8,128)(2,1)S(1)}, u32[]{:S(2)}, u32[]{:S(2)}) collective-permute-start(bf16[512,128]{1,0:T(8,128)(2,1)S(1)} %get-tuple-element.136), channel_id=1, source_target_pairs={{0,12},{4,8},{8,4},{12,0},{16,28},{20,24},{24,20},{28,16},{1,13},{... | collective-permute-start | bytes 393224 | tf_op jit(solution)/shard_map/ppermute | solution.py:213
  56.3 8.7 %collective-permute-start.17 = (bf16[512,128]{1,0:T(8,128)(2,1)S(1)}, bf16[512,128]{1,0:T(8,128)(2,1)S(1)}, u32[]{:S(2)}, u32[]{:S(2)}) collective-permute-start(bf16[512,128]{1,0:T(8,128)(2,1)S(1)} %shard_map.79), channel_id=1, source_target_pairs={{16,0},{20,4},{24,8},{28,12},{17,1},{21,5},{25,9},{29,13},{18,2},{... | collective-permute-start | bytes 393224 | tf_op jit(solution)/shard_map/ppermute | solution.py:226
  60.8 8.4 %collective-permute-start.21 = (bf16[512,128]{1,0:T(8,128)(2,1)S(1)}, bf16[512,128]{1,0:T(8,128)(2,1)S(1)}, u32[]{:S(2)}, u32[]{:S(2)}) collective-permute-start(bf16[512,128]{1,0:T(8,128)(2,1)S(1)} %shard_map.83), channel_id=1, source_target_pairs={{16,0},{20,4},{24,8},{28,12},{17,1},{21,5},{25,9},{29,13},{18,2},{... | collective-permute-start | bytes 393224 | tf_op jit(solution)/shard_map/ppermute | solution.py:226
  65.4 6.3 %collective-permute-start.25 = (bf16[512,128]{1,0:T(8,128)(2,1)S(1)}, bf16[512,128]{1,0:T(8,128)(2,1)S(1)}, u32[]{:S(2)}, u32[]{:S(2)}) collective-permute-start(bf16[512,128]{1,0:T(8,128)(2,1)S(1)} %get-tuple-element.161), channel_id=1, source_target_pairs={{0,4},{4,0},{8,12},{12,8},{16,20},{20,16},{24,28},{28,24},{1,5},{5... | collective-permute-start | bytes 393224 | tf_op jit(solution)/shard_map/ppermute | solution.py:213
  66.3 6.8 %collective-permute-start.26 = (bf16[512,128]{1,0:T(8,128)(2,1)S(1)}, bf16[512,128]{1,0:T(8,128)(2,1)S(1)}, u32[]{:S(2)}, u32[]{:S(2)}) collective-permute-start(bf16[512,128]{1,0:T(8,128)(2,1)S(1)} %get-tuple-element.162), channel_id=1, source_target_pairs={{0,8},{4,12},{8,0},{12,4},{16,24},{20,28},{24,16},{28,20},{1,9},{5... | collective-permute-start | bytes 393224 | tf_op jit(solution)/shard_map/ppermute | solution.py:213
  66.3 8.3 %collective-permute-start.27 = (bf16[512,128]{1,0:T(8,128)(2,1)S(1)}, bf16[512,128]{1,0:T(8,128)(2,1)S(1)}, u32[]{:S(2)}, u32[]{:S(2)}) collective-permute-start(bf16[512,128]{1,0:T(8,128)(2,1)S(1)} %get-tuple-element.163), channel_id=1, source_target_pairs={{0,12},{4,8},{8,4},{12,0},{16,28},{20,24},{24,20},{28,16},{1,13},{... | collective-permute-start | bytes 393224 | tf_op jit(solution)/shard_map/ppermute | solution.py:213
  69.6 7.0 %collective-permute-start.22 = (bf16[512,128]{1,0:T(8,128)(2,1)S(1)}, bf16[512,128]{1,0:T(8,128)(2,1)S(1)}, u32[]{:S(2)}, u32[]{:S(2)}) collective-permute-start(bf16[512,128]{1,0:T(8,128)(2,1)S(1)} %get-tuple-element.154), channel_id=1, source_target_pairs={{0,4},{4,0},{8,12},{12,8},{16,20},{20,16},{24,28},{28,24},{1,5},{5... | collective-permute-start | bytes 393224 | tf_op jit(solution)/shard_map/ppermute | solution.py:213
  70.3 6.4 %collective-permute-start.23 = (bf16[512,128]{1,0:T(8,128)(2,1)S(1)}, bf16[512,128]{1,0:T(8,128)(2,1)S(1)}, u32[]{:S(2)}, u32[]{:S(2)}) collective-permute-start(bf16[512,128]{1,0:T(8,128)(2,1)S(1)} %get-tuple-element.155), channel_id=1, source_target_pairs={{0,8},{4,12},{8,0},{12,4},{16,24},{20,28},{24,16},{28,20},{1,9},{5... | collective-permute-start | bytes 393224 | tf_op jit(solution)/shard_map/ppermute | solution.py:213
  71.7 5.9 %collective-permute-start.24 = (bf16[512,128]{1,0:T(8,128)(2,1)S(1)}, bf16[512,128]{1,0:T(8,128)(2,1)S(1)}, u32[]{:S(2)}, u32[]{:S(2)}) collective-permute-start(bf16[512,128]{1,0:T(8,128)(2,1)S(1)} %get-tuple-element.156), channel_id=1, source_target_pairs={{0,12},{4,8},{8,4},{12,0},{16,28},{20,24},{24,20},{28,16},{1,13},{... | collective-permute-start | bytes 393224 | tf_op jit(solution)/shard_map/ppermute | solution.py:213

commit v6 on v5

v6 whole, which is shorter than its diff:
```python
from functools import partial

import jax
import jax.numpy as jnp
from jax import lax
from jax.experimental import pallas as pl
from jax.experimental.pallas import tpu as pltpu
from jax.sharding import PartitionSpec as P

DH = 128
EPS = 1e-05
CHUNKS = 2
F32 = jnp.float32
BF16 = jnp.bfloat16
NT = (((1,), (1,)), ((), ()))
NN = (((1,), (0,)), ((), ()))
TN = (((0,), (0,)), ((), ()))
VMEM = pl.BlockSpec(memory_space=pltpu.VMEM)
HBM = pl.BlockSpec(memory_space=pltpu.HBM)
barrier = lax.optimization_barrier


def mm(a, b, dims):
    return lax.dot_general(a, b, dims, preferred_element_type=F32)


def head(h):
    return slice(h * DH, (h + 1) * DH)


def head_at(offset, h):
    return pl.ds(pl.multiple_of(offset + h * DH, DH), DH)


def owned(member, j, part):
    return pl.multiple_of((member ^ j) * part, part)


def mask_of(t, later):
    rows = lax.broadcasted_iota(jnp.int32, (t, t), 0)
    cols = lax.broadcasted_iota(jnp.int32, (t, t), 1)
    return rows <= cols if later else rows >= cols


def first_state_kernel(part, m, which, k_hbm, v_hbm, *rest):
    outs, (k_ref, v_ref, sem) = rest[:-3], rest[-3:]
    member = lax.rem(lax.axis_index("seq"), m)
    copies = []
    for j in which:
        at = owned(member, j, part)
        pair = []
        for i, (src, dst) in enumerate(((k_hbm, k_ref), (v_hbm, v_ref))):
            here = pl.ds(at, part)
            copy = pltpu.make_async_copy(src.at[:, here], dst.at[:, here], sem.at[i, j])
            copy.start()
            pair.append(copy)
        copies.append((j, at, pair))
    for out, (j, at, pair) in zip(outs, copies):
        for copy in pair:
            copy.wait()
        for h in range(part // DH):
            a, b = k_ref[:, head_at(at, h)], v_ref[:, head_at(at, h)]
            out[head(h), :] = mm(a, b, TN).astype(BF16)


def state_kernel(chunk, part, m, k_ref, v_ref, *outs):
    member = lax.rem(lax.axis_index("seq"), m)
    for j in reversed(range(m)):
        far = pl.multiple_of(chunk * m * part + owned(member, j, part), part)
        for h in range(part // DH):
            a, b = k_ref[:, head_at(far, h)], v_ref[:, head_at(far, h)]
            outs[j][head(h), :] = mm(a, b, TN).astype(BF16)


def local_kernel(first, q_ref, k_ref, v_ref, c_ref, gain_ref, u_ref, loc_ref):
    mask = mask_of(q_ref.shape[0], False)
    for h in range(u_ref.shape[1] // DH):
        far = head(first + h)
        scores = mm(q_ref[:, far], k_ref[:, far], NT)
        weights = jnp.where(mask, scores, 0.0).astype(BF16)
        loc_ref[:, head(h)] = mm(weights, v_ref[:, far], NN)
        u_ref[:, head(h)] = c_ref[:, far].astype(F32) * gain_ref[:, far]


def attend_kernel(chunk, part, m, which, width, q_ref, loc_ref, u_ref, *rest):
    count = len(which)
    prefixes, before, (att_ref, ss_ref, su_ref) = rest[:count], rest[count:-3], rest[-3:]
    member = lax.rem(lax.axis_index("seq"), m)
    if before:
        ss, su = before[0][...], before[1][...]
    else:
        ss = jnp.zeros(ss_ref.shape, F32)
        su = jnp.zeros(su_ref.shape, F32)
    for pre, j in zip(prefixes, which):
        at = owned(member, j, part)
        for h in range(part // DH):
            here = head_at(at, h)
            far = head_at(chunk * m * part + at, h)
            att = loc_ref[:, here] + mm(q_ref[:, far], pre[head(h), :], NN)
            att_ref[:, here] = att
            ss = ss + att * att
            su = su + att * u_ref[:, here]
    if width:
        r = lax.rsqrt(jnp.sum(ss, axis=1, keepdims=True) / width + EPS)
        su = r * r * r * (jnp.sum(su, axis=1, keepdims=True) / width)
        ss = r
    ss_ref[...] = jnp.broadcast_to(ss, ss_ref.shape)
    su_ref[...] = jnp.broadcast_to(su, su_ref.shape)


def grad_kernel(chunk, part, m, which, q_ref, att_ref, u_ref, r_ref, s_ref, *rest):
    g_ref, outs = rest[-len(which) - 1], rest[-len(which) :]
    member = lax.rem(lax.axis_index("seq"), m)
    r = r_ref[...]
    s = s_ref[...]
    for out, j in zip(outs, which):
        at = owned(member, j, part)
        for h in range(part // DH):
            here = head_at(at, h)
            g = (u_ref[:, here] * r - att_ref[:, here] * s).astype(BF16)
            g_ref[:, here] = g
            far = head_at(chunk * m * part + at, h)
            out[head(h), :] = mm(q_ref[:, far], g, TN).astype(BF16)


def back_local_kernel(first, q_ref, k_ref, v_ref, g_ref, kl_ref, vl_ref):
    mask = mask_of(q_ref.shape[0], True)
    for h in range(g_ref.shape[1] // DH):
        q, k, v = (ref[:, head(first + h)] for ref in (q_ref, k_ref, v_ref))
        g = g_ref[:, head(h)]
        vw = jnp.where(mask, mm(v, g, NT), 0.0).astype(BF16)
        kl_ref[:, head(h)] = mm(vw, q, NN)
        kw = jnp.where(mask, mm(k, q, NT), 0.0).astype(BF16)
        vl_ref[:, head(h)] = mm(kw, g, NN)


def finish_kernel(chunk, part, m, which, k_ref, v_ref, kl_ref, vl_ref, *rest):
    suffixes = rest[: len(which)]
    kg_hbm, vg_hbm, kg_ref, vg_ref, sem = rest[-5:]
    member = lax.rem(lax.axis_index("seq"), m)
    copies = []
    for suf, j in zip(suffixes, which):
        at = owned(member, j, part)
        far = pl.multiple_of(chunk * m * part + at, part)
        for h in range(part // DH):
            here = head_at(at, h)
            s = suf[head(h), :]
            own = head_at(far, h)
            kg_ref[:, here] = (kl_ref[:, here] + mm(v_ref[:, own], s, NT)).astype(BF16)
            vg_ref[:, here] = (vl_ref[:, here] + mm(k_ref[:, own], s, NN)).astype(BF16)
        for i, (src, dst) in enumerate(((kg_ref, kg_hbm), (vg_ref, vg_hbm))):
            copy = pltpu.make_async_copy(src.at[:, pl.ds(at, part)], dst.at[:, pl.ds(far, part)], sem.at[i, j])
            copy.start()
            copies.append(copy)
    for copy in copies:
        copy.wait()


def total_kernel(*refs):
    acc = refs[0][...].astype(F32)
    for ref in refs[1:-1]:
        acc = acc + ref[...].astype(F32)
    refs[-1][...] = acc.astype(refs[-1].dtype)


def give_back_kernel(m, forward, groups, carry, *refs):
    group = lax.axis_index("seq") // m
    use = group > 0 if forward else group < groups - 1
    got, back = refs[:m], refs[m:]
    member = lax.rem(lax.axis_index("seq"), m)
    for j in range(m):
        acc = jnp.where(use, carry[...].astype(F32), 0.0)
        for i in range(m):
            if i != j:
                source, target = member ^ i, member ^ j
                take = (source < target) if forward else (source > target)
                acc = acc + jnp.where(take, got[i][...].astype(F32), 0.0)
        back[j][...] = acc.astype(BF16)


def call(kernel, args, in_specs, out_shape, flops, nbytes, scratch=(), out_specs=None, alias={}):
    return pl.pallas_call(
        kernel,
        in_specs=in_specs,
        out_specs=out_specs or [VMEM] * len(out_shape),
        out_shape=out_shape,
        scratch_shapes=scratch,
        input_output_aliases=alias,
        compiler_params=pltpu.CompilerParams(vmem_limit_bytes=8 << 20),
        cost_estimate=pl.CostEstimate(flops=flops, bytes_accessed=nbytes, transcendentals=0),
    )(*args)


def total_of(got, n):
    m = len(got)
    wire = BF16 if n // m == 2 else F32
    (total,) = call(total_kernel, got, [VMEM] * m, [pltpu.VMEM(got[0].shape, wire)], got[0].size, got[0].size)
    return total


def give_back(got, carry, n, forward):
    m = len(got)
    return call(
        partial(give_back_kernel, m, forward, n // m), (carry, *got), [VMEM] * (m + 1),
        [pltpu.VMEM(got[0].shape, BF16)] * m, got[0].size, got[0].size,
    )


def exchange(parts, n):
    m = len(parts)
    out = [parts[0]] + [None] * (m - 1)
    for j in range(m - 1, 0, -1):
        perm = [(i, (i // m) * m + ((i % m) ^ j)) for i in range(n)]
        out[j] = lax.ppermute(parts[j], "seq", perm)
    return out


def carry_groups(total, n, m, forward):
    groups = n // m
    group = lax.axis_index("seq") // m

    def shift(x, by):
        step = by * m if forward else n - by * m
        return lax.ppermute(x, "seq", [(i, (i + step) % n) for i in range(n)])

    def shift_in(x, by):
        inside = group >= by if forward else group < groups - by
        return jnp.where(inside, shift(x, by), 0.0)

    if groups == 1:
        return total
    if groups == 2:
        return shift(total, 1)
    run = shift_in(total, 1)
    by = 1
    while by < groups - 1:
        run = run + shift_in(run, by)
        by *= 2
    return run


def scan_chunks(first, second_of, n, forward, fill_a, fill_b):
    m = len(first)
    got_a = exchange(first, n)
    second, extra = second_of()
    got_b = exchange(second, n)
    made_a = fill_a(extra)
    made_b = fill_b(extra)
    if forward:
        got_b, made_a, made_b = barrier((got_b, made_a, made_b))
    else:
        got_a, made_a = barrier((got_a, made_a))
    carry_a = carry_groups(total_of(got_a, n), n, m, forward)
    carry_b = carry_groups(total_of(got_b, n), n, m, forward)
    back_a = exchange(give_back(got_a, carry_a, n, forward), n)
    back_b = exchange(give_back(got_b, carry_b, n, forward), n)
    return (back_a, back_b), (made_a, made_b)


def shards(n, queries, keys, values, gain, cotangent):
    rows, width = queries.shape
    m = 4 if n % 4 == 0 else (2 if n % 2 == 0 else 1)
    half = width // CHUNKS
    part = half // m
    gain2 = gain.reshape(1, width)
    wide = pltpu.VMEM((rows, half), F32)
    slim = pltpu.VMEM((rows, half), BF16)
    stat = pltpu.VMEM((rows, DH), F32)
    state = pltpu.VMEM((part, DH), BF16)
    sems = pltpu.SemaphoreType.DMA((2, m))
    unit = 2 * rows * DH * half

    every, far, near = tuple(range(m)), (m - 1,), tuple(range(m - 1))

    def first_states(which):
        return call(
            partial(first_state_kernel, part, m, which),
            tuple(pltpu.with_memory_space_constraint(x, pltpu.HBM) for x in (keys, values)), [HBM, HBM],
            [state] * len(which), unit * len(which) // m, 6 * rows * half * len(which) // m, [slim, slim, sems],
        )

    def states_of(c):
        return call(
            partial(state_kernel, c, part, m), (keys, values), [VMEM, VMEM],
            [state] * m, unit, 4 * rows * half,
        )

    def local_of(c, args):
        return call(
            partial(local_kernel, c * half // DH), (*args, gain2), [VMEM] * 5,
            [wide, wide], 4 * unit, 12 * rows * half,
        )

    parts_a = first_states(every[::-1])[::-1]
    parts_a, queries, keys, values, cotangent = barrier((parts_a, queries, keys, values, cotangent))
    base = (queries, keys, values, cotangent)
    prefix, made = scan_chunks(
        parts_a, lambda: (states_of(1), base), n, True,
        lambda e: local_of(0, e), lambda e: local_of(1, e),
    )

    def attend(c, which, loc, sums, finish):
        return call(
            partial(attend_kernel, c, part, m, which, width if finish else 0),
            (queries, loc, made[c][0], *(prefix[c][j] for j in which), *sums),
            [VMEM] * (3 + len(which) + len(sums)), [wide, stat, stat],
            unit * len(which) // m, 4 * rows * half * len(which) // m, alias={1: 0},
        )

    att_a, *sums = attend(0, every, made[0][1], (), False)
    att_b = made[1][1]
    if m > 1:
        att_b, *sums = attend(1, near, att_b, sums, False)
    att_b, *scale = attend(1, far, att_b, sums, True)
    attended = (att_a, att_b)

    def grads_of(c, which, g):
        k = len(which)
        g, *parts = call(
            partial(grad_kernel, c, part, m, which), (queries, attended[c], made[c][0], *scale, *g),
            [VMEM] * (5 + len(g)), [slim] + [state] * k,
            unit * k // m, 4 * rows * half * k // m, alias={5: 0} if g else {},
        )
        return parts, g

    def back_local_of(c, g):
        return call(
            partial(back_local_kernel, c * half // DH), (queries, keys, values, g), [VMEM] * 4,
            [wide, wide], 8 * unit, 8 * rows * half,
        )

    parts_a, near_a = grads_of(0, far, ())
    if m > 1:
        parts, near_a = grads_of(0, near, (near_a,))
        parts_a = parts + parts_a

    def second_grads():
        parts_b, near_b = grads_of(1, every, ())
        return parts_b, (near_a, near_b)

    suffix, made = scan_chunks(
        parts_a, second_grads, n, False,
        lambda e: back_local_of(0, e[0]), lambda e: back_local_of(1, e[1]),
    )

    outs = ()
    for c, which in ((0, every), (1, every)):
        if not which:
            continue
        k = len(which)
        base = 4 + k
        outs = call(
            partial(finish_kernel, c, part, m, which),
            (keys, values, *made[c], *(suffix[c][j] for j in which), *outs),
            [VMEM] * (4 + k) + [HBM] * len(outs),
            [jax.ShapeDtypeStruct((rows, width), BF16)] * 2, 2 * unit * k // m, 8 * rows * half * k // m,
            [slim, slim, sems], out_specs=[HBM, HBM], alias={base: 0, base + 1: 1} if outs else {},
        )
    return tuple(outs)


def solution(mesh):
    spec = P(("dp", "seq"), None)
    return jax.shard_map(
        partial(shards, mesh.shape["seq"]),
        mesh=mesh,
        in_specs=(spec, spec, spec, P(), spec),
        out_specs=(spec, spec),
        check_vma=False,
    )
```

time: 80.1 us -> 78.6 us (0.981)
  Pallas kernels: 28.5 us -> 23.2 us
  starting transfers between devices: 42 us -> 44.5 us
  waiting for transfers between devices: 8.24 us -> 9.63 us
    pallas_call x20 -> x22, Pallas kernels: 28.5 us -> 23.2 us  [call(): pl.pallas_call(kernel, in_specs=in_specs, out_specs=out_specs or [VMEM] *...]
    ppermute x24, starting transfers between devices: 32.4 us -> 35 us  [exchange(): out[j] = lax.ppermute(parts[j], 'seq', perm)]
    ppermute x4, waiting for transfers between devices: 0.41 us -> 1.85 us  [shift(): return lax.ppermute(x, 'seq', [(i, (i + step) % n) for i in range(n)])]
  transfers between devices with their start and end apart: 28 -> 28, of which waited for: 9 -> 7; matrix products, arithmetic and copies ran while one was open for 0% -> 0% of each run, Pallas kernels for 27% -> 21%
where the time goes in v6:
time: 78.6 us; the launch traced here: 78.4 us
  starting transfers between devices  44.5 us (57%)
  Pallas kernels  23.2 us (30%)
  waiting for transfers between devices  9.63 us (12%)
  between operations  1.05 us (1%)
    ppermute x24, starting transfers between devices, exchange(): out[j] = lax.ppermute(parts[j], 'seq', perm)  35 us
    pallas_call x22, Pallas kernels, call(): pl.pallas_call(kernel, in_specs=in_specs, out_specs=out_specs or [VMEM] *...  23.2 us
    ppermute x4, starting transfers between devices, shift(): return lax.ppermute(x, 'seq', [(i, (i + step) % n) for i in range(n)])  9.47 us
    ppermute x24, waiting for transfers between devices, exchange(): out[j] = lax.ppermute(parts[j], 'seq', perm)  7.78 us
    ppermute x4, waiting for transfers between devices, shift(): return lax.ppermute(x, 'seq', [(i, (i + step) % n) for i in range(n)])  1.85 us
  transfers between devices with their start and end apart: 28, of which 7 were waited for; matrix products, arithmetic and copies ran while one was open for 0% of the time, Pallas kernels for 21%

profile of v6, /device:TPU:0, one launch (start us, length us, event | category | flops | bytes accessed | tf_op | source)
XLA Modules:
  0.0 78.4 jit_solution(852901104655888960)
XLA Ops:
  0.6 2.6 %shard_map.68 = (bf16[512,128]{1,0:T(8,128)(2,1)S(1)}, bf16[512,128]{1,0:T(8,128)(2,1)S(1)}, bf16[512,128]{1,0:T(8,128)(2,1)S(1)}, bf16[512,128]{1,0:T(8,128)(2,1)S(1)}) custom-call(bf16[256,4096]{1,0:T(8,128)(2,1)} %k_ref.6, bf16[256,4096]{1,0:T(8,128)(2,1)} %v_ref.6), custom_call_target="tpu_custom_call" | custom-call | flops 134217728 | bytes 3145728 | tf_op jit(solution)/shard_map/pallas_call | solution.py:182
  3.2 3.0 %collective-permute-start.6 = (bf16[512,128]{1,0:T(8,128)(2,1)S(1)}, bf16[512,128]{1,0:T(8,128)(2,1)S(1)}, u32[]{:S(2)}, u32[]{:S(2)}) collective-permute-start(bf16[512,128]{1,0:T(8,128)(2,1)S(1)} %get-tuple-element.106), channel_id=1, source_target_pairs={{0,4},{4,0},{8,12},{12,8},{16,20},{20,16},{24,28},{28,24},{1,5},{5... | collective-permute-start | bytes 393224 | tf_op jit(solution)/shard_map/ppermute | solution.py:214
  6.3 1.6 %collective-permute-start.7 = (bf16[512,128]{1,0:T(8,128)(2,1)S(1)}, bf16[512,128]{1,0:T(8,128)(2,1)S(1)}, u32[]{:S(2)}, u32[]{:S(2)}) collective-permute-start(bf16[512,128]{1,0:T(8,128)(2,1)S(1)} %get-tuple-element.107), channel_id=1, source_target_pairs={{0,8},{4,12},{8,0},{12,4},{16,24},{20,28},{24,16},{28,20},{1,9},{5... | collective-permute-start | bytes 393224 | tf_op jit(solution)/shard_map/ppermute | solution.py:214
  7.8 0.8 %shard_map.69 = (bf16[512,128]{1,0:T(8,128)(2,1)S(1)}, bf16[512,128]{1,0:T(8,128)(2,1)S(1)}, bf16[512,128]{1,0:T(8,128)(2,1)S(1)}, bf16[512,128]{1,0:T(8,128)(2,1)S(1)}) custom-call(bf16[256,4096]{1,0:T(8,128)(2,1)S(1)} %copy-done.1, bf16[256,4096]{1,0:T(8,128)(2,1)S(1)} %copy-done.2), custom_call_target="tpu_custom_call" | custom-call | flops 134217728 | bytes 2097152 | tf_op jit(solution)/shard_map/pallas_call | solution.py:182
  8.7 2.0 %collective-permute-start = (bf16[512,128]{1,0:T(8,128)(2,1)S(1)}, bf16[512,128]{1,0:T(8,128)(2,1)S(1)}, u32[]{:S(2)}, u32[]{:S(2)}) collective-permute-start(bf16[512,128]{1,0:T(8,128)(2,1)S(1)} %get-tuple-element.86), channel_id=1, source_target_pairs={{0,4},{4,0},{8,12},{12,8},{16,20},{20,16},{24,28},{28,24},{1,5},{5... | collective-permute-start | bytes 393224 | tf_op jit(solution)/shard_map/ppermute | solution.py:214
  10.6 1.6 %collective-permute-start.1 = (bf16[512,128]{1,0:T(8,128)(2,1)S(1)}, bf16[512,128]{1,0:T(8,128)(2,1)S(1)}, u32[]{:S(2)}, u32[]{:S(2)}) collective-permute-start(bf16[512,128]{1,0:T(8,128)(2,1)S(1)} %get-tuple-element.87), channel_id=1, source_target_pairs={{0,8},{4,12},{8,0},{12,4},{16,24},{20,28},{24,16},{28,20},{1,9},{5... | collective-permute-start | bytes 393224 | tf_op jit(solution)/shard_map/ppermute | solution.py:214
  12.2 0.6 collective-permute-start.2
  12.8 2.4 %collective-permute-done.8.refs_3_ = bf16[512,128]{1,0:T(8,128)(2,1)S(1)} collective-permute-done((bf16[512,128]{1,0:T(8,128)(2,1)S(1)}, bf16[512,128]{1,0:T(8,128)(2,1)S(1)}, u32[]{:S(2)}, u32[]{:S(2)}) %collective-permute-start.8) | collective-permute-done | bytes 131104 | tf_op jit(solution)/shard_map/ppermute | solution.py:214
  15.3 2.6 %collective-permute-start.9 = (bf16[512,128]{1,0:T(8,128)(2,1)S(1)}, bf16[512,128]{1,0:T(8,128)(2,1)S(1)}, u32[]{:S(2)}, u32[]{:S(2)}) collective-permute-start(bf16[512,128]{1,0:T(8,128)(2,1)S(1)} %shard_map.74), channel_id=1, source_target_pairs={{0,16},{4,20},{8,24},{12,28},{16,0},{20,4},{24,8},{28,12},{1,17},{... | collective-permute-start | bytes 393224 | tf_op jit(solution)/shard_map/ppermute | solution.py:224
  17.9 1.6 %shard_map.71 = (f32[256,2048]{1,0:T(8,128)S(1)}, f32[256,2048]{1,0:T(8,128)S(1)}) custom-call(bf16[256,4096]{1,0:T(8,128)(2,1)S(1)} %copy-done, bf16[256,4096]{1,0:T(8,128)(2,1)S(1)} %copy-done.1, bf16[256,4096]{1,0:T(8,128)(2,1)S(1)} %copy-done.2, bf16[256,4096]{1,0:T(8,128)(2,1)S(1)} %copy-done.3, f32[1,4096]{1,0:T(1,128)S(1)} %bitcast.1), custom_call_target="tpu_custom_call" | custom-call | flops 536870912 | bytes 6291456 | tf_op jit(solution)/shard_map/pallas_call | solution.py:182
  19.5 1.6 %shard_map.70 = (f32[256,2048]{1,0:T(8,128)S(1)}, f32[256,2048]{1,0:T(8,128)S(1)}) custom-call(bf16[256,4096]{1,0:T(8,128)(2,1)S(1)} %copy-done, bf16[256,4096]{1,0:T(8,128)(2,1)S(1)} %copy-done.1, bf16[256,4096]{1,0:T(8,128)(2,1)S(1)} %copy-done.2, bf16[256,4096]{1,0:T(8,128)(2,1)S(1)} %copy-done.3, f32[1,4096]{1,0:T(1,128)S(1)} %bitcast.2), custom_call_target="tpu_custom_call" | custom-call | flops 536870912 | bytes 6291456 | tf_op jit(solution)/shard_map/pallas_call | solution.py:182
  21.3 2.3 %collective-permute-start.3 = (bf16[512,128]{1,0:T(8,128)(2,1)S(1)}, bf16[512,128]{1,0:T(8,128)(2,1)S(1)}, u32[]{:S(2)}, u32[]{:S(2)}) collective-permute-start(bf16[512,128]{1,0:T(8,128)(2,1)S(1)} %shard_map.72), channel_id=1, source_target_pairs={{0,16},{4,20},{8,24},{12,28},{16,0},{20,4},{24,8},{28,12},{1,17},{... | collective-permute-start | bytes 393224 | tf_op jit(solution)/shard_map/ppermute | solution.py:224
  24.0 3.9 %collective-permute-start.10 = (bf16[512,128]{1,0:T(8,128)(2,1)S(1)}, bf16[512,128]{1,0:T(8,128)(2,1)S(1)}, u32[]{:S(2)}, u32[]{:S(2)}) collective-permute-start(bf16[512,128]{1,0:T(8,128)(2,1)S(1)} %get-tuple-element.110), channel_id=1, source_target_pairs={{0,4},{4,0},{8,12},{12,8},{16,20},{20,16},{24,28},{28,24},{1,5},{5... | collective-permute-start | bytes 393224 | tf_op jit(solution)/shard_map/ppermute | solution.py:214
  28.1 1.2 %collective-permute-start.12 = (bf16[512,128]{1,0:T(8,128)(2,1)S(1)}, bf16[512,128]{1,0:T(8,128)(2,1)S(1)}, u32[]{:S(2)}, u32[]{:S(2)}) collective-permute-start(bf16[512,128]{1,0:T(8,128)(2,1)S(1)} %get-tuple-element.112), channel_id=1, source_target_pairs={{0,12},{4,8},{8,4},{12,0},{16,28},{20,24},{24,20},{28,16},{1,13},{... | collective-permute-start | bytes 393224 | tf_op jit(solution)/shard_map/ppermute | solution.py:214
  29.4 0.8 collective-permute-done.3.carry
  30.1 0.4 shard_map.73
  30.5 1.2 %collective-permute-start.4 = (bf16[512,128]{1,0:T(8,128)(2,1)S(1)}, bf16[512,128]{1,0:T(8,128)(2,1)S(1)}, u32[]{:S(2)}, u32[]{:S(2)}) collective-permute-start(bf16[512,128]{1,0:T(8,128)(2,1)S(1)} %get-tuple-element.101), channel_id=1, source_target_pairs={{0,4},{4,0},{8,12},{12,8},{16,20},{20,16},{24,28},{28,24},{1,5},{5... | collective-permute-start | bytes 393224 | tf_op jit(solution)/shard_map/ppermute | solution.py:214
  31.8 0.6 collective-permute-start.5
  32.4 4.0 %collective-permute-start.13 = (bf16[512,128]{1,0:T(8,128)(2,1)S(1)}, bf16[512,128]{1,0:T(8,128)(2,1)S(1)}, u32[]{:S(2)}, u32[]{:S(2)}) collective-permute-start(bf16[512,128]{1,0:T(8,128)(2,1)S(1)} %get-tuple-element.116), channel_id=1, source_target_pairs={{0,12},{4,8},{8,4},{12,0},{16,28},{20,24},{24,20},{28,16},{1,13},{... | collective-permute-start | bytes 393224 | tf_op jit(solution)/shard_map/ppermute | solution.py:214
  36.4 1.3 %shard_map.76 = (f32[256,2048]{1,0:T(8,128)S(1)}, f32[256,128]{1,0:T(8,128)S(1)}, f32[256,128]{1,0:T(8,128)S(1)}) custom-call(bf16[256,4096]{1,0:T(8,128)(2,1)S(1)} %copy-done, f32[256,2048]{1,0:T(8,128)S(1)} %get-tuple-element.103.loc_ref, f32[256,2048]{1,0:T(8,128)S(1)} %get-tuple-element.104.u_ref, ...), custom_call_target="tpu_custom_call", output_to_operand_aliasing={{0}: (1, {})} | custom-call | flops 134217728 | bytes 2097152 | tf_op jit(solution)/shard_map/pallas_call | solution.py:182
  37.7 0.8 collective-permute-done.4.rest_1_
  38.5 1.0 %shard_map.77 = (f32[256,2048]{1,0:T(8,128)S(1)}, f32[256,128]{1,0:T(8,128)S(1)}, f32[256,128]{1,0:T(8,128)S(1)}) custom-call(bf16[256,4096]{1,0:T(8,128)(2,1)S(1)} %copy-done, f32[256,2048]{1,0:T(8,128)S(1)} %get-tuple-element.94.loc_ref, f32[256,2048]{1,0:T(8,128)S(1)} %get-tuple-element.95.u_ref, ...), custom_call_target="tpu_custom_call", output_to_operand_aliasing={{0}: (1, {})} | custom-call | flops 100663296 | bytes 1572864 | tf_op jit(solution)/shard_map/pallas_call | solution.py:182
  39.5 0.6 collective-permute-done.13.rest_0_
  40.0 0.5 shard_map.78
  40.5 0.5 shard_map.83
  41.0 1.0 %shard_map.84 = (bf16[256,2048]{1,0:T(8,128)(2,1)S(1)}, bf16[512,128]{1,0:T(8,128)(2,1)S(1)}, bf16[512,128]{1,0:T(8,128)(2,1)S(1)}, bf16[512,128]{1,0:T(8,128)(2,1)S(1)}) custom-call(bf16[256,4096]{1,0:T(8,128)(2,1)S(1)} %copy-done, f32[256,2048]{1,0:T(8,128)S(1)} %get-tuple-element.133.att_ref, ...), custom_call_target="tpu_custom_call", output_to_operand_aliasing={{0}: (5, {})} | custom-call | flops 100663296 | bytes 1572864 | tf_op jit(solution)/shard_map/pallas_call | solution.py:182
  42.1 1.4 %collective-permute-start.21 = (bf16[512,128]{1,0:T(8,128)(2,1)S(1)}, bf16[512,128]{1,0:T(8,128)(2,1)S(1)}, u32[]{:S(2)}, u32[]{:S(2)}) collective-permute-start(bf16[512,128]{1,0:T(8,128)(2,1)S(1)} %get-tuple-element.136), channel_id=1, source_target_pairs={{0,4},{4,0},{8,12},{12,8},{16,20},{20,16},{24,28},{28,24},{1,5},{5... | collective-permute-start | bytes 393224 | tf_op jit(solution)/shard_map/ppermute | solution.py:214
  43.5 1.4 %collective-permute-start.22 = (bf16[512,128]{1,0:T(8,128)(2,1)S(1)}, bf16[512,128]{1,0:T(8,128)(2,1)S(1)}, u32[]{:S(2)}, u32[]{:S(2)}) collective-permute-start(bf16[512,128]{1,0:T(8,128)(2,1)S(1)} %get-tuple-element.137), channel_id=1, source_target_pairs={{0,8},{4,12},{8,0},{12,4},{16,24},{20,28},{24,16},{28,20},{1,9},{5... | collective-permute-start | bytes 393224 | tf_op jit(solution)/shard_map/ppermute | solution.py:214
  44.9 0.7 collective-permute-start.23
  45.6 1.3 %shard_map.79 = (bf16[256,2048]{1,0:T(8,128)(2,1)S(1)}, bf16[512,128]{1,0:T(8,128)(2,1)S(1)}, bf16[512,128]{1,0:T(8,128)(2,1)S(1)}, bf16[512,128]{1,0:T(8,128)(2,1)S(1)}, bf16[512,128]{1,0:T(8,128)(2,1)S(1)}) custom-call(bf16[256,4096]{1,0:T(8,128)(2,1)S(1)} %copy-done, f32[256,2048]{1,0:T(8,128)S(1)} %get-tuple-element.119.att_ref, ...), custom_call_target="tpu_custom_call" | custom-call | flops 134217728 | bytes 2097152 | tf_op jit(solution)/shard_map/pallas_call | solution.py:182
  47.0 1.4 %collective-permute-start.14 = (bf16[512,128]{1,0:T(8,128)(2,1)S(1)}, bf16[512,128]{1,0:T(8,128)(2,1)S(1)}, u32[]{:S(2)}, u32[]{:S(2)}) collective-permute-start(bf16[512,128]{1,0:T(8,128)(2,1)S(1)} %get-tuple-element.126), channel_id=1, source_target_pairs={{0,4},{4,0},{8,12},{12,8},{16,20},{20,16},{24,28},{28,24},{1,5},{5... | collective-permute-start | bytes 393224 | tf_op jit(solution)/shard_map/ppermute | solution.py:214
  48.4 1.5 %collective-permute-start.15 = (bf16[512,128]{1,0:T(8,128)(2,1)S(1)}, bf16[512,128]{1,0:T(8,128)(2,1)S(1)}, u32[]{:S(2)}, u32[]{:S(2)}) collective-permute-start(bf16[512,128]{1,0:T(8,128)(2,1)S(1)} %get-tuple-element.127), channel_id=1, source_target_pairs={{0,8},{4,12},{8,0},{12,4},{16,24},{20,28},{24,16},{28,20},{1,9},{5... | collective-permute-start | bytes 393224 | tf_op jit(solution)/shard_map/ppermute | solution.py:214
  49.8 2.6 %shard_map.85 = (f32[256,2048]{1,0:T(8,128)S(1)}, f32[256,2048]{1,0:T(8,128)S(1)}) custom-call(bf16[256,4096]{1,0:T(8,128)(2,1)S(1)} %copy-done, bf16[256,4096]{1,0:T(8,128)(2,1)S(1)} %copy-done.1, bf16[256,4096]{1,0:T(8,128)(2,1)S(1)} %copy-done.2, bf16[256,2048]{1,0:T(8,128)(2,1)S(1)} %get-tuple-element.139.g_ref), custom_call_target="tpu_custom_call" | custom-call | flops 1073741824 | bytes 4194304 | tf_op jit(solution)/shard_map/pallas_call | solution.py:182
  52.4 0.8 collective-permute-start.16
  53.2 2.2 %collective-permute-start.24 = (bf16[512,128]{1,0:T(8,128)(2,1)S(1)}, bf16[512,128]{1,0:T(8,128)(2,1)S(1)}, u32[]{:S(2)}, u32[]{:S(2)}) collective-permute-start(bf16[512,128]{1,0:T(8,128)(2,1)S(1)} %shard_map.86), channel_id=1, source_target_pairs={{0,16},{4,20},{8,24},{12,28},{16,0},{20,4},{24,8},{28,12},{1,17},{... | collective-permute-start | bytes 393224 | tf_op jit(solution)/shard_map/ppermute | solution.py:224
  55.5 2.9 %collective-permute-done.16.refs_3_ = bf16[512,128]{1,0:T(8,128)(2,1)S(1)} collective-permute-done((bf16[512,128]{1,0:T(8,128)(2,1)S(1)}, bf16[512,128]{1,0:T(8,128)(2,1)S(1)}, u32[]{:S(2)}, u32[]{:S(2)}) %collective-permute-start.16) | collective-permute-done | bytes 131104 | tf_op jit(solution)/shard_map/ppermute | solution.py:214
  58.4 2.3 %collective-permute-start.17 = (bf16[512,128]{1,0:T(8,128)(2,1)S(1)}, bf16[512,128]{1,0:T(8,128)(2,1)S(1)}, u32[]{:S(2)}, u32[]{:S(2)}) collective-permute-start(bf16[512,128]{1,0:T(8,128)(2,1)S(1)} %shard_map.81), channel_id=1, source_target_pairs={{0,16},{4,20},{8,24},{12,28},{16,0},{20,4},{24,8},{28,12},{1,17},{... | collective-permute-start | bytes 393224 | tf_op jit(solution)/shard_map/ppermute | solution.py:224
  61.1 1.9 %collective-permute-start.25 = (bf16[512,128]{1,0:T(8,128)(2,1)S(1)}, bf16[512,128]{1,0:T(8,128)(2,1)S(1)}, u32[]{:S(2)}, u32[]{:S(2)}) collective-permute-start(bf16[512,128]{1,0:T(8,128)(2,1)S(1)} %get-tuple-element.149), channel_id=1, source_target_pairs={{0,4},{4,0},{8,12},{12,8},{16,20},{20,16},{24,28},{28,24},{1,5},{5... | collective-permute-start | bytes 393224 | tf_op jit(solution)/shard_map/ppermute | solution.py:214
  63.0 1.8 %collective-permute-start.26 = (bf16[512,128]{1,0:T(8,128)(2,1)S(1)}, bf16[512,128]{1,0:T(8,128)(2,1)S(1)}, u32[]{:S(2)}, u32[]{:S(2)}) collective-permute-start(bf16[512,128]{1,0:T(8,128)(2,1)S(1)} %get-tuple-element.150), channel_id=1, source_target_pairs={{0,8},{4,12},{8,0},{12,4},{16,24},{20,28},{24,16},{28,20},{1,9},{5... | collective-permute-start | bytes 393224 | tf_op jit(solution)/shard_map/ppermute | solution.py:214
  64.7 0.7 collective-permute-start.27
  65.5 1.1 %collective-permute-done.17.carry = bf16[512,128]{1,0:T(8,128)(2,1)S(1)} collective-permute-done((bf16[512,128]{1,0:T(8,128)(2,1)S(1)}, bf16[512,128]{1,0:T(8,128)(2,1)S(1)}, u32[]{:S(2)}, u32[]{:S(2)}) %collective-permute-start.17) | collective-permute-done | bytes 131104 | tf_op jit(solution)/shard_map/ppermute | solution.py:224
  67.0 1.2 %collective-permute-start.18 = (bf16[512,128]{1,0:T(8,128)(2,1)S(1)}, bf16[512,128]{1,0:T(8,128)(2,1)S(1)}, u32[]{:S(2)}, u32[]{:S(2)}) collective-permute-start(bf16[512,128]{1,0:T(8,128)(2,1)S(1)} %get-tuple-element.130), channel_id=1, source_target_pairs={{0,4},{4,0},{8,12},{12,8},{16,20},{20,16},{24,28},{28,24},{1,5},{5... | collective-permute-start | bytes 393224 | tf_op jit(solution)/shard_map/ppermute | solution.py:214
  68.1 0.6 collective-permute-start.19
  68.7 1.8 %collective-permute-start.20 = (bf16[512,128]{1,0:T(8,128)(2,1)S(1)}, bf16[512,128]{1,0:T(8,128)(2,1)S(1)}, u32[]{:S(2)}, u32[]{:S(2)}) collective-permute-start(bf16[512,128]{1,0:T(8,128)(2,1)S(1)} %get-tuple-element.132), channel_id=1, source_target_pairs={{0,12},{4,8},{8,4},{12,0},{16,28},{20,24},{24,20},{28,16},{1,13},{... | collective-permute-start | bytes 393224 | tf_op jit(solution)/shard_map/ppermute | solution.py:214
  70.5 2.6 %shard_map.80 = (f32[256,2048]{1,0:T(8,128)S(1)}, f32[256,2048]{1,0:T(8,128)S(1)}) custom-call(bf16[256,4096]{1,0:T(8,128)(2,1)S(1)} %copy-done, bf16[256,4096]{1,0:T(8,128)(2,1)S(1)} %copy-done.1, bf16[256,4096]{1,0:T(8,128)(2,1)S(1)} %copy-done.2, bf16[256,2048]{1,0:T(8,128)(2,1)S(1)} %get-tuple-element.122.g_ref), custom_call_target="tpu_custom_call" | custom-call | flops 1073741824 | bytes 4194304 | tf_op jit(solution)/shard_map/pallas_call | solution.py:182
  73.1 2.0 %shard_map.88 = (bf16[256,4096]{1,0:T(8,128)(2,1)}, bf16[256,4096]{1,0:T(8,128)(2,1)}) custom-call(bf16[256,4096]{1,0:T(8,128)(2,1)S(1)} %copy-done.1, bf16[256,4096]{1,0:T(8,128)(2,1)S(1)} %copy-done.2, f32[256,2048]{1,0:T(8,128)S(1)} %get-tuple-element.142.kl_ref, f32[256,2048]{1,0:T(8,128)S(1)} %get-tuple-element.143.vl_ref, ...), custom_call_target="tpu_custom_call" | custom-call | flops 268435456 | bytes 4194304 | tf_op jit(solution)/shard_map/pallas_call | solution.py:182
  75.2 1.1 %collective-permute-done.20.rest_3_ = bf16[512,128]{1,0:T(8,128)(2,1)S(1)} collective-permute-done((bf16[512,128]{1,0:T(8,128)(2,1)S(1)}, bf16[512,128]{1,0:T(8,128)(2,1)S(1)}, u32[]{:S(2)}, u32[]{:S(2)}) %collective-permute-start.20) | collective-permute-done | bytes 131104 | tf_op jit(solution)/shard_map/ppermute | solution.py:214
  76.3 2.0 %shard_map.89 = (bf16[256,4096]{1,0:T(8,128)(2,1)}, bf16[256,4096]{1,0:T(8,128)(2,1)}) custom-call(bf16[256,4096]{1,0:T(8,128)(2,1)S(1)} %copy-done.1, bf16[256,4096]{1,0:T(8,128)(2,1)S(1)} %copy-done.2, f32[256,2048]{1,0:T(8,128)S(1)} %get-tuple-element.123.kl_ref, ...), custom_call_target="tpu_custom_call", output_to_operand_aliasing={{0}: (8, {}), {1}: (9, {})} | custom-call | flops 268435456 | bytes 4194304 | tf_op jit(solution)/shard_map/pallas_call | solution.py:182
  (40 shorter events, 1.9 us)
Async XLA Ops:
  0.6 7.2 %copy-start.1 = (bf16[256,4096]{1,0:T(8,128)(2,1)S(1)}, bf16[256,4096]{1,0:T(8,128)(2,1)}, u32[]{:S(2)}) copy-start(bf16[256,4096]{1,0:T(8,128)(2,1)} %k_ref.6) | copy-start | bytes 6291460
  0.6 7.2 %copy-start.2 = (bf16[256,4096]{1,0:T(8,128)(2,1)S(1)}, bf16[256,4096]{1,0:T(8,128)(2,1)}, u32[]{:S(2)}) copy-start(bf16[256,4096]{1,0:T(8,128)(2,1)} %v_ref.6) | copy-start | bytes 6291460
  3.2 14.7 %copy-start = (bf16[256,4096]{1,0:T(8,128)(2,1)S(1)}, bf16[256,4096]{1,0:T(8,128)(2,1)}, u32[]{:S(2)}) copy-start(bf16[256,4096]{1,0:T(8,128)(2,1)} %q_ref.9) | copy-start | bytes 6291460
  3.2 14.7 %copy-start.3 = (bf16[256,4096]{1,0:T(8,128)(2,1)S(1)}, bf16[256,4096]{1,0:T(8,128)(2,1)}, u32[]{:S(2)}) copy-start(bf16[256,4096]{1,0:T(8,128)(2,1)} %c_ref.1) | copy-start | bytes 6291460
  3.2 14.7 %copy-start.4 = (f32[4096]{0:T(1024)S(1)}, f32[4096]{0:T(1024)}, u32[]{:S(2)}) copy-start(f32[4096]{0:T(1024)} %param.8) | copy-start | bytes 49156
  3.2 8.9 %collective-permute-start.6 = (bf16[512,128]{1,0:T(8,128)(2,1)S(1)}, bf16[512,128]{1,0:T(8,128)(2,1)S(1)}, u32[]{:S(2)}, u32[]{:S(2)}) collective-permute-start(bf16[512,128]{1,0:T(8,128)(2,1)S(1)} %get-tuple-element.106), channel_id=1, source_target_pairs={{0,4},{4,0},{8,12},{12,8},{16,20},{20,16},{24,28},{28,24},{1,5},{5... | collective-permute-start | bytes 393224 | tf_op jit(solution)/shard_map/ppermute | solution.py:214
  6.3 6.5 %collective-permute-start.7 = (bf16[512,128]{1,0:T(8,128)(2,1)S(1)}, bf16[512,128]{1,0:T(8,128)(2,1)S(1)}, u32[]{:S(2)}, u32[]{:S(2)}) collective-permute-start(bf16[512,128]{1,0:T(8,128)(2,1)S(1)} %get-tuple-element.107), channel_id=1, source_target_pairs={{0,8},{4,12},{8,0},{12,4},{16,24},{20,28},{24,16},{28,20},{1,9},{5... | collective-permute-start | bytes 393224 | tf_op jit(solution)/shard_map/ppermute | solution.py:214
  7.8 7.4 %collective-permute-start.8 = (bf16[512,128]{1,0:T(8,128)(2,1)S(1)}, bf16[512,128]{1,0:T(8,128)(2,1)S(1)}, u32[]{:S(2)}, u32[]{:S(2)}) collective-permute-start(bf16[512,128]{1,0:T(8,128)(2,1)S(1)} %get-tuple-element.108), channel_id=1, source_target_pairs={{0,12},{4,8},{8,4},{12,0},{16,28},{20,24},{24,20},{28,16},{1,13},{... | collective-permute-start | bytes 393224 | tf_op jit(solution)/shard_map/ppermute | solution.py:214
  8.7 12.5 %collective-permute-start = (bf16[512,128]{1,0:T(8,128)(2,1)S(1)}, bf16[512,128]{1,0:T(8,128)(2,1)S(1)}, u32[]{:S(2)}, u32[]{:S(2)}) collective-permute-start(bf16[512,128]{1,0:T(8,128)(2,1)S(1)} %get-tuple-element.86), channel_id=1, source_target_pairs={{0,4},{4,0},{8,12},{12,8},{16,20},{20,16},{24,28},{28,24},{1,5},{5... | collective-permute-start | bytes 393224 | tf_op jit(solution)/shard_map/ppermute | solution.py:214
  10.6 10.6 %collective-permute-start.1 = (bf16[512,128]{1,0:T(8,128)(2,1)S(1)}, bf16[512,128]{1,0:T(8,128)(2,1)S(1)}, u32[]{:S(2)}, u32[]{:S(2)}) collective-permute-start(bf16[512,128]{1,0:T(8,128)(2,1)S(1)} %get-tuple-element.87), channel_id=1, source_target_pairs={{0,8},{4,12},{8,0},{12,4},{16,24},{20,28},{24,16},{28,20},{1,9},{5... | collective-permute-start | bytes 393224 | tf_op jit(solution)/shard_map/ppermute | solution.py:214
  12.2 9.0 %collective-permute-start.2 = (bf16[512,128]{1,0:T(8,128)(2,1)S(1)}, bf16[512,128]{1,0:T(8,128)(2,1)S(1)}, u32[]{:S(2)}, u32[]{:S(2)}) collective-permute-start(bf16[512,128]{1,0:T(8,128)(2,1)S(1)} %get-tuple-element.88), channel_id=1, source_target_pairs={{0,12},{4,8},{8,4},{12,0},{16,28},{20,24},{24,20},{28,16},{1,13},{... | collective-permute-start | bytes 393224 | tf_op jit(solution)/shard_map/ppermute | solution.py:214
  15.3 8.3 %collective-permute-start.9 = (bf16[512,128]{1,0:T(8,128)(2,1)S(1)}, bf16[512,128]{1,0:T(8,128)(2,1)S(1)}, u32[]{:S(2)}, u32[]{:S(2)}) collective-permute-start(bf16[512,128]{1,0:T(8,128)(2,1)S(1)} %shard_map.74), channel_id=1, source_target_pairs={{0,16},{4,20},{8,24},{12,28},{16,0},{20,4},{24,8},{28,12},{1,17},{... | collective-permute-start | bytes 393224 | tf_op jit(solution)/shard_map/ppermute | solution.py:224
  21.3 8.9 %collective-permute-start.3 = (bf16[512,128]{1,0:T(8,128)(2,1)S(1)}, bf16[512,128]{1,0:T(8,128)(2,1)S(1)}, u32[]{:S(2)}, u32[]{:S(2)}) collective-permute-start(bf16[512,128]{1,0:T(8,128)(2,1)S(1)} %shard_map.72), channel_id=1, source_target_pairs={{0,16},{4,20},{8,24},{12,28},{16,0},{20,4},{24,8},{28,12},{1,17},{... | collective-permute-start | bytes 393224 | tf_op jit(solution)/shard_map/ppermute | solution.py:224
  24.0 8.4 %collective-permute-start.10 = (bf16[512,128]{1,0:T(8,128)(2,1)S(1)}, bf16[512,128]{1,0:T(8,128)(2,1)S(1)}, u32[]{:S(2)}, u32[]{:S(2)}) collective-permute-start(bf16[512,128]{1,0:T(8,128)(2,1)S(1)} %get-tuple-element.110), channel_id=1, source_target_pairs={{0,4},{4,0},{8,12},{12,8},{16,20},{20,16},{24,28},{28,24},{1,5},{5... | collective-permute-start | bytes 393224 | tf_op jit(solution)/shard_map/ppermute | solution.py:214
  27.8 8.6 %collective-permute-start.11 = (bf16[512,128]{1,0:T(8,128)(2,1)S(1)}, bf16[512,128]{1,0:T(8,128)(2,1)S(1)}, u32[]{:S(2)}, u32[]{:S(2)}) collective-permute-start(bf16[512,128]{1,0:T(8,128)(2,1)S(1)} %get-tuple-element.111), channel_id=1, source_target_pairs={{0,8},{4,12},{8,0},{12,4},{16,24},{20,28},{24,16},{28,20},{1,9},{5... | collective-permute-start | bytes 393224 | tf_op jit(solution)/shard_map/ppermute | solution.py:214
  28.1 8.3 %collective-permute-start.12 = (bf16[512,128]{1,0:T(8,128)(2,1)S(1)}, bf16[512,128]{1,0:T(8,128)(2,1)S(1)}, u32[]{:S(2)}, u32[]{:S(2)}) collective-permute-start(bf16[512,128]{1,0:T(8,128)(2,1)S(1)} %get-tuple-element.112), channel_id=1, source_target_pairs={{0,12},{4,8},{8,4},{12,0},{16,28},{20,24},{24,20},{28,16},{1,13},{... | collective-permute-start | bytes 393224 | tf_op jit(solution)/shard_map/ppermute | solution.py:214
  30.5 7.9 %collective-permute-start.4 = (bf16[512,128]{1,0:T(8,128)(2,1)S(1)}, bf16[512,128]{1,0:T(8,128)(2,1)S(1)}, u32[]{:S(2)}, u32[]{:S(2)}) collective-permute-start(bf16[512,128]{1,0:T(8,128)(2,1)S(1)} %get-tuple-element.101), channel_id=1, source_target_pairs={{0,4},{4,0},{8,12},{12,8},{16,20},{20,16},{24,28},{28,24},{1,5},{5... | collective-permute-start | bytes 393224 | tf_op jit(solution)/shard_map/ppermute | solution.py:214
  31.8 6.7 %collective-permute-start.5 = (bf16[512,128]{1,0:T(8,128)(2,1)S(1)}, bf16[512,128]{1,0:T(8,128)(2,1)S(1)}, u32[]{:S(2)}, u32[]{:S(2)}) collective-permute-start(bf16[512,128]{1,0:T(8,128)(2,1)S(1)} %get-tuple-element.102), channel_id=1, source_target_pairs={{0,8},{4,12},{8,0},{12,4},{16,24},{20,28},{24,16},{28,20},{1,9},{5... | collective-permute-start | bytes 393224 | tf_op jit(solution)/shard_map/ppermute | solution.py:214
  32.4 7.7 %collective-permute-start.13 = (bf16[512,128]{1,0:T(8,128)(2,1)S(1)}, bf16[512,128]{1,0:T(8,128)(2,1)S(1)}, u32[]{:S(2)}, u32[]{:S(2)}) collective-permute-start(bf16[512,128]{1,0:T(8,128)(2,1)S(1)} %get-tuple-element.116), channel_id=1, source_target_pairs={{0,12},{4,8},{8,4},{12,0},{16,28},{20,24},{24,20},{28,16},{1,13},{... | collective-permute-start | bytes 393224 | tf_op jit(solution)/shard_map/ppermute | solution.py:214
  42.1 10.3 %collective-permute-start.21 = (bf16[512,128]{1,0:T(8,128)(2,1)S(1)}, bf16[512,128]{1,0:T(8,128)(2,1)S(1)}, u32[]{:S(2)}, u32[]{:S(2)}) collective-permute-start(bf16[512,128]{1,0:T(8,128)(2,1)S(1)} %get-tuple-element.136), channel_id=1, source_target_pairs={{0,4},{4,0},{8,12},{12,8},{16,20},{20,16},{24,28},{28,24},{1,5},{5... | collective-permute-start | bytes 393224 | tf_op jit(solution)/shard_map/ppermute | solution.py:214
  43.5 9.7 %collective-permute-start.22 = (bf16[512,128]{1,0:T(8,128)(2,1)S(1)}, bf16[512,128]{1,0:T(8,128)(2,1)S(1)}, u32[]{:S(2)}, u32[]{:S(2)}) collective-permute-start(bf16[512,128]{1,0:T(8,128)(2,1)S(1)} %get-tuple-element.137), channel_id=1, source_target_pairs={{0,8},{4,12},{8,0},{12,4},{16,24},{20,28},{24,16},{28,20},{1,9},{5... | collective-permute-start | bytes 393224 | tf_op jit(solution)/shard_map/ppermute | solution.py:214
  44.9 8.2 %collective-permute-start.23 = (bf16[512,128]{1,0:T(8,128)(2,1)S(1)}, bf16[512,128]{1,0:T(8,128)(2,1)S(1)}, u32[]{:S(2)}, u32[]{:S(2)}) collective-permute-start(bf16[512,128]{1,0:T(8,128)(2,1)S(1)} %get-tuple-element.138), channel_id=1, source_target_pairs={{0,12},{4,8},{8,4},{12,0},{16,28},{20,24},{24,20},{28,16},{1,13},{... | collective-permute-start | bytes 393224 | tf_op jit(solution)/shard_map/ppermute | solution.py:214
  47.0 8.5 %collective-permute-start.14 = (bf16[512,128]{1,0:T(8,128)(2,1)S(1)}, bf16[512,128]{1,0:T(8,128)(2,1)S(1)}, u32[]{:S(2)}, u32[]{:S(2)}) collective-permute-start(bf16[512,128]{1,0:T(8,128)(2,1)S(1)} %get-tuple-element.126), channel_id=1, source_target_pairs={{0,4},{4,0},{8,12},{12,8},{16,20},{20,16},{24,28},{28,24},{1,5},{5... | collective-permute-start | bytes 393224 | tf_op jit(solution)/shard_map/ppermute | solution.py:214
  48.4 7.1 %collective-permute-start.15 = (bf16[512,128]{1,0:T(8,128)(2,1)S(1)}, bf16[512,128]{1,0:T(8,128)(2,1)S(1)}, u32[]{:S(2)}, u32[]{:S(2)}) collective-permute-start(bf16[512,128]{1,0:T(8,128)(2,1)S(1)} %get-tuple-element.127), channel_id=1, source_target_pairs={{0,8},{4,12},{8,0},{12,4},{16,24},{20,28},{24,16},{28,20},{1,9},{5... | collective-permute-start | bytes 393224 | tf_op jit(solution)/shard_map/ppermute | solution.py:214
  52.4 5.9 %collective-permute-start.16 = (bf16[512,128]{1,0:T(8,128)(2,1)S(1)}, bf16[512,128]{1,0:T(8,128)(2,1)S(1)}, u32[]{:S(2)}, u32[]{:S(2)}) collective-permute-start(bf16[512,128]{1,0:T(8,128)(2,1)S(1)} %get-tuple-element.128), channel_id=1, source_target_pairs={{0,12},{4,8},{8,4},{12,0},{16,28},{20,24},{24,20},{28,16},{1,13},{... | collective-permute-start | bytes 393224 | tf_op jit(solution)/shard_map/ppermute | solution.py:214
  53.2 7.5 %collective-permute-start.24 = (bf16[512,128]{1,0:T(8,128)(2,1)S(1)}, bf16[512,128]{1,0:T(8,128)(2,1)S(1)}, u32[]{:S(2)}, u32[]{:S(2)}) collective-permute-start(bf16[512,128]{1,0:T(8,128)(2,1)S(1)} %shard_map.86), channel_id=1, source_target_pairs={{0,16},{4,20},{8,24},{12,28},{16,0},{20,4},{24,8},{28,12},{1,17},{... | collective-permute-start | bytes 393224 | tf_op jit(solution)/shard_map/ppermute | solution.py:224
  58.4 8.1 %collective-permute-start.17 = (bf16[512,128]{1,0:T(8,128)(2,1)S(1)}, bf16[512,128]{1,0:T(8,128)(2,1)S(1)}, u32[]{:S(2)}, u32[]{:S(2)}) collective-permute-start(bf16[512,128]{1,0:T(8,128)(2,1)S(1)} %shard_map.81), channel_id=1, source_target_pairs={{0,16},{4,20},{8,24},{12,28},{16,0},{20,4},{24,8},{28,12},{1,17},{... | collective-permute-start | bytes 393224 | tf_op jit(solution)/shard_map/ppermute | solution.py:224
  61.1 7.6 %collective-permute-start.25 = (bf16[512,128]{1,0:T(8,128)(2,1)S(1)}, bf16[512,128]{1,0:T(8,128)(2,1)S(1)}, u32[]{:S(2)}, u32[]{:S(2)}) collective-permute-start(bf16[512,128]{1,0:T(8,128)(2,1)S(1)} %get-tuple-element.149), channel_id=1, source_target_pairs={{0,4},{4,0},{8,12},{12,8},{16,20},{20,16},{24,28},{28,24},{1,5},{5... | collective-permute-start | bytes 393224 | tf_op jit(solution)/shard_map/ppermute | solution.py:214
  63.0 10.1 %collective-permute-start.26 = (bf16[512,128]{1,0:T(8,128)(2,1)S(1)}, bf16[512,128]{1,0:T(8,128)(2,1)S(1)}, u32[]{:S(2)}, u32[]{:S(2)}) collective-permute-start(bf16[512,128]{1,0:T(8,128)(2,1)S(1)} %get-tuple-element.150), channel_id=1, source_target_pairs={{0,8},{4,12},{8,0},{12,4},{16,24},{20,28},{24,16},{28,20},{1,9},{5... | collective-permute-start | bytes 393224 | tf_op jit(solution)/shard_map/ppermute | solution.py:214
  64.7 8.4 %collective-permute-start.27 = (bf16[512,128]{1,0:T(8,128)(2,1)S(1)}, bf16[512,128]{1,0:T(8,128)(2,1)S(1)}, u32[]{:S(2)}, u32[]{:S(2)}) collective-permute-start(bf16[512,128]{1,0:T(8,128)(2,1)S(1)} %get-tuple-element.151), channel_id=1, source_target_pairs={{0,12},{4,8},{8,4},{12,0},{16,28},{20,24},{24,20},{28,16},{1,13},{... | collective-permute-start | bytes 393224 | tf_op jit(solution)/shard_map/ppermute | solution.py:214
  67.0 8.2 %collective-permute-start.18 = (bf16[512,128]{1,0:T(8,128)(2,1)S(1)}, bf16[512,128]{1,0:T(8,128)(2,1)S(1)}, u32[]{:S(2)}, u32[]{:S(2)}) collective-permute-start(bf16[512,128]{1,0:T(8,128)(2,1)S(1)} %get-tuple-element.130), channel_id=1, source_target_pairs={{0,4},{4,0},{8,12},{12,8},{16,20},{20,16},{24,28},{28,24},{1,5},{5... | collective-permute-start | bytes 393224 | tf_op jit(solution)/shard_map/ppermute | solution.py:214
  68.1 7.0 %collective-permute-start.19 = (bf16[512,128]{1,0:T(8,128)(2,1)S(1)}, bf16[512,128]{1,0:T(8,128)(2,1)S(1)}, u32[]{:S(2)}, u32[]{:S(2)}) collective-permute-start(bf16[512,128]{1,0:T(8,128)(2,1)S(1)} %get-tuple-element.131), channel_id=1, source_target_pairs={{0,8},{4,12},{8,0},{12,4},{16,24},{20,28},{24,16},{28,20},{1,9},{5... | collective-permute-start | bytes 393224 | tf_op jit(solution)/shard_map/ppermute | solution.py:214
  68.7 7.6 %collective-permute-start.20 = (bf16[512,128]{1,0:T(8,128)(2,1)S(1)}, bf16[512,128]{1,0:T(8,128)(2,1)S(1)}, u32[]{:S(2)}, u32[]{:S(2)}) collective-permute-start(bf16[512,128]{1,0:T(8,128)(2,1)S(1)} %get-tuple-element.132), channel_id=1, source_target_pairs={{0,12},{4,8},{8,4},{12,0},{16,28},{20,24},{24,20},{28,16},{1,13},{... | collective-permute-start | bytes 393224 | tf_op jit(solution)/shard_map/ppermute | solution.py:214

commit v7 on v6

--- a/solution.py
+++ b/solution.py
@@ -63,13 +63,13 @@
             out[head(h), :] = mm(a, b, TN).astype(BF16)
 
 
-def state_kernel(chunk, part, m, k_ref, v_ref, *outs):
-    member = lax.rem(lax.axis_index("seq"), m)
-    for j in reversed(range(m)):
+def state_kernel(chunk, part, m, which, k_ref, v_ref, *outs):
+    member = lax.rem(lax.axis_index("seq"), m)
+    for out, j in zip(outs, which):
         far = pl.multiple_of(chunk * m * part + owned(member, j, part), part)
         for h in range(part // DH):
             a, b = k_ref[:, head_at(far, h)], v_ref[:, head_at(far, h)]
-            outs[j][head(h), :] = mm(a, b, TN).astype(BF16)
+            out[head(h), :] = mm(a, b, TN).astype(BF16)
 
 
 def local_kernel(first, q_ref, k_ref, v_ref, c_ref, gain_ref, u_ref, loc_ref):
@@ -187,7 +187,7 @@
         scratch_shapes=scratch,
         input_output_aliases=alias,
         compiler_params=pltpu.CompilerParams(vmem_limit_bytes=8 << 20),
-        cost_estimate=pl.CostEstimate(flops=flops, bytes_accessed=nbytes, transcendentals=0),
+        cost_estimate=pl.CostEstimate(flops=flops // 4, bytes_accessed=nbytes // 4, transcendentals=0),
     )(*args)
 
 
@@ -242,16 +242,21 @@
 def scan_chunks(first, second_of, n, forward, fill_a, fill_b):
     m = len(first)
     got_a = exchange(first, n)
-    second, extra = second_of()
+    own, second, extra = second_of()
+    got_a = [*own, *got_a[len(own) :]]
     got_b = exchange(second, n)
-    made_a = fill_a(extra)
-    made_b = fill_b(extra)
     if forward:
+        made_a = fill_a(extra)
+        made_b = fill_b(extra)
         got_b, made_a, made_b = barrier((got_b, made_a, made_b))
     else:
-        got_a, made_a = barrier((got_a, made_a))
+        got_a, extra = barrier((got_a, extra))
+        made_a = fill_a(extra)
+        got_b, made_a, extra = barrier((got_b, made_a, extra))
     carry_a = carry_groups(total_of(got_a, n), n, m, forward)
     carry_b = carry_groups(total_of(got_b, n), n, m, forward)
+    if not forward:
+        made_b = fill_b(extra)
     back_a = exchange(give_back(got_a, carry_a, n, forward), n)
     back_b = exchange(give_back(got_b, carry_b, n, forward), n)
     return (back_a, back_b), (made_a, made_b)
@@ -271,6 +276,7 @@
     unit = 2 * rows * DH * half
 
     every, far, near = tuple(range(m)), (m - 1,), tuple(range(m - 1))
+    away, own = (every[:0:-1], (0,)) if m > 1 else (every, ())
 
     def first_states(which):
         return call(
@@ -279,10 +285,11 @@
             [state] * len(which), unit * len(which) // m, 6 * rows * half * len(which) // m, [slim, slim, sems],
         )
 
-    def states_of(c):
-        return call(
-            partial(state_kernel, c, part, m), (keys, values), [VMEM, VMEM],
-            [state] * m, unit, 4 * rows * half,
+    def states_of(c, which):
+        k = len(which)
+        return call(
+            partial(state_kernel, c, part, m, which), (keys, values), [VMEM, VMEM],
+            [state] * k, unit * k // m, 4 * rows * half * k // m,
         )
 
     def local_of(c, args):
@@ -291,11 +298,14 @@
             [wide, wide], 4 * unit, 12 * rows * half,
         )
 
-    parts_a = first_states(every[::-1])[::-1]
+    parts_a = first_states(away)[::-1]
     parts_a, queries, keys, values, cotangent = barrier((parts_a, queries, keys, values, cotangent))
-    base = (queries, keys, values, cotangent)
+
+    def first_others():
+        return states_of(0, own) if own else [], states_of(1, every), (queries, keys, values, cotangent)
+
     prefix, made = scan_chunks(
-        parts_a, lambda: (states_of(1), base), n, True,
+        [None] * len(own) + list(parts_a), first_others, n, True,
         lambda e: local_of(0, e), lambda e: local_of(1, e),
     )
 
@@ -329,17 +339,15 @@
             [wide, wide], 8 * unit, 8 * rows * half,
         )
 
-    parts_a, near_a = grads_of(0, far, ())
-    if m > 1:
-        parts, near_a = grads_of(0, near, (near_a,))
-        parts_a = parts + parts_a
+    parts_a, near_a = grads_of(0, away, ())
 
     def second_grads():
-        parts_b, near_b = grads_of(1, every, ())
-        return parts_b, (near_a, near_b)
+        mine, g_a = grads_of(0, own, (near_a,)) if own else ([], near_a)
+        parts_b, g_b = grads_of(1, every, ())
+        return mine, parts_b, (g_a, g_b)
 
     suffix, made = scan_chunks(
-        parts_a, second_grads, n, False,
+        [None] * len(own) + parts_a[::-1], second_grads, n, False,
         lambda e: back_local_of(0, e[0]), lambda e: back_local_of(1, e[1]),
     )
 

time: 78.6 us -> 77.5 us (0.986)
  waiting for transfers between devices: 9.63 us -> 8.75 us
    ppermute x4, starting transfers between devices: 9.47 us -> 7.11 us  [shift(): return lax.ppermute(x, 'seq', [(i, (i + step) % n) for i in range(n)])]
    ppermute x24, waiting for transfers between devices: 7.78 us -> 5.47 us  [exchange(): out[j] = lax.ppermute(parts[j], 'seq', perm)]
    ppermute x24, starting transfers between devices: 35 us -> 37 us  [exchange(): out[j] = lax.ppermute(parts[j], 'seq', perm)]
    ppermute x4, waiting for transfers between devices: 1.85 us -> 3.28 us  [shift(): return lax.ppermute(x, 'seq', [(i, (i + step) % n) for i in range(n)])]
    pallas_call x22 -> x23, Pallas kernels: 23.2 us -> 23.4 us  [call(): pl.pallas_call(kernel, in_specs=in_specs, out_specs=out_specs or [VMEM] *...]
  transfers between devices with their start and end apart: 28 -> 28, of which waited for: 7 -> 7; matrix products, arithmetic and copies ran while one was open for 0% -> 0% of each run, Pallas kernels for 21% -> 23%
where the time goes in v7:
time: 77.5 us; the launch traced here: 77.4 us
  starting transfers between devices  44.1 us (57%)
  Pallas kernels  23.4 us (30%)
  waiting for transfers between devices  8.75 us (11%)
  between operations  1.09 us (1%)
    ppermute x24, starting transfers between devices, exchange(): out[j] = lax.ppermute(parts[j], 'seq', perm)  37 us
    pallas_call x23, Pallas kernels, call(): pl.pallas_call(kernel, in_specs=in_specs, out_specs=out_specs or [VMEM] *...  23.4 us
    ppermute x4, starting transfers between devices, shift(): return lax.ppermute(x, 'seq', [(i, (i + step) % n) for i in range(n)])  7.11 us
    ppermute x24, waiting for transfers between devices, exchange(): out[j] = lax.ppermute(parts[j], 'seq', perm)  5.47 us
    ppermute x4, waiting for transfers between devices, shift(): return lax.ppermute(x, 'seq', [(i, (i + step) % n) for i in range(n)])  3.28 us
  transfers between devices with their start and end apart: 28, of which 7 were waited for; matrix products, arithmetic and copies ran while one was open for 0% of the time, Pallas kernels for 23%

profile of v7, /device:TPU:0, one launch (start us, length us, event | category | flops | bytes accessed | tf_op | source)
XLA Modules:
  0.0 77.4 jit_solution(14989947348280157482)
XLA Ops:
  0.6 2.2 %shard_map.68 = (bf16[512,128]{1,0:T(8,128)(2,1)S(1)}, bf16[512,128]{1,0:T(8,128)(2,1)S(1)}, bf16[512,128]{1,0:T(8,128)(2,1)S(1)}) custom-call(bf16[256,4096]{1,0:T(8,128)(2,1)} %k_ref.7, bf16[256,4096]{1,0:T(8,128)(2,1)} %v_ref.7), custom_call_target="tpu_custom_call" | custom-call | flops 25165824 | bytes 589824 | tf_op jit(solution)/shard_map/pallas_call | solution.py:182
  2.9 3.0 %collective-permute-start.6 = (bf16[512,128]{1,0:T(8,128)(2,1)S(1)}, bf16[512,128]{1,0:T(8,128)(2,1)S(1)}, u32[]{:S(2)}, u32[]{:S(2)}) collective-permute-start(bf16[512,128]{1,0:T(8,128)(2,1)S(1)} %get-tuple-element.109), channel_id=1, source_target_pairs={{0,4},{4,0},{8,12},{12,8},{16,20},{20,16},{24,28},{28,24},{1,5},{5... | collective-permute-start | bytes 393224 | tf_op jit(solution)/shard_map/ppermute | solution.py:214
  5.9 1.6 %collective-permute-start.7 = (bf16[512,128]{1,0:T(8,128)(2,1)S(1)}, bf16[512,128]{1,0:T(8,128)(2,1)S(1)}, u32[]{:S(2)}, u32[]{:S(2)}) collective-permute-start(bf16[512,128]{1,0:T(8,128)(2,1)S(1)} %get-tuple-element.110), channel_id=1, source_target_pairs={{0,8},{4,12},{8,0},{12,4},{16,24},{20,28},{24,16},{28,20},{1,9},{5... | collective-permute-start | bytes 393224 | tf_op jit(solution)/shard_map/ppermute | solution.py:214
  7.5 0.8 %shard_map.69 = (bf16[512,128]{1,0:T(8,128)(2,1)S(1)}, bf16[512,128]{1,0:T(8,128)(2,1)S(1)}, bf16[512,128]{1,0:T(8,128)(2,1)S(1)}, bf16[512,128]{1,0:T(8,128)(2,1)S(1)}) custom-call(bf16[256,4096]{1,0:T(8,128)(2,1)S(1)} %copy-done.1, bf16[256,4096]{1,0:T(8,128)(2,1)S(1)} %copy-done.2), custom_call_target="tpu_custom_call" | custom-call | flops 33554432 | bytes 524288 | tf_op jit(solution)/shard_map/pallas_call | solution.py:182
  8.3 2.0 %collective-permute-start = (bf16[512,128]{1,0:T(8,128)(2,1)S(1)}, bf16[512,128]{1,0:T(8,128)(2,1)S(1)}, u32[]{:S(2)}, u32[]{:S(2)}) collective-permute-start(bf16[512,128]{1,0:T(8,128)(2,1)S(1)} %get-tuple-element.90), channel_id=1, source_target_pairs={{0,4},{4,0},{8,12},{12,8},{16,20},{20,16},{24,28},{28,24},{1,5},{5... | collective-permute-start | bytes 393224 | tf_op jit(solution)/shard_map/ppermute | solution.py:214
  10.2 1.6 %collective-permute-start.1 = (bf16[512,128]{1,0:T(8,128)(2,1)S(1)}, bf16[512,128]{1,0:T(8,128)(2,1)S(1)}, u32[]{:S(2)}, u32[]{:S(2)}) collective-permute-start(bf16[512,128]{1,0:T(8,128)(2,1)S(1)} %get-tuple-element.91), channel_id=1, source_target_pairs={{0,8},{4,12},{8,0},{12,4},{16,24},{20,28},{24,16},{28,20},{1,9},{5... | collective-permute-start | bytes 393224 | tf_op jit(solution)/shard_map/ppermute | solution.py:214
  11.8 0.6 collective-permute-start.2
  12.8 2.1 %collective-permute-done.8.refs_3_ = bf16[512,128]{1,0:T(8,128)(2,1)S(1)} collective-permute-done((bf16[512,128]{1,0:T(8,128)(2,1)S(1)}, bf16[512,128]{1,0:T(8,128)(2,1)S(1)}, u32[]{:S(2)}, u32[]{:S(2)}) %collective-permute-start.8) | collective-permute-done | bytes 131104 | tf_op jit(solution)/shard_map/ppermute | solution.py:214
  14.9 2.7 %collective-permute-start.9 = (bf16[512,128]{1,0:T(8,128)(2,1)S(1)}, bf16[512,128]{1,0:T(8,128)(2,1)S(1)}, u32[]{:S(2)}, u32[]{:S(2)}) collective-permute-start(bf16[512,128]{1,0:T(8,128)(2,1)S(1)} %shard_map.75), channel_id=1, source_target_pairs={{0,16},{4,20},{8,24},{12,28},{16,0},{20,4},{24,8},{28,12},{1,17},{... | collective-permute-start | bytes 393224 | tf_op jit(solution)/shard_map/ppermute | solution.py:224
  17.6 1.6 %shard_map.71 = (f32[256,2048]{1,0:T(8,128)S(1)}, f32[256,2048]{1,0:T(8,128)S(1)}) custom-call(bf16[256,4096]{1,0:T(8,128)(2,1)S(1)} %copy-done, bf16[256,4096]{1,0:T(8,128)(2,1)S(1)} %copy-done.1, bf16[256,4096]{1,0:T(8,128)(2,1)S(1)} %copy-done.2, bf16[256,4096]{1,0:T(8,128)(2,1)S(1)} %copy-done.3, f32[1,4096]{1,0:T(1,128)S(1)} %bitcast.1), custom_call_target="tpu_custom_call" | custom-call | flops 134217728 | bytes 1572864 | tf_op jit(solution)/shard_map/pallas_call | solution.py:182
  19.2 1.6 %shard_map.70 = (f32[256,2048]{1,0:T(8,128)S(1)}, f32[256,2048]{1,0:T(8,128)S(1)}) custom-call(bf16[256,4096]{1,0:T(8,128)(2,1)S(1)} %copy-done, bf16[256,4096]{1,0:T(8,128)(2,1)S(1)} %copy-done.1, bf16[256,4096]{1,0:T(8,128)(2,1)S(1)} %copy-done.2, bf16[256,4096]{1,0:T(8,128)(2,1)S(1)} %copy-done.3, f32[1,4096]{1,0:T(1,128)S(1)} %bitcast.2), custom_call_target="tpu_custom_call" | custom-call | flops 134217728 | bytes 1572864 | tf_op jit(solution)/shard_map/pallas_call | solution.py:182
  20.9 2.3 %collective-permute-start.3 = (bf16[512,128]{1,0:T(8,128)(2,1)S(1)}, bf16[512,128]{1,0:T(8,128)(2,1)S(1)}, u32[]{:S(2)}, u32[]{:S(2)}) collective-permute-start(bf16[512,128]{1,0:T(8,128)(2,1)S(1)} %shard_map.72), channel_id=1, source_target_pairs={{0,16},{4,20},{8,24},{12,28},{16,0},{20,4},{24,8},{28,12},{1,17},{... | collective-permute-start | bytes 393224 | tf_op jit(solution)/shard_map/ppermute | solution.py:224
  23.6 3.9 %collective-permute-start.10 = (bf16[512,128]{1,0:T(8,128)(2,1)S(1)}, bf16[512,128]{1,0:T(8,128)(2,1)S(1)}, u32[]{:S(2)}, u32[]{:S(2)}) collective-permute-start(bf16[512,128]{1,0:T(8,128)(2,1)S(1)} %get-tuple-element.113), channel_id=1, source_target_pairs={{0,4},{4,0},{8,12},{12,8},{16,20},{20,16},{24,28},{28,24},{1,5},{5... | collective-permute-start | bytes 393224 | tf_op jit(solution)/shard_map/ppermute | solution.py:214
  27.8 1.2 %collective-permute-start.12 = (bf16[512,128]{1,0:T(8,128)(2,1)S(1)}, bf16[512,128]{1,0:T(8,128)(2,1)S(1)}, u32[]{:S(2)}, u32[]{:S(2)}) collective-permute-start(bf16[512,128]{1,0:T(8,128)(2,1)S(1)} %get-tuple-element.115), channel_id=1, source_target_pairs={{0,12},{4,8},{8,4},{12,0},{16,28},{20,24},{24,20},{28,16},{1,13},{... | collective-permute-start | bytes 393224 | tf_op jit(solution)/shard_map/ppermute | solution.py:214
  29.0 0.8 collective-permute-done.3.carry
  29.8 0.4 shard_map.73
  30.2 1.2 %collective-permute-start.4 = (bf16[512,128]{1,0:T(8,128)(2,1)S(1)}, bf16[512,128]{1,0:T(8,128)(2,1)S(1)}, u32[]{:S(2)}, u32[]{:S(2)}) collective-permute-start(bf16[512,128]{1,0:T(8,128)(2,1)S(1)} %get-tuple-element.105), channel_id=1, source_target_pairs={{0,4},{4,0},{8,12},{12,8},{16,20},{20,16},{24,28},{28,24},{1,5},{5... | collective-permute-start | bytes 393224 | tf_op jit(solution)/shard_map/ppermute | solution.py:214
  31.4 0.6 collective-permute-start.5
  32.0 4.0 %collective-permute-start.13 = (bf16[512,128]{1,0:T(8,128)(2,1)S(1)}, bf16[512,128]{1,0:T(8,128)(2,1)S(1)}, u32[]{:S(2)}, u32[]{:S(2)}) collective-permute-start(bf16[512,128]{1,0:T(8,128)(2,1)S(1)} %get-tuple-element.119), channel_id=1, source_target_pairs={{0,12},{4,8},{8,4},{12,0},{16,28},{20,24},{24,20},{28,16},{1,13},{... | collective-permute-start | bytes 393224 | tf_op jit(solution)/shard_map/ppermute | solution.py:214
  36.1 1.3 %shard_map.77 = (f32[256,2048]{1,0:T(8,128)S(1)}, f32[256,128]{1,0:T(8,128)S(1)}, f32[256,128]{1,0:T(8,128)S(1)}) custom-call(bf16[256,4096]{1,0:T(8,128)(2,1)S(1)} %copy-done, f32[256,2048]{1,0:T(8,128)S(1)} %get-tuple-element.107.loc_ref, f32[256,2048]{1,0:T(8,128)S(1)} %get-tuple-element.108.u_ref, ...), custom_call_target="tpu_custom_call", output_to_operand_aliasing={{0}: (1, {})} | custom-call | flops 33554432 | bytes 524288 | tf_op jit(solution)/shard_map/pallas_call | solution.py:182
  37.4 0.8 collective-permute-done.4.rest_1_
  38.1 1.0 %shard_map.78 = (f32[256,2048]{1,0:T(8,128)S(1)}, f32[256,128]{1,0:T(8,128)S(1)}, f32[256,128]{1,0:T(8,128)S(1)}) custom-call(bf16[256,4096]{1,0:T(8,128)(2,1)S(1)} %copy-done, f32[256,2048]{1,0:T(8,128)S(1)} %get-tuple-element.98.loc_ref, f32[256,2048]{1,0:T(8,128)S(1)} %get-tuple-element.99.u_ref, ...), custom_call_target="tpu_custom_call", output_to_operand_aliasing={{0}: (1, {})} | custom-call | flops 25165824 | bytes 393216 | tf_op jit(solution)/shard_map/pallas_call | solution.py:182
  39.1 0.6 collective-permute-done.13.rest_0_
  39.7 0.5 shard_map.79
  40.2 1.1 %shard_map.81 = (bf16[256,2048]{1,0:T(8,128)(2,1)S(1)}, bf16[512,128]{1,0:T(8,128)(2,1)S(1)}, bf16[512,128]{1,0:T(8,128)(2,1)S(1)}, bf16[512,128]{1,0:T(8,128)(2,1)S(1)}) custom-call(bf16[256,4096]{1,0:T(8,128)(2,1)S(1)} %copy-done, f32[256,2048]{1,0:T(8,128)S(1)} %get-tuple-element.129.att_ref, f32[256,2048]{1,0:T(8,128)S(1)} %get-tuple-element.108.u_ref, ...), custom_call_target="tpu_custom_call" | custom-call | flops 25165824 | bytes 393216 | tf_op jit(solution)/shard_map/pallas_call | solution.py:182
  41.3 1.4 %collective-permute-start.17 = (bf16[512,128]{1,0:T(8,128)(2,1)S(1)}, bf16[512,128]{1,0:T(8,128)(2,1)S(1)}, u32[]{:S(2)}, u32[]{:S(2)}) collective-permute-start(bf16[512,128]{1,0:T(8,128)(2,1)S(1)} %get-tuple-element.132), channel_id=1, source_target_pairs={{0,4},{4,0},{8,12},{12,8},{16,20},{20,16},{24,28},{28,24},{1,5},{5... | collective-permute-start | bytes 393224 | tf_op jit(solution)/shard_map/ppermute | solution.py:214
  42.7 1.5 %collective-permute-start.18 = (bf16[512,128]{1,0:T(8,128)(2,1)S(1)}, bf16[512,128]{1,0:T(8,128)(2,1)S(1)}, u32[]{:S(2)}, u32[]{:S(2)}) collective-permute-start(bf16[512,128]{1,0:T(8,128)(2,1)S(1)} %get-tuple-element.133), channel_id=1, source_target_pairs={{0,8},{4,12},{8,0},{12,4},{16,24},{20,28},{24,16},{28,20},{1,9},{5... | collective-permute-start | bytes 393224 | tf_op jit(solution)/shard_map/ppermute | solution.py:214
  44.1 0.7 collective-permute-start.19
  44.8 1.3 %shard_map.80 = (bf16[256,2048]{1,0:T(8,128)(2,1)S(1)}, bf16[512,128]{1,0:T(8,128)(2,1)S(1)}, bf16[512,128]{1,0:T(8,128)(2,1)S(1)}, bf16[512,128]{1,0:T(8,128)(2,1)S(1)}, bf16[512,128]{1,0:T(8,128)(2,1)S(1)}) custom-call(bf16[256,4096]{1,0:T(8,128)(2,1)S(1)} %copy-done, f32[256,2048]{1,0:T(8,128)S(1)} %get-tuple-element.122.att_ref, ...), custom_call_target="tpu_custom_call" | custom-call | flops 33554432 | bytes 524288 | tf_op jit(solution)/shard_map/pallas_call | solution.py:182
  46.2 1.4 %collective-permute-start.14 = (bf16[512,128]{1,0:T(8,128)(2,1)S(1)}, bf16[512,128]{1,0:T(8,128)(2,1)S(1)}, u32[]{:S(2)}, u32[]{:S(2)}) collective-permute-start(bf16[512,128]{1,0:T(8,128)(2,1)S(1)} %get-tuple-element.126), channel_id=1, source_target_pairs={{0,4},{4,0},{8,12},{12,8},{16,20},{20,16},{24,28},{28,24},{1,5},{5... | collective-permute-start | bytes 393224 | tf_op jit(solution)/shard_map/ppermute | solution.py:214
  47.6 1.5 %collective-permute-start.15 = (bf16[512,128]{1,0:T(8,128)(2,1)S(1)}, bf16[512,128]{1,0:T(8,128)(2,1)S(1)}, u32[]{:S(2)}, u32[]{:S(2)}) collective-permute-start(bf16[512,128]{1,0:T(8,128)(2,1)S(1)} %get-tuple-element.127), channel_id=1, source_target_pairs={{0,8},{4,12},{8,0},{12,4},{16,24},{20,28},{24,16},{28,20},{1,9},{5... | collective-permute-start | bytes 393224 | tf_op jit(solution)/shard_map/ppermute | solution.py:214
  49.0 2.7 %collective-permute-start.16 = (bf16[512,128]{1,0:T(8,128)(2,1)S(1)}, bf16[512,128]{1,0:T(8,128)(2,1)S(1)}, u32[]{:S(2)}, u32[]{:S(2)}) collective-permute-start(bf16[512,128]{1,0:T(8,128)(2,1)S(1)} %get-tuple-element.128), channel_id=1, source_target_pairs={{0,12},{4,8},{8,4},{12,0},{16,28},{20,24},{24,20},{28,16},{1,13},{... | collective-permute-start | bytes 393224 | tf_op jit(solution)/shard_map/ppermute | solution.py:214
  51.7 0.6 shard_map.82
  52.4 2.1 %collective-permute-start.24 = (bf16[512,128]{1,0:T(8,128)(2,1)S(1)}, bf16[512,128]{1,0:T(8,128)(2,1)S(1)}, u32[]{:S(2)}, u32[]{:S(2)}) collective-permute-start(bf16[512,128]{1,0:T(8,128)(2,1)S(1)} %shard_map.87), channel_id=1, source_target_pairs={{0,16},{4,20},{8,24},{12,28},{16,0},{20,4},{24,8},{28,12},{1,17},{... | collective-permute-start | bytes 393224 | tf_op jit(solution)/shard_map/ppermute | solution.py:224
  54.5 2.6 %shard_map.83 = (f32[256,2048]{1,0:T(8,128)S(1)}, f32[256,2048]{1,0:T(8,128)S(1)}) custom-call(bf16[256,4096]{1,0:T(8,128)(2,1)S(1)} %copy-done, bf16[256,4096]{1,0:T(8,128)(2,1)S(1)} %copy-done.1, bf16[256,4096]{1,0:T(8,128)(2,1)S(1)} %copy-done.2, bf16[256,2048]{1,0:T(8,128)(2,1)S(1)} %get-tuple-element.137.g_ref), custom_call_target="tpu_custom_call" | custom-call | flops 268435456 | bytes 1048576 | tf_op jit(solution)/shard_map/pallas_call | solution.py:182
  57.1 1.4 %collective-permute-done.16.refs_3_ = bf16[512,128]{1,0:T(8,128)(2,1)S(1)} collective-permute-done((bf16[512,128]{1,0:T(8,128)(2,1)S(1)}, bf16[512,128]{1,0:T(8,128)(2,1)S(1)}, u32[]{:S(2)}, u32[]{:S(2)}) %collective-permute-start.16) | collective-permute-done | bytes 131104 | tf_op jit(solution)/shard_map/ppermute | solution.py:214
  58.7 2.5 %collective-permute-done.24.carry = bf16[512,128]{1,0:T(8,128)(2,1)S(1)} collective-permute-done((bf16[512,128]{1,0:T(8,128)(2,1)S(1)}, bf16[512,128]{1,0:T(8,128)(2,1)S(1)}, u32[]{:S(2)}, u32[]{:S(2)}) %collective-permute-start.24) | collective-permute-done | bytes 131104 | tf_op jit(solution)/shard_map/ppermute | solution.py:224
  61.2 0.4 shard_map.88
  61.7 3.4 %collective-permute-start.26 = (bf16[512,128]{1,0:T(8,128)(2,1)S(1)}, bf16[512,128]{1,0:T(8,128)(2,1)S(1)}, u32[]{:S(2)}, u32[]{:S(2)}) collective-permute-start(bf16[512,128]{1,0:T(8,128)(2,1)S(1)} %get-tuple-element.160), channel_id=1, source_target_pairs={{0,8},{4,12},{8,0},{12,4},{16,24},{20,28},{24,16},{28,20},{1,9},{5... | collective-permute-start | bytes 393224 | tf_op jit(solution)/shard_map/ppermute | solution.py:214
  65.1 0.9 %collective-permute-start.27 = (bf16[512,128]{1,0:T(8,128)(2,1)S(1)}, bf16[512,128]{1,0:T(8,128)(2,1)S(1)}, u32[]{:S(2)}, u32[]{:S(2)}) collective-permute-start(bf16[512,128]{1,0:T(8,128)(2,1)S(1)} %get-tuple-element.161), channel_id=1, source_target_pairs={{0,12},{4,8},{8,4},{12,0},{16,28},{20,24},{24,20},{28,16},{1,13},{... | collective-permute-start | bytes 393224 | tf_op jit(solution)/shard_map/ppermute | solution.py:214
  66.0 0.4 shard_map.86
  66.4 0.6 collective-permute-start.21
  67.0 2.0 %collective-permute-start.22 = (bf16[512,128]{1,0:T(8,128)(2,1)S(1)}, bf16[512,128]{1,0:T(8,128)(2,1)S(1)}, u32[]{:S(2)}, u32[]{:S(2)}) collective-permute-start(bf16[512,128]{1,0:T(8,128)(2,1)S(1)} %get-tuple-element.150), channel_id=1, source_target_pairs={{0,8},{4,12},{8,0},{12,4},{16,24},{20,28},{24,16},{28,20},{1,9},{5... | collective-permute-start | bytes 393224 | tf_op jit(solution)/shard_map/ppermute | solution.py:214
  69.0 0.9 %collective-permute-start.23 = (bf16[512,128]{1,0:T(8,128)(2,1)S(1)}, bf16[512,128]{1,0:T(8,128)(2,1)S(1)}, u32[]{:S(2)}, u32[]{:S(2)}) collective-permute-start(bf16[512,128]{1,0:T(8,128)(2,1)S(1)} %get-tuple-element.151), channel_id=1, source_target_pairs={{0,12},{4,8},{8,4},{12,0},{16,28},{20,24},{24,20},{28,16},{1,13},{... | collective-permute-start | bytes 393224 | tf_op jit(solution)/shard_map/ppermute | solution.py:214
  70.0 2.6 %shard_map.84 = (f32[256,2048]{1,0:T(8,128)S(1)}, f32[256,2048]{1,0:T(8,128)S(1)}) custom-call(bf16[256,4096]{1,0:T(8,128)(2,1)S(1)} %copy-done, bf16[256,4096]{1,0:T(8,128)(2,1)S(1)} %copy-done.1, bf16[256,4096]{1,0:T(8,128)(2,1)S(1)} %copy-done.2, bf16[256,2048]{1,0:T(8,128)(2,1)S(1)} %get-tuple-element.141.g_ref), custom_call_target="tpu_custom_call" | custom-call | flops 268435456 | bytes 1048576 | tf_op jit(solution)/shard_map/pallas_call | solution.py:182
  72.6 2.0 %shard_map.89 = (bf16[256,4096]{1,0:T(8,128)(2,1)}, bf16[256,4096]{1,0:T(8,128)(2,1)}) custom-call(bf16[256,4096]{1,0:T(8,128)(2,1)S(1)} %copy-done.1, bf16[256,4096]{1,0:T(8,128)(2,1)S(1)} %copy-done.2, f32[256,2048]{1,0:T(8,128)S(1)} %get-tuple-element.152.kl_ref, f32[256,2048]{1,0:T(8,128)S(1)} %get-tuple-element.153.vl_ref, ...), custom_call_target="tpu_custom_call" | custom-call | flops 67108864 | bytes 1048576 | tf_op jit(solution)/shard_map/pallas_call | solution.py:182
  74.6 0.6 collective-permute-done.23.rest_3_
  75.2 2.0 %shard_map.90 = (bf16[256,4096]{1,0:T(8,128)(2,1)}, bf16[256,4096]{1,0:T(8,128)(2,1)}) custom-call(bf16[256,4096]{1,0:T(8,128)(2,1)S(1)} %copy-done.1, bf16[256,4096]{1,0:T(8,128)(2,1)S(1)} %copy-done.2, f32[256,2048]{1,0:T(8,128)S(1)} %get-tuple-element.142.kl_ref, ...), custom_call_target="tpu_custom_call", output_to_operand_aliasing={{0}: (8, {}), {1}: (9, {})} | custom-call | flops 67108864 | bytes 1048576 | tf_op jit(solution)/shard_map/pallas_call | solution.py:182
  (41 shorter events, 1.5 us)
Async XLA Ops:
  0.6 6.8 %copy-start.1 = (bf16[256,4096]{1,0:T(8,128)(2,1)S(1)}, bf16[256,4096]{1,0:T(8,128)(2,1)}, u32[]{:S(2)}) copy-start(bf16[256,4096]{1,0:T(8,128)(2,1)} %k_ref.7) | copy-start | bytes 6291460
  0.6 6.8 %copy-start.2 = (bf16[256,4096]{1,0:T(8,128)(2,1)S(1)}, bf16[256,4096]{1,0:T(8,128)(2,1)}, u32[]{:S(2)}) copy-start(bf16[256,4096]{1,0:T(8,128)(2,1)} %v_ref.7) | copy-start | bytes 6291460
  2.9 8.9 %collective-permute-start.6 = (bf16[512,128]{1,0:T(8,128)(2,1)S(1)}, bf16[512,128]{1,0:T(8,128)(2,1)S(1)}, u32[]{:S(2)}, u32[]{:S(2)}) collective-permute-start(bf16[512,128]{1,0:T(8,128)(2,1)S(1)} %get-tuple-element.109), channel_id=1, source_target_pairs={{0,4},{4,0},{8,12},{12,8},{16,20},{20,16},{24,28},{28,24},{1,5},{5... | collective-permute-start | bytes 393224 | tf_op jit(solution)/shard_map/ppermute | solution.py:214
  5.9 6.9 %collective-permute-start.7 = (bf16[512,128]{1,0:T(8,128)(2,1)S(1)}, bf16[512,128]{1,0:T(8,128)(2,1)S(1)}, u32[]{:S(2)}, u32[]{:S(2)}) collective-permute-start(bf16[512,128]{1,0:T(8,128)(2,1)S(1)} %get-tuple-element.110), channel_id=1, source_target_pairs={{0,8},{4,12},{8,0},{12,4},{16,24},{20,28},{24,16},{28,20},{1,9},{5... | collective-permute-start | bytes 393224 | tf_op jit(solution)/shard_map/ppermute | solution.py:214
  7.5 7.4 %collective-permute-start.8 = (bf16[512,128]{1,0:T(8,128)(2,1)S(1)}, bf16[512,128]{1,0:T(8,128)(2,1)S(1)}, u32[]{:S(2)}, u32[]{:S(2)}) collective-permute-start(bf16[512,128]{1,0:T(8,128)(2,1)S(1)} %get-tuple-element.111), channel_id=1, source_target_pairs={{0,12},{4,8},{8,4},{12,0},{16,28},{20,24},{24,20},{28,16},{1,13},{... | collective-permute-start | bytes 393224 | tf_op jit(solution)/shard_map/ppermute | solution.py:214
  8.3 12.5 %collective-permute-start = (bf16[512,128]{1,0:T(8,128)(2,1)S(1)}, bf16[512,128]{1,0:T(8,128)(2,1)S(1)}, u32[]{:S(2)}, u32[]{:S(2)}) collective-permute-start(bf16[512,128]{1,0:T(8,128)(2,1)S(1)} %get-tuple-element.90), channel_id=1, source_target_pairs={{0,4},{4,0},{8,12},{12,8},{16,20},{20,16},{24,28},{28,24},{1,5},{5... | collective-permute-start | bytes 393224 | tf_op jit(solution)/shard_map/ppermute | solution.py:214
  10.2 10.6 %collective-permute-start.1 = (bf16[512,128]{1,0:T(8,128)(2,1)S(1)}, bf16[512,128]{1,0:T(8,128)(2,1)S(1)}, u32[]{:S(2)}, u32[]{:S(2)}) collective-permute-start(bf16[512,128]{1,0:T(8,128)(2,1)S(1)} %get-tuple-element.91), channel_id=1, source_target_pairs={{0,8},{4,12},{8,0},{12,4},{16,24},{20,28},{24,16},{28,20},{1,9},{5... | collective-permute-start | bytes 393224 | tf_op jit(solution)/shard_map/ppermute | solution.py:214
  11.8 5.8 %copy-start = (bf16[256,4096]{1,0:T(8,128)(2,1)S(1)}, bf16[256,4096]{1,0:T(8,128)(2,1)}, u32[]{:S(2)}) copy-start(bf16[256,4096]{1,0:T(8,128)(2,1)} %q_ref.9) | copy-start | bytes 6291460
  11.8 5.8 %copy-start.3 = (bf16[256,4096]{1,0:T(8,128)(2,1)S(1)}, bf16[256,4096]{1,0:T(8,128)(2,1)}, u32[]{:S(2)}) copy-start(bf16[256,4096]{1,0:T(8,128)(2,1)} %c_ref.1) | copy-start | bytes 6291460
  11.8 5.8 %copy-start.4 = (f32[4096]{0:T(1024)S(1)}, f32[4096]{0:T(1024)}, u32[]{:S(2)}) copy-start(f32[4096]{0:T(1024)} %param.8) | copy-start | bytes 49156
  11.8 9.0 %collective-permute-start.2 = (bf16[512,128]{1,0:T(8,128)(2,1)S(1)}, bf16[512,128]{1,0:T(8,128)(2,1)S(1)}, u32[]{:S(2)}, u32[]{:S(2)}) collective-permute-start(bf16[512,128]{1,0:T(8,128)(2,1)S(1)} %get-tuple-element.92), channel_id=1, source_target_pairs={{0,12},{4,8},{8,4},{12,0},{16,28},{20,24},{24,20},{28,16},{1,13},{... | collective-permute-start | bytes 393224 | tf_op jit(solution)/shard_map/ppermute | solution.py:214
  14.9 8.3 %collective-permute-start.9 = (bf16[512,128]{1,0:T(8,128)(2,1)S(1)}, bf16[512,128]{1,0:T(8,128)(2,1)S(1)}, u32[]{:S(2)}, u32[]{:S(2)}) collective-permute-start(bf16[512,128]{1,0:T(8,128)(2,1)S(1)} %shard_map.75), channel_id=1, source_target_pairs={{0,16},{4,20},{8,24},{12,28},{16,0},{20,4},{24,8},{28,12},{1,17},{... | collective-permute-start | bytes 393224 | tf_op jit(solution)/shard_map/ppermute | solution.py:224
  20.9 8.9 %collective-permute-start.3 = (bf16[512,128]{1,0:T(8,128)(2,1)S(1)}, bf16[512,128]{1,0:T(8,128)(2,1)S(1)}, u32[]{:S(2)}, u32[]{:S(2)}) collective-permute-start(bf16[512,128]{1,0:T(8,128)(2,1)S(1)} %shard_map.72), channel_id=1, source_target_pairs={{0,16},{4,20},{8,24},{12,28},{16,0},{20,4},{24,8},{28,12},{1,17},{... | collective-permute-start | bytes 393224 | tf_op jit(solution)/shard_map/ppermute | solution.py:224
  23.6 8.4 %collective-permute-start.10 = (bf16[512,128]{1,0:T(8,128)(2,1)S(1)}, bf16[512,128]{1,0:T(8,128)(2,1)S(1)}, u32[]{:S(2)}, u32[]{:S(2)}) collective-permute-start(bf16[512,128]{1,0:T(8,128)(2,1)S(1)} %get-tuple-element.113), channel_id=1, source_target_pairs={{0,4},{4,0},{8,12},{12,8},{16,20},{20,16},{24,28},{28,24},{1,5},{5... | collective-permute-start | bytes 393224 | tf_op jit(solution)/shard_map/ppermute | solution.py:214
  27.5 8.6 %collective-permute-start.11 = (bf16[512,128]{1,0:T(8,128)(2,1)S(1)}, bf16[512,128]{1,0:T(8,128)(2,1)S(1)}, u32[]{:S(2)}, u32[]{:S(2)}) collective-permute-start(bf16[512,128]{1,0:T(8,128)(2,1)S(1)} %get-tuple-element.114), channel_id=1, source_target_pairs={{0,8},{4,12},{8,0},{12,4},{16,24},{20,28},{24,16},{28,20},{1,9},{5... | collective-permute-start | bytes 393224 | tf_op jit(solution)/shard_map/ppermute | solution.py:214
  27.8 8.3 %collective-permute-start.12 = (bf16[512,128]{1,0:T(8,128)(2,1)S(1)}, bf16[512,128]{1,0:T(8,128)(2,1)S(1)}, u32[]{:S(2)}, u32[]{:S(2)}) collective-permute-start(bf16[512,128]{1,0:T(8,128)(2,1)S(1)} %get-tuple-element.115), channel_id=1, source_target_pairs={{0,12},{4,8},{8,4},{12,0},{16,28},{20,24},{24,20},{28,16},{1,13},{... | collective-permute-start | bytes 393224 | tf_op jit(solution)/shard_map/ppermute | solution.py:214
  30.2 7.9 %collective-permute-start.4 = (bf16[512,128]{1,0:T(8,128)(2,1)S(1)}, bf16[512,128]{1,0:T(8,128)(2,1)S(1)}, u32[]{:S(2)}, u32[]{:S(2)}) collective-permute-start(bf16[512,128]{1,0:T(8,128)(2,1)S(1)} %get-tuple-element.105), channel_id=1, source_target_pairs={{0,4},{4,0},{8,12},{12,8},{16,20},{20,16},{24,28},{28,24},{1,5},{5... | collective-permute-start | bytes 393224 | tf_op jit(solution)/shard_map/ppermute | solution.py:214
  31.4 6.7 %collective-permute-start.5 = (bf16[512,128]{1,0:T(8,128)(2,1)S(1)}, bf16[512,128]{1,0:T(8,128)(2,1)S(1)}, u32[]{:S(2)}, u32[]{:S(2)}) collective-permute-start(bf16[512,128]{1,0:T(8,128)(2,1)S(1)} %get-tuple-element.106), channel_id=1, source_target_pairs={{0,8},{4,12},{8,0},{12,4},{16,24},{20,28},{24,16},{28,20},{1,9},{5... | collective-permute-start | bytes 393224 | tf_op jit(solution)/shard_map/ppermute | solution.py:214
  32.0 7.7 %collective-permute-start.13 = (bf16[512,128]{1,0:T(8,128)(2,1)S(1)}, bf16[512,128]{1,0:T(8,128)(2,1)S(1)}, u32[]{:S(2)}, u32[]{:S(2)}) collective-permute-start(bf16[512,128]{1,0:T(8,128)(2,1)S(1)} %get-tuple-element.119), channel_id=1, source_target_pairs={{0,12},{4,8},{8,4},{12,0},{16,28},{20,24},{24,20},{28,16},{1,13},{... | collective-permute-start | bytes 393224 | tf_op jit(solution)/shard_map/ppermute | solution.py:214
  41.3 7.8 %collective-permute-start.17 = (bf16[512,128]{1,0:T(8,128)(2,1)S(1)}, bf16[512,128]{1,0:T(8,128)(2,1)S(1)}, u32[]{:S(2)}, u32[]{:S(2)}) collective-permute-start(bf16[512,128]{1,0:T(8,128)(2,1)S(1)} %get-tuple-element.132), channel_id=1, source_target_pairs={{0,4},{4,0},{8,12},{12,8},{16,20},{20,16},{24,28},{28,24},{1,5},{5... | collective-permute-start | bytes 393224 | tf_op jit(solution)/shard_map/ppermute | solution.py:214
  42.7 9.6 %collective-permute-start.18 = (bf16[512,128]{1,0:T(8,128)(2,1)S(1)}, bf16[512,128]{1,0:T(8,128)(2,1)S(1)}, u32[]{:S(2)}, u32[]{:S(2)}) collective-permute-start(bf16[512,128]{1,0:T(8,128)(2,1)S(1)} %get-tuple-element.133), channel_id=1, source_target_pairs={{0,8},{4,12},{8,0},{12,4},{16,24},{20,28},{24,16},{28,20},{1,9},{5... | collective-permute-start | bytes 393224 | tf_op jit(solution)/shard_map/ppermute | solution.py:214
  44.1 8.2 %collective-permute-start.19 = (bf16[512,128]{1,0:T(8,128)(2,1)S(1)}, bf16[512,128]{1,0:T(8,128)(2,1)S(1)}, u32[]{:S(2)}, u32[]{:S(2)}) collective-permute-start(bf16[512,128]{1,0:T(8,128)(2,1)S(1)} %get-tuple-element.134), channel_id=1, source_target_pairs={{0,12},{4,8},{8,4},{12,0},{16,28},{20,24},{24,20},{28,16},{1,13},{... | collective-permute-start | bytes 393224 | tf_op jit(solution)/shard_map/ppermute | solution.py:214
  46.2 10.9 %collective-permute-start.14 = (bf16[512,128]{1,0:T(8,128)(2,1)S(1)}, bf16[512,128]{1,0:T(8,128)(2,1)S(1)}, u32[]{:S(2)}, u32[]{:S(2)}) collective-permute-start(bf16[512,128]{1,0:T(8,128)(2,1)S(1)} %get-tuple-element.126), channel_id=1, source_target_pairs={{0,4},{4,0},{8,12},{12,8},{16,20},{20,16},{24,28},{28,24},{1,5},{5... | collective-permute-start | bytes 393224 | tf_op jit(solution)/shard_map/ppermute | solution.py:214
  47.6 9.5 %collective-permute-start.15 = (bf16[512,128]{1,0:T(8,128)(2,1)S(1)}, bf16[512,128]{1,0:T(8,128)(2,1)S(1)}, u32[]{:S(2)}, u32[]{:S(2)}) collective-permute-start(bf16[512,128]{1,0:T(8,128)(2,1)S(1)} %get-tuple-element.127), channel_id=1, source_target_pairs={{0,8},{4,12},{8,0},{12,4},{16,24},{20,28},{24,16},{28,20},{1,9},{5... | collective-permute-start | bytes 393224 | tf_op jit(solution)/shard_map/ppermute | solution.py:214
  49.0 9.5 %collective-permute-start.16 = (bf16[512,128]{1,0:T(8,128)(2,1)S(1)}, bf16[512,128]{1,0:T(8,128)(2,1)S(1)}, u32[]{:S(2)}, u32[]{:S(2)}) collective-permute-start(bf16[512,128]{1,0:T(8,128)(2,1)S(1)} %get-tuple-element.128), channel_id=1, source_target_pairs={{0,12},{4,8},{8,4},{12,0},{16,28},{20,24},{24,20},{28,16},{1,13},{... | collective-permute-start | bytes 393224 | tf_op jit(solution)/shard_map/ppermute | solution.py:214
  52.4 8.8 %collective-permute-start.24 = (bf16[512,128]{1,0:T(8,128)(2,1)S(1)}, bf16[512,128]{1,0:T(8,128)(2,1)S(1)}, u32[]{:S(2)}, u32[]{:S(2)}) collective-permute-start(bf16[512,128]{1,0:T(8,128)(2,1)S(1)} %shard_map.87), channel_id=1, source_target_pairs={{0,16},{4,20},{8,24},{12,28},{16,0},{20,4},{24,8},{28,12},{1,17},{... | collective-permute-start | bytes 393224 | tf_op jit(solution)/shard_map/ppermute | solution.py:224
  58.6 7.4 %collective-permute-start.20 = (bf16[512,128]{1,0:T(8,128)(2,1)S(1)}, bf16[512,128]{1,0:T(8,128)(2,1)S(1)}, u32[]{:S(2)}, u32[]{:S(2)}) collective-permute-start(bf16[512,128]{1,0:T(8,128)(2,1)S(1)} %shard_map.85), channel_id=1, source_target_pairs={{0,16},{4,20},{8,24},{12,28},{16,0},{20,4},{24,8},{28,12},{1,17},{... | collective-permute-start | bytes 393224 | tf_op jit(solution)/shard_map/ppermute | solution.py:224
  61.6 7.5 %collective-permute-start.25 = (bf16[512,128]{1,0:T(8,128)(2,1)S(1)}, bf16[512,128]{1,0:T(8,128)(2,1)S(1)}, u32[]{:S(2)}, u32[]{:S(2)}) collective-permute-start(bf16[512,128]{1,0:T(8,128)(2,1)S(1)} %get-tuple-element.159), channel_id=1, source_target_pairs={{0,4},{4,0},{8,12},{12,8},{16,20},{20,16},{24,28},{28,24},{1,5},{5... | collective-permute-start | bytes 393224 | tf_op jit(solution)/shard_map/ppermute | solution.py:214
  61.7 10.9 %collective-permute-start.26 = (bf16[512,128]{1,0:T(8,128)(2,1)S(1)}, bf16[512,128]{1,0:T(8,128)(2,1)S(1)}, u32[]{:S(2)}, u32[]{:S(2)}) collective-permute-start(bf16[512,128]{1,0:T(8,128)(2,1)S(1)} %get-tuple-element.160), channel_id=1, source_target_pairs={{0,8},{4,12},{8,0},{12,4},{16,24},{20,28},{24,16},{28,20},{1,9},{5... | collective-permute-start | bytes 393224 | tf_op jit(solution)/shard_map/ppermute | solution.py:214
  65.1 7.5 %collective-permute-start.27 = (bf16[512,128]{1,0:T(8,128)(2,1)S(1)}, bf16[512,128]{1,0:T(8,128)(2,1)S(1)}, u32[]{:S(2)}, u32[]{:S(2)}) collective-permute-start(bf16[512,128]{1,0:T(8,128)(2,1)S(1)} %get-tuple-element.161), channel_id=1, source_target_pairs={{0,12},{4,8},{8,4},{12,0},{16,28},{20,24},{24,20},{28,16},{1,13},{... | collective-permute-start | bytes 393224 | tf_op jit(solution)/shard_map/ppermute | solution.py:214
  66.4 8.2 %collective-permute-start.21 = (bf16[512,128]{1,0:T(8,128)(2,1)S(1)}, bf16[512,128]{1,0:T(8,128)(2,1)S(1)}, u32[]{:S(2)}, u32[]{:S(2)}) collective-permute-start(bf16[512,128]{1,0:T(8,128)(2,1)S(1)} %get-tuple-element.149), channel_id=1, source_target_pairs={{0,4},{4,0},{8,12},{12,8},{16,20},{20,16},{24,28},{28,24},{1,5},{5... | collective-permute-start | bytes 393224 | tf_op jit(solution)/shard_map/ppermute | solution.py:214
  67.0 7.6 %collective-permute-start.22 = (bf16[512,128]{1,0:T(8,128)(2,1)S(1)}, bf16[512,128]{1,0:T(8,128)(2,1)S(1)}, u32[]{:S(2)}, u32[]{:S(2)}) collective-permute-start(bf16[512,128]{1,0:T(8,128)(2,1)S(1)} %get-tuple-element.150), channel_id=1, source_target_pairs={{0,8},{4,12},{8,0},{12,4},{16,24},{20,28},{24,16},{28,20},{1,9},{5... | collective-permute-start | bytes 393224 | tf_op jit(solution)/shard_map/ppermute | solution.py:214
  69.0 6.2 %collective-permute-start.23 = (bf16[512,128]{1,0:T(8,128)(2,1)S(1)}, bf16[512,128]{1,0:T(8,128)(2,1)S(1)}, u32[]{:S(2)}, u32[]{:S(2)}) collective-permute-start(bf16[512,128]{1,0:T(8,128)(2,1)S(1)} %get-tuple-element.151), channel_id=1, source_target_pairs={{0,12},{4,8},{8,4},{12,0},{16,28},{20,24},{24,20},{28,16},{1,13},{... | collective-permute-start | bytes 393224 | tf_op jit(solution)/shard_map/ppermute | solution.py:214

commit v8 on v7

--- a/solution.py
+++ b/solution.py
@@ -187,7 +187,7 @@
         scratch_shapes=scratch,
         input_output_aliases=alias,
         compiler_params=pltpu.CompilerParams(vmem_limit_bytes=8 << 20),
-        cost_estimate=pl.CostEstimate(flops=flops // 4, bytes_accessed=nbytes // 4, transcendentals=0),
+        cost_estimate=pl.CostEstimate(flops=flops, bytes_accessed=nbytes, transcendentals=0),
     )(*args)
 
 
@@ -246,9 +246,9 @@
     got_a = [*own, *got_a[len(own) :]]
     got_b = exchange(second, n)
     if forward:
+        made_b = fill_b(extra)
+        got_b, made_b, extra = barrier((got_b, made_b, extra))
         made_a = fill_a(extra)
-        made_b = fill_b(extra)
-        got_b, made_a, made_b = barrier((got_b, made_a, made_b))
     else:
         got_a, extra = barrier((got_a, extra))
         made_a = fill_a(extra)

time: 77.5 us -> 77.5 us (level)
  no operation moved by 1% of the time
where the time goes in v8:
time: 77.5 us; the launch traced here: 77.3 us
  starting transfers between devices  44.2 us (57%)
  Pallas kernels  23.4 us (30%)
  waiting for transfers between devices  8.58 us (11%)
  between operations  1.1 us (1%)
    ppermute x24, starting transfers between devices, exchange(): out[j] = lax.ppermute(parts[j], 'seq', perm)  36.8 us
    pallas_call x23, Pallas kernels, call(): pl.pallas_call(kernel, in_specs=in_specs, out_specs=out_specs or [VMEM] *...  23.4 us
    ppermute x4, starting transfers between devices, shift(): return lax.ppermute(x, 'seq', [(i, (i + step) % n) for i in range(n)])  7.44 us
    ppermute x24, waiting for transfers between devices, exchange(): out[j] = lax.ppermute(parts[j], 'seq', perm)  5.34 us
    ppermute x4, waiting for transfers between devices, shift(): return lax.ppermute(x, 'seq', [(i, (i + step) % n) for i in range(n)])  3.24 us
  transfers between devices with their start and end apart: 28, of which 7 were waited for; matrix products, arithmetic and copies ran while one was open for 0% of the time, Pallas kernels for 23%

profile of v8, /device:TPU:0, one launch (start us, length us, event | category | flops | bytes accessed | tf_op | source)
XLA Modules:
  0.0 77.3 jit_solution(14120636958952149940)
XLA Ops:
  0.6 2.2 %shard_map.68 = (bf16[512,128]{1,0:T(8,128)(2,1)S(1)}, bf16[512,128]{1,0:T(8,128)(2,1)S(1)}, bf16[512,128]{1,0:T(8,128)(2,1)S(1)}) custom-call(bf16[256,4096]{1,0:T(8,128)(2,1)} %k_ref.7, bf16[256,4096]{1,0:T(8,128)(2,1)} %v_ref.7), custom_call_target="tpu_custom_call" | custom-call | flops 100663296 | bytes 2359296 | tf_op jit(solution)/shard_map/pallas_call | solution.py:182
  2.9 3.0 %collective-permute-start.6 = (bf16[512,128]{1,0:T(8,128)(2,1)S(1)}, bf16[512,128]{1,0:T(8,128)(2,1)S(1)}, u32[]{:S(2)}, u32[]{:S(2)}) collective-permute-start(bf16[512,128]{1,0:T(8,128)(2,1)S(1)} %get-tuple-element.113), channel_id=1, source_target_pairs={{0,4},{4,0},{8,12},{12,8},{16,20},{20,16},{24,28},{28,24},{1,5},{5... | collective-permute-start | bytes 393224 | tf_op jit(solution)/shard_map/ppermute | solution.py:214
  5.9 1.6 %collective-permute-start.7 = (bf16[512,128]{1,0:T(8,128)(2,1)S(1)}, bf16[512,128]{1,0:T(8,128)(2,1)S(1)}, u32[]{:S(2)}, u32[]{:S(2)}) collective-permute-start(bf16[512,128]{1,0:T(8,128)(2,1)S(1)} %get-tuple-element.114), channel_id=1, source_target_pairs={{0,8},{4,12},{8,0},{12,4},{16,24},{20,28},{24,16},{28,20},{1,9},{5... | collective-permute-start | bytes 393224 | tf_op jit(solution)/shard_map/ppermute | solution.py:214
  7.5 0.8 %shard_map.69 = (bf16[512,128]{1,0:T(8,128)(2,1)S(1)}, bf16[512,128]{1,0:T(8,128)(2,1)S(1)}, bf16[512,128]{1,0:T(8,128)(2,1)S(1)}, bf16[512,128]{1,0:T(8,128)(2,1)S(1)}) custom-call(bf16[256,4096]{1,0:T(8,128)(2,1)S(1)} %copy-done.1, bf16[256,4096]{1,0:T(8,128)(2,1)S(1)} %copy-done.2), custom_call_target="tpu_custom_call" | custom-call | flops 134217728 | bytes 2097152 | tf_op jit(solution)/shard_map/pallas_call | solution.py:182
  8.3 2.0 %collective-permute-start = (bf16[512,128]{1,0:T(8,128)(2,1)S(1)}, bf16[512,128]{1,0:T(8,128)(2,1)S(1)}, u32[]{:S(2)}, u32[]{:S(2)}) collective-permute-start(bf16[512,128]{1,0:T(8,128)(2,1)S(1)} %get-tuple-element.92), channel_id=1, source_target_pairs={{0,4},{4,0},{8,12},{12,8},{16,20},{20,16},{24,28},{28,24},{1,5},{5... | collective-permute-start | bytes 393224 | tf_op jit(solution)/shard_map/ppermute | solution.py:214
  10.2 1.6 %collective-permute-start.1 = (bf16[512,128]{1,0:T(8,128)(2,1)S(1)}, bf16[512,128]{1,0:T(8,128)(2,1)S(1)}, u32[]{:S(2)}, u32[]{:S(2)}) collective-permute-start(bf16[512,128]{1,0:T(8,128)(2,1)S(1)} %get-tuple-element.93), channel_id=1, source_target_pairs={{0,8},{4,12},{8,0},{12,4},{16,24},{20,28},{24,16},{28,20},{1,9},{5... | collective-permute-start | bytes 393224 | tf_op jit(solution)/shard_map/ppermute | solution.py:214
  11.8 0.6 collective-permute-start.2
  12.8 2.1 %collective-permute-done.8.refs_3_ = bf16[512,128]{1,0:T(8,128)(2,1)S(1)} collective-permute-done((bf16[512,128]{1,0:T(8,128)(2,1)S(1)}, bf16[512,128]{1,0:T(8,128)(2,1)S(1)}, u32[]{:S(2)}, u32[]{:S(2)}) %collective-permute-start.8) | collective-permute-done | bytes 131104 | tf_op jit(solution)/shard_map/ppermute | solution.py:214
  14.9 2.7 %collective-permute-start.9 = (bf16[512,128]{1,0:T(8,128)(2,1)S(1)}, bf16[512,128]{1,0:T(8,128)(2,1)S(1)}, u32[]{:S(2)}, u32[]{:S(2)}) collective-permute-start(bf16[512,128]{1,0:T(8,128)(2,1)S(1)} %shard_map.75), channel_id=1, source_target_pairs={{0,16},{4,20},{8,24},{12,28},{16,0},{20,4},{24,8},{28,12},{1,17},{... | collective-permute-start | bytes 393224 | tf_op jit(solution)/shard_map/ppermute | solution.py:224
  17.6 1.6 %shard_map.70 = (f32[256,2048]{1,0:T(8,128)S(1)}, f32[256,2048]{1,0:T(8,128)S(1)}) custom-call(bf16[256,4096]{1,0:T(8,128)(2,1)S(1)} %copy-done, bf16[256,4096]{1,0:T(8,128)(2,1)S(1)} %copy-done.1, bf16[256,4096]{1,0:T(8,128)(2,1)S(1)} %copy-done.2, bf16[256,4096]{1,0:T(8,128)(2,1)S(1)} %copy-done.3, f32[1,4096]{1,0:T(1,128)S(1)} %bitcast.1), custom_call_target="tpu_custom_call" | custom-call | flops 536870912 | bytes 6291456 | tf_op jit(solution)/shard_map/pallas_call | solution.py:182
  19.3 1.3 %collective-permute-done.2.refs_3_ = bf16[512,128]{1,0:T(8,128)(2,1)S(1)} collective-permute-done((bf16[512,128]{1,0:T(8,128)(2,1)S(1)}, bf16[512,128]{1,0:T(8,128)(2,1)S(1)}, u32[]{:S(2)}, u32[]{:S(2)}) %collective-permute-start.2) | collective-permute-done | bytes 131104 | tf_op jit(solution)/shard_map/ppermute | solution.py:214
  20.6 2.6 %collective-permute-start.3 = (bf16[512,128]{1,0:T(8,128)(2,1)S(1)}, bf16[512,128]{1,0:T(8,128)(2,1)S(1)}, u32[]{:S(2)}, u32[]{:S(2)}) collective-permute-start(bf16[512,128]{1,0:T(8,128)(2,1)S(1)} %shard_map.71), channel_id=1, source_target_pairs={{0,16},{4,20},{8,24},{12,28},{16,0},{20,4},{24,8},{28,12},{1,17},{... | collective-permute-start | bytes 393224 | tf_op jit(solution)/shard_map/ppermute | solution.py:224
  23.2 0.4 shard_map.76
  23.6 3.9 %collective-permute-start.10 = (bf16[512,128]{1,0:T(8,128)(2,1)S(1)}, bf16[512,128]{1,0:T(8,128)(2,1)S(1)}, u32[]{:S(2)}, u32[]{:S(2)}) collective-permute-start(bf16[512,128]{1,0:T(8,128)(2,1)S(1)} %get-tuple-element.117), channel_id=1, source_target_pairs={{0,4},{4,0},{8,12},{12,8},{16,20},{20,16},{24,28},{28,24},{1,5},{5... | collective-permute-start | bytes 393224 | tf_op jit(solution)/shard_map/ppermute | solution.py:214
  27.8 1.2 %collective-permute-start.12 = (bf16[512,128]{1,0:T(8,128)(2,1)S(1)}, bf16[512,128]{1,0:T(8,128)(2,1)S(1)}, u32[]{:S(2)}, u32[]{:S(2)}) collective-permute-start(bf16[512,128]{1,0:T(8,128)(2,1)S(1)} %get-tuple-element.119), channel_id=1, source_target_pairs={{0,12},{4,8},{8,4},{12,0},{16,28},{20,24},{24,20},{28,16},{1,13},{... | collective-permute-start | bytes 393224 | tf_op jit(solution)/shard_map/ppermute | solution.py:214
  29.0 0.7 collective-permute-done.3.carry
  29.7 0.4 shard_map.72
  30.1 1.3 %collective-permute-start.4 = (bf16[512,128]{1,0:T(8,128)(2,1)S(1)}, bf16[512,128]{1,0:T(8,128)(2,1)S(1)}, u32[]{:S(2)}, u32[]{:S(2)}) collective-permute-start(bf16[512,128]{1,0:T(8,128)(2,1)S(1)} %get-tuple-element.105), channel_id=1, source_target_pairs={{0,4},{4,0},{8,12},{12,8},{16,20},{20,16},{24,28},{28,24},{1,5},{5... | collective-permute-start | bytes 393224 | tf_op jit(solution)/shard_map/ppermute | solution.py:214
  31.8 4.3 %collective-permute-start.13 = (bf16[512,128]{1,0:T(8,128)(2,1)S(1)}, bf16[512,128]{1,0:T(8,128)(2,1)S(1)}, u32[]{:S(2)}, u32[]{:S(2)}) collective-permute-start(bf16[512,128]{1,0:T(8,128)(2,1)S(1)} %get-tuple-element.123), channel_id=1, source_target_pairs={{0,12},{4,8},{8,4},{12,0},{16,28},{20,24},{24,20},{28,16},{1,13},{... | collective-permute-start | bytes 393224 | tf_op jit(solution)/shard_map/ppermute | solution.py:214
  36.0 1.6 %shard_map.73 = (f32[256,2048]{1,0:T(8,128)S(1)}, f32[256,2048]{1,0:T(8,128)S(1)}) custom-call(bf16[256,4096]{1,0:T(8,128)(2,1)S(1)} %copy-done, bf16[256,4096]{1,0:T(8,128)(2,1)S(1)} %copy-done.1, bf16[256,4096]{1,0:T(8,128)(2,1)S(1)} %copy-done.2, bf16[256,4096]{1,0:T(8,128)(2,1)S(1)} %copy-done.3, f32[1,4096]{1,0:T(1,128)S(1)} %bitcast.2), custom_call_target="tpu_custom_call" | custom-call | flops 536870912 | bytes 6291456 | tf_op jit(solution)/shard_map/pallas_call | solution.py:182
  37.7 1.3 %shard_map.77 = (f32[256,2048]{1,0:T(8,128)S(1)}, f32[256,128]{1,0:T(8,128)S(1)}, f32[256,128]{1,0:T(8,128)S(1)}) custom-call(bf16[256,4096]{1,0:T(8,128)(2,1)S(1)} %copy-done, f32[256,2048]{1,0:T(8,128)S(1)} %get-tuple-element.111.loc_ref, f32[256,2048]{1,0:T(8,128)S(1)} %get-tuple-element.112.u_ref, ...), custom_call_target="tpu_custom_call", output_to_operand_aliasing={{0}: (1, {})} | custom-call | flops 134217728 | bytes 2097152 | tf_op jit(solution)/shard_map/pallas_call | solution.py:182
  39.0 1.0 %shard_map.78 = (f32[256,2048]{1,0:T(8,128)S(1)}, f32[256,128]{1,0:T(8,128)S(1)}, f32[256,128]{1,0:T(8,128)S(1)}) custom-call(bf16[256,4096]{1,0:T(8,128)(2,1)S(1)} %copy-done, f32[256,2048]{1,0:T(8,128)S(1)} %get-tuple-element.98.loc_ref, f32[256,2048]{1,0:T(8,128)S(1)} %get-tuple-element.99.u_ref, ...), custom_call_target="tpu_custom_call", output_to_operand_aliasing={{0}: (1, {})} | custom-call | flops 100663296 | bytes 1572864 | tf_op jit(solution)/shard_map/pallas_call | solution.py:182
  40.0 0.5 shard_map.79
  40.5 1.1 %shard_map.81 = (bf16[256,2048]{1,0:T(8,128)(2,1)S(1)}, bf16[512,128]{1,0:T(8,128)(2,1)S(1)}, bf16[512,128]{1,0:T(8,128)(2,1)S(1)}, bf16[512,128]{1,0:T(8,128)(2,1)S(1)}) custom-call(bf16[256,4096]{1,0:T(8,128)(2,1)S(1)} %copy-done, f32[256,2048]{1,0:T(8,128)S(1)} %get-tuple-element.133.att_ref, f32[256,2048]{1,0:T(8,128)S(1)} %get-tuple-element.112.u_ref, ...), custom_call_target="tpu_custom_call" | custom-call | flops 100663296 | bytes 1572864 | tf_op jit(solution)/shard_map/pallas_call | solution.py:182
  41.6 1.1 %collective-permute-start.17 = (bf16[512,128]{1,0:T(8,128)(2,1)S(1)}, bf16[512,128]{1,0:T(8,128)(2,1)S(1)}, u32[]{:S(2)}, u32[]{:S(2)}) collective-permute-start(bf16[512,128]{1,0:T(8,128)(2,1)S(1)} %get-tuple-element.136), channel_id=1, source_target_pairs={{0,4},{4,0},{8,12},{12,8},{16,20},{20,16},{24,28},{28,24},{1,5},{5... | collective-permute-start | bytes 393224 | tf_op jit(solution)/shard_map/ppermute | solution.py:214
  42.7 1.4 %collective-permute-start.18 = (bf16[512,128]{1,0:T(8,128)(2,1)S(1)}, bf16[512,128]{1,0:T(8,128)(2,1)S(1)}, u32[]{:S(2)}, u32[]{:S(2)}) collective-permute-start(bf16[512,128]{1,0:T(8,128)(2,1)S(1)} %get-tuple-element.137), channel_id=1, source_target_pairs={{0,8},{4,12},{8,0},{12,4},{16,24},{20,28},{24,16},{28,20},{1,9},{5... | collective-permute-start | bytes 393224 | tf_op jit(solution)/shard_map/ppermute | solution.py:214
  44.1 1.0 %collective-permute-start.19 = (bf16[512,128]{1,0:T(8,128)(2,1)S(1)}, bf16[512,128]{1,0:T(8,128)(2,1)S(1)}, u32[]{:S(2)}, u32[]{:S(2)}) collective-permute-start(bf16[512,128]{1,0:T(8,128)(2,1)S(1)} %get-tuple-element.138), channel_id=1, source_target_pairs={{0,12},{4,8},{8,4},{12,0},{16,28},{20,24},{24,20},{28,16},{1,13},{... | collective-permute-start | bytes 393224 | tf_op jit(solution)/shard_map/ppermute | solution.py:214
  45.2 1.3 %shard_map.80 = (bf16[256,2048]{1,0:T(8,128)(2,1)S(1)}, bf16[512,128]{1,0:T(8,128)(2,1)S(1)}, bf16[512,128]{1,0:T(8,128)(2,1)S(1)}, bf16[512,128]{1,0:T(8,128)(2,1)S(1)}, bf16[512,128]{1,0:T(8,128)(2,1)S(1)}) custom-call(bf16[256,4096]{1,0:T(8,128)(2,1)S(1)} %copy-done, f32[256,2048]{1,0:T(8,128)S(1)} %get-tuple-element.126.att_ref, ...), custom_call_target="tpu_custom_call" | custom-call | flops 134217728 | bytes 2097152 | tf_op jit(solution)/shard_map/pallas_call | solution.py:182
  46.5 1.1 %collective-permute-start.14 = (bf16[512,128]{1,0:T(8,128)(2,1)S(1)}, bf16[512,128]{1,0:T(8,128)(2,1)S(1)}, u32[]{:S(2)}, u32[]{:S(2)}) collective-permute-start(bf16[512,128]{1,0:T(8,128)(2,1)S(1)} %get-tuple-element.130), channel_id=1, source_target_pairs={{0,4},{4,0},{8,12},{12,8},{16,20},{20,16},{24,28},{28,24},{1,5},{5... | collective-permute-start | bytes 393224 | tf_op jit(solution)/shard_map/ppermute | solution.py:214
  47.6 1.4 %collective-permute-start.15 = (bf16[512,128]{1,0:T(8,128)(2,1)S(1)}, bf16[512,128]{1,0:T(8,128)(2,1)S(1)}, u32[]{:S(2)}, u32[]{:S(2)}) collective-permute-start(bf16[512,128]{1,0:T(8,128)(2,1)S(1)} %get-tuple-element.131), channel_id=1, source_target_pairs={{0,8},{4,12},{8,0},{12,4},{16,24},{20,28},{24,16},{28,20},{1,9},{5... | collective-permute-start | bytes 393224 | tf_op jit(solution)/shard_map/ppermute | solution.py:214
  49.0 2.7 %collective-permute-start.16 = (bf16[512,128]{1,0:T(8,128)(2,1)S(1)}, bf16[512,128]{1,0:T(8,128)(2,1)S(1)}, u32[]{:S(2)}, u32[]{:S(2)}) collective-permute-start(bf16[512,128]{1,0:T(8,128)(2,1)S(1)} %get-tuple-element.132), channel_id=1, source_target_pairs={{0,12},{4,8},{8,4},{12,0},{16,28},{20,24},{24,20},{28,16},{1,13},{... | collective-permute-start | bytes 393224 | tf_op jit(solution)/shard_map/ppermute | solution.py:214
  51.7 0.6 shard_map.82
  52.4 2.1 %collective-permute-start.24 = (bf16[512,128]{1,0:T(8,128)(2,1)S(1)}, bf16[512,128]{1,0:T(8,128)(2,1)S(1)}, u32[]{:S(2)}, u32[]{:S(2)}) collective-permute-start(bf16[512,128]{1,0:T(8,128)(2,1)S(1)} %shard_map.87), channel_id=1, source_target_pairs={{0,16},{4,20},{8,24},{12,28},{16,0},{20,4},{24,8},{28,12},{1,17},{... | collective-permute-start | bytes 393224 | tf_op jit(solution)/shard_map/ppermute | solution.py:224
  54.5 2.6 %shard_map.83 = (f32[256,2048]{1,0:T(8,128)S(1)}, f32[256,2048]{1,0:T(8,128)S(1)}) custom-call(bf16[256,4096]{1,0:T(8,128)(2,1)S(1)} %copy-done, bf16[256,4096]{1,0:T(8,128)(2,1)S(1)} %copy-done.1, bf16[256,4096]{1,0:T(8,128)(2,1)S(1)} %copy-done.2, bf16[256,2048]{1,0:T(8,128)(2,1)S(1)} %get-tuple-element.141.g_ref), custom_call_target="tpu_custom_call" | custom-call | flops 1073741824 | bytes 4194304 | tf_op jit(solution)/shard_map/pallas_call | solution.py:182
  57.1 1.4 %collective-permute-done.16.refs_3_ = bf16[512,128]{1,0:T(8,128)(2,1)S(1)} collective-permute-done((bf16[512,128]{1,0:T(8,128)(2,1)S(1)}, bf16[512,128]{1,0:T(8,128)(2,1)S(1)}, u32[]{:S(2)}, u32[]{:S(2)}) %collective-permute-start.16) | collective-permute-done | bytes 131104 | tf_op jit(solution)/shard_map/ppermute | solution.py:214
  58.6 2.5 %collective-permute-done.24.carry = bf16[512,128]{1,0:T(8,128)(2,1)S(1)} collective-permute-done((bf16[512,128]{1,0:T(8,128)(2,1)S(1)}, bf16[512,128]{1,0:T(8,128)(2,1)S(1)}, u32[]{:S(2)}, u32[]{:S(2)}) %collective-permute-start.24) | collective-permute-done | bytes 131104 | tf_op jit(solution)/shard_map/ppermute | solution.py:224
  61.1 0.4 shard_map.88
  61.5 0.8 %collective-permute-start.25 = (bf16[512,128]{1,0:T(8,128)(2,1)S(1)}, bf16[512,128]{1,0:T(8,128)(2,1)S(1)}, u32[]{:S(2)}, u32[]{:S(2)}) collective-permute-start(bf16[512,128]{1,0:T(8,128)(2,1)S(1)} %get-tuple-element.163), channel_id=1, source_target_pairs={{0,4},{4,0},{8,12},{12,8},{16,20},{20,16},{24,28},{28,24},{1,5},{5... | collective-permute-start | bytes 393224 | tf_op jit(solution)/shard_map/ppermute | solution.py:214
  62.4 2.7 %collective-permute-start.26 = (bf16[512,128]{1,0:T(8,128)(2,1)S(1)}, bf16[512,128]{1,0:T(8,128)(2,1)S(1)}, u32[]{:S(2)}, u32[]{:S(2)}) collective-permute-start(bf16[512,128]{1,0:T(8,128)(2,1)S(1)} %get-tuple-element.164), channel_id=1, source_target_pairs={{0,8},{4,12},{8,0},{12,4},{16,24},{20,28},{24,16},{28,20},{1,9},{5... | collective-permute-start | bytes 393224 | tf_op jit(solution)/shard_map/ppermute | solution.py:214
  65.1 1.0 %collective-permute-start.27 = (bf16[512,128]{1,0:T(8,128)(2,1)S(1)}, bf16[512,128]{1,0:T(8,128)(2,1)S(1)}, u32[]{:S(2)}, u32[]{:S(2)}) collective-permute-start(bf16[512,128]{1,0:T(8,128)(2,1)S(1)} %get-tuple-element.165), channel_id=1, source_target_pairs={{0,12},{4,8},{8,4},{12,0},{16,28},{20,24},{24,20},{28,16},{1,13},{... | collective-permute-start | bytes 393224 | tf_op jit(solution)/shard_map/ppermute | solution.py:214
  66.1 0.4 shard_map.86
  66.5 0.6 collective-permute-start.21
  67.1 2.0 %collective-permute-start.22 = (bf16[512,128]{1,0:T(8,128)(2,1)S(1)}, bf16[512,128]{1,0:T(8,128)(2,1)S(1)}, u32[]{:S(2)}, u32[]{:S(2)}) collective-permute-start(bf16[512,128]{1,0:T(8,128)(2,1)S(1)} %get-tuple-element.154), channel_id=1, source_target_pairs={{0,8},{4,12},{8,0},{12,4},{16,24},{20,28},{24,16},{28,20},{1,9},{5... | collective-permute-start | bytes 393224 | tf_op jit(solution)/shard_map/ppermute | solution.py:214
  69.1 1.0 %collective-permute-start.23 = (bf16[512,128]{1,0:T(8,128)(2,1)S(1)}, bf16[512,128]{1,0:T(8,128)(2,1)S(1)}, u32[]{:S(2)}, u32[]{:S(2)}) collective-permute-start(bf16[512,128]{1,0:T(8,128)(2,1)S(1)} %get-tuple-element.155), channel_id=1, source_target_pairs={{0,12},{4,8},{8,4},{12,0},{16,28},{20,24},{24,20},{28,16},{1,13},{... | collective-permute-start | bytes 393224 | tf_op jit(solution)/shard_map/ppermute | solution.py:214
  70.0 2.6 %shard_map.84 = (f32[256,2048]{1,0:T(8,128)S(1)}, f32[256,2048]{1,0:T(8,128)S(1)}) custom-call(bf16[256,4096]{1,0:T(8,128)(2,1)S(1)} %copy-done, bf16[256,4096]{1,0:T(8,128)(2,1)S(1)} %copy-done.1, bf16[256,4096]{1,0:T(8,128)(2,1)S(1)} %copy-done.2, bf16[256,2048]{1,0:T(8,128)(2,1)S(1)} %get-tuple-element.145.g_ref), custom_call_target="tpu_custom_call" | custom-call | flops 1073741824 | bytes 4194304 | tf_op jit(solution)/shard_map/pallas_call | solution.py:182
  72.6 2.0 %shard_map.89 = (bf16[256,4096]{1,0:T(8,128)(2,1)}, bf16[256,4096]{1,0:T(8,128)(2,1)}) custom-call(bf16[256,4096]{1,0:T(8,128)(2,1)S(1)} %copy-done.1, bf16[256,4096]{1,0:T(8,128)(2,1)S(1)} %copy-done.2, f32[256,2048]{1,0:T(8,128)S(1)} %get-tuple-element.156.kl_ref, f32[256,2048]{1,0:T(8,128)S(1)} %get-tuple-element.157.vl_ref, ...), custom_call_target="tpu_custom_call" | custom-call | flops 268435456 | bytes 4194304 | tf_op jit(solution)/shard_map/pallas_call | solution.py:182
  74.7 0.5 collective-permute-done.23.rest_3_
  75.2 2.0 %shard_map.90 = (bf16[256,4096]{1,0:T(8,128)(2,1)}, bf16[256,4096]{1,0:T(8,128)(2,1)}) custom-call(bf16[256,4096]{1,0:T(8,128)(2,1)S(1)} %copy-done.1, bf16[256,4096]{1,0:T(8,128)(2,1)S(1)} %copy-done.2, f32[256,2048]{1,0:T(8,128)S(1)} %get-tuple-element.146.kl_ref, ...), custom_call_target="tpu_custom_call", output_to_operand_aliasing={{0}: (8, {}), {1}: (9, {})} | custom-call | flops 268435456 | bytes 4194304 | tf_op jit(solution)/shard_map/pallas_call | solution.py:182
  (41 shorter events, 1.5 us)
Async XLA Ops:
  0.6 6.8 %copy-start.1 = (bf16[256,4096]{1,0:T(8,128)(2,1)S(1)}, bf16[256,4096]{1,0:T(8,128)(2,1)}, u32[]{:S(2)}) copy-start(bf16[256,4096]{1,0:T(8,128)(2,1)} %k_ref.7) | copy-start | bytes 6291460
  0.6 6.8 %copy-start.2 = (bf16[256,4096]{1,0:T(8,128)(2,1)S(1)}, bf16[256,4096]{1,0:T(8,128)(2,1)}, u32[]{:S(2)}) copy-start(bf16[256,4096]{1,0:T(8,128)(2,1)} %v_ref.7) | copy-start | bytes 6291460
  2.9 8.9 %collective-permute-start.6 = (bf16[512,128]{1,0:T(8,128)(2,1)S(1)}, bf16[512,128]{1,0:T(8,128)(2,1)S(1)}, u32[]{:S(2)}, u32[]{:S(2)}) collective-permute-start(bf16[512,128]{1,0:T(8,128)(2,1)S(1)} %get-tuple-element.113), channel_id=1, source_target_pairs={{0,4},{4,0},{8,12},{12,8},{16,20},{20,16},{24,28},{28,24},{1,5},{5... | collective-permute-start | bytes 393224 | tf_op jit(solution)/shard_map/ppermute | solution.py:214
  5.9 6.9 %collective-permute-start.7 = (bf16[512,128]{1,0:T(8,128)(2,1)S(1)}, bf16[512,128]{1,0:T(8,128)(2,1)S(1)}, u32[]{:S(2)}, u32[]{:S(2)}) collective-permute-start(bf16[512,128]{1,0:T(8,128)(2,1)S(1)} %get-tuple-element.114), channel_id=1, source_target_pairs={{0,8},{4,12},{8,0},{12,4},{16,24},{20,28},{24,16},{28,20},{1,9},{5... | collective-permute-start | bytes 393224 | tf_op jit(solution)/shard_map/ppermute | solution.py:214
  7.5 7.4 %collective-permute-start.8 = (bf16[512,128]{1,0:T(8,128)(2,1)S(1)}, bf16[512,128]{1,0:T(8,128)(2,1)S(1)}, u32[]{:S(2)}, u32[]{:S(2)}) collective-permute-start(bf16[512,128]{1,0:T(8,128)(2,1)S(1)} %get-tuple-element.115), channel_id=1, source_target_pairs={{0,12},{4,8},{8,4},{12,0},{16,28},{20,24},{24,20},{28,16},{1,13},{... | collective-permute-start | bytes 393224 | tf_op jit(solution)/shard_map/ppermute | solution.py:214
  8.3 10.9 %collective-permute-start = (bf16[512,128]{1,0:T(8,128)(2,1)S(1)}, bf16[512,128]{1,0:T(8,128)(2,1)S(1)}, u32[]{:S(2)}, u32[]{:S(2)}) collective-permute-start(bf16[512,128]{1,0:T(8,128)(2,1)S(1)} %get-tuple-element.92), channel_id=1, source_target_pairs={{0,4},{4,0},{8,12},{12,8},{16,20},{20,16},{24,28},{28,24},{1,5},{5... | collective-permute-start | bytes 393224 | tf_op jit(solution)/shard_map/ppermute | solution.py:214
  10.2 9.0 %collective-permute-start.1 = (bf16[512,128]{1,0:T(8,128)(2,1)S(1)}, bf16[512,128]{1,0:T(8,128)(2,1)S(1)}, u32[]{:S(2)}, u32[]{:S(2)}) collective-permute-start(bf16[512,128]{1,0:T(8,128)(2,1)S(1)} %get-tuple-element.93), channel_id=1, source_target_pairs={{0,8},{4,12},{8,0},{12,4},{16,24},{20,28},{24,16},{28,20},{1,9},{5... | collective-permute-start | bytes 393224 | tf_op jit(solution)/shard_map/ppermute | solution.py:214
  11.8 5.8 %copy-start = (bf16[256,4096]{1,0:T(8,128)(2,1)S(1)}, bf16[256,4096]{1,0:T(8,128)(2,1)}, u32[]{:S(2)}) copy-start(bf16[256,4096]{1,0:T(8,128)(2,1)} %q_ref.9) | copy-start | bytes 6291460
  11.8 5.8 %copy-start.3 = (bf16[256,4096]{1,0:T(8,128)(2,1)S(1)}, bf16[256,4096]{1,0:T(8,128)(2,1)}, u32[]{:S(2)}) copy-start(bf16[256,4096]{1,0:T(8,128)(2,1)} %c_ref.1) | copy-start | bytes 6291460
  11.8 5.8 %copy-start.4 = (f32[4096]{0:T(1024)S(1)}, f32[4096]{0:T(1024)}, u32[]{:S(2)}) copy-start(f32[4096]{0:T(1024)} %param.8) | copy-start | bytes 49156
  11.8 8.7 %collective-permute-start.2 = (bf16[512,128]{1,0:T(8,128)(2,1)S(1)}, bf16[512,128]{1,0:T(8,128)(2,1)S(1)}, u32[]{:S(2)}, u32[]{:S(2)}) collective-permute-start(bf16[512,128]{1,0:T(8,128)(2,1)S(1)} %get-tuple-element.94), channel_id=1, source_target_pairs={{0,12},{4,8},{8,4},{12,0},{16,28},{20,24},{24,20},{28,16},{1,13},{... | collective-permute-start | bytes 393224 | tf_op jit(solution)/shard_map/ppermute | solution.py:214
  14.9 8.3 %collective-permute-start.9 = (bf16[512,128]{1,0:T(8,128)(2,1)S(1)}, bf16[512,128]{1,0:T(8,128)(2,1)S(1)}, u32[]{:S(2)}, u32[]{:S(2)}) collective-permute-start(bf16[512,128]{1,0:T(8,128)(2,1)S(1)} %shard_map.75), channel_id=1, source_target_pairs={{0,16},{4,20},{8,24},{12,28},{16,0},{20,4},{24,8},{28,12},{1,17},{... | collective-permute-start | bytes 393224 | tf_op jit(solution)/shard_map/ppermute | solution.py:224
  20.6 9.1 %collective-permute-start.3 = (bf16[512,128]{1,0:T(8,128)(2,1)S(1)}, bf16[512,128]{1,0:T(8,128)(2,1)S(1)}, u32[]{:S(2)}, u32[]{:S(2)}) collective-permute-start(bf16[512,128]{1,0:T(8,128)(2,1)S(1)} %shard_map.71), channel_id=1, source_target_pairs={{0,16},{4,20},{8,24},{12,28},{16,0},{20,4},{24,8},{28,12},{1,17},{... | collective-permute-start | bytes 393224 | tf_op jit(solution)/shard_map/ppermute | solution.py:224
  23.6 8.2 %collective-permute-start.10 = (bf16[512,128]{1,0:T(8,128)(2,1)S(1)}, bf16[512,128]{1,0:T(8,128)(2,1)S(1)}, u32[]{:S(2)}, u32[]{:S(2)}) collective-permute-start(bf16[512,128]{1,0:T(8,128)(2,1)S(1)} %get-tuple-element.117), channel_id=1, source_target_pairs={{0,4},{4,0},{8,12},{12,8},{16,20},{20,16},{24,28},{28,24},{1,5},{5... | collective-permute-start | bytes 393224 | tf_op jit(solution)/shard_map/ppermute | solution.py:214
  27.5 10.2 %collective-permute-start.11 = (bf16[512,128]{1,0:T(8,128)(2,1)S(1)}, bf16[512,128]{1,0:T(8,128)(2,1)S(1)}, u32[]{:S(2)}, u32[]{:S(2)}) collective-permute-start(bf16[512,128]{1,0:T(8,128)(2,1)S(1)} %get-tuple-element.118), channel_id=1, source_target_pairs={{0,8},{4,12},{8,0},{12,4},{16,24},{20,28},{24,16},{28,20},{1,9},{5... | collective-permute-start | bytes 393224 | tf_op jit(solution)/shard_map/ppermute | solution.py:214
  27.8 9.9 %collective-permute-start.12 = (bf16[512,128]{1,0:T(8,128)(2,1)S(1)}, bf16[512,128]{1,0:T(8,128)(2,1)S(1)}, u32[]{:S(2)}, u32[]{:S(2)}) collective-permute-start(bf16[512,128]{1,0:T(8,128)(2,1)S(1)} %get-tuple-element.119), channel_id=1, source_target_pairs={{0,12},{4,8},{8,4},{12,0},{16,28},{20,24},{24,20},{28,16},{1,13},{... | collective-permute-start | bytes 393224 | tf_op jit(solution)/shard_map/ppermute | solution.py:214
  30.1 8.9 %collective-permute-start.4 = (bf16[512,128]{1,0:T(8,128)(2,1)S(1)}, bf16[512,128]{1,0:T(8,128)(2,1)S(1)}, u32[]{:S(2)}, u32[]{:S(2)}) collective-permute-start(bf16[512,128]{1,0:T(8,128)(2,1)S(1)} %get-tuple-element.105), channel_id=1, source_target_pairs={{0,4},{4,0},{8,12},{12,8},{16,20},{20,16},{24,28},{28,24},{1,5},{5... | collective-permute-start | bytes 393224 | tf_op jit(solution)/shard_map/ppermute | solution.py:214
  31.4 7.6 %collective-permute-start.5 = (bf16[512,128]{1,0:T(8,128)(2,1)S(1)}, bf16[512,128]{1,0:T(8,128)(2,1)S(1)}, u32[]{:S(2)}, u32[]{:S(2)}) collective-permute-start(bf16[512,128]{1,0:T(8,128)(2,1)S(1)} %get-tuple-element.106), channel_id=1, source_target_pairs={{0,8},{4,12},{8,0},{12,4},{16,24},{20,28},{24,16},{28,20},{1,9},{5... | collective-permute-start | bytes 393224 | tf_op jit(solution)/shard_map/ppermute | solution.py:214
  31.8 8.2 %collective-permute-start.13 = (bf16[512,128]{1,0:T(8,128)(2,1)S(1)}, bf16[512,128]{1,0:T(8,128)(2,1)S(1)}, u32[]{:S(2)}, u32[]{:S(2)}) collective-permute-start(bf16[512,128]{1,0:T(8,128)(2,1)S(1)} %get-tuple-element.123), channel_id=1, source_target_pairs={{0,12},{4,8},{8,4},{12,0},{16,28},{20,24},{24,20},{28,16},{1,13},{... | collective-permute-start | bytes 393224 | tf_op jit(solution)/shard_map/ppermute | solution.py:214
  41.6 7.4 %collective-permute-start.17 = (bf16[512,128]{1,0:T(8,128)(2,1)S(1)}, bf16[512,128]{1,0:T(8,128)(2,1)S(1)}, u32[]{:S(2)}, u32[]{:S(2)}) collective-permute-start(bf16[512,128]{1,0:T(8,128)(2,1)S(1)} %get-tuple-element.136), channel_id=1, source_target_pairs={{0,4},{4,0},{8,12},{12,8},{16,20},{20,16},{24,28},{28,24},{1,5},{5... | collective-permute-start | bytes 393224 | tf_op jit(solution)/shard_map/ppermute | solution.py:214
  42.7 9.6 %collective-permute-start.18 = (bf16[512,128]{1,0:T(8,128)(2,1)S(1)}, bf16[512,128]{1,0:T(8,128)(2,1)S(1)}, u32[]{:S(2)}, u32[]{:S(2)}) collective-permute-start(bf16[512,128]{1,0:T(8,128)(2,1)S(1)} %get-tuple-element.137), channel_id=1, source_target_pairs={{0,8},{4,12},{8,0},{12,4},{16,24},{20,28},{24,16},{28,20},{1,9},{5... | collective-permute-start | bytes 393224 | tf_op jit(solution)/shard_map/ppermute | solution.py:214
  44.1 8.2 %collective-permute-start.19 = (bf16[512,128]{1,0:T(8,128)(2,1)S(1)}, bf16[512,128]{1,0:T(8,128)(2,1)S(1)}, u32[]{:S(2)}, u32[]{:S(2)}) collective-permute-start(bf16[512,128]{1,0:T(8,128)(2,1)S(1)} %get-tuple-element.138), channel_id=1, source_target_pairs={{0,12},{4,8},{8,4},{12,0},{16,28},{20,24},{24,20},{28,16},{1,13},{... | collective-permute-start | bytes 393224 | tf_op jit(solution)/shard_map/ppermute | solution.py:214
  46.5 10.6 %collective-permute-start.14 = (bf16[512,128]{1,0:T(8,128)(2,1)S(1)}, bf16[512,128]{1,0:T(8,128)(2,1)S(1)}, u32[]{:S(2)}, u32[]{:S(2)}) collective-permute-start(bf16[512,128]{1,0:T(8,128)(2,1)S(1)} %get-tuple-element.130), channel_id=1, source_target_pairs={{0,4},{4,0},{8,12},{12,8},{16,20},{20,16},{24,28},{28,24},{1,5},{5... | collective-permute-start | bytes 393224 | tf_op jit(solution)/shard_map/ppermute | solution.py:214
  47.6 9.5 %collective-permute-start.15 = (bf16[512,128]{1,0:T(8,128)(2,1)S(1)}, bf16[512,128]{1,0:T(8,128)(2,1)S(1)}, u32[]{:S(2)}, u32[]{:S(2)}) collective-permute-start(bf16[512,128]{1,0:T(8,128)(2,1)S(1)} %get-tuple-element.131), channel_id=1, source_target_pairs={{0,8},{4,12},{8,0},{12,4},{16,24},{20,28},{24,16},{28,20},{1,9},{5... | collective-permute-start | bytes 393224 | tf_op jit(solution)/shard_map/ppermute | solution.py:214
  49.0 9.4 %collective-permute-start.16 = (bf16[512,128]{1,0:T(8,128)(2,1)S(1)}, bf16[512,128]{1,0:T(8,128)(2,1)S(1)}, u32[]{:S(2)}, u32[]{:S(2)}) collective-permute-start(bf16[512,128]{1,0:T(8,128)(2,1)S(1)} %get-tuple-element.132), channel_id=1, source_target_pairs={{0,12},{4,8},{8,4},{12,0},{16,28},{20,24},{24,20},{28,16},{1,13},{... | collective-permute-start | bytes 393224 | tf_op jit(solution)/shard_map/ppermute | solution.py:214
  52.4 8.7 %collective-permute-start.24 = (bf16[512,128]{1,0:T(8,128)(2,1)S(1)}, bf16[512,128]{1,0:T(8,128)(2,1)S(1)}, u32[]{:S(2)}, u32[]{:S(2)}) collective-permute-start(bf16[512,128]{1,0:T(8,128)(2,1)S(1)} %shard_map.87), channel_id=1, source_target_pairs={{0,16},{4,20},{8,24},{12,28},{16,0},{20,4},{24,8},{28,12},{1,17},{... | collective-permute-start | bytes 393224 | tf_op jit(solution)/shard_map/ppermute | solution.py:224
  58.5 7.5 %collective-permute-start.20 = (bf16[512,128]{1,0:T(8,128)(2,1)S(1)}, bf16[512,128]{1,0:T(8,128)(2,1)S(1)}, u32[]{:S(2)}, u32[]{:S(2)}) collective-permute-start(bf16[512,128]{1,0:T(8,128)(2,1)S(1)} %shard_map.85), channel_id=1, source_target_pairs={{0,16},{4,20},{8,24},{12,28},{16,0},{20,4},{24,8},{28,12},{1,17},{... | collective-permute-start | bytes 393224 | tf_op jit(solution)/shard_map/ppermute | solution.py:224
  61.5 7.5 %collective-permute-start.25 = (bf16[512,128]{1,0:T(8,128)(2,1)S(1)}, bf16[512,128]{1,0:T(8,128)(2,1)S(1)}, u32[]{:S(2)}, u32[]{:S(2)}) collective-permute-start(bf16[512,128]{1,0:T(8,128)(2,1)S(1)} %get-tuple-element.163), channel_id=1, source_target_pairs={{0,4},{4,0},{8,12},{12,8},{16,20},{20,16},{24,28},{28,24},{1,5},{5... | collective-permute-start | bytes 393224 | tf_op jit(solution)/shard_map/ppermute | solution.py:214
  62.4 10.2 %collective-permute-start.26 = (bf16[512,128]{1,0:T(8,128)(2,1)S(1)}, bf16[512,128]{1,0:T(8,128)(2,1)S(1)}, u32[]{:S(2)}, u32[]{:S(2)}) collective-permute-start(bf16[512,128]{1,0:T(8,128)(2,1)S(1)} %get-tuple-element.164), channel_id=1, source_target_pairs={{0,8},{4,12},{8,0},{12,4},{16,24},{20,28},{24,16},{28,20},{1,9},{5... | collective-permute-start | bytes 393224 | tf_op jit(solution)/shard_map/ppermute | solution.py:214
  65.1 7.5 %collective-permute-start.27 = (bf16[512,128]{1,0:T(8,128)(2,1)S(1)}, bf16[512,128]{1,0:T(8,128)(2,1)S(1)}, u32[]{:S(2)}, u32[]{:S(2)}) collective-permute-start(bf16[512,128]{1,0:T(8,128)(2,1)S(1)} %get-tuple-element.165), channel_id=1, source_target_pairs={{0,12},{4,8},{8,4},{12,0},{16,28},{20,24},{24,20},{28,16},{1,13},{... | collective-permute-start | bytes 393224 | tf_op jit(solution)/shard_map/ppermute | solution.py:214
  66.5 8.2 %collective-permute-start.21 = (bf16[512,128]{1,0:T(8,128)(2,1)S(1)}, bf16[512,128]{1,0:T(8,128)(2,1)S(1)}, u32[]{:S(2)}, u32[]{:S(2)}) collective-permute-start(bf16[512,128]{1,0:T(8,128)(2,1)S(1)} %get-tuple-element.153), channel_id=1, source_target_pairs={{0,4},{4,0},{8,12},{12,8},{16,20},{20,16},{24,28},{28,24},{1,5},{5... | collective-permute-start | bytes 393224 | tf_op jit(solution)/shard_map/ppermute | solution.py:214
  67.1 7.6 %collective-permute-start.22 = (bf16[512,128]{1,0:T(8,128)(2,1)S(1)}, bf16[512,128]{1,0:T(8,128)(2,1)S(1)}, u32[]{:S(2)}, u32[]{:S(2)}) collective-permute-start(bf16[512,128]{1,0:T(8,128)(2,1)S(1)} %get-tuple-element.154), channel_id=1, source_target_pairs={{0,8},{4,12},{8,0},{12,4},{16,24},{20,28},{24,16},{28,20},{1,9},{5... | collective-permute-start | bytes 393224 | tf_op jit(solution)/shard_map/ppermute | solution.py:214
  69.1 6.1 %collective-permute-start.23 = (bf16[512,128]{1,0:T(8,128)(2,1)S(1)}, bf16[512,128]{1,0:T(8,128)(2,1)S(1)}, u32[]{:S(2)}, u32[]{:S(2)}) collective-permute-start(bf16[512,128]{1,0:T(8,128)(2,1)S(1)} %get-tuple-element.155), channel_id=1, source_target_pairs={{0,12},{4,8},{8,4},{12,0},{16,28},{20,24},{24,20},{28,16},{1,13},{... | collective-permute-start | bytes 393224 | tf_op jit(solution)/shard_map/ppermute | solution.py:214

commit v9 on v8

--- a/solution.py
+++ b/solution.py
@@ -187,7 +187,7 @@
         scratch_shapes=scratch,
         input_output_aliases=alias,
         compiler_params=pltpu.CompilerParams(vmem_limit_bytes=8 << 20),
-        cost_estimate=pl.CostEstimate(flops=flops, bytes_accessed=nbytes, transcendentals=0),
+        cost_estimate=pl.CostEstimate(flops=flops // 4, bytes_accessed=nbytes // 4, transcendentals=0),
     )(*args)
 
 
@@ -256,8 +256,12 @@
     carry_a = carry_groups(total_of(got_a, n), n, m, forward)
     carry_b = carry_groups(total_of(got_b, n), n, m, forward)
     if not forward:
+        back = give_back(got_a, carry_a, n, forward)
+        back, extra = barrier((back, extra))
         made_b = fill_b(extra)
-    back_a = exchange(give_back(got_a, carry_a, n, forward), n)
+        back_a = exchange(back, n)
+    else:
+        back_a = exchange(give_back(got_a, carry_a, n, forward), n)
     back_b = exchange(give_back(got_b, carry_b, n, forward), n)
     return (back_a, back_b), (made_a, made_b)
 

time: 77.5 us -> 77.3 us (level)
  waiting for transfers between devices: 8.58 us -> 5.88 us
  starting transfers between devices: 44.2 us -> 46.8 us
    ppermute x4, waiting for transfers between devices: 3.24 us -> 0.73 us  [shift(): return lax.ppermute(x, 'seq', [(i, (i + step) % n) for i in range(n)])]
    ppermute x24, starting transfers between devices: 36.8 us -> 38.7 us  [exchange(): out[j] = lax.ppermute(parts[j], 'seq', perm)]
  transfers between devices with their start and end apart: 28 -> 28, of which waited for: 7 -> 6; matrix products, arithmetic and copies ran while one was open for 0% -> 0% of each run, Pallas kernels for 23% -> 23%
where the time goes in v9:
time: 77.3 us; the launch traced here: 77.1 us
  starting transfers between devices  46.8 us (61%)
  Pallas kernels  23.4 us (30%)
  waiting for transfers between devices  5.88 us (8%)
  between operations  1.1 us (1%)
    ppermute x24, starting transfers between devices, exchange(): out[j] = lax.ppermute(parts[j], 'seq', perm)  38.7 us
    pallas_call x23, Pallas kernels, call(): pl.pallas_call(kernel, in_specs=in_specs, out_specs=out_specs or [VMEM] *...  23.4 us
    ppermute x4, starting transfers between devices, shift(): return lax.ppermute(x, 'seq', [(i, (i + step) % n) for i in range(n)])  8.05 us
    ppermute x24, waiting for transfers between devices, exchange(): out[j] = lax.ppermute(parts[j], 'seq', perm)  5.14 us
  transfers between devices with their start and end apart: 28, of which 6 were waited for; matrix products, arithmetic and copies ran while one was open for 0% of the time, Pallas kernels for 23%

profile of v9, /device:TPU:0, one launch (start us, length us, event | category | flops | bytes accessed | tf_op | source)
XLA Modules:
  0.0 77.1 jit_solution(247950815449484025)
XLA Ops:
  0.6 2.2 %shard_map.68 = (bf16[512,128]{1,0:T(8,128)(2,1)S(1)}, bf16[512,128]{1,0:T(8,128)(2,1)S(1)}, bf16[512,128]{1,0:T(8,128)(2,1)S(1)}) custom-call(bf16[256,4096]{1,0:T(8,128)(2,1)} %k_ref.7, bf16[256,4096]{1,0:T(8,128)(2,1)} %v_ref.7), custom_call_target="tpu_custom_call" | custom-call | flops 25165824 | bytes 589824 | tf_op jit(solution)/shard_map/pallas_call | solution.py:182
  2.9 3.0 %collective-permute-start.3 = (bf16[512,128]{1,0:T(8,128)(2,1)S(1)}, bf16[512,128]{1,0:T(8,128)(2,1)S(1)}, u32[]{:S(2)}, u32[]{:S(2)}) collective-permute-start(bf16[512,128]{1,0:T(8,128)(2,1)S(1)} %get-tuple-element.109), channel_id=1, source_target_pairs={{0,4},{4,0},{8,12},{12,8},{16,20},{20,16},{24,28},{28,24},{1,5},{5... | collective-permute-start | bytes 393224 | tf_op jit(solution)/shard_map/ppermute | solution.py:214
  5.9 1.6 %collective-permute-start.4 = (bf16[512,128]{1,0:T(8,128)(2,1)S(1)}, bf16[512,128]{1,0:T(8,128)(2,1)S(1)}, u32[]{:S(2)}, u32[]{:S(2)}) collective-permute-start(bf16[512,128]{1,0:T(8,128)(2,1)S(1)} %get-tuple-element.110), channel_id=1, source_target_pairs={{0,8},{4,12},{8,0},{12,4},{16,24},{20,28},{24,16},{28,20},{1,9},{5... | collective-permute-start | bytes 393224 | tf_op jit(solution)/shard_map/ppermute | solution.py:214
  7.5 0.8 %shard_map.69 = (bf16[512,128]{1,0:T(8,128)(2,1)S(1)}, bf16[512,128]{1,0:T(8,128)(2,1)S(1)}, bf16[512,128]{1,0:T(8,128)(2,1)S(1)}, bf16[512,128]{1,0:T(8,128)(2,1)S(1)}) custom-call(bf16[256,4096]{1,0:T(8,128)(2,1)S(1)} %copy-done.1, bf16[256,4096]{1,0:T(8,128)(2,1)S(1)} %copy-done.2), custom_call_target="tpu_custom_call" | custom-call | flops 33554432 | bytes 524288 | tf_op jit(solution)/shard_map/pallas_call | solution.py:182
  8.3 2.0 %collective-permute-start = (bf16[512,128]{1,0:T(8,128)(2,1)S(1)}, bf16[512,128]{1,0:T(8,128)(2,1)S(1)}, u32[]{:S(2)}, u32[]{:S(2)}) collective-permute-start(bf16[512,128]{1,0:T(8,128)(2,1)S(1)} %get-tuple-element.97), channel_id=1, source_target_pairs={{0,4},{4,0},{8,12},{12,8},{16,20},{20,16},{24,28},{28,24},{1,5},{5... | collective-permute-start | bytes 393224 | tf_op jit(solution)/shard_map/ppermute | solution.py:214
  10.2 1.6 %collective-permute-start.1 = (bf16[512,128]{1,0:T(8,128)(2,1)S(1)}, bf16[512,128]{1,0:T(8,128)(2,1)S(1)}, u32[]{:S(2)}, u32[]{:S(2)}) collective-permute-start(bf16[512,128]{1,0:T(8,128)(2,1)S(1)} %get-tuple-element.98), channel_id=1, source_target_pairs={{0,8},{4,12},{8,0},{12,4},{16,24},{20,28},{24,16},{28,20},{1,9},{5... | collective-permute-start | bytes 393224 | tf_op jit(solution)/shard_map/ppermute | solution.py:214
  11.8 0.6 collective-permute-start.2
  12.8 2.1 %collective-permute-done.5.refs_3_ = bf16[512,128]{1,0:T(8,128)(2,1)S(1)} collective-permute-done((bf16[512,128]{1,0:T(8,128)(2,1)S(1)}, bf16[512,128]{1,0:T(8,128)(2,1)S(1)}, u32[]{:S(2)}, u32[]{:S(2)}) %collective-permute-start.5) | collective-permute-done | bytes 131104 | tf_op jit(solution)/shard_map/ppermute | solution.py:214
  14.9 2.7 %collective-permute-start.6 = (bf16[512,128]{1,0:T(8,128)(2,1)S(1)}, bf16[512,128]{1,0:T(8,128)(2,1)S(1)}, u32[]{:S(2)}, u32[]{:S(2)}) collective-permute-start(bf16[512,128]{1,0:T(8,128)(2,1)S(1)} %shard_map.73), channel_id=1, source_target_pairs={{0,16},{4,20},{8,24},{12,28},{16,0},{20,4},{24,8},{28,12},{1,17},{... | collective-permute-start | bytes 393224 | tf_op jit(solution)/shard_map/ppermute | solution.py:224
  17.6 1.6 %shard_map.70 = (f32[256,2048]{1,0:T(8,128)S(1)}, f32[256,2048]{1,0:T(8,128)S(1)}) custom-call(bf16[256,4096]{1,0:T(8,128)(2,1)S(1)} %copy-done, bf16[256,4096]{1,0:T(8,128)(2,1)S(1)} %copy-done.1, bf16[256,4096]{1,0:T(8,128)(2,1)S(1)} %copy-done.2, bf16[256,4096]{1,0:T(8,128)(2,1)S(1)} %copy-done.3, f32[1,4096]{1,0:T(1,128)S(1)} %bitcast.1), custom_call_target="tpu_custom_call" | custom-call | flops 134217728 | bytes 1572864 | tf_op jit(solution)/shard_map/pallas_call | solution.py:182
  19.3 1.3 %collective-permute-done.2.refs_3_ = bf16[512,128]{1,0:T(8,128)(2,1)S(1)} collective-permute-done((bf16[512,128]{1,0:T(8,128)(2,1)S(1)}, bf16[512,128]{1,0:T(8,128)(2,1)S(1)}, u32[]{:S(2)}, u32[]{:S(2)}) %collective-permute-start.2) | collective-permute-done | bytes 131104 | tf_op jit(solution)/shard_map/ppermute | solution.py:214
  20.6 2.6 %collective-permute-start.10 = (bf16[512,128]{1,0:T(8,128)(2,1)S(1)}, bf16[512,128]{1,0:T(8,128)(2,1)S(1)}, u32[]{:S(2)}, u32[]{:S(2)}) collective-permute-start(bf16[512,128]{1,0:T(8,128)(2,1)S(1)} %shard_map.76), channel_id=1, source_target_pairs={{0,16},{4,20},{8,24},{12,28},{16,0},{20,4},{24,8},{28,12},{1,17},{... | collective-permute-start | bytes 393224 | tf_op jit(solution)/shard_map/ppermute | solution.py:224
  23.2 0.4 shard_map.74
  23.6 3.9 %collective-permute-start.7 = (bf16[512,128]{1,0:T(8,128)(2,1)S(1)}, bf16[512,128]{1,0:T(8,128)(2,1)S(1)}, u32[]{:S(2)}, u32[]{:S(2)}) collective-permute-start(bf16[512,128]{1,0:T(8,128)(2,1)S(1)} %get-tuple-element.113), channel_id=1, source_target_pairs={{0,4},{4,0},{8,12},{12,8},{16,20},{20,16},{24,28},{28,24},{1,5},{5... | collective-permute-start | bytes 393224 | tf_op jit(solution)/shard_map/ppermute | solution.py:214
  27.5 0.3 collective-permute-start.8
  27.8 1.2 %collective-permute-start.9 = (bf16[512,128]{1,0:T(8,128)(2,1)S(1)}, bf16[512,128]{1,0:T(8,128)(2,1)S(1)}, u32[]{:S(2)}, u32[]{:S(2)}) collective-permute-start(bf16[512,128]{1,0:T(8,128)(2,1)S(1)} %get-tuple-element.115), channel_id=1, source_target_pairs={{0,12},{4,8},{8,4},{12,0},{16,28},{20,24},{24,20},{28,16},{1,13},{... | collective-permute-start | bytes 393224 | tf_op jit(solution)/shard_map/ppermute | solution.py:214
  29.0 0.7 collective-permute-done.10.carry
  29.7 0.4 shard_map.77
  30.1 1.3 %collective-permute-start.11 = (bf16[512,128]{1,0:T(8,128)(2,1)S(1)}, bf16[512,128]{1,0:T(8,128)(2,1)S(1)}, u32[]{:S(2)}, u32[]{:S(2)}) collective-permute-start(bf16[512,128]{1,0:T(8,128)(2,1)S(1)} %get-tuple-element.124), channel_id=1, source_target_pairs={{0,4},{4,0},{8,12},{12,8},{16,20},{20,16},{24,28},{28,24},{1,5},{5... | collective-permute-start | bytes 393224 | tf_op jit(solution)/shard_map/ppermute | solution.py:214
  31.4 0.3 collective-permute-start.12
  31.8 4.3 %collective-permute-start.13 = (bf16[512,128]{1,0:T(8,128)(2,1)S(1)}, bf16[512,128]{1,0:T(8,128)(2,1)S(1)}, u32[]{:S(2)}, u32[]{:S(2)}) collective-permute-start(bf16[512,128]{1,0:T(8,128)(2,1)S(1)} %get-tuple-element.129), channel_id=1, source_target_pairs={{0,12},{4,8},{8,4},{12,0},{16,28},{20,24},{24,20},{28,16},{1,13},{... | collective-permute-start | bytes 393224 | tf_op jit(solution)/shard_map/ppermute | solution.py:214
  36.0 1.6 %shard_map.71 = (f32[256,2048]{1,0:T(8,128)S(1)}, f32[256,2048]{1,0:T(8,128)S(1)}) custom-call(bf16[256,4096]{1,0:T(8,128)(2,1)S(1)} %copy-done, bf16[256,4096]{1,0:T(8,128)(2,1)S(1)} %copy-done.1, bf16[256,4096]{1,0:T(8,128)(2,1)S(1)} %copy-done.2, bf16[256,4096]{1,0:T(8,128)(2,1)S(1)} %copy-done.3, f32[1,4096]{1,0:T(1,128)S(1)} %bitcast.2), custom_call_target="tpu_custom_call" | custom-call | flops 134217728 | bytes 1572864 | tf_op jit(solution)/shard_map/pallas_call | solution.py:182
  37.7 1.3 %shard_map.75 = (f32[256,2048]{1,0:T(8,128)S(1)}, f32[256,128]{1,0:T(8,128)S(1)}, f32[256,128]{1,0:T(8,128)S(1)}) custom-call(bf16[256,4096]{1,0:T(8,128)(2,1)S(1)} %copy-done, f32[256,2048]{1,0:T(8,128)S(1)} %get-tuple-element.107.loc_ref, f32[256,2048]{1,0:T(8,128)S(1)} %get-tuple-element.108.u_ref, ...), custom_call_target="tpu_custom_call", output_to_operand_aliasing={{0}: (1, {})} | custom-call | flops 33554432 | bytes 524288 | tf_op jit(solution)/shard_map/pallas_call | solution.py:182
  39.0 1.0 %shard_map.78 = (f32[256,2048]{1,0:T(8,128)S(1)}, f32[256,128]{1,0:T(8,128)S(1)}, f32[256,128]{1,0:T(8,128)S(1)}) custom-call(bf16[256,4096]{1,0:T(8,128)(2,1)S(1)} %copy-done, f32[256,2048]{1,0:T(8,128)S(1)} %get-tuple-element.117.loc_ref, f32[256,2048]{1,0:T(8,128)S(1)} %get-tuple-element.118.u_ref, ...), custom_call_target="tpu_custom_call", output_to_operand_aliasing={{0}: (1, {})} | custom-call | flops 25165824 | bytes 393216 | tf_op jit(solution)/shard_map/pallas_call | solution.py:182
  40.0 0.5 shard_map.79
  40.5 1.1 %shard_map.80 = (bf16[256,2048]{1,0:T(8,128)(2,1)S(1)}, bf16[512,128]{1,0:T(8,128)(2,1)S(1)}, bf16[512,128]{1,0:T(8,128)(2,1)S(1)}, bf16[512,128]{1,0:T(8,128)(2,1)S(1)}) custom-call(bf16[256,4096]{1,0:T(8,128)(2,1)S(1)} %copy-done, f32[256,2048]{1,0:T(8,128)S(1)} %get-tuple-element.116.att_ref, f32[256,2048]{1,0:T(8,128)S(1)} %get-tuple-element.108.u_ref, ...), custom_call_target="tpu_custom_call" | custom-call | flops 25165824 | bytes 393216 | tf_op jit(solution)/shard_map/pallas_call | solution.py:182
  41.6 1.1 %collective-permute-start.14 = (bf16[512,128]{1,0:T(8,128)(2,1)S(1)}, bf16[512,128]{1,0:T(8,128)(2,1)S(1)}, u32[]{:S(2)}, u32[]{:S(2)}) collective-permute-start(bf16[512,128]{1,0:T(8,128)(2,1)S(1)} %get-tuple-element.136), channel_id=1, source_target_pairs={{0,4},{4,0},{8,12},{12,8},{16,20},{20,16},{24,28},{28,24},{1,5},{5... | collective-permute-start | bytes 393224 | tf_op jit(solution)/shard_map/ppermute | solution.py:214
  42.7 1.4 %collective-permute-start.15 = (bf16[512,128]{1,0:T(8,128)(2,1)S(1)}, bf16[512,128]{1,0:T(8,128)(2,1)S(1)}, u32[]{:S(2)}, u32[]{:S(2)}) collective-permute-start(bf16[512,128]{1,0:T(8,128)(2,1)S(1)} %get-tuple-element.137), channel_id=1, source_target_pairs={{0,8},{4,12},{8,0},{12,4},{16,24},{20,28},{24,16},{28,20},{1,9},{5... | collective-permute-start | bytes 393224 | tf_op jit(solution)/shard_map/ppermute | solution.py:214
  44.1 1.0 %collective-permute-start.16 = (bf16[512,128]{1,0:T(8,128)(2,1)S(1)}, bf16[512,128]{1,0:T(8,128)(2,1)S(1)}, u32[]{:S(2)}, u32[]{:S(2)}) collective-permute-start(bf16[512,128]{1,0:T(8,128)(2,1)S(1)} %get-tuple-element.138), channel_id=1, source_target_pairs={{0,12},{4,8},{8,4},{12,0},{16,28},{20,24},{24,20},{28,16},{1,13},{... | collective-permute-start | bytes 393224 | tf_op jit(solution)/shard_map/ppermute | solution.py:214
  45.2 1.3 %shard_map.82 = (bf16[256,2048]{1,0:T(8,128)(2,1)S(1)}, bf16[512,128]{1,0:T(8,128)(2,1)S(1)}, bf16[512,128]{1,0:T(8,128)(2,1)S(1)}, bf16[512,128]{1,0:T(8,128)(2,1)S(1)}, bf16[512,128]{1,0:T(8,128)(2,1)S(1)}) custom-call(bf16[256,4096]{1,0:T(8,128)(2,1)S(1)} %copy-done, f32[256,2048]{1,0:T(8,128)S(1)} %get-tuple-element.140.att_ref, ...), custom_call_target="tpu_custom_call" | custom-call | flops 33554432 | bytes 524288 | tf_op jit(solution)/shard_map/pallas_call | solution.py:182
  46.5 1.1 %collective-permute-start.18 = (bf16[512,128]{1,0:T(8,128)(2,1)S(1)}, bf16[512,128]{1,0:T(8,128)(2,1)S(1)}, u32[]{:S(2)}, u32[]{:S(2)}) collective-permute-start(bf16[512,128]{1,0:T(8,128)(2,1)S(1)} %get-tuple-element.151), channel_id=1, source_target_pairs={{0,4},{4,0},{8,12},{12,8},{16,20},{20,16},{24,28},{28,24},{1,5},{5... | collective-permute-start | bytes 393224 | tf_op jit(solution)/shard_map/ppermute | solution.py:214
  47.6 1.4 %collective-permute-start.19 = (bf16[512,128]{1,0:T(8,128)(2,1)S(1)}, bf16[512,128]{1,0:T(8,128)(2,1)S(1)}, u32[]{:S(2)}, u32[]{:S(2)}) collective-permute-start(bf16[512,128]{1,0:T(8,128)(2,1)S(1)} %get-tuple-element.152), channel_id=1, source_target_pairs={{0,8},{4,12},{8,0},{12,4},{16,24},{20,28},{24,16},{28,20},{1,9},{5... | collective-permute-start | bytes 393224 | tf_op jit(solution)/shard_map/ppermute | solution.py:214
  49.0 0.6 shard_map.81
  49.6 2.1 %collective-permute-start.20 = (bf16[512,128]{1,0:T(8,128)(2,1)S(1)}, bf16[512,128]{1,0:T(8,128)(2,1)S(1)}, u32[]{:S(2)}, u32[]{:S(2)}) collective-permute-start(bf16[512,128]{1,0:T(8,128)(2,1)S(1)} %get-tuple-element.153), channel_id=1, source_target_pairs={{0,12},{4,8},{8,4},{12,0},{16,28},{20,24},{24,20},{28,16},{1,13},{... | collective-permute-start | bytes 393224 | tf_op jit(solution)/shard_map/ppermute | solution.py:214
  51.8 2.7 %collective-permute-start.17 = (bf16[512,128]{1,0:T(8,128)(2,1)S(1)}, bf16[512,128]{1,0:T(8,128)(2,1)S(1)}, u32[]{:S(2)}, u32[]{:S(2)}) collective-permute-start(bf16[512,128]{1,0:T(8,128)(2,1)S(1)} %shard_map.83), channel_id=1, source_target_pairs={{0,16},{4,20},{8,24},{12,28},{16,0},{20,4},{24,8},{28,12},{1,17},{... | collective-permute-start | bytes 393224 | tf_op jit(solution)/shard_map/ppermute | solution.py:224
  54.5 2.6 %shard_map.85 = (f32[256,2048]{1,0:T(8,128)S(1)}, f32[256,2048]{1,0:T(8,128)S(1)}) custom-call(bf16[256,4096]{1,0:T(8,128)(2,1)S(1)} %copy-done, bf16[256,4096]{1,0:T(8,128)(2,1)S(1)} %copy-done.1, bf16[256,4096]{1,0:T(8,128)(2,1)S(1)} %copy-done.2, bf16[256,2048]{1,0:T(8,128)(2,1)S(1)} %get-tuple-element.154.g_ref), custom_call_target="tpu_custom_call" | custom-call | flops 268435456 | bytes 1048576 | tf_op jit(solution)/shard_map/pallas_call | solution.py:182
  57.1 1.4 %collective-permute-done.20.refs_3_ = bf16[512,128]{1,0:T(8,128)(2,1)S(1)} collective-permute-done((bf16[512,128]{1,0:T(8,128)(2,1)S(1)}, bf16[512,128]{1,0:T(8,128)(2,1)S(1)}, u32[]{:S(2)}, u32[]{:S(2)}) %collective-permute-start.20) | collective-permute-done | bytes 131104 | tf_op jit(solution)/shard_map/ppermute | solution.py:214
  58.6 0.4 shard_map.84
  59.0 3.3 %collective-permute-start.25 = (bf16[512,128]{1,0:T(8,128)(2,1)S(1)}, bf16[512,128]{1,0:T(8,128)(2,1)S(1)}, u32[]{:S(2)}, u32[]{:S(2)}) collective-permute-start(bf16[512,128]{1,0:T(8,128)(2,1)S(1)} %get-tuple-element.173), channel_id=1, source_target_pairs={{0,4},{4,0},{8,12},{12,8},{16,20},{20,16},{24,28},{28,24},{1,5},{5... | collective-permute-start | bytes 393224 | tf_op jit(solution)/shard_map/ppermute | solution.py:214
  62.4 2.7 %collective-permute-start.26 = (bf16[512,128]{1,0:T(8,128)(2,1)S(1)}, bf16[512,128]{1,0:T(8,128)(2,1)S(1)}, u32[]{:S(2)}, u32[]{:S(2)}) collective-permute-start(bf16[512,128]{1,0:T(8,128)(2,1)S(1)} %get-tuple-element.174), channel_id=1, source_target_pairs={{0,8},{4,12},{8,0},{12,4},{16,24},{20,28},{24,16},{28,20},{1,9},{5... | collective-permute-start | bytes 393224 | tf_op jit(solution)/shard_map/ppermute | solution.py:214
  65.1 1.0 %collective-permute-start.27 = (bf16[512,128]{1,0:T(8,128)(2,1)S(1)}, bf16[512,128]{1,0:T(8,128)(2,1)S(1)}, u32[]{:S(2)}, u32[]{:S(2)}) collective-permute-start(bf16[512,128]{1,0:T(8,128)(2,1)S(1)} %get-tuple-element.175), channel_id=1, source_target_pairs={{0,12},{4,8},{8,4},{12,0},{16,28},{20,24},{24,20},{28,16},{1,13},{... | collective-permute-start | bytes 393224 | tf_op jit(solution)/shard_map/ppermute | solution.py:214
  66.1 0.4 shard_map.88
  66.5 0.6 collective-permute-start.22
  67.1 2.0 %collective-permute-start.23 = (bf16[512,128]{1,0:T(8,128)(2,1)S(1)}, bf16[512,128]{1,0:T(8,128)(2,1)S(1)}, u32[]{:S(2)}, u32[]{:S(2)}) collective-permute-start(bf16[512,128]{1,0:T(8,128)(2,1)S(1)} %get-tuple-element.168), channel_id=1, source_target_pairs={{0,8},{4,12},{8,0},{12,4},{16,24},{20,28},{24,16},{28,20},{1,9},{5... | collective-permute-start | bytes 393224 | tf_op jit(solution)/shard_map/ppermute | solution.py:214
  69.1 1.0 %collective-permute-start.24 = (bf16[512,128]{1,0:T(8,128)(2,1)S(1)}, bf16[512,128]{1,0:T(8,128)(2,1)S(1)}, u32[]{:S(2)}, u32[]{:S(2)}) collective-permute-start(bf16[512,128]{1,0:T(8,128)(2,1)S(1)} %get-tuple-element.169), channel_id=1, source_target_pairs={{0,12},{4,8},{8,4},{12,0},{16,28},{20,24},{24,20},{28,16},{1,13},{... | collective-permute-start | bytes 393224 | tf_op jit(solution)/shard_map/ppermute | solution.py:214
  70.1 2.6 %shard_map.86 = (f32[256,2048]{1,0:T(8,128)S(1)}, f32[256,2048]{1,0:T(8,128)S(1)}) custom-call(bf16[256,4096]{1,0:T(8,128)(2,1)S(1)} %copy-done, bf16[256,4096]{1,0:T(8,128)(2,1)S(1)} %copy-done.1, bf16[256,4096]{1,0:T(8,128)(2,1)S(1)} %copy-done.2, bf16[256,2048]{1,0:T(8,128)(2,1)S(1)} %get-tuple-element.159.g_ref), custom_call_target="tpu_custom_call" | custom-call | flops 268435456 | bytes 1048576 | tf_op jit(solution)/shard_map/pallas_call | solution.py:182
  72.7 2.0 %shard_map.89 = (bf16[256,4096]{1,0:T(8,128)(2,1)}, bf16[256,4096]{1,0:T(8,128)(2,1)}) custom-call(bf16[256,4096]{1,0:T(8,128)(2,1)S(1)} %copy-done.1, bf16[256,4096]{1,0:T(8,128)(2,1)S(1)} %copy-done.2, f32[256,2048]{1,0:T(8,128)S(1)} %get-tuple-element.170.kl_ref, f32[256,2048]{1,0:T(8,128)S(1)} %get-tuple-element.171.vl_ref, ...), custom_call_target="tpu_custom_call" | custom-call | flops 67108864 | bytes 1048576 | tf_op jit(solution)/shard_map/pallas_call | solution.py:182
  75.0 2.0 %shard_map.90 = (bf16[256,4096]{1,0:T(8,128)(2,1)}, bf16[256,4096]{1,0:T(8,128)(2,1)}) custom-call(bf16[256,4096]{1,0:T(8,128)(2,1)S(1)} %copy-done.1, bf16[256,4096]{1,0:T(8,128)(2,1)S(1)} %copy-done.2, f32[256,2048]{1,0:T(8,128)S(1)} %get-tuple-element.160.kl_ref, ...), custom_call_target="tpu_custom_call", output_to_operand_aliasing={{0}: (8, {}), {1}: (9, {})} | custom-call | flops 67108864 | bytes 1048576 | tf_op jit(solution)/shard_map/pallas_call | solution.py:182
  (41 shorter events, 1.1 us)
Async XLA Ops:
  0.6 6.8 %copy-start.2 = (bf16[256,4096]{1,0:T(8,128)(2,1)S(1)}, bf16[256,4096]{1,0:T(8,128)(2,1)}, u32[]{:S(2)}) copy-start(bf16[256,4096]{1,0:T(8,128)(2,1)} %v_ref.7) | copy-start | bytes 6291460
  0.6 6.8 %copy-start.1 = (bf16[256,4096]{1,0:T(8,128)(2,1)S(1)}, bf16[256,4096]{1,0:T(8,128)(2,1)}, u32[]{:S(2)}) copy-start(bf16[256,4096]{1,0:T(8,128)(2,1)} %k_ref.7) | copy-start | bytes 6291460
  2.9 8.9 %collective-permute-start.3 = (bf16[512,128]{1,0:T(8,128)(2,1)S(1)}, bf16[512,128]{1,0:T(8,128)(2,1)S(1)}, u32[]{:S(2)}, u32[]{:S(2)}) collective-permute-start(bf16[512,128]{1,0:T(8,128)(2,1)S(1)} %get-tuple-element.109), channel_id=1, source_target_pairs={{0,4},{4,0},{8,12},{12,8},{16,20},{20,16},{24,28},{28,24},{1,5},{5... | collective-permute-start | bytes 393224 | tf_op jit(solution)/shard_map/ppermute | solution.py:214
  5.9 6.9 %collective-permute-start.4 = (bf16[512,128]{1,0:T(8,128)(2,1)S(1)}, bf16[512,128]{1,0:T(8,128)(2,1)S(1)}, u32[]{:S(2)}, u32[]{:S(2)}) collective-permute-start(bf16[512,128]{1,0:T(8,128)(2,1)S(1)} %get-tuple-element.110), channel_id=1, source_target_pairs={{0,8},{4,12},{8,0},{12,4},{16,24},{20,28},{24,16},{28,20},{1,9},{5... | collective-permute-start | bytes 393224 | tf_op jit(solution)/shard_map/ppermute | solution.py:214
  7.5 7.4 %collective-permute-start.5 = (bf16[512,128]{1,0:T(8,128)(2,1)S(1)}, bf16[512,128]{1,0:T(8,128)(2,1)S(1)}, u32[]{:S(2)}, u32[]{:S(2)}) collective-permute-start(bf16[512,128]{1,0:T(8,128)(2,1)S(1)} %get-tuple-element.111), channel_id=1, source_target_pairs={{0,12},{4,8},{8,4},{12,0},{16,28},{20,24},{24,20},{28,16},{1,13},{... | collective-permute-start | bytes 393224 | tf_op jit(solution)/shard_map/ppermute | solution.py:214
  8.3 10.9 %collective-permute-start = (bf16[512,128]{1,0:T(8,128)(2,1)S(1)}, bf16[512,128]{1,0:T(8,128)(2,1)S(1)}, u32[]{:S(2)}, u32[]{:S(2)}) collective-permute-start(bf16[512,128]{1,0:T(8,128)(2,1)S(1)} %get-tuple-element.97), channel_id=1, source_target_pairs={{0,4},{4,0},{8,12},{12,8},{16,20},{20,16},{24,28},{28,24},{1,5},{5... | collective-permute-start | bytes 393224 | tf_op jit(solution)/shard_map/ppermute | solution.py:214
  10.2 9.0 %collective-permute-start.1 = (bf16[512,128]{1,0:T(8,128)(2,1)S(1)}, bf16[512,128]{1,0:T(8,128)(2,1)S(1)}, u32[]{:S(2)}, u32[]{:S(2)}) collective-permute-start(bf16[512,128]{1,0:T(8,128)(2,1)S(1)} %get-tuple-element.98), channel_id=1, source_target_pairs={{0,8},{4,12},{8,0},{12,4},{16,24},{20,28},{24,16},{28,20},{1,9},{5... | collective-permute-start | bytes 393224 | tf_op jit(solution)/shard_map/ppermute | solution.py:214
  11.8 5.8 %copy-start = (bf16[256,4096]{1,0:T(8,128)(2,1)S(1)}, bf16[256,4096]{1,0:T(8,128)(2,1)}, u32[]{:S(2)}) copy-start(bf16[256,4096]{1,0:T(8,128)(2,1)} %q_ref.9) | copy-start | bytes 6291460
  11.8 5.8 %copy-start.3 = (bf16[256,4096]{1,0:T(8,128)(2,1)S(1)}, bf16[256,4096]{1,0:T(8,128)(2,1)}, u32[]{:S(2)}) copy-start(bf16[256,4096]{1,0:T(8,128)(2,1)} %c_ref.1) | copy-start | bytes 6291460
  11.8 5.8 %copy-start.4 = (f32[4096]{0:T(1024)S(1)}, f32[4096]{0:T(1024)}, u32[]{:S(2)}) copy-start(f32[4096]{0:T(1024)} %param.8) | copy-start | bytes 49156
  11.8 8.7 %collective-permute-start.2 = (bf16[512,128]{1,0:T(8,128)(2,1)S(1)}, bf16[512,128]{1,0:T(8,128)(2,1)S(1)}, u32[]{:S(2)}, u32[]{:S(2)}) collective-permute-start(bf16[512,128]{1,0:T(8,128)(2,1)S(1)} %get-tuple-element.99), channel_id=1, source_target_pairs={{0,12},{4,8},{8,4},{12,0},{16,28},{20,24},{24,20},{28,16},{1,13},{... | collective-permute-start | bytes 393224 | tf_op jit(solution)/shard_map/ppermute | solution.py:214
  14.9 8.3 %collective-permute-start.6 = (bf16[512,128]{1,0:T(8,128)(2,1)S(1)}, bf16[512,128]{1,0:T(8,128)(2,1)S(1)}, u32[]{:S(2)}, u32[]{:S(2)}) collective-permute-start(bf16[512,128]{1,0:T(8,128)(2,1)S(1)} %shard_map.73), channel_id=1, source_target_pairs={{0,16},{4,20},{8,24},{12,28},{16,0},{20,4},{24,8},{28,12},{1,17},{... | collective-permute-start | bytes 393224 | tf_op jit(solution)/shard_map/ppermute | solution.py:224
  20.6 9.1 %collective-permute-start.10 = (bf16[512,128]{1,0:T(8,128)(2,1)S(1)}, bf16[512,128]{1,0:T(8,128)(2,1)S(1)}, u32[]{:S(2)}, u32[]{:S(2)}) collective-permute-start(bf16[512,128]{1,0:T(8,128)(2,1)S(1)} %shard_map.76), channel_id=1, source_target_pairs={{0,16},{4,20},{8,24},{12,28},{16,0},{20,4},{24,8},{28,12},{1,17},{... | collective-permute-start | bytes 393224 | tf_op jit(solution)/shard_map/ppermute | solution.py:224
  23.6 8.2 %collective-permute-start.7 = (bf16[512,128]{1,0:T(8,128)(2,1)S(1)}, bf16[512,128]{1,0:T(8,128)(2,1)S(1)}, u32[]{:S(2)}, u32[]{:S(2)}) collective-permute-start(bf16[512,128]{1,0:T(8,128)(2,1)S(1)} %get-tuple-element.113), channel_id=1, source_target_pairs={{0,4},{4,0},{8,12},{12,8},{16,20},{20,16},{24,28},{28,24},{1,5},{5... | collective-permute-start | bytes 393224 | tf_op jit(solution)/shard_map/ppermute | solution.py:214
  27.5 10.2 %collective-permute-start.8 = (bf16[512,128]{1,0:T(8,128)(2,1)S(1)}, bf16[512,128]{1,0:T(8,128)(2,1)S(1)}, u32[]{:S(2)}, u32[]{:S(2)}) collective-permute-start(bf16[512,128]{1,0:T(8,128)(2,1)S(1)} %get-tuple-element.114), channel_id=1, source_target_pairs={{0,8},{4,12},{8,0},{12,4},{16,24},{20,28},{24,16},{28,20},{1,9},{5... | collective-permute-start | bytes 393224 | tf_op jit(solution)/shard_map/ppermute | solution.py:214
  27.8 9.9 %collective-permute-start.9 = (bf16[512,128]{1,0:T(8,128)(2,1)S(1)}, bf16[512,128]{1,0:T(8,128)(2,1)S(1)}, u32[]{:S(2)}, u32[]{:S(2)}) collective-permute-start(bf16[512,128]{1,0:T(8,128)(2,1)S(1)} %get-tuple-element.115), channel_id=1, source_target_pairs={{0,12},{4,8},{8,4},{12,0},{16,28},{20,24},{24,20},{28,16},{1,13},{... | collective-permute-start | bytes 393224 | tf_op jit(solution)/shard_map/ppermute | solution.py:214
  30.1 8.9 %collective-permute-start.11 = (bf16[512,128]{1,0:T(8,128)(2,1)S(1)}, bf16[512,128]{1,0:T(8,128)(2,1)S(1)}, u32[]{:S(2)}, u32[]{:S(2)}) collective-permute-start(bf16[512,128]{1,0:T(8,128)(2,1)S(1)} %get-tuple-element.124), channel_id=1, source_target_pairs={{0,4},{4,0},{8,12},{12,8},{16,20},{20,16},{24,28},{28,24},{1,5},{5... | collective-permute-start | bytes 393224 | tf_op jit(solution)/shard_map/ppermute | solution.py:214
  31.4 7.6 %collective-permute-start.12 = (bf16[512,128]{1,0:T(8,128)(2,1)S(1)}, bf16[512,128]{1,0:T(8,128)(2,1)S(1)}, u32[]{:S(2)}, u32[]{:S(2)}) collective-permute-start(bf16[512,128]{1,0:T(8,128)(2,1)S(1)} %get-tuple-element.125), channel_id=1, source_target_pairs={{0,8},{4,12},{8,0},{12,4},{16,24},{20,28},{24,16},{28,20},{1,9},{5... | collective-permute-start | bytes 393224 | tf_op jit(solution)/shard_map/ppermute | solution.py:214
  31.8 8.2 %collective-permute-start.13 = (bf16[512,128]{1,0:T(8,128)(2,1)S(1)}, bf16[512,128]{1,0:T(8,128)(2,1)S(1)}, u32[]{:S(2)}, u32[]{:S(2)}) collective-permute-start(bf16[512,128]{1,0:T(8,128)(2,1)S(1)} %get-tuple-element.129), channel_id=1, source_target_pairs={{0,12},{4,8},{8,4},{12,0},{16,28},{20,24},{24,20},{28,16},{1,13},{... | collective-permute-start | bytes 393224 | tf_op jit(solution)/shard_map/ppermute | solution.py:214
  41.6 8.0 %collective-permute-start.14 = (bf16[512,128]{1,0:T(8,128)(2,1)S(1)}, bf16[512,128]{1,0:T(8,128)(2,1)S(1)}, u32[]{:S(2)}, u32[]{:S(2)}) collective-permute-start(bf16[512,128]{1,0:T(8,128)(2,1)S(1)} %get-tuple-element.136), channel_id=1, source_target_pairs={{0,4},{4,0},{8,12},{12,8},{16,20},{20,16},{24,28},{28,24},{1,5},{5... | collective-permute-start | bytes 393224 | tf_op jit(solution)/shard_map/ppermute | solution.py:214
  42.7 9.0 %collective-permute-start.15 = (bf16[512,128]{1,0:T(8,128)(2,1)S(1)}, bf16[512,128]{1,0:T(8,128)(2,1)S(1)}, u32[]{:S(2)}, u32[]{:S(2)}) collective-permute-start(bf16[512,128]{1,0:T(8,128)(2,1)S(1)} %get-tuple-element.137), channel_id=1, source_target_pairs={{0,8},{4,12},{8,0},{12,4},{16,24},{20,28},{24,16},{28,20},{1,9},{5... | collective-permute-start | bytes 393224 | tf_op jit(solution)/shard_map/ppermute | solution.py:214
  44.1 7.6 %collective-permute-start.16 = (bf16[512,128]{1,0:T(8,128)(2,1)S(1)}, bf16[512,128]{1,0:T(8,128)(2,1)S(1)}, u32[]{:S(2)}, u32[]{:S(2)}) collective-permute-start(bf16[512,128]{1,0:T(8,128)(2,1)S(1)} %get-tuple-element.138), channel_id=1, source_target_pairs={{0,12},{4,8},{8,4},{12,0},{16,28},{20,24},{24,20},{28,16},{1,13},{... | collective-permute-start | bytes 393224 | tf_op jit(solution)/shard_map/ppermute | solution.py:214
  46.5 10.6 %collective-permute-start.18 = (bf16[512,128]{1,0:T(8,128)(2,1)S(1)}, bf16[512,128]{1,0:T(8,128)(2,1)S(1)}, u32[]{:S(2)}, u32[]{:S(2)}) collective-permute-start(bf16[512,128]{1,0:T(8,128)(2,1)S(1)} %get-tuple-element.151), channel_id=1, source_target_pairs={{0,4},{4,0},{8,12},{12,8},{16,20},{20,16},{24,28},{28,24},{1,5},{5... | collective-permute-start | bytes 393224 | tf_op jit(solution)/shard_map/ppermute | solution.py:214
  47.6 9.5 %collective-permute-start.19 = (bf16[512,128]{1,0:T(8,128)(2,1)S(1)}, bf16[512,128]{1,0:T(8,128)(2,1)S(1)}, u32[]{:S(2)}, u32[]{:S(2)}) collective-permute-start(bf16[512,128]{1,0:T(8,128)(2,1)S(1)} %get-tuple-element.152), channel_id=1, source_target_pairs={{0,8},{4,12},{8,0},{12,4},{16,24},{20,28},{24,16},{28,20},{1,9},{5... | collective-permute-start | bytes 393224 | tf_op jit(solution)/shard_map/ppermute | solution.py:214
  49.6 8.8 %collective-permute-start.20 = (bf16[512,128]{1,0:T(8,128)(2,1)S(1)}, bf16[512,128]{1,0:T(8,128)(2,1)S(1)}, u32[]{:S(2)}, u32[]{:S(2)}) collective-permute-start(bf16[512,128]{1,0:T(8,128)(2,1)S(1)} %get-tuple-element.153), channel_id=1, source_target_pairs={{0,12},{4,8},{8,4},{12,0},{16,28},{20,24},{24,20},{28,16},{1,13},{... | collective-permute-start | bytes 393224 | tf_op jit(solution)/shard_map/ppermute | solution.py:214
  51.8 6.9 %collective-permute-start.17 = (bf16[512,128]{1,0:T(8,128)(2,1)S(1)}, bf16[512,128]{1,0:T(8,128)(2,1)S(1)}, u32[]{:S(2)}, u32[]{:S(2)}) collective-permute-start(bf16[512,128]{1,0:T(8,128)(2,1)S(1)} %shard_map.83), channel_id=1, source_target_pairs={{0,16},{4,20},{8,24},{12,28},{16,0},{20,4},{24,8},{28,12},{1,17},{... | collective-permute-start | bytes 393224 | tf_op jit(solution)/shard_map/ppermute | solution.py:224
  58.5 7.5 %collective-permute-start.21 = (bf16[512,128]{1,0:T(8,128)(2,1)S(1)}, bf16[512,128]{1,0:T(8,128)(2,1)S(1)}, u32[]{:S(2)}, u32[]{:S(2)}) collective-permute-start(bf16[512,128]{1,0:T(8,128)(2,1)S(1)} %shard_map.87), channel_id=1, source_target_pairs={{0,16},{4,20},{8,24},{12,28},{16,0},{20,4},{24,8},{28,12},{1,17},{... | collective-permute-start | bytes 393224 | tf_op jit(solution)/shard_map/ppermute | solution.py:224
  59.0 10.0 %collective-permute-start.25 = (bf16[512,128]{1,0:T(8,128)(2,1)S(1)}, bf16[512,128]{1,0:T(8,128)(2,1)S(1)}, u32[]{:S(2)}, u32[]{:S(2)}) collective-permute-start(bf16[512,128]{1,0:T(8,128)(2,1)S(1)} %get-tuple-element.173), channel_id=1, source_target_pairs={{0,4},{4,0},{8,12},{12,8},{16,20},{20,16},{24,28},{28,24},{1,5},{5... | collective-permute-start | bytes 393224 | tf_op jit(solution)/shard_map/ppermute | solution.py:214
  62.4 10.3 %collective-permute-start.26 = (bf16[512,128]{1,0:T(8,128)(2,1)S(1)}, bf16[512,128]{1,0:T(8,128)(2,1)S(1)}, u32[]{:S(2)}, u32[]{:S(2)}) collective-permute-start(bf16[512,128]{1,0:T(8,128)(2,1)S(1)} %get-tuple-element.174), channel_id=1, source_target_pairs={{0,8},{4,12},{8,0},{12,4},{16,24},{20,28},{24,16},{28,20},{1,9},{5... | collective-permute-start | bytes 393224 | tf_op jit(solution)/shard_map/ppermute | solution.py:214
  65.1 7.6 %collective-permute-start.27 = (bf16[512,128]{1,0:T(8,128)(2,1)S(1)}, bf16[512,128]{1,0:T(8,128)(2,1)S(1)}, u32[]{:S(2)}, u32[]{:S(2)}) collective-permute-start(bf16[512,128]{1,0:T(8,128)(2,1)S(1)} %get-tuple-element.175), channel_id=1, source_target_pairs={{0,12},{4,8},{8,4},{12,0},{16,28},{20,24},{24,20},{28,16},{1,13},{... | collective-permute-start | bytes 393224 | tf_op jit(solution)/shard_map/ppermute | solution.py:214
  66.5 8.2 %collective-permute-start.22 = (bf16[512,128]{1,0:T(8,128)(2,1)S(1)}, bf16[512,128]{1,0:T(8,128)(2,1)S(1)}, u32[]{:S(2)}, u32[]{:S(2)}) collective-permute-start(bf16[512,128]{1,0:T(8,128)(2,1)S(1)} %get-tuple-element.167), channel_id=1, source_target_pairs={{0,4},{4,0},{8,12},{12,8},{16,20},{20,16},{24,28},{28,24},{1,5},{5... | collective-permute-start | bytes 393224 | tf_op jit(solution)/shard_map/ppermute | solution.py:214
  67.1 7.6 %collective-permute-start.23 = (bf16[512,128]{1,0:T(8,128)(2,1)S(1)}, bf16[512,128]{1,0:T(8,128)(2,1)S(1)}, u32[]{:S(2)}, u32[]{:S(2)}) collective-permute-start(bf16[512,128]{1,0:T(8,128)(2,1)S(1)} %get-tuple-element.168), channel_id=1, source_target_pairs={{0,8},{4,12},{8,0},{12,4},{16,24},{20,28},{24,16},{28,20},{1,9},{5... | collective-permute-start | bytes 393224 | tf_op jit(solution)/shard_map/ppermute | solution.py:214
  69.1 5.9 %collective-permute-start.24 = (bf16[512,128]{1,0:T(8,128)(2,1)S(1)}, bf16[512,128]{1,0:T(8,128)(2,1)S(1)}, u32[]{:S(2)}, u32[]{:S(2)}) collective-permute-start(bf16[512,128]{1,0:T(8,128)(2,1)S(1)} %get-tuple-element.169), channel_id=1, source_target_pairs={{0,12},{4,8},{8,4},{12,0},{16,28},{20,24},{24,20},{28,16},{1,13},{... | collective-permute-start | bytes 393224 | tf_op jit(solution)/shard_map/ppermute | solution.py:214
